TPU v7x, 32 devices: a whole 2x2x4 slice. The times are simulated.
32 devices in a mesh: rep: 4 (over x, core), shard: 8 (over z, y).
Axes of the slice: x: 2, y: 2, z: 4, core: 2. Of those that a mesh axis runs over, the one named last changes fastest.
Arguments:
- inputs: bfloat16 [32, 1024, 512], P(('rep', 'shard')), may hold values from -6 to 6
- segments: int32 [32, 1024], P(('rep', 'shard')), may hold values from 0 to 7, never falling along the last dimension, each value on 1 to 512 neighbouring positions
- valid_mask: int32 [32, 1024], P(('rep', 'shard')), may hold values from 0 to 1, as said below
- teacher: bfloat16 [32, 1024, 512], P(('rep', 'shard')), may hold values from -6 to 6
- query_weight: bfloat16 [512, 512], P('shard'), may hold values from -0.5 to 0.5
- key_weight: bfloat16 [512, 512], P('shard'), may hold values from -0.25 to 0.25
- value_weight: bfloat16 [512, 512], P('shard'), may hold values from -0.25 to 0.25
- control_weight: bfloat16 [512, 512], P('shard'), may hold values from -0.75 to 0.75
- output_weight: bfloat16 [512, 512], P('shard'), may hold values from -0.75 to 0.75
- gain_first: bfloat16 [512], P('shard'), may hold values from 0.5 to 1.5
- shift_first: bfloat16 [512], P('shard'), may hold values from -4 to 4
- expand_weight: bfloat16 [512, 2048], P('shard'), may hold values from -0.25 to 0.25
- expand_bias: bfloat16 [2048], P('shard'), may hold values from -4 to 4
- contract_weight: bfloat16 [2048, 512], P('shard'), may hold values from -0.1875 to 0.1875
- contract_bias: bfloat16 [512], P('shard'), may hold values from -4 to 4
- gain_second: bfloat16 [512], P('shard'), may hold values from 0.5 to 1.5
- shift_second: bfloat16 [512], P('shard'), may hold values from -4 to 4
Outputs:
- layer_out: bfloat16 [32, 1024, 512], P(('rep', 'shard'))
- grad_inputs: float32 [32, 1024, 512], P(('rep', 'shard'))
- loss_value: float32 [], replicated
- grad_query_weight: float32 [512, 512], P('shard')
- grad_key_weight: float32 [512, 512], P('shard')
- grad_value_weight: float32 [512, 512], P('shard')
- grad_control_weight: float32 [512, 512], P('shard')
- grad_output_weight: float32 [512, 512], P('shard')
- grad_gain_first: float32 [512], P('shard')
- grad_shift_first: float32 [512], P('shard')
- grad_expand_weight: float32 [512, 2048], P('shard')
- grad_expand_bias: float32 [2048], P('shard')
- grad_contract_weight: float32 [2048, 512], P('shard')
- grad_contract_bias: float32 [512], P('shard')
- grad_gain_second: float32 [512], P('shard')
- grad_shift_second: float32 [512], P('shard')
Inputs may be any that keep to these rules, and one draw needn't show every extreme that they name: `valid_mask`: 1 marks a token that counts toward the loss; the first token of every sequence always counts. `segments`: within each sequence ids start at 0 and never fall; each document has 1 to 512 tokens, and one has exactly 512.
All inputs are finite; a program needn't handle non-finite values.
Results may differ from a plain program's by a relative error of at most 0.017.
Values may be sent and summed in bfloat16 or wider, within the bound.
No kernel may reach another device: no remote copies, remote signals or barrier semaphores. Data moves between devices by JAX's collectives and lax.ppermute only.
A program may use at most 128 MiB of HBM per device.

v0:
```python
from functools import partial

import jax
import jax.numpy as jnp
from jax import lax
from jax.sharding import PartitionSpec as P

HEADS = 8


EPSILON = 1e-05
HIGHEST = lax.Precision.HIGHEST
THREEPASS = lax.Precision.HIGH


def layer_norm(activations, gain, shift):
    row_mean = jnp.mean(activations, axis=-1, keepdims=True)
    centred = activations - row_mean
    variance = jnp.mean(centred * centred, axis=-1, keepdims=True)
    return centred * lax.rsqrt(variance + EPSILON) * gain + shift


def doc_mask(segment_row):
    places = jnp.arange(segment_row.shape[0], dtype=jnp.int32)
    earlier = places[None, :] <= places[:, None]
    same_document = segment_row[:, None] == segment_row[None, :]
    return jnp.where(earlier & same_document, 1.0, 0.0).astype(jnp.bfloat16)


def product(left, right):
    return jnp.dot(left, right, preferred_element_type=jnp.float32)


def head_scores(queries, key_rows):
    return product(queries, key_rows.T) * queries.shape[-1] ** (-0.5)


def slot_rest(causal, scores, value_rows, control):
    weights = jnp.exp(control)
    totals = jnp.dot(causal, weights, precision=THREEPASS, preferred_element_type=jnp.float32)
    slot_scores = jnp.dot(scores * causal, weights, precision=HIGHEST) / totals
    slot_shares = jax.nn.softmax(slot_scores, axis=-1)
    mixing = jnp.dot(slot_shares / totals, weights.T, precision=HIGHEST) * causal
    return jnp.dot(mixing, value_rows, precision=THREEPASS, preferred_element_type=jnp.float32)


def head_forward(causal, head_bundle):
    queries, key_rows, value_rows, control = head_bundle
    return slot_rest(causal, head_scores(queries, key_rows), value_rows, control)


def head_backward(causal, head_bundle):
    queries, key_rows, value_rows, control, grad_mixed = head_bundle
    scores = head_scores(queries, key_rows)
    outcome, pullback = jax.vjp(partial(slot_rest, causal), scores, value_rows, control)
    grad_scores, grad_values, grad_control = pullback(grad_mixed)
    scale = queries.shape[-1] ** (-0.5)
    grad_queries = (
        jnp.dot(grad_scores, key_rows, precision=THREEPASS, preferred_element_type=jnp.float32)
        * scale
    )
    grad_keys = (
        jnp.dot(grad_scores.T, queries, precision=THREEPASS, preferred_element_type=jnp.float32)
        * scale
    )
    return (grad_queries, grad_keys, grad_values.astype(jnp.float32), grad_control)


def mix_forward(bundle):
    queries, key_rows, value_rows, control, segment_row = bundle
    causal = doc_mask(segment_row)
    return lax.map(partial(head_forward, causal), (queries, key_rows, value_rows, control))


def mix_backward(bundle):
    queries, key_rows, value_rows, control, grad_mixed, segment_row = bundle
    causal = doc_mask(segment_row)
    return lax.map(
        partial(head_backward, causal), (queries, key_rows, value_rows, control, grad_mixed)
    )


def split_heads(matrix, sequence_count):
    return matrix.reshape(sequence_count, -1, HEADS, matrix.shape[1] // HEADS).transpose(0, 2, 1, 3)


def merge_heads(stacked):
    sequence_count, head_count, length, head_width = stacked.shape
    return stacked.transpose(0, 2, 1, 3).reshape(sequence_count * length, head_count * head_width)


def local(
    inputs,
    segments,
    valid_mask,
    teacher,
    query_weight,
    key_weight,
    value_weight,
    control_weight,
    output_weight,
    gain_first,
    shift_first,
    expand_weight,
    expand_bias,
    contract_weight,
    contract_bias,
    gain_second,
    shift_second,
):
    sequence_count, length, width = inputs.shape
    total_rows = sequence_count * length
    valid_rows = valid_mask.reshape(total_rows, 1).astype(jnp.float32)
    local_count = jnp.sum(valid_rows)
    count_all = lax.psum(local_count, ("rep", "shard"))
    mixer_set = (
        lax.all_gather(query_weight, "shard", axis=0, tiled=True),
        lax.all_gather(key_weight, "shard", axis=0, tiled=True),
        lax.all_gather(value_weight, "shard", axis=0, tiled=True),
        lax.all_gather(control_weight, "shard", axis=0, tiled=True),
        lax.all_gather(output_weight, "shard", axis=0, tiled=True),
        lax.all_gather(gain_first, "shard", axis=0, tiled=True),
        lax.all_gather(shift_first, "shard", axis=0, tiled=True),
    )
    query_full, key_full, value_full, control_full, out_full, gain_one, shift_one = mixer_set
    layer_in = inputs.reshape(total_rows, width).astype(jnp.float32)
    normed_one, first_back = jax.vjp(
        layer_norm, layer_in, gain_one.astype(jnp.float32), shift_one.astype(jnp.float32)
    )
    normed_one = normed_one.astype(jnp.bfloat16)
    queries = product(normed_one, query_full).astype(jnp.bfloat16)
    key_rows = product(normed_one, key_full).astype(jnp.bfloat16)
    value_rows = product(normed_one, value_full).astype(jnp.bfloat16)
    control = product(normed_one, control_full)
    head_queries = split_heads(queries, sequence_count)
    head_keys = split_heads(key_rows, sequence_count)
    head_values = split_heads(value_rows, sequence_count)
    head_control = split_heads(control, sequence_count)
    mixed = lax.map(mix_forward, (head_queries, head_keys, head_values, head_control, segments))
    mixed_low = merge_heads(mixed).astype(jnp.bfloat16)
    hidden_one = layer_in + product(mixed_low, out_full)
    branch_set = (
        lax.all_gather(expand_weight, "shard", axis=0, tiled=True),
        lax.all_gather(expand_bias, "shard", axis=0, tiled=True),
        lax.all_gather(contract_weight, "shard", axis=0, tiled=True),
        lax.all_gather(contract_bias, "shard", axis=0, tiled=True),
        lax.all_gather(gain_second, "shard", axis=0, tiled=True),
        lax.all_gather(shift_second, "shard", axis=0, tiled=True),
    )
    expand_full, expand_shift, contract_full, contract_shift, gain_two, shift_two = branch_set
    normed_two, second_back = jax.vjp(
        layer_norm, hidden_one, gain_two.astype(jnp.float32), shift_two.astype(jnp.float32)
    )
    normed_two = normed_two.astype(jnp.bfloat16)
    before_relu = product(normed_two, expand_full) + expand_shift.astype(jnp.float32)
    after_relu = jnp.maximum(before_relu, 0.0).astype(jnp.bfloat16)
    result = hidden_one + (product(after_relu, contract_full) + contract_shift.astype(jnp.float32))
    layer_out = result.astype(jnp.bfloat16).reshape(sequence_count, length, width)
    error = result - teacher.reshape(total_rows, width).astype(jnp.float32)
    local_loss = jnp.sum(valid_rows * error * error)
    loss_all = lax.psum(local_loss, ("rep", "shard"))
    loss_value = loss_all / (2.0 * count_all)
    total_tokens = total_rows * lax.axis_size("rep") * lax.axis_size("shard")
    grad_result = total_tokens / count_all * valid_rows * error
    branch_set = (
        lax.all_gather(expand_weight, "shard", axis=0, tiled=True),
        lax.all_gather(expand_bias, "shard", axis=0, tiled=True),
        lax.all_gather(contract_weight, "shard", axis=0, tiled=True),
        lax.all_gather(contract_bias, "shard", axis=0, tiled=True),
        lax.all_gather(gain_second, "shard", axis=0, tiled=True),
        lax.all_gather(shift_second, "shard", axis=0, tiled=True),
    )
    expand_full, expand_shift, contract_full, contract_shift, gain_two, shift_two = branch_set
    grad_second_low = grad_result.astype(jnp.bfloat16)
    grad_contract = product(after_relu.T, grad_second_low)
    grad_contract_shift = jnp.sum(grad_second_low.astype(jnp.float32), axis=0)
    grad_after = product(grad_second_low, contract_full.T)
    grad_before = jnp.where(before_relu > 0, grad_after, 0.0).astype(jnp.bfloat16)
    grad_expand = product(normed_two.T, grad_before)
    grad_expand_shift = jnp.sum(grad_before.astype(jnp.float32), axis=0)
    grad_normed_two = product(grad_before, expand_full.T)
    grad_hidden_part, grad_gain_two, grad_shift_two = second_back(grad_normed_two)
    grad_hidden = grad_result + grad_hidden_part
    mixer_set = (
        lax.all_gather(query_weight, "shard", axis=0, tiled=True),
        lax.all_gather(key_weight, "shard", axis=0, tiled=True),
        lax.all_gather(value_weight, "shard", axis=0, tiled=True),
        lax.all_gather(control_weight, "shard", axis=0, tiled=True),
        lax.all_gather(output_weight, "shard", axis=0, tiled=True),
        lax.all_gather(gain_first, "shard", axis=0, tiled=True),
        lax.all_gather(shift_first, "shard", axis=0, tiled=True),
    )
    query_full, key_full, value_full, control_full, out_full, gain_one, shift_one = mixer_set
    grad_mixer_low = grad_hidden.astype(jnp.bfloat16)
    grad_output = product(mixed_low.T, grad_mixer_low)
    grad_mixed = product(grad_mixer_low, out_full.T)
    head_grads = lax.map(
        mix_backward,
        (
            head_queries,
            head_keys,
            head_values,
            head_control,
            split_heads(grad_mixed, sequence_count),
            segments,
        ),
    )
    grad_queries = merge_heads(head_grads[0]).astype(jnp.bfloat16)
    grad_key_rows = merge_heads(head_grads[1]).astype(jnp.bfloat16)
    grad_value_rows = merge_heads(head_grads[2]).astype(jnp.bfloat16)
    grad_control = merge_heads(head_grads[3]).astype(jnp.bfloat16)
    grad_query = product(normed_one.T, grad_queries)
    grad_key = product(normed_one.T, grad_key_rows)
    grad_value = product(normed_one.T, grad_value_rows)
    grad_control_full = product(normed_one.T, grad_control)
    grad_normed_one = (
        product(grad_queries, query_full.T)
        + product(grad_key_rows, key_full.T)
        + product(grad_value_rows, value_full.T)
        + product(grad_control, control_full.T)
    )
    grad_layer_in, grad_gain_one, grad_shift_one = first_back(grad_normed_one)
    grad_inputs = (grad_hidden + grad_layer_in).reshape(sequence_count, length, width)
    branch_parts = (
        lax.psum_scatter(
            grad_expand.astype(jnp.bfloat16), "shard", scatter_dimension=0, tiled=True
        ).astype(jnp.float32),
        lax.psum_scatter(
            grad_expand_shift.astype(jnp.bfloat16), "shard", scatter_dimension=0, tiled=True
        ).astype(jnp.float32),
        lax.psum_scatter(
            grad_contract.astype(jnp.bfloat16), "shard", scatter_dimension=0, tiled=True
        ).astype(jnp.float32),
        lax.psum_scatter(
            grad_contract_shift.astype(jnp.bfloat16), "shard", scatter_dimension=0, tiled=True
        ).astype(jnp.float32),
        lax.psum_scatter(
            grad_gain_two.astype(jnp.bfloat16), "shard", scatter_dimension=0, tiled=True
        ).astype(jnp.float32),
        lax.psum_scatter(
            grad_shift_two.astype(jnp.bfloat16), "shard", scatter_dimension=0, tiled=True
        ).astype(jnp.float32),
    )
    mixer_parts = (
        lax.psum_scatter(
            grad_query.astype(jnp.bfloat16), "shard", scatter_dimension=0, tiled=True
        ).astype(jnp.float32),
        lax.psum_scatter(
            grad_key.astype(jnp.bfloat16), "shard", scatter_dimension=0, tiled=True
        ).astype(jnp.float32),
        lax.psum_scatter(
            grad_value.astype(jnp.bfloat16), "shard", scatter_dimension=0, tiled=True
        ).astype(jnp.float32),
        lax.psum_scatter(
            grad_control_full.astype(jnp.bfloat16), "shard", scatter_dimension=0, tiled=True
        ).astype(jnp.float32),
        lax.psum_scatter(
            grad_output.astype(jnp.bfloat16), "shard", scatter_dimension=0, tiled=True
        ).astype(jnp.float32),
        lax.psum_scatter(
            grad_gain_one.astype(jnp.bfloat16), "shard", scatter_dimension=0, tiled=True
        ).astype(jnp.float32),
        lax.psum_scatter(
            grad_shift_one.astype(jnp.bfloat16), "shard", scatter_dimension=0, tiled=True
        ).astype(jnp.float32),
    )
    (
        part_expand,
        part_expand_shift,
        part_contract,
        part_contract_shift,
        part_gain_two,
        part_shift_two,
    ) = branch_parts
    part_query, part_key, part_value, part_control, part_output, part_gain_one, part_shift_one = (
        mixer_parts
    )
    summed = (
        lax.psum(part_query.astype(jnp.bfloat16), "rep").astype(jnp.float32),
        lax.psum(part_key.astype(jnp.bfloat16), "rep").astype(jnp.float32),
        lax.psum(part_value.astype(jnp.bfloat16), "rep").astype(jnp.float32),
        lax.psum(part_control.astype(jnp.bfloat16), "rep").astype(jnp.float32),
        lax.psum(part_output.astype(jnp.bfloat16), "rep").astype(jnp.float32),
        lax.psum(part_gain_one.astype(jnp.bfloat16), "rep").astype(jnp.float32),
        lax.psum(part_shift_one.astype(jnp.bfloat16), "rep").astype(jnp.float32),
        lax.psum(part_expand.astype(jnp.bfloat16), "rep").astype(jnp.float32),
        lax.psum(part_expand_shift.astype(jnp.bfloat16), "rep").astype(jnp.float32),
        lax.psum(part_contract.astype(jnp.bfloat16), "rep").astype(jnp.float32),
        lax.psum(part_contract_shift.astype(jnp.bfloat16), "rep").astype(jnp.float32),
        lax.psum(part_gain_two.astype(jnp.bfloat16), "rep").astype(jnp.float32),
        lax.psum(part_shift_two.astype(jnp.bfloat16), "rep").astype(jnp.float32),
    )
    return (
        layer_out,
        grad_inputs,
        loss_value,
        summed[0],
        summed[1],
        summed[2],
        summed[3],
        summed[4],
        summed[5],
        summed[6],
        summed[7],
        summed[8],
        summed[9],
        summed[10],
        summed[11],
        summed[12],
    )


def solution(mesh):
    in_specs = (
        P(("rep", "shard"), None, None),
        P(("rep", "shard"), None),
        P(("rep", "shard"), None),
        P(("rep", "shard"), None, None),
        P("shard", None),
        P("shard", None),
        P("shard", None),
        P("shard", None),
        P("shard", None),
        P("shard"),
        P("shard"),
        P("shard", None),
        P("shard"),
        P("shard", None),
        P("shard"),
        P("shard"),
        P("shard"),
    )
    out_specs = (
        P(("rep", "shard"), None, None),
        P(("rep", "shard"), None, None),
        P(),
        P("shard", None),
        P("shard", None),
        P("shard", None),
        P("shard", None),
        P("shard", None),
        P("shard"),
        P("shard"),
        P("shard", None),
        P("shard"),
        P("shard", None),
        P("shard"),
        P("shard"),
        P("shard"),
    )
    return jax.shard_map(local, mesh=mesh, in_specs=in_specs, out_specs=out_specs, check_vma=False)
```

profile of v0, /device:TPU:13, one launch (start us, length us, event | category | flops | bytes accessed | tf_op | source)
XLA Modules:
  0.0 1277.0 jit_solution(18241503229063410139)
XLA Ops:
  15.0 13.0 %all-reduce.13 = (bf16[512]{0:T(512)(128)(2,1)S(1)}, bf16[512]{0:T(512)(128)(2,1)S(1)}, bf16[512]{0:T(512)(128)(2,1)S(1)}, bf16[512]{0:T(512)(128)(2,1)S(1)}, bf16[512]{0:T(512)(128)(2,1)S(1)}) all-reduce(bf16[512]{0:T(512)(128)(2,1)S(1)} %dynamic-update-slice.1, ...), channel_id=1, replica_groups=mesh['rep'=4,'shard'=8] {'shard'}, use_global_device_ids=true, to_apply=%add.1 | all-reduce | flops 2560 | bytes 10240
  28.0 28.5 %all_gather.48 = bf16[512,512]{1,0:T(8,128)(2,1)S(1)} all-gather(bf16[64,512]{1,0:T(8,128)(2,1)} %param.25), channel_id=1, replica_groups=mesh['rep'=4,'shard'=8] {'shard'}, dimensions={0}, use_global_device_ids=true | all-gather | bytes 589824 | tf_op jit(solution)/shard_map/all_gather | solution.py:117
  56.5 25.5 %all_gather.49 = bf16[512,512]{1,0:T(8,128)(2,1)S(1)} all-gather(bf16[64,512]{1,0:T(8,128)(2,1)} %param.26), channel_id=1, replica_groups=mesh['rep'=4,'shard'=8] {'shard'}, dimensions={0}, use_global_device_ids=true | all-gather | bytes 589824 | tf_op jit(solution)/shard_map/all_gather | solution.py:118
  82.0 28.5 %all_gather.51 = bf16[512,512]{1,0:T(8,128)(2,1)S(1)} all-gather(bf16[64,512]{1,0:T(8,128)(2,1)} %param.27), channel_id=1, replica_groups=mesh['rep'=4,'shard'=8] {'shard'}, dimensions={0}, use_global_device_ids=true | all-gather | bytes 589824 | tf_op jit(solution)/shard_map/all_gather | solution.py:119
  110.6 24.9 %all_gather.50 = bf16[512,512]{1,0:T(8,128)(2,1)S(1)} all-gather(bf16[64,512]{1,0:T(8,128)(2,1)S(1)} %copy-done.27), channel_id=1, replica_groups=mesh['rep'=4,'shard'=8] {'shard'}, dimensions={0}, use_global_device_ids=true | all-gather | bytes 589824 | tf_op jit(solution)/shard_map/all_gather | solution.py:120
  153.3 126.4 %while.48 = (s32[]{:T(128)}, bf16[8,1024,64]{1,2,0:T(8,128)(2,1)S(1)}, bf16[8,1024,64]{2,1,0:T(8,128)(2,1)}, bf16[8,1024,64]{2,1,0:T(8,128)(2,1)}, f32[8,1024,64...) while((s32[]{:T(128)}, bf16[8,1024,64]{1,2,0:T(8,128)(2,1)S(1)}, ...), condition=%wide.region_5.6_spmd.clone, body=%wide.region_2.5_spmd.clone.sunk | while | flops 2571565056 | bytes 21272672 | solution.py:72
  158.2 4.9 fusion.317
  174.0 4.9 fusion.317
  189.7 4.9 fusion.317
  205.4 4.9 fusion.317
  221.2 4.9 fusion.317
  236.9 4.9 fusion.317
  252.7 4.9 fusion.317
  268.4 4.9 fusion.317
  279.8 16.2 %all-gather = bf16[8,1,256]{2,1,0:T(2,128)(2,1)S(1)} all-gather(bf16[1,1,256]{2,1,0:T(2,128)(2,1)S(1)} %reshape.342), channel_id=1, replica_groups=mesh['rep'=4,'shard'=8] {'shard'}, dimensions={0}, use_global_device_ids=true | all-gather | bytes 4608 | tf_op jit(solution)/shard_map/all_gather | solution.py:144
  298.8 22.6 %all_gather.52 = bf16[512,512]{1,0:T(8,128)(2,1)S(1)} all-gather(bf16[64,512]{1,0:T(8,128)(2,1)S(1)} %copy-done.28), channel_id=1, replica_groups=mesh['rep'=4,'shard'=8] {'shard'}, dimensions={0}, use_global_device_ids=true | all-gather | bytes 589824 | tf_op jit(solution)/shard_map/all_gather | solution.py:121
  324.0 7.4 fusion.220
  331.4 8.4 fusion.205
  339.9 79.4 %all-reduce.11 = (f32[]{:T(128)}, f32[]{:T(128)}) all-reduce(f32[]{:T(128)} %convert_reduce_fusion.1, f32[]{:T(128)} %get-tuple-element.343), channel_id=1, replica_groups=mesh['rep'=4,'shard'=8] {'rep','shard'}, use_global_device_ids=true, to_apply=%region_9.10 | all-reduce | flops 2 | bytes 16 | tf_op jit(solution)/shard_map/psum | solution.py:115
  422.6 6.9 fusion.235
  458.0 363.5 %while.49 = (s32[]{:T(128)}, bf16[8,1024,64]{1,2,0:T(8,128)(2,1)}, bf16[8,1024,64]{1,2,0:T(8,128)(2,1)}, bf16[8,1024,64]{1,2,0:T(8,128)(2,1)}, bf16[8,1024,64]{1...) while((s32[]{:T(128)}, bf16[8,1024,64]{1,2,0:T(8,128)(2,1)}, ...), condition=%wide.region_16.17_spmd.clone, body=%wide.region_12.16_spmd.clone.sunk | while | flops 7448756224 | bytes 66475184 | solution.py:78
  525.6 4.8 fusion.336
  833.1 7.4 convolution_convert_fusion
  841.1 6.0 convolution_convert_fusion.1
  856.7 27.7 %reduce-scatter.8.cloned.1.call-done = bf16[64,512]{1,0:T(8,128)(2,1)} async-done(((bf16[512,512]{1,0:T(8,128)(2,1)}), bf16[64,512]{1,0:T(8,128)(2,1)}) %reduce-scatter.8.cloned.1.call-update) | async-done | bytes 65552 | tf_op jit(solution)/shard_map/reduce_scatter | solution.py:245
  884.4 64.1 %reduce-scatter.14.cloned.1.call-done = bf16[64,512]{1,0:T(8,128)(2,1)} async-done(((bf16[512,512]{1,0:T(8,128)(2,1)}), bf16[64,512]{1,0:T(8,128)(2,1)}) %reduce-scatter.14.cloned.1.call-update) | async-done | bytes 65552 | tf_op jit(solution)/shard_map/reduce_scatter | solution.py:254
  948.5 64.6 %reduce-scatter.10.cloned.1.call-done = bf16[64,512]{1,0:T(8,128)(2,1)} async-done(((bf16[512,512]{1,0:T(8,128)(2,1)}), bf16[64,512]{1,0:T(8,128)(2,1)}) %reduce-scatter.10.cloned.1.call-update) | async-done | bytes 65552 | tf_op jit(solution)/shard_map/reduce_scatter | solution.py:248
  1013.1 64.3 %reduce-scatter.12.cloned.1.call-done = bf16[64,512]{1,0:T(8,128)(2,1)} async-done(((bf16[512,512]{1,0:T(8,128)(2,1)}), bf16[64,512]{1,0:T(8,128)(2,1)}) %reduce-scatter.12.cloned.1.call-update) | async-done | bytes 65552 | tf_op jit(solution)/shard_map/reduce_scatter | solution.py:251
  1077.4 70.7 %reduce-scatter.20.cloned.1.call-done = bf16[256,512]{1,0:T(8,128)(2,1)} async-done(((bf16[2048,512]{1,0:T(8,128)(2,1)}), bf16[256,512]{1,0:T(8,128)(2,1)}) %reduce-scatter.20.cloned.1.call-update) | async-done | bytes 262160 | tf_op jit(solution)/shard_map/reduce_scatter | solution.py:231
  1148.1 70.8 %reduce-scatter.18.cloned.1.call-done = bf16[64,2048]{1,0:T(8,128)(2,1)} async-done(((bf16[512,2048]{1,0:T(8,128)(2,1)}), bf16[64,2048]{1,0:T(8,128)(2,1)}) %reduce-scatter.18.cloned.1.call-update) | async-done | bytes 262160 | tf_op jit(solution)/shard_map/reduce_scatter | solution.py:225
  1221.9 12.3 all-reduce.12
  1234.6 10.9 all-reduce.14
  (415 shorter events, 522.0 us)
Async XLA Ops:
  7.2 103.4 %copy-start.27 = (bf16[64,512]{1,0:T(8,128)(2,1)S(1)}, bf16[64,512]{1,0:T(8,128)(2,1)}, u32[]{:S(2)}) copy-start(bf16[64,512]{1,0:T(8,128)(2,1)} %param.28) | copy-start | bytes 196612
  7.2 316.8 %all-gather.4.cloned.1.call-start = ((), (), s32[]{:S(2)}) async-start(), calls=%async_computation.7 | async-start | bytes 2359296 | tf_op jit(solution)/shard_map/all_gather | solution.py:143
  7.9 323.5 %all-gather.6.cloned.1.call-start = ((), (), s32[]{:S(2)}) async-start(), calls=%async_computation.8 | async-start | bytes 2359296 | tf_op jit(solution)/shard_map/all_gather | solution.py:145
  8.7 848.0 %reduce-scatter.16.cloned.1.call-start = ((), (), s32[]{:S(2)}) async-start(), calls=%async_computation.13 | async-start | bytes 589824 | tf_op jit(solution)/shard_map/reduce_scatter | solution.py:257
  28.0 122.9 %copy-start.39 = (f32[512]{0:T(512)}, f32[512]{0:T(512)S(1)}, u32[]{:S(2)}) copy-start(f32[512]{0:T(512)S(1)} %convert_element_type.286) | copy-start | bytes 6148
  28.0 122.9 %copy-start.33 = (f32[512]{0:T(512)}, f32[512]{0:T(512)S(1)}, u32[]{:S(2)}) copy-start(f32[512]{0:T(512)S(1)} %convert_element_type.285) | copy-start | bytes 6148
  56.5 91.7 %copy-start.23 = (bf16[512,512]{1,0:T(8,128)(2,1)}, bf16[512,512]{1,0:T(8,128)(2,1)S(1)}, u32[]{:S(2)}) copy-start(bf16[512,512]{1,0:T(8,128)(2,1)S(1)} %all_gather.48) | copy-start | bytes 1572868
  82.0 57.1 %copy-start.19 = (bf16[512,512]{1,0:T(8,128)(2,1)}, bf16[512,512]{1,0:T(8,128)(2,1)S(1)}, u32[]{:S(2)}) copy-start(bf16[512,512]{1,0:T(8,128)(2,1)S(1)} %all_gather.49) | copy-start | bytes 1572868
  110.6 33.1 %copy-start.21 = (bf16[512,512]{1,0:T(8,128)(2,1)}, bf16[512,512]{1,0:T(8,128)(2,1)S(1)}, u32[]{:S(2)}) copy-start(bf16[512,512]{1,0:T(8,128)(2,1)S(1)} %all_gather.51) | copy-start | bytes 1572868
  138.0 183.5 %copy-start = (bf16[1,1024,512]{1,2,0:T(8,128)(2,1)}, bf16[1,1024,512]{1,2,0:T(8,128)(2,1)S(1)}, u32[]{:S(2)}) copy-start(bf16[1,1024,512]{1,2,0:T(8,128)(2,1)S(1)} %copy.51) | copy-start | bytes 3145732
  153.2 126.4 %copy-start.47 = (bf16[256]{0:T(256)(128)(2,1)S(1)}, bf16[256]{0:T(256)(128)(2,1)}, u32[]{:S(2)}) copy-start(bf16[256]{0:T(256)(128)(2,1)} %param.33) | copy-start | bytes 1540
  153.3 126.5 %copy-start.35 = (s32[1,1024]{1,0:T(1,128)S(1)}, s32[1,1024]{1,0:T(1,128)}, u32[]{:S(2)}) copy-start(s32[1,1024]{1,0:T(1,128)} %param.23) | copy-start | bytes 12292
  279.7 41.8 %copy-start.6 = (bf16[8,1024,64]{1,2,0:T(8,128)(2,1)}, bf16[8,1024,64]{1,2,0:T(8,128)(2,1)S(1)}, u32[]{:S(2)}) copy-start(bf16[8,1024,64]{1,2,0:T(8,128)(2,1)S(1)} %get-tuple-element.167) | copy-start | bytes 3145732
  279.7 19.2 %copy-start.28 = (bf16[64,512]{1,0:T(8,128)(2,1)S(1)}, bf16[64,512]{1,0:T(8,128)(2,1)}, u32[]{:S(2)}) copy-start(bf16[64,512]{1,0:T(8,128)(2,1)} %param.29) | copy-start | bytes 196612
  279.7 44.3 %copy-start.41 = (f32[512]{0:T(512)}, f32[512]{0:T(512)S(1)}, u32[]{:S(2)}) copy-start(f32[512]{0:T(512)S(1)} %convert_element_type.298) | copy-start | bytes 6148
  449.6 434.7 %reduce-scatter.8.cloned.1.call-start = ((), (), s32[]{:S(2)}) async-start(), calls=%async_computation.9 | async-start | bytes 589824 | tf_op jit(solution)/shard_map/reduce_scatter | solution.py:245
  457.9 363.6 %copy-start.1 = (bf16[1,1024,512]{1,2,0:T(8,128)(2,1)S(1)}, bf16[1,1024,512]{1,2,0:T(8,128)(2,1)}, u32[]{:S(2)}) copy-start(bf16[1,1024,512]{1,2,0:T(8,128)(2,1)} %copy-done) | copy-start | bytes 3145732
  457.9 363.6 %copy-start.26 = (f32[1024]{0:T(1024)S(1)}, f32[1024]{0:T(1024)}, u32[]{:S(2)}) copy-start(f32[1024]{0:T(1024)} %copy-done.25) | copy-start | bytes 12292
  457.9 363.6 %copy-start.30 = (f32[1024]{0:T(1024)S(1)}, f32[1024]{0:T(1024)}, u32[]{:S(2)}) copy-start(f32[1024]{0:T(1024)} %copy-done.29) | copy-start | bytes 12292
  457.9 363.6 %copy-start.34 = (f32[512]{0:T(512)S(1)}, f32[512]{0:T(512)}, u32[]{:S(2)}) copy-start(f32[512]{0:T(512)} %copy-done.33) | copy-start | bytes 6148
  458.0 363.6 %copy-start.40 = (f32[512]{0:T(512)S(1)}, f32[512]{0:T(512)}, u32[]{:S(2)}) copy-start(f32[512]{0:T(512)} %copy-done.39) | copy-start | bytes 6148
  824.4 124.2 %reduce-scatter.14.cloned.1.call-start = ((), (), s32[]{:S(2)}) async-start(), calls=%async_computation.12 | async-start | bytes 589824 | tf_op jit(solution)/shard_map/reduce_scatter | solution.py:254
  827.3 185.8 %reduce-scatter.10.cloned.1.call-start = ((), (), s32[]{:S(2)}) async-start(), calls=%async_computation.10 | async-start | bytes 589824 | tf_op jit(solution)/shard_map/reduce_scatter | solution.py:248
  830.2 247.2 %reduce-scatter.12.cloned.1.call-start = ((), (), s32[]{:S(2)}) async-start(), calls=%async_computation.11 | async-start | bytes 589824 | tf_op jit(solution)/shard_map/reduce_scatter | solution.py:251
  833.0 315.0 %reduce-scatter.20.cloned.1.call-start = ((), (), s32[]{:S(2)}) async-start(), calls=%async_computation.15 | async-start | bytes 2359296 | tf_op jit(solution)/shard_map/reduce_scatter | solution.py:231
  840.5 378.4 %reduce-scatter.18.cloned.1.call-start = ((), (), s32[]{:S(2)}) async-start(), calls=%async_computation.14 | async-start | bytes 2359296 | tf_op jit(solution)/shard_map/reduce_scatter | solution.py:225
  847.1 410.6 %all-reduce.18.cloned.1.call-start = ((), (), s32[]{:S(2)}) async-start(), calls=%async_computation.16 | async-start | bytes 1703936 | tf_op jit(solution)/shard_map/psum | solution.py:279
  856.6 365.2 %copy-start.36 = (bf16[512]{0:T(512)(128)(2,1)S(1)}, bf16[512]{0:T(512)(128)(2,1)}, u32[]{:S(2)}) copy-start(bf16[512]{0:T(512)(128)(2,1)} %get-tuple-element.260) | copy-start | bytes 3076
  856.6 365.2 %copy-start.37 = (bf16[2048]{0:T(1024)(128)(2,1)S(1)}, bf16[2048]{0:T(1024)(128)(2,1)}, u32[]{:S(2)}) copy-start(bf16[2048]{0:T(1024)(128)(2,1)} %get-tuple-element.346) | copy-start | bytes 12292
  856.6 365.2 %copy-start.38 = (bf16[512]{0:T(512)(128)(2,1)S(1)}, bf16[512]{0:T(512)(128)(2,1)}, u32[]{:S(2)}) copy-start(bf16[512]{0:T(512)(128)(2,1)} %get-tuple-element.330) | copy-start | bytes 3076
  856.6 365.2 %copy-start.43 = (bf16[512]{0:T(512)(128)(2,1)S(1)}, bf16[512]{0:T(512)(128)(2,1)}, u32[]{:S(2)}) copy-start(bf16[512]{0:T(512)(128)(2,1)} %get-tuple-element.348) | copy-start | bytes 3076
  856.7 392.0 %copy-start.3 = (f32[1024,512]{0,1:T(8,128)S(1)}, f32[1024,512]{0,1:T(8,128)}, u32[]{:S(2)}) copy-start(f32[1024,512]{0,1:T(8,128)} %copy-done.2) | copy-start | bytes 6291460
  (34 other events, 99.1 us)
Sparse Core Ops, SparseCore 0:
  10.1 57.0 all-gather.3
  69.3 55.4 all-gather.5
  449.8 59.8 reduce-scatter.15
  824.5 59.8 reduce-scatter.7
  887.6 60.8 reduce-scatter.13
  952.1 60.9 reduce-scatter.9
  1016.4 60.9 reduce-scatter.11
  1081.3 66.7 reduce-scatter.19
  1152.0 66.7 reduce-scatter.17
  1221.8 35.8 all-reduce.17
where the time goes:
time: 1290 us; the launch traced here: 1280 us
  matrix products  519 us (40%)
  waiting for transfers between devices  366 us (28%)
  blocking collectives  262 us (20%)
  local copies, waits for them, and re-layouts  49.7 us (4%)
  other arithmetic  30.4 us (2%)
  loops' own time  30.1 us (2%)
  between operations  20.2 us (2%)
    dot_general x32, matrix products, slot_rest(): slot_scores = jnp.dot(scores * causal, weights, precision=HIGHEST) / totals  134 us
    dot_general x32, matrix products, slot_rest(): jnp.dot(slot_shares / totals, weights.T, precision=HIGHEST) * causal  127 us
    dot_general x37, matrix products, product(): return jnp.dot(left, right, preferred_element_type=jnp.float32)  99.4 us
    psum x1, blocking collectives, local(): count_all = lax.psum(local_count, ('rep', 'shard'))  79.4 us
    reduce_scatter x1, waiting for transfers between devices, local(): lax.psum_scatter(grad_expand.astype(jnp.bfloat16), 'shard', scatter_dimen...  70.8 us
    reduce_scatter x1, waiting for transfers between devices, local(): lax.psum_scatter(grad_contract.astype(jnp.bfloat16), 'shard', scatter_dim...  70.7 us
    dot_general x24, matrix products, slot_rest(): jnp.dot(mixing, value_rows, precision=THREEPASS, preferred_element_type=j...  69.2 us
    reduce_scatter x1, waiting for transfers between devices, local(): lax.psum_scatter(grad_key.astype(jnp.bfloat16), 'shard', scatter_dimensio...  64.6 us
  transfers between devices with their start and end apart: 10, of which 7 were waited for; matrix products, arithmetic and copies ran while one was open for 43% of the time, Pallas kernels for 0%

commit v1 on v0

v1 whole, which is shorter than its diff:
```python
import functools

import jax
import jax.numpy as jnp
from jax import lax
from jax.experimental import pallas as pl
from jax.experimental.pallas import tpu as pltpu
from jax.sharding import PartitionSpec as P

HEADS = 8
EPSILON = 1e-05
CHUNK = 256
QUAD = 256
F32 = jnp.float32
BF16 = jnp.bfloat16
VMEM_LIMIT = 60 << 20


def nn(left, right):
    return jnp.dot(left, right, preferred_element_type=F32)


def nt(left, right):
    return lax.dot_general(left, right, (((1,), (1,)), ((), ())), preferred_element_type=F32)


def tn(left, right):
    return lax.dot_general(left, right, (((0,), (0,)), ((), ())), preferred_element_type=F32)


def head_lanes():
    lane = lax.broadcasted_iota(jnp.int32, (1, QUAD), 1) // 64
    return [jnp.where(lane == h, 1.0, 0.0).astype(BF16) for h in range(4)]


def block_diagonal():
    rows = lax.broadcasted_iota(jnp.int32, (QUAD, QUAD), 0) // 64
    columns = lax.broadcasted_iota(jnp.int32, (QUAD, QUAD), 1) // 64
    return jnp.where(rows == columns, 1.0, 0.0)


def as_column(row):
    return jnp.broadcast_to(row, (CHUNK, CHUNK)).T


def causal_mask(column, row):
    at = lax.broadcasted_iota(jnp.int32, (CHUNK, CHUNK), 0)
    source = lax.broadcasted_iota(jnp.int32, (CHUNK, CHUNK), 1)
    return jnp.where((column == row) & (source <= at), 1.0, 0.0)


def causal_mask_transposed(column, row):
    source = lax.broadcasted_iota(jnp.int32, (CHUNK, CHUNK), 0)
    at = lax.broadcasted_iota(jnp.int32, (CHUNK, CHUNK), 1)
    return jnp.where((column == row) & (source <= at), 1.0, 0.0)


def per_head(values, reduce, fill):
    lane = lax.broadcasted_iota(jnp.int32, (1, 128), 1)
    first = lane < 64
    tiles = []
    for tile in range(values.shape[1] // 128):
        part = values[:, tile * 128 : (tile + 1) * 128]
        one = reduce(jnp.where(first, part, fill), axis=-1, keepdims=True)
        two = reduce(jnp.where(first, fill, part), axis=-1, keepdims=True)
        tiles.append(jnp.where(first, one, two))
    return jnp.concatenate(tiles, axis=1)


def standardise(values):
    mean = jnp.mean(values, axis=-1, keepdims=True)
    centred = values - mean
    variance = jnp.mean(centred * centred, axis=-1, keepdims=True)
    scale = lax.rsqrt(variance + EPSILON)
    return centred * scale, scale


def norm_backward(gradient, gain, normal, scale):
    upstream = gradient * gain
    one = jnp.mean(upstream, axis=-1, keepdims=True)
    two = jnp.mean(upstream * normal, axis=-1, keepdims=True)
    return (upstream - one - normal * two) * scale


def spread(rows, shards):
    width = 512 // shards
    lane = lax.broadcasted_iota(jnp.int32, (8, 128), 1)
    tiles = [None] * 4
    for s in range(shards):
        tile, offset = divmod(s * width, 128)
        moved = pltpu.roll(rows[s], offset, 1) if offset else rows[s]
        inside = (lane >= offset) & (lane < offset + width)
        tiles[tile] = jnp.where(inside, moved, 0.0 if tiles[tile] is None else tiles[tile])
    return jnp.concatenate(tiles, axis=1)


def piece_of(vectors, s, width):
    tile, offset = divmod(s * width, 128)
    part = vectors[:, tile * 128 : (tile + 1) * 128]
    return pltpu.roll(part, 128 - offset, 1) if offset else part


def attention_forward(
    shards,
    seg_s,
    pos_s,
    x_ref,
    seg_ref,
    mine_ref,
    theirs_ref,
    q_ref,
    k_ref,
    v_ref,
    e_ref,
    p_ref,
    s_ref,
    rz_ref,
    mix_ref,
    one_ref,
    two_ref,
    w_ref,
    vec_ref,
    eb_ref,
    count_ref,
    held,
    first_state,
    second_state,
    total_state,
    sems,
):
    step = pl.program_id(0)
    nb = 512 // shards // 16
    mine, core = pos_s[0], pos_s[1]

    @pl.when(step == 0)
    def _():
        for half, source in enumerate((mine_ref, theirs_ref)):
            column = pl.multiple_of(((core + half) % 2) * 256, 256)
            for j in range(shards):
                owner = mine ^ j
                for m in range(4):
                    pltpu.make_async_copy(
                        source.at[j, pl.ds(m * nb, nb)],
                        w_ref.at[m, pl.ds(owner * nb, nb), :, pl.ds(column, 256)],
                        sems.at[0],
                    ).start()
                pltpu.make_async_copy(
                    source.at[j, 4 * nb], held.at[half, owner], sems.at[1]
                ).start()
        first_state[...] = jnp.zeros_like(first_state)
        second_state[...] = jnp.zeros_like(second_state)
        total_state[...] = jnp.zeros_like(total_state)
        pltpu.make_async_copy(held, held, sems.at[1]).wait()
        own = [held[0, s].astype(F32) for s in range(shards)]
        other = [held[1, s].astype(F32) for s in range(shards)]
        vec_ref[...] = spread([part[:8, :128] for part in own], shards)
        width = 2048 // shards
        lane = lax.broadcasted_iota(jnp.int32, (8, 128), 1)
        if width >= 128:
            for s in range(shards):
                eb_ref[:, s * width : (s + 1) * width] = own[s][8:16, :width]
        else:
            for tile in range(16):
                built = jnp.zeros((8, 128), F32)
                for k in range(128 // width):
                    part = own[tile * (128 // width) + k][8:16, :128]
                    moved = pltpu.roll(part, k * width, 1) if k else part
                    built = jnp.where((lane >= k * width) & (lane < (k + 1) * width), moved, built)
                eb_ref[:, tile * 128 : (tile + 1) * 128] = built
        count_ref[...] = sum(part[:8, :128] for part in own + other)
        pltpu.make_async_copy(w_ref, w_ref, sems.at[0]).wait()

    start = step * CHUNK
    segment_last = seg_s[start + CHUNK - 1]
    segment_before = jnp.where(step == 0, -1, seg_s[jnp.maximum(start - 1, 0)])
    keep = jnp.where(segment_last == segment_before, 1.0, 0.0)
    row = seg_ref[...]
    column = as_column(row)
    causal = causal_mask(column, row).astype(BF16)
    enters = jnp.where(column == segment_before.astype(F32), 1.0, 0.0)
    leaves = jnp.where(column == segment_last.astype(F32), 1.0, 0.0).astype(BF16)
    lanes = head_lanes()
    diagonal = block_diagonal()

    normal, _ = standardise(x_ref[...].astype(F32))
    normed = (normal * vec_ref[0:1, :] + vec_ref[1:2, :]).astype(BF16)
    for g in range(2):
        at = slice(g * QUAD, (g + 1) * QUAD)
        weight = lambda m: w_ref[m, :, :, at].reshape(512, QUAD)
        queries = nn(normed, weight(0)).astype(BF16)
        keys = nn(normed, weight(1)).astype(BF16)
        values = nn(normed, weight(2)).astype(BF16)
        slots = jnp.exp(nn(normed, weight(3))).astype(BF16)
        q_ref[:, at] = queries
        k_ref[:, at] = keys
        v_ref[:, at] = values
        e_ref[:, at] = slots
        totals = nn(causal, slots) + enters * total_state[0:1, at]
        total_state[0:1, at] = totals[CHUNK - 1 : CHUNK, :]
        inverse = 1.0 / totals
        rz_ref[:, at] = inverse
        one = first_state[g].astype(BF16)
        two = second_state[g].astype(BF16)
        one_ref[0, g] = one
        two_ref[0, g] = two
        scores = jnp.concatenate(
            [nt(queries * lanes[h], keys).astype(BF16) * causal for h in range(4)], axis=1
        )
        gathered = nn(scores, jnp.concatenate([slots * lanes[h] for h in range(4)], axis=0))
        gathered += enters * nn(queries, one)
        slot_scores = gathered * (inverse * 0.125)
        raised = jnp.exp(slot_scores - per_head(slot_scores, jnp.max, -jnp.inf))
        shares = raised / per_head(raised, jnp.sum, 0.0)
        s_ref[:, at] = slot_scores.astype(BF16)
        p_ref[:, at] = shares.astype(BF16)
        scaled = (shares * inverse).astype(BF16)
        mixing = jnp.concatenate(
            [nt(scaled * lanes[h], slots).astype(BF16) * causal for h in range(4)], axis=1
        )
        mixed = nn(mixing, jnp.concatenate([values * lanes[h] for h in range(4)], axis=0))
        mixed += enters * nn(scaled, two)
        mix_ref[:, at] = mixed.astype(BF16)
        first_state[g] = keep * first_state[g] + diagonal * tn(keys * leaves, slots)
        second_state[g] = keep * second_state[g] + diagonal * tn(slots * leaves, values)


def feed_forward(
    shards,
    tokens,
    pos_s,
    x_ref,
    mix_ref,
    teacher_ref,
    valid_ref,
    vec_ref,
    eb_ref,
    count_ref,
    mine_ref,
    theirs_ref,
    out_ref,
    hidden_ref,
    grad_mix_ref,
    keep_ref,
    send_ref,
    loss_ref,
    wo,
    we,
    wc,
    act,
    d_wo,
    d_we,
    d_wc,
    d_vec,
    d_eb,
    sems,
):
    step = pl.program_id(0)
    r = 512 // shards
    nb = r // 16
    mine, core = pos_s[0], pos_s[1]

    @pl.when(step == 0)
    def _():
        for half, source in enumerate((mine_ref, theirs_ref)):
            column = pl.multiple_of(((core + half) % 2) * 256, 256)
            for j in range(shards):
                owner = mine ^ j
                pltpu.make_async_copy(
                    source.at[j, 0],
                    wo.at[pl.ds(owner * nb, nb), :, pl.ds(column, 256)],
                    sems.at[0],
                ).start()
                pltpu.make_async_copy(
                    source.at[j, 1:5],
                    we.at[:, pl.ds(owner * nb, nb), :, pl.ds(column, 256)],
                    sems.at[1],
                ).start()
                pltpu.make_async_copy(
                    source.at[j, 5:9],
                    wc.at[pl.ds(owner * 4, 4), :, :, pl.ds(column, 256)],
                    sems.at[2],
                ).start()
        for ref in (d_wo, d_we, d_wc, d_vec, d_eb, loss_ref):
            ref[...] = jnp.zeros_like(ref)
        pltpu.make_async_copy(wo, wo, sems.at[0]).wait()
        pltpu.make_async_copy(we, we, sems.at[1]).wait()
        pltpu.make_async_copy(wc, wc, sems.at[2]).wait()

    gain, shift, bias = vec_ref[2:3, :], vec_ref[3:4, :], vec_ref[4:5, :]
    weight_out = wo[...].reshape(512, 512)
    expand = lambda b: we[b].reshape(512, 512)
    contract = wc.reshape(2048, 512)
    mixed = mix_ref[...]
    hidden = x_ref[...].astype(F32) + nn(mixed, weight_out)
    normal, scale = standardise(hidden)
    normed = (normal * gain + shift).astype(BF16)
    for b in range(4):
        at = slice(b * 512, (b + 1) * 512)
        before = nn(normed, expand(b)) + eb_ref[0:1, at]
        act[:, at] = jnp.maximum(before, 0.0).astype(BF16)
    result = hidden + (nn(act[...], contract[...]) + bias)
    out_ref[...] = result.astype(BF16)
    valid = as_column(valid_ref[...])
    valid = jnp.concatenate([valid, valid], axis=1)
    error = result - teacher_ref[...].astype(F32)
    masked = valid * error
    loss_ref[...] += jnp.sum(masked * error)
    count = 256.0 * count_ref[6:7, 0:1] + count_ref[6:7, 1:2]
    grad_result = masked * (tokens / count)
    low = grad_result.astype(BF16)
    d_normed = None
    for b in range(4):
        at = slice(b * 512, (b + 1) * 512)
        active = act[:, at]
        d_wc[at, :] += tn(active, low)
        grad = jnp.where(active > 0, nt(low, contract[at, :]), 0.0)
        grad = grad.astype(BF16)
        d_we[b] += tn(normed, grad)
        d_eb[0:1, at] += jnp.sum(grad.astype(F32), axis=0, keepdims=True)
        part = nt(grad, expand(b))
        d_normed = part if d_normed is None else d_normed + part
    d_vec[0:1, :] += jnp.sum(d_normed * normal, axis=0, keepdims=True)
    d_vec[1:2, :] += jnp.sum(d_normed, axis=0, keepdims=True)
    d_vec[2:3, :] += jnp.sum(low.astype(F32), axis=0, keepdims=True)
    grad_hidden = grad_result + norm_backward(d_normed, gain, normal, scale)
    hidden_ref[...] = grad_hidden
    grad_low = grad_hidden.astype(BF16)
    d_wo[...] += tn(mixed, grad_low)
    grad_mix_ref[...] = nt(grad_low, weight_out).astype(BF16)

    @pl.when(step == pl.num_programs(0) - 1)
    def _():
        def write(ref, at):
            ref[:, 0:r, :] = d_wo[:, at].reshape(shards, r, 256).astype(BF16)
            for b in range(4):
                ref[:, (1 + b) * r : (2 + b) * r, :] = (
                    d_we[b, :, at].reshape(shards, r, 256).astype(BF16)
                )
            ref[:, 5 * r : 9 * r, :] = d_wc[:, at].reshape(shards, 4 * r, 256).astype(BF16)
            width = 2048 // shards
            for s in range(shards):
                top = piece_of(d_vec[...], s, r)
                top = jnp.concatenate([top, jnp.zeros_like(top)], axis=1)
                if width >= 128:
                    low_rows = d_eb[:, s * width : (s + 1) * width]
                else:
                    low_rows = piece_of(d_eb[...], s, width)
                if low_rows.shape[1] < 256:
                    pad = jnp.zeros((8, 256 - low_rows.shape[1]), F32)
                    low_rows = jnp.concatenate([low_rows, pad], axis=1)
                both = jnp.concatenate([top, low_rows], axis=0)
                ref[s, 9 * r : 9 * r + 16, :] = both.astype(BF16)

        left, right = slice(0, 256), slice(256, 512)

        @pl.when(core == 0)
        def _():
            write(keep_ref, left)
            write(send_ref, right)

        @pl.when(core == 1)
        def _():
            write(keep_ref, right)
            write(send_ref, left)


def attention_backward(last, shards, seg_s, pos_s, *refs):
    x_ref, seg_ref, q_ref, k_ref, v_ref, e_ref, p_ref, s_ref, rz_ref, g_ref = refs[:10]
    one_ref, two_ref, w_ref, vec_ref = refs[10:14]
    refs = refs[14:]
    if last:
        part_ref, hidden_ref = refs[:2]
        refs = refs[2:]
    out_ref, keep_ref, send_ref = refs[:3]
    first_state, second_state, total_state, d_w, d_vec = refs[3:]
    step = pl.program_id(0)
    chunks = pl.num_programs(0)
    chunk = chunks - 1 - step
    r = 512 // shards
    core = pos_s[1]

    @pl.when(step == 0)
    def _():
        for ref in (first_state, second_state, total_state, d_w, d_vec):
            ref[...] = jnp.zeros_like(ref)

    start = chunk * CHUNK
    length = chunks * CHUNK
    segment_first = seg_s[start]
    segment_before = jnp.where(chunk == 0, -1, seg_s[jnp.maximum(start - 1, 0)])
    segment_after = jnp.where(step == 0, -1, seg_s[jnp.minimum(start + CHUNK, length - 1)])
    keep = jnp.where(segment_first == segment_after, 1.0, 0.0)
    row = seg_ref[...]
    column = as_column(row)
    causal = causal_mask(column, row).astype(BF16)
    turned = causal_mask_transposed(column, row).astype(BF16)
    enters = jnp.where(column == segment_before.astype(F32), 1.0, 0.0)
    goes_on = jnp.where(column == segment_after.astype(F32), 1.0, 0.0)
    opens = jnp.where(column == segment_first.astype(F32), 1.0, 0.0).astype(BF16)
    lanes = head_lanes()
    diagonal = block_diagonal()

    def heads(values):
        return [values * lanes[h] for h in range(4)]

    def beside(parts):
        return jnp.concatenate(parts, axis=1)

    def stacked(parts):
        return jnp.concatenate(parts, axis=0)

    queries, keys, values, slots = q_ref[...], k_ref[...], v_ref[...], e_ref[...]
    shares, slot_scores = p_ref[...].astype(F32), s_ref[...].astype(F32)
    inverse, grad = rz_ref[...], g_ref[...]
    scaled = shares * inverse
    scaled_low = scaled.astype(BF16)
    one, two = one_ref[0, 0], two_ref[0, 0]
    one_back, two_back = first_state[...].astype(BF16), second_state[...].astype(BF16)
    grad_heads, slot_heads, value_heads = heads(grad), heads(slots), heads(values)
    slot_stack = stacked(slot_heads)

    d_mixing = beside([nt(part, values).astype(BF16) * causal for part in grad_heads])
    d_scaled = nn(d_mixing, slot_stack) + enters * nt(grad, two)
    d_shares = d_scaled * inverse
    product = shares * d_shares
    d_scores = product - shares * per_head(product, jnp.sum, 0.0)
    d_gathered = d_scores * inverse
    d_totals = -(d_scaled * scaled + d_scores * slot_scores) * inverse
    d_low = (d_gathered * 0.125).astype(BF16)
    d_low_heads = heads(d_low)

    d_raw = beside([nt(part, slots).astype(BF16) * causal for part in d_low_heads])
    d_queries = nn(d_raw, stacked(heads(keys))) + enters * nt(d_low, one)
    d_raw_t = beside([nt(part, d_low).astype(BF16) * turned for part in slot_heads])
    d_keys = nn(d_raw_t, stacked(heads(queries))) + goes_on * nt(slots, one_back)
    mixing_t = beside([nt(part, scaled_low).astype(BF16) * turned for part in slot_heads])
    d_values = nn(mixing_t, stacked(grad_heads)) + goes_on * nn(slots, two_back)
    scores_t = beside([nt(part, queries).astype(BF16) * turned for part in heads(keys)])
    d_slots = nn(scores_t, stacked(d_low_heads))
    d_mixing_t = beside([nt(part, grad).astype(BF16) * turned for part in value_heads])
    d_slots += nn(d_mixing_t, stacked(heads(scaled_low)))
    d_totals_low = d_totals.astype(BF16)
    rest = (d_totals - d_totals_low.astype(F32)).astype(BF16)
    sums = nn(turned, d_totals_low) + nn(turned, rest) + goes_on * total_state[0:1, :]
    d_slots += goes_on * (nn(keys, one_back) + nt(values, two_back)) + sums
    d_control = d_slots * slots.astype(F32)

    total_state[0:1, :] = sums[0:1, :]
    first_state[...] = keep * first_state[...] + diagonal * tn(queries * opens, d_low)
    second_state[...] = keep * second_state[...] + diagonal * tn(scaled_low * opens, grad)

    normal, scale = standardise(x_ref[...].astype(F32))
    gain = vec_ref[0:1, :]
    normed = (normal * gain + vec_ref[1:2, :]).astype(BF16)
    grads = [part.astype(BF16) for part in (d_queries, d_keys, d_values, d_control)]
    d_w[...] += tn(normed, beside(grads))
    d_normed = sum(nt(grads[m], w_ref[m].reshape(512, QUAD)) for m in range(4))
    if last:
        d_normed += part_ref[...]
        d_vec[0:1, :] += jnp.sum(d_normed * normal, axis=0, keepdims=True)
        d_vec[1:2, :] += jnp.sum(d_normed, axis=0, keepdims=True)
        out_ref[...] = hidden_ref[...] + norm_backward(d_normed, gain, normal, scale)
    else:
        out_ref[...] = d_normed

    @pl.when(step == chunks - 1)
    def _():
        def write(ref, half):
            for m in range(4):
                at = slice(m * QUAD + half * 128, m * QUAD + half * 128 + 128)
                ref[:, m * r : (m + 1) * r, :] = d_w[:, at].reshape(shards, r, 128).astype(BF16)
            if last:
                for s in range(shards):
                    top = piece_of(d_vec[...], s, r)
                    both = jnp.concatenate([top, jnp.zeros_like(top)], axis=0)
                    ref[s, 4 * r : 4 * r + 16, :] = both.astype(BF16)

        @pl.when(core == 0)
        def _():
            write(keep_ref, 0)
            write(send_ref, 1)

        @pl.when(core == 1)
        def _():
            write(keep_ref, 1)
            write(send_ref, 0)


def whole(shape):
    return pl.BlockSpec(shape, lambda *_: (0,) * len(shape))


def anywhere():
    return pl.BlockSpec(memory_space=pl.ANY)


def shaped(shape, dtype):
    return jax.ShapeDtypeStruct(shape, dtype)


def params():
    return pltpu.CompilerParams(
        dimension_semantics=("arbitrary",), vmem_limit_bytes=VMEM_LIMIT
    )


def call_forward(shards, seg_row, segments, position, x, mine, theirs):
    length = x.shape[0]
    chunks = length // CHUNK
    tile = lambda width: pl.BlockSpec((CHUNK, width), lambda c, *_: (c, 0))
    state = pl.BlockSpec((1, 2, QUAD, QUAD), lambda c, *_: (c, 0, 0, 0))
    low = shaped((length, 512), BF16)
    states = shaped((chunks, 2, QUAD, QUAD), BF16)
    grid_spec = pltpu.PrefetchScalarGridSpec(
        num_scalar_prefetch=2,
        grid=(chunks,),
        in_specs=[
            tile(512),
            pl.BlockSpec((1, CHUNK), lambda c, *_: (0, c)),
            anywhere(),
            anywhere(),
        ],
        out_specs=[tile(512)] * 8
        + [state] * 2
        + [whole((4, 32, 16, 512)), whole((8, 512)), whole((8, 2048)), whole((8, 128))],
        scratch_shapes=[
            pltpu.VMEM((2, shards, 16, 256), BF16),
            pltpu.VMEM((2, QUAD, QUAD), F32),
            pltpu.VMEM((2, QUAD, QUAD), F32),
            pltpu.VMEM((8, 512), F32),
            pltpu.SemaphoreType.DMA((2,)),
        ],
    )
    return pl.pallas_call(
        functools.partial(attention_forward, shards),
        grid_spec=grid_spec,
        out_shape=[low] * 6
        + [shaped((length, 512), F32), low, states, states]
        + [
            shaped((4, 32, 16, 512), BF16),
            shaped((8, 512), F32),
            shaped((8, 2048), F32),
            shaped((8, 128), F32),
        ],
        compiler_params=params(),
        cost_estimate=pl.CostEstimate(
            flops=12_000_000_000, bytes_accessed=18_000_000, transcendentals=1_000_000
        ),
        name="attention_forward",
    )(segments, position, x, seg_row, mine, theirs)


def call_feed_forward(
    shards, tokens, position, x, mixed, teacher, valid_row, vectors, bias, count, mine, theirs
):
    length = x.shape[0]
    chunks = length // CHUNK
    r = 512 // shards
    tile = lambda width: pl.BlockSpec((CHUNK, width), lambda c, *_: (c, 0))
    payload = (shards, 9 * r + 16, 256)
    grid_spec = pltpu.PrefetchScalarGridSpec(
        num_scalar_prefetch=1,
        grid=(chunks,),
        in_specs=[
            tile(512),
            tile(512),
            tile(512),
            pl.BlockSpec((1, CHUNK), lambda c, *_: (0, c)),
            whole((8, 512)),
            whole((8, 2048)),
            whole((8, 128)),
            anywhere(),
            anywhere(),
        ],
        out_specs=[tile(512)] * 3 + [whole(payload), whole(payload), whole((8, 128))],
        scratch_shapes=[
            pltpu.VMEM((32, 16, 512), BF16),
            pltpu.VMEM((4, 32, 16, 512), BF16),
            pltpu.VMEM((shards * 4, r // 16, 16, 512), BF16),
            pltpu.VMEM((CHUNK, 2048), BF16),
            pltpu.VMEM((512, 512), F32),
            pltpu.VMEM((4, 512, 512), F32),
            pltpu.VMEM((2048, 512), F32),
            pltpu.VMEM((8, 512), F32),
            pltpu.VMEM((8, 2048), F32),
            pltpu.SemaphoreType.DMA((3,)),
        ],
    )
    return pl.pallas_call(
        functools.partial(feed_forward, shards, tokens),
        grid_spec=grid_spec,
        out_shape=[
            shaped((length, 512), BF16),
            shaped((length, 512), F32),
            shaped((length, 512), BF16),
            shaped(payload, BF16),
            shaped(payload, BF16),
            shaped((8, 128), F32),
        ],
        compiler_params=params(),
        cost_estimate=pl.CostEstimate(
            flops=15_000_000_000, bytes_accessed=18_000_000, transcendentals=0
        ),
        name="feed_forward",
    )(position, x, mixed, teacher, valid_row, vectors, bias, count, mine, theirs)


def call_backward(
    quad, shards, seg_row, segments, position, x, saved, grad_mix, weights, vectors, extra
):
    length = x.shape[0]
    chunks = length // CHUNK
    r = 512 // shards
    last = quad == 1
    back = lambda c: chunks - 1 - c
    wide = pl.BlockSpec((CHUNK, 512), lambda c, *_: (back(c), 0))
    tile = pl.BlockSpec((CHUNK, QUAD), lambda c, *_: (back(c), quad))
    state = pl.BlockSpec((1, 1, QUAD, QUAD), lambda c, *_: (back(c), quad, 0, 0))
    rows = 4 * r + 16 if last else 4 * r
    payload = (shards, rows, 128)
    grid_spec = pltpu.PrefetchScalarGridSpec(
        num_scalar_prefetch=2,
        grid=(chunks,),
        in_specs=[
            wide,
            pl.BlockSpec((1, CHUNK), lambda c, *_: (0, back(c))),
        ]
        + [tile] * 8
        + [state] * 2
        + [
            pl.BlockSpec((4, 32, 16, QUAD), lambda c, *_: (0, 0, 0, quad)),
            whole((8, 512)),
        ]
        + [wide] * len(extra),
        out_specs=[wide, whole(payload), whole(payload)],
        scratch_shapes=[
            pltpu.VMEM((QUAD, QUAD), F32),
            pltpu.VMEM((QUAD, QUAD), F32),
            pltpu.VMEM((8, QUAD), F32),
            pltpu.VMEM((512, 4 * QUAD), F32),
            pltpu.VMEM((8, 512), F32),
        ],
    )
    return pl.pallas_call(
        functools.partial(attention_backward, last, shards),
        grid_spec=grid_spec,
        out_shape=[shaped((length, 512), F32), shaped(payload, BF16), shaped(payload, BF16)],
        compiler_params=params(),
        cost_estimate=pl.CostEstimate(
            flops=15_000_000_000, bytes_accessed=12_000_000, transcendentals=0
        ),
        name=f"attention_backward_{quad}",
    )(segments, position, x, seg_row, *saved, grad_mix[0], *grad_mix[1:], weights, vectors, *extra)


def swap(value, axis, bit):
    n = lax.axis_size(axis)
    return lax.ppermute(value, axis, [(i, i ^ bit) for i in range(n)])


def swap_both(value, rep_bit, shard_bit):
    n, m = lax.axis_size("rep"), lax.axis_size("shard")
    pairs = [
        (a * m + b, (a ^ rep_bit) * m + (b ^ shard_bit)) for a in range(n) for b in range(m)
    ]
    return lax.ppermute(value, ("rep", "shard"), pairs)


def bit_groups(shards):
    bits = shards.bit_length() - 1
    return [(low, min(2, bits - low)) for low in range(1, bits, 2)]


def gather(payload):
    shards = lax.axis_size("shard")
    held = payload[None]
    for low, width in [(0, 1)] + bit_groups(shards):
        arrived = [swap(held, "shard", a << low) for a in range(1, 1 << width)]
        held = jnp.concatenate([held] + arrived, axis=0)
    return held, swap(held, "rep", 1)


def add_low(*parts):
    return sum(part.astype(F32) for part in parts).astype(BF16)


def reduce_shares(keep, send):
    shards = lax.axis_size("shard")
    me = lax.axis_index("shard")
    rows, columns = keep.shape[1:]
    current = (keep, swap(send, "rep", 1))
    for low, width in reversed(bit_groups(shards)):
        ways = 1 << width
        mine = (me >> low) & (ways - 1)
        views = [part.reshape(ways, -1, rows, columns) for part in current]
        pieces = [
            add_low(*(lax.dynamic_index_in_dim(v, mine ^ a, 0, keepdims=False) for v in views))
            for a in range(ways)
        ]
        arrived = [swap(pieces[a], "shard", a << low) for a in range(1, ways)]
        current = (pieces[0], *arrived)
    both = add_low(*current)
    own = lax.dynamic_index_in_dim(both, me & 1, 0, keepdims=False)
    other = lax.dynamic_index_in_dim(both, (me & 1) ^ 1, 0, keepdims=False)
    from_y = swap(other, "shard", 1)
    from_x = swap(own, "rep", 2)
    from_xy = swap_both(other, 2, 1)
    here = own.astype(F32) + from_y.astype(F32)
    there = from_x.astype(F32) + from_xy.astype(F32)
    total = (here + there).astype(BF16)
    bit = 4
    while bit < lax.axis_size("rep"):
        total = add_low(total, swap(total, "rep", bit))
        bit *= 2
    sibling = swap(total, "rep", 1)
    first = lax.axis_index("rep") % 2 == 0
    left = jnp.where(first, total, sibling).astype(F32)
    right = jnp.where(first, sibling, total).astype(F32)
    return left, right


def local(
    inputs,
    segments,
    valid_mask,
    teacher,
    query_weight,
    key_weight,
    value_weight,
    control_weight,
    output_weight,
    gain_first,
    shift_first,
    expand_weight,
    expand_bias,
    contract_weight,
    contract_bias,
    gain_second,
    shift_second,
):
    _, length, width = inputs.shape
    shards, reps = lax.axis_size("shard"), lax.axis_size("rep")
    r = width // shards
    core = lax.axis_index("rep") % 2
    position = jnp.stack([lax.axis_index("shard"), core]).astype(jnp.int32)

    count = jnp.sum(valid_mask)
    count_pair = jnp.stack([count // 256, count % 256]).astype(BF16)

    def padded(vector):
        return jnp.pad(vector, (0, 256 - vector.shape[0]))

    blank = jnp.zeros((256,), BF16)
    rows = [gain_first, shift_first, gain_second, shift_second, contract_bias, blank, count_pair]
    rows += [blank, expand_bias] + [blank] * 7
    vec_block = jnp.stack([padded(v) for v in rows])[None]

    def my_half(matrix):
        halves = matrix.reshape(matrix.shape[0], -1, 2, 256)
        return lax.dynamic_index_in_dim(halves, core, 2, keepdims=False)

    mixer = jnp.stack([query_weight, key_weight, value_weight, control_weight])
    mixer = my_half(mixer.reshape(4 * r, width)).reshape(4 * r // 16, 16, 256)
    mine_a, theirs_a = gather(jnp.concatenate([mixer, vec_block], axis=0))
    branch = jnp.concatenate(
        [
            my_half(output_weight).reshape(1, r // 16, 16, 256),
            my_half(expand_weight).transpose(1, 0, 2).reshape(4, r // 16, 16, 256),
            my_half(contract_weight).reshape(4, r // 16, 16, 256),
        ],
        axis=0,
    )
    branch, mine_a = lax.optimization_barrier((branch, mine_a))
    mine_b, theirs_b = gather(branch)

    x = inputs.reshape(length, width)
    seg_row = segments.astype(F32)
    seg_flat = segments.reshape(length)
    forward = call_forward(shards, seg_row, seg_flat, position, x, mine_a, theirs_a)
    saved, mixed, one, two = forward[:7], forward[7], forward[8], forward[9]
    weights, vectors, bias, count_part = forward[10:]
    bit = 2
    while bit < reps:
        count_part = count_part + swap(count_part, "rep", bit)
        bit *= 2

    layer_out, grad_hidden, grad_mix, keep_f, send_f, loss = call_feed_forward(
        shards,
        float(length * shards * reps),
        position,
        x,
        mixed,
        teacher.reshape(length, width),
        valid_mask.astype(F32),
        vectors,
        bias,
        count_part,
        mine_b,
        theirs_b,
    )
    back = functools.partial(
        call_backward,
        shards=shards,
        seg_row=seg_row,
        segments=seg_flat,
        position=position,
        x=x,
        saved=saved,
        grad_mix=(grad_mix, one, two),
        weights=weights,
        vectors=vectors,
    )
    part, keep_0, send_0 = back(0, extra=())
    grad_inputs, keep_1, send_1 = back(1, extra=(part, grad_hidden))

    left_f, right_f = reduce_shares(keep_f, send_f)
    left_0, right_0 = reduce_shares(keep_0, send_0)
    left_1, right_1 = reduce_shares(keep_1, send_1)

    for axis, size in (("rep", reps), ("shard", shards)):
        bit = 1
        while bit < size:
            loss = loss + swap(loss, axis, bit)
            bit *= 2
    count_all = 256.0 * count_part[6, 0] + count_part[6, 1]
    loss_value = loss[0, 0] / (2.0 * count_all)

    mats = []
    for m in range(4):
        at = slice(m * r, (m + 1) * r)
        mats.append(
            jnp.concatenate([left_0[at], right_0[at], left_1[at], right_1[at]], axis=1)
        )
    grad_output = jnp.concatenate([left_f[:r], right_f[:r]], axis=1)
    expand_parts = []
    for b in range(4):
        at = slice((1 + b) * r, (2 + b) * r)
        expand_parts += [left_f[at], right_f[at]]
    grad_expand = jnp.concatenate(expand_parts, axis=1)
    grad_contract = jnp.concatenate([left_f[5 * r : 9 * r], right_f[5 * r : 9 * r]], axis=1)
    vec_f, vec_1 = left_f[9 * r :], left_1[4 * r :]
    return (
        layer_out.reshape(inputs.shape),
        grad_inputs.reshape(inputs.shape),
        loss_value,
        *mats,
        grad_output,
        vec_1[0, :r],
        vec_1[1, :r],
        grad_expand,
        vec_f[8, : 4 * r],
        grad_contract,
        vec_f[2, :r],
        vec_f[0, :r],
        vec_f[1, :r],
    )


def solution(mesh):
    every = P(("rep", "shard"), None, None)
    every_row = P(("rep", "shard"), None)
    matrix, vector = P("shard", None), P("shard")
    in_specs = (
        every,
        every_row,
        every_row,
        every,
        *[matrix] * 5,
        *[vector] * 2,
        matrix,
        vector,
        matrix,
        *[vector] * 3,
    )
    out_specs = (
        every,
        every,
        P(),
        *[matrix] * 5,
        *[vector] * 2,
        matrix,
        vector,
        matrix,
        *[vector] * 3,
    )
    return jax.shard_map(local, mesh=mesh, in_specs=in_specs, out_specs=out_specs, check_vma=False)
```

time: 1290 us -> 326 us (0.25)
  matrix products: 519 us -> 0 us
  blocking collectives: 262 us -> 0 us
  waiting for transfers between devices: 366 us -> 165 us
  Pallas kernels: 0 us -> 86.6 us
  starting transfers between devices: 0.41 us -> 46.7 us
  local copies, waits for them, and re-layouts: 49.7 us -> 5.47 us
  loops' own time: 30.1 us -> 0 us
  other arithmetic: 30.4 us -> 13.8 us
  between operations: 20.2 us -> 7.12 us
    dot_general x165 -> x0, matrix products: 519 us -> none  [the longest x32 134 us: slot_rest(): slot_scores = jnp.dot(scores * causal, weights, precision=HIGHEST) / totals]
    reduce_scatter x7 -> x0, waiting for transfers between devices: 362 us -> none  [the longest x1 70.8 us: local(): lax.psum_scatter(grad_expand.astype(jnp.bfloat16), 'shard', scatter_dimen...]
    ppermute x0 -> x40, waiting for transfers between devices: none -> 165 us  [the longest x37 165 us: swap(): return lax.ppermute(value, axis, [(i, i ^ bit) for i in range(n)])]
    all_gather x6 -> x0, blocking collectives: 146 us -> none  [the longest x1 28.5 us: local(): lax.all_gather(value_weight, 'shard', axis=0, tiled=True)]
    psum x2 -> x0, blocking collectives: 90.3 us -> none  [the longest x1 79.4 us: local(): count_all = lax.psum(local_count, ('rep', 'shard'))]
    pallas_call x0 -> x4, Pallas kernels: none -> 86.6 us  [the longest x2 35.5 us: call_backward(): pl.pallas_call(functools.partial(attention_backward, last, shards), grid_...]
    ppermute x0 -> x40, starting transfers between devices: none -> 46.7 us  [the longest x37 41.1 us: swap(): return lax.ppermute(value, axis, [(i, i ^ bit) for i in range(n)])]
    another operation x2 -> x0, loops' own time: 30.1 us -> none  [the longest x1 29.3 us: mix_backward(): lax.map(partial(head_backward, causal), (queries, key_rows, value_rows, c...]
  transfers between devices with their start and end apart: 10 -> 40, of which waited for: 7 -> 22; matrix products, arithmetic and copies ran while one was open for 43% -> 4% of each run, Pallas kernels for 0% -> 12%
where the time goes in v1:
time: 326 us; the launch traced here: 325 us
  waiting for transfers between devices  165 us (51%)
  Pallas kernels  86.6 us (27%)
  starting transfers between devices  46.7 us (14%)
  other arithmetic  13.8 us (4%)
  between operations  7.12 us (2%)
  local copies, waits for them, and re-layouts  5.47 us (2%)
    ppermute x37, waiting for transfers between devices, swap(): return lax.ppermute(value, axis, [(i, i ^ bit) for i in range(n)])  165 us
    ppermute x37, starting transfers between devices, swap(): return lax.ppermute(value, axis, [(i, i ^ bit) for i in range(n)])  41.1 us
    pallas_call x2, Pallas kernels, call_backward(): pl.pallas_call(functools.partial(attention_backward, last, shards), grid_...  35.5 us
    pallas_call x1, Pallas kernels, call_feed_forward(): pl.pallas_call(functools.partial(feed_forward, shards, tokens), grid_spec...  30.4 us
    pallas_call x1, Pallas kernels, call_forward(): pl.pallas_call(functools.partial(attention_forward, shards), grid_spec=gr...  20.8 us
  transfers between devices with their start and end apart: 40, of which 22 were waited for; matrix products, arithmetic and copies ran while one was open for 4% of the time, Pallas kernels for 12%

profile of v1, /device:TPU:13, one launch (start us, length us, event | category | flops | bytes accessed | tf_op | source)
XLA Modules:
  0.0 324.7 jit_solution(12037042300468077854)
XLA Ops:
  0.7 2.0 fusion.29
  8.4 3.6 %collective-permute-done = bf16[1,17,16,256]{3,2,1,0:T(8,128)(2,1)S(1)} collective-permute-done((bf16[1,17,16,256]{3,2,1,0:T(8,128)(2,1)S(1)}, bf16[1,17,16,256]{3,2,1,0:T(8,128)(2,1)S(1)}, u32[]{:S(2)}, u32[]{:S(2)}) %collective-permute-start) | collective-permute-done | bytes 139296 | tf_op jit(solution)/shard_map/ppermute | solution.py:658
  12.4 2.4 collective-permute-start.2
  15.0 5.6 %collective-permute-done.1 = bf16[2,17,16,256]{3,2,1,0:T(8,128)(2,1)S(1)} collective-permute-done((bf16[2,17,16,256]{3,2,1,0:T(8,128)(2,1)S(1)}, bf16[2,17,16,256]{3,2,1,0:T(8,128)(2,1)S(1)}, u32[]{:S(2)}, u32[]{:S(2)}) %collective-permute-start.1) | collective-permute-done | bytes 278560 | tf_op jit(solution)/shard_map/ppermute | solution.py:658
  20.7 5.1 %collective-permute-done.2 = bf16[2,17,16,256]{3,2,1,0:T(8,128)(2,1)S(1)} collective-permute-done((bf16[2,17,16,256]{3,2,1,0:T(8,128)(2,1)S(1)}, bf16[2,17,16,256]{3,2,1,0:T(8,128)(2,1)S(1)}, u32[]{:S(2)}, u32[]{:S(2)}) %collective-permute-start.2) | collective-permute-done | bytes 278560 | tf_op jit(solution)/shard_map/ppermute | solution.py:658
  25.8 11.9 %collective-permute-done.3 = bf16[2,17,16,256]{3,2,1,0:T(8,128)(2,1)S(1)} collective-permute-done((bf16[2,17,16,256]{3,2,1,0:T(8,128)(2,1)S(1)}, bf16[2,17,16,256]{3,2,1,0:T(8,128)(2,1)S(1)}, u32[]{:S(2)}, u32[]{:S(2)}) %collective-permute-start.3) | collective-permute-done | bytes 278560 | tf_op jit(solution)/shard_map/ppermute | solution.py:658
  38.1 5.3 %collective-permute-done.6 = bf16[1,9,4,16,256]{4,3,2,1,0:T(8,128)(2,1)S(1)} collective-permute-done((bf16[1,9,4,16,256]{4,3,2,1,0:T(8,128)(2,1)S(1)}, bf16[1,9,4,16,256]{4,3,2,1,0:T(8,128)(2,1)S(1)}, u32[]{:S(2)}, u32[]{:S(2)}) %collective-permute-start.6) | collective-permute-done | bytes 294944 | tf_op jit(solution)/shard_map/ppermute | solution.py:658
  43.6 2.5 collective-permute-start.8
  46.3 18.2 %collective-permute-done.7 = bf16[2,9,4,16,256]{4,3,2,1,0:T(8,128)(2,1)S(1)} collective-permute-done((bf16[2,9,4,16,256]{4,3,2,1,0:T(8,128)(2,1)S(1)}, bf16[2,9,4,16,256]{4,3,2,1,0:T(8,128)(2,1)S(1)}, u32[]{:S(2)}, u32[]{:S(2)}) %collective-permute-start.7) | collective-permute-done | bytes 589856 | tf_op jit(solution)/shard_map/ppermute | solution.py:658
  64.5 3.7 %collective-permute-done.8 = bf16[2,9,4,16,256]{4,3,2,1,0:T(8,128)(2,1)S(1)} collective-permute-done((bf16[2,9,4,16,256]{4,3,2,1,0:T(8,128)(2,1)S(1)}, bf16[2,9,4,16,256]{4,3,2,1,0:T(8,128)(2,1)S(1)}, u32[]{:S(2)}, u32[]{:S(2)}) %collective-permute-start.8) | collective-permute-done | bytes 589856 | tf_op jit(solution)/shard_map/ppermute | solution.py:658
  68.3 25.2 %collective-permute-done.9 = bf16[2,9,4,16,256]{4,3,2,1,0:T(8,128)(2,1)S(1)} collective-permute-done((bf16[2,9,4,16,256]{4,3,2,1,0:T(8,128)(2,1)S(1)}, bf16[2,9,4,16,256]{4,3,2,1,0:T(8,128)(2,1)S(1)}, u32[]{:S(2)}, u32[]{:S(2)}) %collective-permute-start.9) | collective-permute-done | bytes 589856 | tf_op jit(solution)/shard_map/ppermute | solution.py:658
  93.5 5.1 %collective-permute-start.10 = (bf16[8,9,4,16,256]{4,3,2,1,0:T(8,128)(2,1)S(1)}, bf16[8,9,4,16,256]{4,3,2,1,0:T(8,128)(2,1)}, u32[]{:S(2)}, u32[]{:S(2)}) collective-permute-start(bf16[8,9,4,16,256]{4,3,2,1,0:T(8,128)(2,1)S(1)} %constant_dynamic-update-slice_fusion.5.mine_ref), channel_id=1, source_target_pairs={{0,8},{8,0},{16,24},{24,16},{1,9},{9,1},{17,25},{25,17},{2,10},{10... | collective-permute-start | bytes 7077896 | tf_op jit(solution)/shard_map/ppermute | solution.py:658
  99.9 4.6 %collective-permute-done.4.theirs_ref = bf16[8,17,16,256]{3,2,1,0:T(8,128)(2,1)} collective-permute-done((bf16[8,17,16,256]{3,2,1,0:T(8,128)(2,1)S(1)}, bf16[8,17,16,256]{3,2,1,0:T(8,128)(2,1)}, u32[]{:S(2)}, u32[]{:S(2)}) %collective-permute-start.4) | collective-permute-done | bytes 1114144 | tf_op jit(solution)/shard_map/ppermute | solution.py:658
  104.5 20.8 %attention_forward.1 = (bf16[1024,512]{1,0:T(8,128)(2,1)}, bf16[1024,512]{1,0:T(8,128)(2,1)}, bf16[1024,512]{1,0:T(8,128)(2,1)}, bf16[1024,512]{1,0:T(8,128)(2,1...) custom-call(s32[1024]{0:T(1024)} %bitcast.114, ...), custom_call_target="tpu_custom_call" | custom-call | flops 12000000000 | bytes 18000000 | tf_op jit(solution)/shard_map/attention_forward/pallas_call | solution.py:534
  129.3 30.4 %feed_forward.1 = (bf16[1024,512]{1,0:T(8,128)(2,1)}, f32[1024,512]{1,0:T(8,128)}, bf16[1024,512]{1,0:T(8,128)(2,1)}, bf16[8,592,256]{2,1,0:T(8,128)(2,1)}, bf16...) custom-call(s32[2]{0:T(128)} %pad_add_fusion.pos_s, bf16[1024,512]{1,0:T(8,128)(2,1)} %bitcast.120, ...), custom_call_target="tpu_custom_call" | custom-call | flops 15000000512 | bytes 18000000 | tf_op jit(solution)/shard_map/feed_forward/pallas_call | solution.py:589
  159.7 17.6 %attention_backward_0.1 = (f32[1024,512]{1,0:T(8,128)}, bf16[8,256,128]{2,1,0:T(8,128)(2,1)}, bf16[8,256,128]{2,1,0:T(8,128)(2,1)}) custom-call(s32[1024]{0:T(1024)} %bitcast.115, s32[2]{0:T(128)} %pad_add_fusion.pos_s, bf16[1024,512]{1,0:T(8,128)(2,1)} %bitcast.121, f32[1,1024]{1,0:T(1,128)} %convert_element_type.294.seg_ref.refs_1_, ...), custom_call_target="tpu_custom_call" | custom-call | flops 15000000512 | bytes 12000000 | tf_op jit(solution)/shard_map/attention_backward_0/pallas_call | solution.py:644
  178.9 17.9 %attention_backward_1.1 = (f32[1024,512]{1,0:T(8,128)}, bf16[8,272,128]{2,1,0:T(8,128)(2,1)}, bf16[8,272,128]{2,1,0:T(8,128)(2,1)}) custom-call(s32[1024]{0:T(1024)} %bitcast.116, s32[2]{0:T(128)} %pad_add_fusion.pos_s, bf16[1024,512]{1,0:T(8,128)(2,1)} %bitcast.122, f32[1,1024]{1,0:T(1,128)} %convert_element_type.294.seg_ref.refs_1_, ...), custom_call_target="tpu_custom_call" | custom-call | flops 15000000512 | bytes 12000000 | tf_op jit(solution)/shard_map/attention_backward_1/pallas_call | solution.py:644
  201.5 2.2 collective-permute-done.13
  203.7 2.5 collective-permute-done.14
  215.3 2.4 collective-permute-start.25
  221.9 2.2 collective-permute-start.22
  224.1 3.2 collective-permute-done.26
  228.5 5.2 %collective-permute-done.27 = bf16[2,272,128]{2,1,0:T(8,128)(2,1)S(1)} collective-permute-done((bf16[2,272,128]{2,1,0:T(8,128)(2,1)S(1)}, bf16[2,272,128]{2,1,0:T(8,128)(2,1)S(1)}, u32[]{:S(2)}, u32[]{:S(2)}) %collective-permute-start.27) | collective-permute-done | bytes 139296 | tf_op jit(solution)/shard_map/ppermute | solution.py:658
  234.1 2.2 collective-permute-start.30
  236.6 6.1 %collective-permute-start.23 = (bf16[256,128]{1,0:T(8,128)(2,1)S(1)}, bf16[256,128]{1,0:T(8,128)(2,1)S(1)}, u32[]{:S(2)}, u32[]{:S(2)}) collective-permute-start(bf16[256,128]{1,0:T(8,128)(2,1)S(1)} %add_convert_fusion.14), channel_id=1, source_target_pairs={{0,8},{8,0},{16,24},{24,16},{1,9},{9,1},{17,25},{25,17},{2,10},{10... | collective-permute-start | bytes 196616 | tf_op jit(solution)/shard_map/ppermute | solution.py:658
  242.7 2.8 collective-permute-start.31
  246.2 2.5 collective-permute-start.35
  248.8 21.1 %collective-permute-done.33 = bf16[2,592,256]{2,1,0:T(8,128)(2,1)S(1)} collective-permute-done((bf16[2,592,256]{2,1,0:T(8,128)(2,1)S(1)}, bf16[2,592,256]{2,1,0:T(8,128)(2,1)S(1)}, u32[]{:S(2)}, u32[]{:S(2)}) %collective-permute-start.33) | collective-permute-done | bytes 606240 | tf_op jit(solution)/shard_map/ppermute | solution.py:658
  269.9 3.2 collective-permute-done.34
  273.0 28.2 %collective-permute-done.35 = bf16[2,592,256]{2,1,0:T(8,128)(2,1)S(1)} collective-permute-done((bf16[2,592,256]{2,1,0:T(8,128)(2,1)S(1)}, bf16[2,592,256]{2,1,0:T(8,128)(2,1)S(1)}, u32[]{:S(2)}, u32[]{:S(2)}) %collective-permute-start.35) | collective-permute-done | bytes 606240 | tf_op jit(solution)/shard_map/ppermute | solution.py:658
  306.5 9.4 %collective-permute-done.36 = bf16[592,256]{1,0:T(8,128)(2,1)S(1)} collective-permute-done((bf16[592,256]{1,0:T(8,128)(2,1)S(1)}, bf16[592,256]{1,0:T(8,128)(2,1)S(1)}, u32[]{:S(2)}, u32[]{:S(2)}) %collective-permute-start.36) | collective-permute-done | bytes 303136 | tf_op jit(solution)/shard_map/ppermute | solution.py:658
  317.0 2.4 collective-permute-start.39
  (174 shorter events, 40.3 us)
Async XLA Ops:
  12.1 8.5 %collective-permute-start.1 = (bf16[2,17,16,256]{3,2,1,0:T(8,128)(2,1)S(1)}, bf16[2,17,16,256]{3,2,1,0:T(8,128)(2,1)S(1)}, u32[]{:S(2)}, u32[]{:S(2)}) collective-permute-start(bf16[2,17,16,256]{3,2,1,0:T(8,128)(2,1)S(1)} %pad_maximum_fusion.3), channel_id=1, source_target_pairs={{0,2},{1,3},{2,0},{3,1},{4,6},{5,7},{6,4},{7,5},{8,10},{9,11},{10,... | collective-permute-start | bytes 835592 | tf_op jit(solution)/shard_map/ppermute | solution.py:658
  12.4 13.4 %collective-permute-start.2 = (bf16[2,17,16,256]{3,2,1,0:T(8,128)(2,1)S(1)}, bf16[2,17,16,256]{3,2,1,0:T(8,128)(2,1)S(1)}, u32[]{:S(2)}, u32[]{:S(2)}) collective-permute-start(bf16[2,17,16,256]{3,2,1,0:T(8,128)(2,1)S(1)} %pad_maximum_fusion.3), channel_id=1, source_target_pairs={{0,4},{1,5},{2,6},{3,7},{4,0},{5,1},{6,2},{7,3},{8,12},{9,13},{10,... | collective-permute-start | bytes 835592 | tf_op jit(solution)/shard_map/ppermute | solution.py:658
  14.8 23.0 %collective-permute-start.3 = (bf16[2,17,16,256]{3,2,1,0:T(8,128)(2,1)S(1)}, bf16[2,17,16,256]{3,2,1,0:T(8,128)(2,1)S(1)}, u32[]{:S(2)}, u32[]{:S(2)}) collective-permute-start(bf16[2,17,16,256]{3,2,1,0:T(8,128)(2,1)S(1)} %pad_maximum_fusion.3), channel_id=1, source_target_pairs={{0,6},{1,7},{2,4},{3,5},{4,2},{5,3},{6,0},{7,1},{8,14},{9,15},{10,... | collective-permute-start | bytes 835592 | tf_op jit(solution)/shard_map/ppermute | solution.py:658
  37.8 5.6 %collective-permute-start.6 = (bf16[1,9,4,16,256]{4,3,2,1,0:T(8,128)(2,1)S(1)}, bf16[1,9,4,16,256]{4,3,2,1,0:T(8,128)(2,1)S(1)}, u32[]{:S(2)}, u32[]{:S(2)}) collective-permute-start(bf16[1,9,4,16,256]{4,3,2,1,0:T(8,128)(2,1)S(1)} %bitcast.91), channel_id=1, source_target_pairs={{0,1},{1,0},{2,3},{3,2},{4,5},{5,4},{6,7},{7,6},{8,9},{9,8},{10,11... | collective-permute-start | bytes 884744 | tf_op jit(solution)/shard_map/ppermute | solution.py:658
  43.5 21.0 %collective-permute-start.7 = (bf16[2,9,4,16,256]{4,3,2,1,0:T(8,128)(2,1)S(1)}, bf16[2,9,4,16,256]{4,3,2,1,0:T(8,128)(2,1)S(1)}, u32[]{:S(2)}, u32[]{:S(2)}) collective-permute-start(bf16[2,9,4,16,256]{4,3,2,1,0:T(8,128)(2,1)S(1)} %pad_maximum_fusion), channel_id=1, source_target_pairs={{0,2},{1,3},{2,0},{3,1},{4,6},{5,7},{6,4},{7,5},{8,10},{9,11},{10,... | collective-permute-start | bytes 1769480 | tf_op jit(solution)/shard_map/ppermute | solution.py:658
  43.6 24.7 %collective-permute-start.8 = (bf16[2,9,4,16,256]{4,3,2,1,0:T(8,128)(2,1)S(1)}, bf16[2,9,4,16,256]{4,3,2,1,0:T(8,128)(2,1)S(1)}, u32[]{:S(2)}, u32[]{:S(2)}) collective-permute-start(bf16[2,9,4,16,256]{4,3,2,1,0:T(8,128)(2,1)S(1)} %pad_maximum_fusion), channel_id=1, source_target_pairs={{0,4},{1,5},{2,6},{3,7},{4,0},{5,1},{6,2},{7,3},{8,12},{9,13},{10,... | collective-permute-start | bytes 1769480 | tf_op jit(solution)/shard_map/ppermute | solution.py:658
  46.1 47.4 %collective-permute-start.9 = (bf16[2,9,4,16,256]{4,3,2,1,0:T(8,128)(2,1)S(1)}, bf16[2,9,4,16,256]{4,3,2,1,0:T(8,128)(2,1)S(1)}, u32[]{:S(2)}, u32[]{:S(2)}) collective-permute-start(bf16[2,9,4,16,256]{4,3,2,1,0:T(8,128)(2,1)S(1)} %pad_maximum_fusion), channel_id=1, source_target_pairs={{0,6},{1,7},{2,4},{3,5},{4,2},{5,3},{6,0},{7,1},{8,14},{9,15},{10,... | collective-permute-start | bytes 1769480 | tf_op jit(solution)/shard_map/ppermute | solution.py:658
  93.5 35.8 %collective-permute-start.10 = (bf16[8,9,4,16,256]{4,3,2,1,0:T(8,128)(2,1)S(1)}, bf16[8,9,4,16,256]{4,3,2,1,0:T(8,128)(2,1)}, u32[]{:S(2)}, u32[]{:S(2)}) collective-permute-start(bf16[8,9,4,16,256]{4,3,2,1,0:T(8,128)(2,1)S(1)} %constant_dynamic-update-slice_fusion.5.mine_ref), channel_id=1, source_target_pairs={{0,8},{8,0},{16,24},{24,16},{1,9},{9,1},{17,25},{25,17},{2,10},{10... | collective-permute-start | bytes 7077896 | tf_op jit(solution)/shard_map/ppermute | solution.py:658
  98.6 5.9 %collective-permute-start.4 = (bf16[8,17,16,256]{3,2,1,0:T(8,128)(2,1)S(1)}, bf16[8,17,16,256]{3,2,1,0:T(8,128)(2,1)}, u32[]{:S(2)}, u32[]{:S(2)}) collective-permute-start(bf16[8,17,16,256]{3,2,1,0:T(8,128)(2,1)S(1)} %constant_dynamic-update-slice_fusion.mine_ref), channel_id=1, source_target_pairs={{0,8},{8,0},{16,24},{24,16},{1,9},{9,1},{17,25},{25,17},{2,10},{10... | collective-permute-start | bytes 3342344 | tf_op jit(solution)/shard_map/ppermute | solution.py:658
  177.3 29.9 %collective-permute-start.16 = (bf16[8,256,128]{2,1,0:T(8,128)(2,1)}, bf16[8,256,128]{2,1,0:T(8,128)(2,1)}, u32[]{:S(2)}, u32[]{:S(2)}) collective-permute-start(bf16[8,256,128]{2,1,0:T(8,128)(2,1)} %get-tuple-element.67), channel_id=1, source_target_pairs={{0,8},{8,0},{16,24},{24,16},{1,9},{9,1},{17,25},{25,17},{2,10},{10... | collective-permute-start | bytes 1572872 | tf_op jit(solution)/shard_map/ppermute | solution.py:658
  196.8 18.4 %collective-permute-start.24 = (bf16[8,272,128]{2,1,0:T(8,128)(2,1)}, bf16[8,272,128]{2,1,0:T(8,128)(2,1)S(1)}, u32[]{:S(2)}, u32[]{:S(2)}) collective-permute-start(bf16[8,272,128]{2,1,0:T(8,128)(2,1)} %get-tuple-element.69), channel_id=1, source_target_pairs={{0,8},{8,0},{16,24},{24,16},{1,9},{9,1},{17,25},{25,17},{2,10},{10... | collective-permute-start | bytes 1671176 | tf_op jit(solution)/shard_map/ppermute | solution.py:658
  196.8 48.7 %collective-permute-start.32 = (bf16[8,592,256]{2,1,0:T(8,128)(2,1)}, bf16[8,592,256]{2,1,0:T(8,128)(2,1)S(1)}, u32[]{:S(2)}, u32[]{:S(2)}) collective-permute-start(bf16[8,592,256]{2,1,0:T(8,128)(2,1)} %get-tuple-element.71), channel_id=1, source_target_pairs={{0,8},{8,0},{16,24},{24,16},{1,9},{9,1},{17,25},{25,17},{2,10},{10... | collective-permute-start | bytes 7274504 | tf_op jit(solution)/shard_map/ppermute | solution.py:658
  208.5 9.1 %collective-permute-start.17 = (bf16[2,256,128]{2,1,0:T(8,128)(2,1)S(1)}, bf16[2,256,128]{2,1,0:T(8,128)(2,1)S(1)}, u32[]{:S(2)}, u32[]{:S(2)}) collective-permute-start(bf16[2,256,128]{2,1,0:T(8,128)(2,1)S(1)} %get-tuple-element.78), channel_id=1, source_target_pairs={{0,2},{1,3},{2,0},{3,1},{4,6},{5,7},{6,4},{7,5},{8,10},{9,11},{10,... | collective-permute-start | bytes 393224 | tf_op jit(solution)/shard_map/ppermute | solution.py:658
  210.1 7.6 %collective-permute-start.18 = (bf16[2,256,128]{2,1,0:T(8,128)(2,1)S(1)}, bf16[2,256,128]{2,1,0:T(8,128)(2,1)S(1)}, u32[]{:S(2)}, u32[]{:S(2)}) collective-permute-start(bf16[2,256,128]{2,1,0:T(8,128)(2,1)S(1)} %get-tuple-element.80), channel_id=1, source_target_pairs={{0,4},{1,5},{2,6},{3,7},{4,0},{5,1},{6,2},{7,3},{8,12},{9,13},{10,... | collective-permute-start | bytes 393224 | tf_op jit(solution)/shard_map/ppermute | solution.py:658
  210.1 10.4 %collective-permute-start.19 = (bf16[2,256,128]{2,1,0:T(8,128)(2,1)S(1)}, bf16[2,256,128]{2,1,0:T(8,128)(2,1)S(1)}, u32[]{:S(2)}, u32[]{:S(2)}) collective-permute-start(bf16[2,256,128]{2,1,0:T(8,128)(2,1)S(1)} %get-tuple-element.79), channel_id=1, source_target_pairs={{0,6},{1,7},{2,4},{3,5},{4,2},{5,3},{6,0},{7,1},{8,14},{9,15},{10,... | collective-permute-start | bytes 393224 | tf_op jit(solution)/shard_map/ppermute | solution.py:658
  215.3 6.6 %collective-permute-start.25 = (bf16[2,272,128]{2,1,0:T(8,128)(2,1)S(1)}, bf16[2,272,128]{2,1,0:T(8,128)(2,1)S(1)}, u32[]{:S(2)}, u32[]{:S(2)}) collective-permute-start(bf16[2,272,128]{2,1,0:T(8,128)(2,1)S(1)} %get-tuple-element.75), channel_id=1, source_target_pairs={{0,2},{1,3},{2,0},{3,1},{4,6},{5,7},{6,4},{7,5},{8,10},{9,11},{10,... | collective-permute-start | bytes 417800 | tf_op jit(solution)/shard_map/ppermute | solution.py:658
  217.6 9.6 %collective-permute-start.26 = (bf16[2,272,128]{2,1,0:T(8,128)(2,1)S(1)}, bf16[2,272,128]{2,1,0:T(8,128)(2,1)S(1)}, u32[]{:S(2)}, u32[]{:S(2)}) collective-permute-start(bf16[2,272,128]{2,1,0:T(8,128)(2,1)S(1)} %get-tuple-element.77), channel_id=1, source_target_pairs={{0,4},{1,5},{2,6},{3,7},{4,0},{5,1},{6,2},{7,3},{8,12},{9,13},{10,... | collective-permute-start | bytes 417800 | tf_op jit(solution)/shard_map/ppermute | solution.py:658
  217.7 16.0 %collective-permute-start.27 = (bf16[2,272,128]{2,1,0:T(8,128)(2,1)S(1)}, bf16[2,272,128]{2,1,0:T(8,128)(2,1)S(1)}, u32[]{:S(2)}, u32[]{:S(2)}) collective-permute-start(bf16[2,272,128]{2,1,0:T(8,128)(2,1)S(1)} %get-tuple-element.76), channel_id=1, source_target_pairs={{0,6},{1,7},{2,4},{3,5},{4,2},{5,3},{6,0},{7,1},{8,14},{9,15},{10,... | collective-permute-start | bytes 417800 | tf_op jit(solution)/shard_map/ppermute | solution.py:658
  221.6 12.5 %collective-permute-start.20 = (bf16[256,128]{1,0:T(8,128)(2,1)S(1)}, bf16[256,128]{1,0:T(8,128)(2,1)S(1)}, u32[]{:S(2)}, u32[]{:S(2)}) collective-permute-start(bf16[256,128]{1,0:T(8,128)(2,1)S(1)} %get-tuple-element.117), channel_id=1, source_target_pairs={{0,1},{1,0},{2,3},{3,2},{4,5},{5,4},{6,7},{7,6},{8,9},{9,8},{10,11... | collective-permute-start | bytes 196616 | tf_op jit(solution)/shard_map/ppermute | solution.py:658
  221.9 14.7 %collective-permute-start.22 = (bf16[256,128]{1,0:T(8,128)(2,1)S(1)}, bf16[256,128]{1,0:T(8,128)(2,1)S(1)}, u32[]{:S(2)}, u32[]{:S(2)}) collective-permute-start(bf16[256,128]{1,0:T(8,128)(2,1)S(1)} %get-tuple-element.117), channel_id=1, source_target_pairs={{0,17},{1,16},{2,19},{3,18},{4,21},{5,20},{6,23},{7,22},{8,25},{9,... | collective-permute-start | bytes 196616 | tf_op jit(solution)/shard_map/ppermute | solution.py:666
  227.2 9.0 %collective-permute-start.21 = (bf16[256,128]{1,0:T(8,128)(2,1)S(1)}, bf16[256,128]{1,0:T(8,128)(2,1)S(1)}, u32[]{:S(2)}, u32[]{:S(2)}) collective-permute-start(bf16[256,128]{1,0:T(8,128)(2,1)S(1)} %get-tuple-element.116), channel_id=1, source_target_pairs={{0,16},{8,24},{16,0},{24,8},{1,17},{9,25},{17,1},{25,9},{2,18},{10... | collective-permute-start | bytes 196616 | tf_op jit(solution)/shard_map/ppermute | solution.py:658
  233.8 8.9 %collective-permute-start.28 = (bf16[272,128]{1,0:T(8,128)(2,1)S(1)}, bf16[272,128]{1,0:T(8,128)(2,1)S(1)}, u32[]{:S(2)}, u32[]{:S(2)}) collective-permute-start(bf16[272,128]{1,0:T(8,128)(2,1)S(1)} %get-tuple-element.105), channel_id=1, source_target_pairs={{0,1},{1,0},{2,3},{3,2},{4,5},{5,4},{6,7},{7,6},{8,9},{9,8},{10,11... | collective-permute-start | bytes 208904 | tf_op jit(solution)/shard_map/ppermute | solution.py:658
  234.1 8.6 %collective-permute-start.30 = (bf16[272,128]{1,0:T(8,128)(2,1)S(1)}, bf16[272,128]{1,0:T(8,128)(2,1)S(1)}, u32[]{:S(2)}, u32[]{:S(2)}) collective-permute-start(bf16[272,128]{1,0:T(8,128)(2,1)S(1)} %get-tuple-element.105), channel_id=1, source_target_pairs={{0,17},{1,16},{2,19},{3,18},{4,21},{5,20},{6,23},{7,22},{8,25},{9,... | collective-permute-start | bytes 208904 | tf_op jit(solution)/shard_map/ppermute | solution.py:666
  236.3 6.4 %collective-permute-start.29 = (bf16[272,128]{1,0:T(8,128)(2,1)S(1)}, bf16[272,128]{1,0:T(8,128)(2,1)S(1)}, u32[]{:S(2)}, u32[]{:S(2)}) collective-permute-start(bf16[272,128]{1,0:T(8,128)(2,1)S(1)} %get-tuple-element.104), channel_id=1, source_target_pairs={{0,16},{8,24},{16,0},{24,8},{1,17},{9,25},{17,1},{25,9},{2,18},{10... | collective-permute-start | bytes 208904 | tf_op jit(solution)/shard_map/ppermute | solution.py:658
  236.6 8.9 %collective-permute-start.23 = (bf16[256,128]{1,0:T(8,128)(2,1)S(1)}, bf16[256,128]{1,0:T(8,128)(2,1)S(1)}, u32[]{:S(2)}, u32[]{:S(2)}) collective-permute-start(bf16[256,128]{1,0:T(8,128)(2,1)S(1)} %add_convert_fusion.14), channel_id=1, source_target_pairs={{0,8},{8,0},{16,24},{24,16},{1,9},{9,1},{17,25},{25,17},{2,10},{10... | collective-permute-start | bytes 196616 | tf_op jit(solution)/shard_map/ppermute | solution.py:658
  242.7 6.0 %collective-permute-start.31 = (bf16[272,128]{1,0:T(8,128)(2,1)S(1)}, bf16[272,128]{1,0:T(8,128)(2,1)S(1)}, u32[]{:S(2)}, u32[]{:S(2)}) collective-permute-start(bf16[272,128]{1,0:T(8,128)(2,1)S(1)} %add_convert_fusion.13), channel_id=1, source_target_pairs={{0,8},{8,0},{16,24},{24,16},{1,9},{9,1},{17,25},{25,17},{2,10},{10... | collective-permute-start | bytes 208904 | tf_op jit(solution)/shard_map/ppermute | solution.py:658
  246.0 23.9 %collective-permute-start.33 = (bf16[2,592,256]{2,1,0:T(8,128)(2,1)S(1)}, bf16[2,592,256]{2,1,0:T(8,128)(2,1)S(1)}, u32[]{:S(2)}, u32[]{:S(2)}) collective-permute-start(bf16[2,592,256]{2,1,0:T(8,128)(2,1)S(1)} %get-tuple-element.72), channel_id=1, source_target_pairs={{0,2},{1,3},{2,0},{3,1},{4,6},{5,7},{6,4},{7,5},{8,10},{9,11},{10,... | collective-permute-start | bytes 1818632 | tf_op jit(solution)/shard_map/ppermute | solution.py:658
  246.1 27.0 %collective-permute-start.34 = (bf16[2,592,256]{2,1,0:T(8,128)(2,1)S(1)}, bf16[2,592,256]{2,1,0:T(8,128)(2,1)S(1)}, u32[]{:S(2)}, u32[]{:S(2)}) collective-permute-start(bf16[2,592,256]{2,1,0:T(8,128)(2,1)S(1)} %get-tuple-element.74), channel_id=1, source_target_pairs={{0,4},{1,5},{2,6},{3,7},{4,0},{5,1},{6,2},{7,3},{8,12},{9,13},{10,... | collective-permute-start | bytes 1818632 | tf_op jit(solution)/shard_map/ppermute | solution.py:658
  246.2 55.1 %collective-permute-start.35 = (bf16[2,592,256]{2,1,0:T(8,128)(2,1)S(1)}, bf16[2,592,256]{2,1,0:T(8,128)(2,1)S(1)}, u32[]{:S(2)}, u32[]{:S(2)}) collective-permute-start(bf16[2,592,256]{2,1,0:T(8,128)(2,1)S(1)} %get-tuple-element.73), channel_id=1, source_target_pairs={{0,6},{1,7},{2,4},{3,5},{4,2},{5,3},{6,0},{7,1},{8,14},{9,15},{10,... | collective-permute-start | bytes 1818632 | tf_op jit(solution)/shard_map/ppermute | solution.py:658
  301.8 14.1 %collective-permute-start.36 = (bf16[592,256]{1,0:T(8,128)(2,1)S(1)}, bf16[592,256]{1,0:T(8,128)(2,1)S(1)}, u32[]{:S(2)}, u32[]{:S(2)}) collective-permute-start(bf16[592,256]{1,0:T(8,128)(2,1)S(1)} %get-tuple-element.91), channel_id=1, source_target_pairs={{0,1},{1,0},{2,3},{3,2},{4,5},{5,4},{6,7},{7,6},{8,9},{9,8},{10,11... | collective-permute-start | bytes 909320 | tf_op jit(solution)/shard_map/ppermute | solution.py:658
  303.0 13.9 %collective-permute-start.38 = (bf16[592,256]{1,0:T(8,128)(2,1)S(1)}, bf16[592,256]{1,0:T(8,128)(2,1)S(1)}, u32[]{:S(2)}, u32[]{:S(2)}) collective-permute-start(bf16[592,256]{1,0:T(8,128)(2,1)S(1)} %get-tuple-element.91), channel_id=1, source_target_pairs={{0,17},{1,16},{2,19},{3,18},{4,21},{5,20},{6,23},{7,22},{8,25},{9,... | collective-permute-start | bytes 909320 | tf_op jit(solution)/shard_map/ppermute | solution.py:666
  304.2 12.6 %collective-permute-start.37 = (bf16[592,256]{1,0:T(8,128)(2,1)S(1)}, bf16[592,256]{1,0:T(8,128)(2,1)S(1)}, u32[]{:S(2)}, u32[]{:S(2)}) collective-permute-start(bf16[592,256]{1,0:T(8,128)(2,1)S(1)} %get-tuple-element.90), channel_id=1, source_target_pairs={{0,16},{8,24},{16,0},{24,8},{1,17},{9,25},{17,1},{25,9},{2,18},{10... | collective-permute-start | bytes 909320 | tf_op jit(solution)/shard_map/ppermute | solution.py:658
  (24 other events, 221.6 us)

commit v2 on v1

v2 whole, which is shorter than its diff:
```python
import functools

import jax
import jax.numpy as jnp
from jax import lax
from jax.experimental import pallas as pl
from jax.experimental.pallas import tpu as pltpu
from jax.sharding import PartitionSpec as P

HEADS = 8
EPSILON = 1e-05
CHUNK = 256
QUAD = 256
F32 = jnp.float32
BF16 = jnp.bfloat16
VMEM_LIMIT = 60 << 20
LOSS_DIGITS = 30
LOSS_ZERO = 10
COST = pl.CostEstimate(flops=1000, bytes_accessed=1000, transcendentals=0)


def place():
    rep = lax.axis_index("rep")
    return lax.axis_index("shard"), rep % 2, (rep // 2) % 2


def slots_of(shards):
    ways = shards // 2
    low, high = range(ways // 2), range(ways // 2, ways)
    first = [(z, y, x) for x in (0, 1) for y in (0, 1) for z in low]
    second = [(z, y, x) for y in (0, 1) for x in (0, 1) for z in high]
    return first + second


def nn(left, right):
    return jnp.dot(left, right, preferred_element_type=F32)


def nt(left, right):
    return lax.dot_general(left, right, (((1,), (1,)), ((), ())), preferred_element_type=F32)


def tn(left, right):
    return lax.dot_general(left, right, (((0,), (0,)), ((), ())), preferred_element_type=F32)


def head_lanes():
    lane = lax.broadcasted_iota(jnp.int32, (1, QUAD), 1) // 64
    return [jnp.where(lane == h, 1.0, 0.0).astype(BF16) for h in range(4)]


def block_diagonal():
    rows = lax.broadcasted_iota(jnp.int32, (QUAD, QUAD), 0) // 64
    columns = lax.broadcasted_iota(jnp.int32, (QUAD, QUAD), 1) // 64
    return jnp.where(rows == columns, 1.0, 0.0)


def as_column(row):
    return jnp.broadcast_to(row, (CHUNK, CHUNK)).T


def causal_mask(column, row):
    at = lax.broadcasted_iota(jnp.int32, (CHUNK, CHUNK), 0)
    source = lax.broadcasted_iota(jnp.int32, (CHUNK, CHUNK), 1)
    return jnp.where((column == row) & (source <= at), 1.0, 0.0)


def causal_mask_transposed(column, row):
    source = lax.broadcasted_iota(jnp.int32, (CHUNK, CHUNK), 0)
    at = lax.broadcasted_iota(jnp.int32, (CHUNK, CHUNK), 1)
    return jnp.where((column == row) & (source <= at), 1.0, 0.0)


def per_head(values, reduce, fill):
    lane = lax.broadcasted_iota(jnp.int32, (1, 128), 1)
    first = lane < 64
    tiles = []
    for tile in range(values.shape[1] // 128):
        part = values[:, tile * 128 : (tile + 1) * 128]
        one = reduce(jnp.where(first, part, fill), axis=-1, keepdims=True)
        two = reduce(jnp.where(first, fill, part), axis=-1, keepdims=True)
        tiles.append(jnp.where(first, one, two))
    return jnp.concatenate(tiles, axis=1)


def standardise(values):
    mean = jnp.mean(values, axis=-1, keepdims=True)
    centred = values - mean
    variance = jnp.mean(centred * centred, axis=-1, keepdims=True)
    scale = lax.rsqrt(variance + EPSILON)
    return centred * scale, scale


def norm_backward(gradient, gain, normal, scale):
    upstream = gradient * gain
    one = jnp.mean(upstream, axis=-1, keepdims=True)
    two = jnp.mean(upstream * normal, axis=-1, keepdims=True)
    return (upstream - one - normal * two) * scale


def spread(rows, shards):
    width = 512 // shards
    lane = lax.broadcasted_iota(jnp.int32, (8, 128), 1)
    tiles = [None] * 4
    for s in range(shards):
        tile, offset = divmod(s * width, 128)
        moved = pltpu.roll(rows[s], offset, 1) if offset else rows[s]
        inside = (lane >= offset) & (lane < offset + width)
        tiles[tile] = jnp.where(inside, moved, 0.0 if tiles[tile] is None else tiles[tile])
    return jnp.concatenate(tiles, axis=1)


def digits_of(value):
    lane = lax.broadcasted_iota(jnp.int32, (8, 128), 1)
    scale = jnp.zeros((8, 128), F32)
    for k in range(LOSS_DIGITS):
        scale = jnp.where(lane == k, 8.0 ** (LOSS_ZERO - k), scale)
    shifted = value * scale
    return jnp.floor(shifted) - 8.0 * jnp.floor(shifted * 0.125)


def piece_of(vectors, s, width):
    tile, offset = divmod(s * width, 128)
    part = vectors[:, tile * 128 : (tile + 1) * 128]
    return pltpu.roll(part, 128 - offset, 1) if offset else part


def pack(shards, *refs):
    query, key, value, control, output, expand, contract = refs[:7]
    gain_1, shift_1, gain_2, shift_2, bias_2, bias_1, valid = refs[7:14]
    mixer_ref, branch_ref = refs[14:]
    r = 512 // shards
    _, core, cross = place()

    def write(half, third):
        at = slice(half * 256, half * 256 + 256)
        for m, ref in enumerate(((query, key), (value, control))[third]):
            mixer_ref[m * r : (m + 1) * r] = ref[:, at]
        if third == 0:
            for b in range(4):
                part = expand[:, b * 512 + half * 256 : b * 512 + half * 256 + 256]
                branch_ref[b * r : (b + 1) * r] = part
        else:
            branch_ref[0 : 4 * r] = contract[:, at]
        branch_ref[4 * r : 4 * r + r // 2] = output[third * (r // 2) : (third + 1) * (r // 2), at]

    for half in range(2):
        for third in range(2):
            pl.when((core == half) & (cross == third))(functools.partial(write, half, third))

    row = lax.broadcasted_iota(jnp.int32, (16, 256), 0)
    lane = lax.broadcasted_iota(jnp.int32, (16, 256), 1)
    block = jnp.zeros((16, 256), F32)
    for k, ref in ((0, gain_1), (1, shift_1), (2, gain_2), (3, shift_2), (4, bias_2), (8, bias_1)):
        part = ref[...].astype(F32)
        width = part.shape[1]
        if width < 256:
            part = jnp.concatenate([part, jnp.zeros((1, 256 - width), F32)], axis=1)
        block = jnp.where(row == k, part, block)
    count = jnp.sum(valid[...].astype(F32))
    high = jnp.floor(count / 256.0)
    block = jnp.where((row == 6) & (lane == 0), high, block)
    block = jnp.where((row == 6) & (lane == 1), count - 256.0 * high, block)
    mixer_ref[2 * r : 2 * r + 16] = block.astype(BF16)


def attention_forward(quad, shards, seg_s, x_ref, seg_ref, *refs):
    step = pl.program_id(0)
    r = 512 // shards
    at = slice(quad * QUAD, (quad + 1) * QUAD)
    if quad == 0:
        mine_ref, theirs_ref = refs[:2]
        q_ref, k_ref, v_ref, e_ref, p_ref, s_ref, rz_ref, mix_ref, one_ref, two_ref = refs[2:12]
        w_ref, vec_ref, eb_ref = refs[12:15]
        held, first_state, second_state, total_state, sems = refs[15:]
        weight = lambda m: w_ref[m, :, at]
    else:
        w_ref, vec_ref = refs[:2]
        q_ref, k_ref, v_ref, e_ref, p_ref, s_ref, rz_ref, mix_ref, one_ref, two_ref = refs[2:12]
        first_state, second_state, total_state = refs[12:]
        weight = lambda m: w_ref[m]

    @pl.when(step == 0)
    def _():
        first_state[...] = jnp.zeros_like(first_state)
        second_state[...] = jnp.zeros_like(second_state)
        total_state[...] = jnp.zeros_like(total_state)

    def assemble():
        me, core, cross = place()
        for half, source in enumerate((mine_ref, theirs_ref)):
            column = pl.multiple_of(((core + half) % 2) * 256, 256)
            for slot, (z, y, x) in enumerate(slots_of(shards)):
                owner = me ^ (2 * z + y)
                third = cross ^ x
                for m in range(2):
                    pltpu.make_async_copy(
                        source.at[slot, pl.ds(m * r, r)],
                        w_ref.at[
                            2 * third + m,
                            pl.ds(pl.multiple_of(owner * r, r), r),
                            pl.ds(column, 256),
                        ],
                        sems.at[0],
                    ).start()
                if half == 0 and x == 0:
                    pltpu.make_async_copy(
                        source.at[slot, pl.ds(2 * r, 16)], held.at[owner], sems.at[1]
                    ).start()
        pltpu.make_async_copy(held, held, sems.at[1]).wait()
        own = [held[s].astype(F32) for s in range(shards)]
        vec_ref[...] = spread([part[:8, :128] for part in own], shards)
        width = 2048 // shards
        lane = lax.broadcasted_iota(jnp.int32, (8, 128), 1)
        if width >= 128:
            for s in range(shards):
                eb_ref[:, s * width : (s + 1) * width] = own[s][8:16, :width]
        else:
            for tile in range(16):
                built = jnp.zeros((8, 128), F32)
                for k in range(128 // width):
                    part = own[tile * (128 // width) + k][8:16, :128]
                    moved = pltpu.roll(part, k * width, 1) if k else part
                    built = jnp.where((lane >= k * width) & (lane < (k + 1) * width), moved, built)
                eb_ref[:, tile * 128 : (tile + 1) * 128] = built
        pltpu.make_async_copy(w_ref, w_ref, sems.at[0]).wait()

    if quad == 0:
        pl.when(step == 0)(assemble)

    start = step * CHUNK
    segment_last = seg_s[0, start + CHUNK - 1]
    segment_before = jnp.where(step == 0, -1, seg_s[0, jnp.maximum(start - 1, 0)])
    keep = jnp.where(segment_last == segment_before, 1.0, 0.0)
    row = seg_ref[...].astype(F32)
    column = as_column(row)
    causal = causal_mask(column, row).astype(BF16)
    enters = jnp.where(column == segment_before.astype(F32), 1.0, 0.0)
    leaves = jnp.where(column == segment_last.astype(F32), 1.0, 0.0).astype(BF16)
    lanes = head_lanes()
    diagonal = block_diagonal()

    normal, _ = standardise(x_ref[...].astype(F32))
    normed = (normal * vec_ref[0:1, :] + vec_ref[1:2, :]).astype(BF16)
    queries = nn(normed, weight(0)).astype(BF16)
    keys = nn(normed, weight(1)).astype(BF16)
    values = nn(normed, weight(2)).astype(BF16)
    slots = jnp.exp(nn(normed, weight(3))).astype(BF16)
    q_ref[...] = queries
    k_ref[...] = keys
    v_ref[...] = values
    e_ref[...] = slots
    totals = nn(causal, slots) + enters * total_state[0:1, :]
    total_state[0:1, :] = totals[CHUNK - 1 : CHUNK, :]
    inverse = 1.0 / totals
    rz_ref[...] = inverse
    one = first_state[...].astype(BF16)
    two = second_state[...].astype(BF16)
    one_ref[0] = one
    two_ref[0] = two
    scores = jnp.concatenate(
        [nt(queries * lanes[h], keys).astype(BF16) * causal for h in range(4)], axis=1
    )
    gathered = nn(scores, jnp.concatenate([slots * lanes[h] for h in range(4)], axis=0))
    gathered += enters * nn(queries, one)
    slot_scores = gathered * (inverse * 0.125)
    raised = jnp.exp(slot_scores - per_head(slot_scores, jnp.max, -jnp.inf))
    shares = raised / per_head(raised, jnp.sum, 0.0)
    s_ref[...] = slot_scores.astype(BF16)
    p_ref[...] = shares.astype(BF16)
    scaled = (shares * inverse).astype(BF16)
    mixing = jnp.concatenate(
        [nt(scaled * lanes[h], slots).astype(BF16) * causal for h in range(4)], axis=1
    )
    mixed = nn(mixing, jnp.concatenate([values * lanes[h] for h in range(4)], axis=0))
    mixed += enters * nn(scaled, two)
    mix_ref[...] = mixed.astype(BF16)
    first_state[...] = keep * first_state[...] + diagonal * tn(keys * leaves, slots)
    second_state[...] = keep * second_state[...] + diagonal * tn(slots * leaves, values)


def feed_forward(
    shards,
    tokens,
    x_ref,
    mix_0_ref,
    mix_1_ref,
    teacher_ref,
    valid_ref,
    vec_ref,
    eb_ref,
    count_ref,
    mine_ref,
    theirs_ref,
    out_ref,
    hidden_ref,
    grad_mix_ref,
    keep_1_ref,
    send_1_ref,
    keep_2_ref,
    send_2_ref,
    wo,
    we,
    wc,
    act,
    d_wo,
    d_we,
    d_wc,
    d_vec,
    d_eb,
    loss_ref,
    sems,
):
    step = pl.program_id(0)
    r = 512 // shards
    me, core, cross = place()

    @pl.when(step == 0)
    def _():
        loss_ref[...] = jnp.zeros_like(loss_ref)
        for half, source in enumerate((mine_ref, theirs_ref)):
            column = pl.multiple_of(((core + half) % 2) * 256, 256)
            for slot, (z, y, x) in enumerate(slots_of(shards)):
                owner = me ^ (2 * z + y)
                third = cross ^ x
                pltpu.make_async_copy(
                    source.at[slot, pl.ds(4 * r, r // 2)],
                    wo.at[2 * owner + third, :, pl.ds(column, 256)],
                    sems.at[0],
                ).start()

                def expansion():
                    for b in range(4):
                        pltpu.make_async_copy(
                            source.at[slot, pl.ds(b * r, r)],
                            we.at[
                                b, pl.ds(pl.multiple_of(owner * r, r), r), pl.ds(column, 256)
                            ],
                            sems.at[1],
                        ).start()

                def contraction():
                    pltpu.make_async_copy(
                        source.at[slot, pl.ds(0, 4 * r)],
                        wc.at[
                            pl.ds(pl.multiple_of(owner * 4 * r, 4 * r), 4 * r), pl.ds(column, 256)
                        ],
                        sems.at[2],
                    ).start()

                pl.when(third == 0)(expansion)
                pl.when(third == 1)(contraction)
        for ref in (d_wo, d_we, d_wc, d_vec, d_eb):
            ref[...] = jnp.zeros_like(ref)
        pltpu.make_async_copy(wo, wo, sems.at[0]).wait()
        pltpu.make_async_copy(we, we, sems.at[1]).wait()
        pltpu.make_async_copy(wc, wc, sems.at[2]).wait()

    gain, shift, bias = vec_ref[2:3, :], vec_ref[3:4, :], vec_ref[4:5, :]
    weight_out = wo[...].reshape(512, 512)
    mixed = jnp.concatenate([mix_0_ref[...], mix_1_ref[...]], axis=1)
    hidden = x_ref[...].astype(F32) + nn(mixed, weight_out)
    normal, scale = standardise(hidden)
    normed = (normal * gain + shift).astype(BF16)
    for b in range(4):
        at = slice(b * 512, (b + 1) * 512)
        before = nn(normed, we[b]) + eb_ref[0:1, at]
        act[:, at] = jnp.maximum(before, 0.0).astype(BF16)
    result = hidden + (nn(act[...], wc[...]) + bias)
    out_ref[...] = result.astype(BF16)
    valid = as_column(valid_ref[...].astype(F32))
    valid = jnp.concatenate([valid, valid], axis=1)
    error = result - teacher_ref[...].astype(F32)
    masked = valid * error
    loss_ref[...] += jnp.sum(masked * error)
    count = 256.0 * count_ref[0:1, 0:1] + count_ref[0:1, 1:2]
    grad_result = masked * (tokens / count)
    low = grad_result.astype(BF16)
    d_normed = None
    for b in range(4):
        at = slice(b * 512, (b + 1) * 512)
        active = act[:, at]
        d_wc[at, :] += tn(active, low)
        grad = jnp.where(active > 0, nt(low, wc[at, :]), 0.0)
        grad = grad.astype(BF16)
        d_we[b] += tn(normed, grad)
        d_eb[0:1, at] += jnp.sum(grad.astype(F32), axis=0, keepdims=True)
        part = nt(grad, we[b])
        d_normed = part if d_normed is None else d_normed + part
    d_vec[0:1, :] += jnp.sum(d_normed * normal, axis=0, keepdims=True)
    d_vec[1:2, :] += jnp.sum(d_normed, axis=0, keepdims=True)
    d_vec[2:3, :] += jnp.sum(low.astype(F32), axis=0, keepdims=True)
    grad_hidden = grad_result + norm_backward(d_normed, gain, normal, scale)
    hidden_ref[...] = grad_hidden
    grad_low = grad_hidden.astype(BF16)
    d_wo[...] += tn(mixed, grad_low)
    grad_mix_ref[...] = nt(grad_low, weight_out).astype(BF16)

    @pl.when(step == pl.num_programs(0) - 1)
    def _():
        width = 2048 // shards
        digits = digits_of(loss_ref[...])

        def write(first_ref, second_ref, at):
            for s in range(shards):
                y, z = (me ^ s) & 1, (me ^ s) >> 1
                rows = slice(s * r, (s + 1) * r)
                top = jnp.concatenate([piece_of(d_vec[...], s, r), digits], axis=1)
                if width >= 128:
                    low_rows = d_eb[:, s * width : (s + 1) * width]
                else:
                    low_rows = piece_of(d_eb[...], s, width)
                if low_rows.shape[1] < 256:
                    pad = jnp.zeros((8, 256 - low_rows.shape[1]), F32)
                    low_rows = jnp.concatenate([low_rows, pad], axis=1)
                both = jnp.concatenate([top, low_rows], axis=0).astype(BF16)
                for half in range(2):
                    x = cross ^ half
                    start = s * 4 * r + half * 2 * r
                    first_ref[y, x, z] = d_wc[start : start + 2 * r, at].astype(BF16)
                    for b in range(2):
                        part = d_we[2 * half + b, rows, at]
                        second_ref[x, y, z, b * r : (b + 1) * r, :] = part.astype(BF16)
                    second_ref[x, y, z, 2 * r : 2 * r + 16, :] = both
                    start = s * r + half * (r // 2)
                    part = d_wo[start : start + r // 2, at]
                    second_ref[x, y, z, 2 * r + 16 :, :] = part.astype(BF16)

        left, right = slice(0, 256), slice(256, 512)

        @pl.when(core == 0)
        def _():
            write(keep_1_ref, keep_2_ref, left)
            write(send_1_ref, send_2_ref, right)

        @pl.when(core == 1)
        def _():
            write(keep_1_ref, keep_2_ref, right)
            write(send_1_ref, send_2_ref, left)


def attention_backward(last, shards, seg_s, *refs):
    x_ref, seg_ref, q_ref, k_ref, v_ref, e_ref, p_ref, s_ref, rz_ref, g_ref = refs[:10]
    one_ref, two_ref, w_ref, vec_ref = refs[10:14]
    refs = refs[14:]
    if last:
        part_ref, hidden_ref = refs[:2]
        refs = refs[2:]
    out_ref, keep_ref, send_ref = refs[:3]
    first_state, second_state, total_state, d_w, d_vec = refs[3:]
    step = pl.program_id(0)
    chunks = pl.num_programs(0)
    chunk = chunks - 1 - step
    r = 512 // shards
    me, core, cross = place()

    @pl.when(step == 0)
    def _():
        for ref in (first_state, second_state, total_state, d_w, d_vec):
            ref[...] = jnp.zeros_like(ref)

    start = chunk * CHUNK
    length = chunks * CHUNK
    segment_first = seg_s[0, start]
    segment_before = jnp.where(chunk == 0, -1, seg_s[0, jnp.maximum(start - 1, 0)])
    segment_after = jnp.where(step == 0, -1, seg_s[0, jnp.minimum(start + CHUNK, length - 1)])
    keep = jnp.where(segment_first == segment_after, 1.0, 0.0)
    row = seg_ref[...].astype(F32)
    column = as_column(row)
    causal = causal_mask(column, row).astype(BF16)
    turned = causal_mask_transposed(column, row).astype(BF16)
    enters = jnp.where(column == segment_before.astype(F32), 1.0, 0.0)
    goes_on = jnp.where(column == segment_after.astype(F32), 1.0, 0.0)
    opens = jnp.where(column == segment_first.astype(F32), 1.0, 0.0).astype(BF16)
    lanes = head_lanes()
    diagonal = block_diagonal()

    def heads(values):
        return [values * lanes[h] for h in range(4)]

    def beside(parts):
        return jnp.concatenate(parts, axis=1)

    def stacked(parts):
        return jnp.concatenate(parts, axis=0)

    queries, keys, values, slots = q_ref[...], k_ref[...], v_ref[...], e_ref[...]
    shares, slot_scores = p_ref[...].astype(F32), s_ref[...].astype(F32)
    inverse, grad = rz_ref[...], g_ref[...]
    scaled = shares * inverse
    scaled_low = scaled.astype(BF16)
    one, two = one_ref[0], two_ref[0]
    one_back, two_back = first_state[...].astype(BF16), second_state[...].astype(BF16)
    grad_heads, slot_heads, value_heads = heads(grad), heads(slots), heads(values)
    slot_stack = stacked(slot_heads)

    d_mixing = beside([nt(part, values).astype(BF16) * causal for part in grad_heads])
    d_scaled = nn(d_mixing, slot_stack) + enters * nt(grad, two)
    d_shares = d_scaled * inverse
    product = shares * d_shares
    d_scores = product - shares * per_head(product, jnp.sum, 0.0)
    d_gathered = d_scores * inverse
    d_totals = -(d_scaled * scaled + d_scores * slot_scores) * inverse
    d_low = (d_gathered * 0.125).astype(BF16)
    d_low_heads = heads(d_low)

    d_raw = beside([nt(part, slots).astype(BF16) * causal for part in d_low_heads])
    d_queries = nn(d_raw, stacked(heads(keys))) + enters * nt(d_low, one)
    d_raw_t = beside([nt(part, d_low).astype(BF16) * turned for part in slot_heads])
    d_keys = nn(d_raw_t, stacked(heads(queries))) + goes_on * nt(slots, one_back)
    mixing_t = beside([nt(part, scaled_low).astype(BF16) * turned for part in slot_heads])
    d_values = nn(mixing_t, stacked(grad_heads)) + goes_on * nn(slots, two_back)
    scores_t = beside([nt(part, queries).astype(BF16) * turned for part in heads(keys)])
    d_slots = nn(scores_t, stacked(d_low_heads))
    d_mixing_t = beside([nt(part, grad).astype(BF16) * turned for part in value_heads])
    d_slots += nn(d_mixing_t, stacked(heads(scaled_low)))
    d_totals_low = d_totals.astype(BF16)
    rest = (d_totals - d_totals_low.astype(F32)).astype(BF16)
    sums = nn(turned, d_totals_low) + nn(turned, rest) + goes_on * total_state[0:1, :]
    d_slots += goes_on * (nn(keys, one_back) + nt(values, two_back)) + sums
    d_control = d_slots * slots.astype(F32)

    total_state[0:1, :] = sums[0:1, :]
    first_state[...] = keep * first_state[...] + diagonal * tn(queries * opens, d_low)
    second_state[...] = keep * second_state[...] + diagonal * tn(scaled_low * opens, grad)

    normal, scale = standardise(x_ref[...].astype(F32))
    gain = vec_ref[0:1, :]
    normed = (normal * gain + vec_ref[1:2, :]).astype(BF16)
    grads = [part.astype(BF16) for part in (d_queries, d_keys, d_values, d_control)]
    d_w[...] += tn(normed, beside(grads))
    d_normed = sum(nt(grads[m], w_ref[m]) for m in range(4))
    if last:
        d_normed += part_ref[...]
        d_vec[0:1, :] += jnp.sum(d_normed * normal, axis=0, keepdims=True)
        d_vec[1:2, :] += jnp.sum(d_normed, axis=0, keepdims=True)
        out_ref[...] = hidden_ref[...] + norm_backward(d_normed, gain, normal, scale)
    else:
        out_ref[...] = d_normed

    @pl.when(step == chunks - 1)
    def _():
        def write(ref, half):
            for s in range(shards):
                y, z = (me ^ s) & 1, (me ^ s) >> 1
                for m in range(4):
                    x = cross ^ (m // 2)
                    lead = (x, y, z) if last else (y, x, z)
                    at = slice(m * QUAD + half * 128, m * QUAD + half * 128 + 128)
                    part = d_w[s * r : (s + 1) * r, at].astype(BF16)
                    ref[(*lead, slice((m % 2) * r, (m % 2 + 1) * r), slice(None))] = part
                for x in range(2):
                    lead = (x, y, z) if last else (y, x, z)
                    top = piece_of(d_vec[...], s, r)
                    both = jnp.concatenate([top, jnp.zeros_like(top)], axis=0)
                    ref[(*lead, slice(2 * r, 2 * r + 16), slice(None))] = both.astype(BF16)

        @pl.when(core == 0)
        def _():
            write(keep_ref, 0)
            write(send_ref, 1)

        @pl.when(core == 1)
        def _():
            write(keep_ref, 1)
            write(send_ref, 0)


def whole(shape):
    return pl.BlockSpec(shape, lambda *_: (0,) * len(shape))


def anywhere():
    return pl.BlockSpec(memory_space=pl.ANY)


def shaped(shape, dtype):
    return jax.ShapeDtypeStruct(shape, dtype)


def params():
    return pltpu.CompilerParams(
        dimension_semantics=("arbitrary",), vmem_limit_bytes=VMEM_LIMIT
    )


def call_pack(shards, matrices, vectors, valid):
    r = 512 // shards
    operands = [*matrices, *[v[None] for v in vectors], valid]
    mixer, branch = (2 * r + 16, 256), (4 * r + r // 2, 256)
    return pl.pallas_call(
        functools.partial(pack, shards),
        grid=(1,),
        in_specs=[whole(v.shape) for v in operands],
        out_specs=[whole(mixer), whole(branch)],
        out_shape=[shaped(mixer, BF16), shaped(branch, BF16)],
        compiler_params=params(),
        cost_estimate=COST,
        name="pack",
    )(*operands)


def call_forward(quad, shards, segments, x, operands):
    length = x.shape[0]
    chunks = length // CHUNK
    wide = pl.BlockSpec((CHUNK, 512), lambda c, *_: (c, 0))
    tile = pl.BlockSpec((CHUNK, QUAD), lambda c, *_: (c, 0))
    state = pl.BlockSpec((1, QUAD, QUAD), lambda c, *_: (c, 0, 0))
    low = shaped((length, QUAD), BF16)
    states = shaped((chunks, QUAD, QUAD), BF16)
    if quad == 0:
        in_specs = [anywhere(), anywhere()]
        out_specs = [whole((4, 512, 512)), whole((8, 512)), whole((8, 2048))]
        out_shape = [shaped((4, 512, 512), BF16), shaped((8, 512), F32), shaped((8, 2048), F32)]
        first = [pltpu.VMEM((shards, 16, 256), BF16)]
        last = [pltpu.SemaphoreType.DMA((2,))]
    else:
        in_specs = [pl.BlockSpec((4, 512, QUAD), lambda c, *_: (0, 0, 1)), whole((8, 512))]
        out_specs, out_shape, first, last = [], [], [], []
    grid_spec = pltpu.PrefetchScalarGridSpec(
        num_scalar_prefetch=1,
        grid=(chunks,),
        in_specs=[wide, pl.BlockSpec((1, CHUNK), lambda c, *_: (0, c)), *in_specs],
        out_specs=[tile] * 8 + [state] * 2 + out_specs,
        scratch_shapes=first
        + [
            pltpu.VMEM((QUAD, QUAD), F32),
            pltpu.VMEM((QUAD, QUAD), F32),
            pltpu.VMEM((8, QUAD), F32),
        ]
        + last,
    )
    return pl.pallas_call(
        functools.partial(attention_forward, quad, shards),
        grid_spec=grid_spec,
        out_shape=[low] * 6 + [shaped((length, QUAD), F32), low, states, states] + out_shape,
        compiler_params=params(),
        cost_estimate=COST,
        name=f"attention_forward_{quad}",
    )(segments, x, segments, *operands)


def call_feed_forward(shards, tokens, *operands):
    length = operands[0].shape[0]
    chunks = length // CHUNK
    r = 512 // shards
    tile = lambda width: pl.BlockSpec((CHUNK, width), lambda c: (c, 0))
    first = (2, 2, shards // 2, 2 * r, 256)
    second = (2, 2, shards // 2, 2 * r + 16 + r // 2, 256)
    return pl.pallas_call(
        functools.partial(feed_forward, shards, tokens),
        grid=(chunks,),
        in_specs=[
            tile(512),
            tile(QUAD),
            tile(QUAD),
            tile(512),
            pl.BlockSpec((1, CHUNK), lambda c: (0, c)),
            whole((8, 512)),
            whole((8, 2048)),
            whole((1, 2)),
            anywhere(),
            anywhere(),
        ],
        out_specs=[tile(512)] * 3 + [whole(first)] * 2 + [whole(second)] * 2,
        out_shape=[
            shaped((length, 512), BF16),
            shaped((length, 512), F32),
            shaped((length, 512), BF16),
            *[shaped(first, BF16)] * 2,
            *[shaped(second, BF16)] * 2,
        ],
        scratch_shapes=[
            pltpu.VMEM((2 * shards, r // 2, 512), BF16),
            pltpu.VMEM((4, 512, 512), BF16),
            pltpu.VMEM((2048, 512), BF16),
            pltpu.VMEM((CHUNK, 2048), BF16),
            pltpu.VMEM((512, 512), F32),
            pltpu.VMEM((4, 512, 512), F32),
            pltpu.VMEM((2048, 512), F32),
            pltpu.VMEM((8, 512), F32),
            pltpu.VMEM((8, 2048), F32),
            pltpu.VMEM((8, 128), F32),
            pltpu.SemaphoreType.DMA((3,)),
        ],
        compiler_params=params(),
        cost_estimate=COST,
        name="feed_forward",
    )(*operands)


def call_backward(quad, shards, segments, x, saved, grad_mix, states, weights, vectors, extra):
    length = x.shape[0]
    chunks = length // CHUNK
    r = 512 // shards
    last = quad == 1
    back = lambda c: chunks - 1 - c
    wide = pl.BlockSpec((CHUNK, 512), lambda c, *_: (back(c), 0))
    own = pl.BlockSpec((CHUNK, QUAD), lambda c, *_: (back(c), 0))
    tile = pl.BlockSpec((CHUNK, QUAD), lambda c, *_: (back(c), quad))
    state = pl.BlockSpec((1, QUAD, QUAD), lambda c, *_: (back(c), 0, 0))
    payload = (2, 2, shards // 2, 2 * r + 16, 128)
    grid_spec = pltpu.PrefetchScalarGridSpec(
        num_scalar_prefetch=1,
        grid=(chunks,),
        in_specs=[
            wide,
            pl.BlockSpec((1, CHUNK), lambda c, *_: (0, back(c))),
            *[own] * 7,
            tile,
            *[state] * 2,
            pl.BlockSpec((4, 512, QUAD), lambda c, *_: (0, 0, quad)),
            whole((8, 512)),
            *[wide] * len(extra),
        ],
        out_specs=[wide, whole(payload), whole(payload)],
        scratch_shapes=[
            pltpu.VMEM((QUAD, QUAD), F32),
            pltpu.VMEM((QUAD, QUAD), F32),
            pltpu.VMEM((8, QUAD), F32),
            pltpu.VMEM((512, 4 * QUAD), F32),
            pltpu.VMEM((8, 512), F32),
        ],
    )
    return pl.pallas_call(
        functools.partial(attention_backward, last, shards),
        grid_spec=grid_spec,
        out_shape=[shaped((length, 512), F32), shaped(payload, BF16), shaped(payload, BF16)],
        compiler_params=params(),
        cost_estimate=COST,
        name=f"attention_backward_{quad}",
    )(segments, x, segments, *saved, grad_mix, *states, weights, vectors, *extra)


def swap(value, axis, bit):
    n = lax.axis_size(axis)
    return lax.ppermute(value, axis, [(i, i ^ bit) for i in range(n)])


def bit_groups(shards):
    bits = shards.bit_length() - 1
    return [(low, min(2, bits - low)) for low in range(1, bits, 2)]


def after(value, *others):
    return lax.optimization_barrier((value, *others))[0]


def add_low(*parts):
    return sum(part.astype(F32) for part in parts).astype(BF16)


def local(
    inputs,
    segments,
    valid_mask,
    teacher,
    query_weight,
    key_weight,
    value_weight,
    control_weight,
    output_weight,
    gain_first,
    shift_first,
    expand_weight,
    expand_bias,
    contract_weight,
    contract_bias,
    gain_second,
    shift_second,
):
    _, length, width = inputs.shape
    shards, reps = lax.axis_size("shard"), lax.axis_size("rep")
    r = width // shards
    core = lax.axis_index("rep") % 2
    cross = (lax.axis_index("rep") // 2) % 2
    groups = bit_groups(shards)

    matrices = (query_weight, key_weight, value_weight, control_weight, output_weight)
    matrices += (expand_weight, contract_weight)
    biases = (gain_first, shift_first, gain_second, shift_second, contract_bias, expand_bias)
    mixer, branch = call_pack(shards, matrices, biases, valid_mask)

    def along_z(payload):
        held = [payload[None]]
        for low, bits in groups:
            if len(held) > 1:
                held = [jnp.concatenate(held, axis=0)]
            held += [swap(held[0], "shard", a << low) for a in range(1, 1 << bits)]
        return held

    def halves(held):
        half = shards // 4
        if len(held) == 4:
            groups_of = [[], held[:2], held[2:]]
            return jnp.concatenate(held[:2], axis=0), jnp.concatenate(held[2:], axis=0)
        joined = jnp.concatenate(held, axis=0)
        return joined[:half], joined[half:]

    def step_one(first, second):
        return swap(first, "shard", 1), swap(second, "rep", 2)

    def join(first, second, arrived):
        return jnp.concatenate([first, arrived[0]]), jnp.concatenate([second, arrived[1]])

    def step_two(first, second):
        return swap(first, "rep", 2), swap(second, "shard", 1)

    held_a = along_z(mixer)
    branch = after(branch, held_a[1:])
    held_b = along_z(branch)
    first, second = halves(held_a)
    arrived = step_one(first, second)
    first, second = join(first, second, arrived)
    arrived = step_two(first, second)
    mine_a = jnp.concatenate([first, arrived[0], second, arrived[1]])
    theirs_a = swap(mine_a, "rep", 1)

    first, second = halves(after(held_b, arrived))
    pending = step_one(first, second)

    own_slots = [n for n, slot in enumerate(slots_of(shards)) if slot[2] == 0]
    count = sum(
        part[n : n + 1, 2 * r + 6, :2].astype(F32) for part in (mine_a, theirs_a) for n in own_slots
    )
    bit = 2
    while bit < reps:
        count = count + swap(count, "rep", bit)
        bit *= 2

    x = inputs.reshape(length, width)
    forward_0 = call_forward(0, shards, segments, after(x, first, second), (mine_a, theirs_a))
    weights, vectors, bias = forward_0[10:]
    first, second = join(first, second, after(pending, forward_0[7]))
    pending = step_two(first, second)
    vectors = after(vectors, first, second)
    forward_1 = call_forward(1, shards, segments, x, (weights, vectors))
    mixed = (forward_0[7], forward_1[7])
    pending = after(pending, forward_1[7])
    mine_b = jnp.concatenate([first, pending[0], second, pending[1]])
    theirs_b = swap(mine_b, "rep", 1)

    layer_out, grad_hidden, grad_mix, keep_c, send_c, keep_e, send_e = call_feed_forward(
        shards,
        float(length * shards * reps),
        x,
        *mixed,
        teacher.reshape(length, width),
        valid_mask,
        vectors,
        bias,
        count,
        mine_b,
        theirs_b,
    )

    def core_swap(keep, send):
        return keep, swap(send, "rep", 1)

    def split(parts):
        return add_low(*(part[0] for part in parts)), add_low(*(part[1] for part in parts))

    def cross_first(parts):
        keep, send = split(parts)
        return keep, swap(send, "rep", 2)

    def row_first(parts):
        keep, send = split(parts)
        return keep, swap(send, "shard", 1)

    def z_stage(parts_list):
        current = parts_list
        for low, bits in reversed(groups):
            span = 1 << (low - 1)
            pieces = [
                jnp.concatenate(
                    [
                        add_low(*(part[a * span : (a + 1) * span] for part in parts))
                        for parts in current
                    ],
                    axis=1,
                )
                for a in range(1 << bits)
            ]
            arrived = [swap(pieces[a], "shard", a << low) for a in range(1, 1 << bits)]
            current = [(pieces[0], *arrived)]
        return current[0]

    def finish(parts):
        total = add_low(*(part[0] for part in parts))
        bit = 4
        while bit < reps:
            total = add_low(total, swap(total, "rep", bit))
            bit *= 2
        over = swap(total, "rep", 2)
        near = jnp.where(cross == 0, total, over)
        far = jnp.where(cross == 0, over, total)
        both = jnp.stack([near, far])
        sibling = swap(both, "rep", 1)
        left = jnp.where(core == 0, both, sibling)
        right = jnp.where(core == 0, sibling, both)
        return jnp.concatenate([left, right], axis=2).astype(F32)

    def back(quad, saved, grad_mix, extra):
        return call_backward(
            quad, shards, segments, x, saved[:7], grad_mix, saved[8:10], weights, vectors, extra
        )

    c_parts = row_first(core_swap(keep_c, send_c))
    e_parts = cross_first(core_swap(keep_e, send_e))
    grad_mix = after(grad_mix, c_parts[0], e_parts[0])
    part, keep_0, send_0 = back(0, forward_0, grad_mix, ())
    c_parts = (c_parts[0], after(c_parts[1], part))
    e_parts = (e_parts[0], after(e_parts[1], part))
    c_parts, e_parts = cross_first(c_parts), row_first(e_parts)
    parts_0 = core_swap(keep_0, send_0)
    part = after(part, c_parts[0], e_parts[0])
    grad_inputs, keep_1, send_1 = back(1, forward_1, grad_mix, (part, grad_hidden))

    parts_0 = (parts_0[0], after(parts_0[1], grad_inputs))
    c_parts = (c_parts[0], after(c_parts[1], grad_inputs))
    e_parts = (e_parts[0], after(e_parts[1], grad_inputs))
    parts_1 = core_swap(keep_1, send_1)
    f_parts = z_stage([c_parts, e_parts])
    parts_0, parts_1 = row_first(parts_0), cross_first(parts_1)
    parts_0, parts_1 = cross_first(parts_0), row_first(parts_1)
    q_parts = z_stage([parts_0, parts_1])
    final_f = finish(f_parts)
    final_q = finish(q_parts)

    grad_contract = final_f[:, : 2 * r].reshape(4 * r, width)
    rest = final_f[:, 2 * r :]
    grad_expand = jnp.concatenate(
        [rest[h, b * r : (b + 1) * r] for h in range(2) for b in range(2)], axis=1
    )
    vec_f = rest[0, 2 * r : 2 * r + 16, :256]
    grad_output = rest[:, 2 * r + 16 :].reshape(r, width)
    mats = []
    for m in range(4):
        parts = [
            final_q[m // 2, q * (2 * r + 16) + (m % 2) * r : q * (2 * r + 16) + (m % 2 + 1) * r]
            for q in range(2)
        ]
        mats.append(jnp.concatenate(parts, axis=1))
    vec_1 = final_q[0, 4 * r + 32 - 16 : 4 * r + 32, :128]
    powers = jnp.array([8.0 ** (k - LOSS_ZERO) for k in range(LOSS_DIGITS)], F32)
    loss_sum = jnp.sum(vec_f[0, 128 : 128 + LOSS_DIGITS] * powers)
    loss_value = loss_sum / (2.0 * (256.0 * count[0, 0] + count[0, 1]))
    return (
        layer_out.reshape(inputs.shape),
        grad_inputs.reshape(inputs.shape),
        loss_value,
        *mats,
        grad_output,
        vec_1[0, :r],
        vec_1[1, :r],
        grad_expand,
        vec_f[8, : 4 * r],
        grad_contract,
        vec_f[2, :r],
        vec_f[0, :r],
        vec_f[1, :r],
    )


def solution(mesh):
    every = P(("rep", "shard"), None, None)
    every_row = P(("rep", "shard"), None)
    matrix, vector = P("shard", None), P("shard")
    in_specs = (
        every,
        every_row,
        every_row,
        every,
        *[matrix] * 5,
        *[vector] * 2,
        matrix,
        vector,
        matrix,
        *[vector] * 3,
    )
    out_specs = (
        every,
        every,
        P(),
        *[matrix] * 5,
        *[vector] * 2,
        matrix,
        vector,
        matrix,
        *[vector] * 3,
    )
    return jax.shard_map(local, mesh=mesh, in_specs=in_specs, out_specs=out_specs, check_vma=False)
```

time: 326 us -> 231 us (0.71)
  waiting for transfers between devices: 165 us -> 60.9 us
  local copies, waits for them, and re-layouts: 5.47 us -> 11.8 us
  Pallas kernels: 86.6 us -> 92 us
    ppermute x37 -> x39, waiting for transfers between devices: 165 us -> 60.9 us  [swap(): return lax.ppermute(value, axis, [(i, i ^ bit) for i in range(n)])]
    unnamed x49 -> x52, local copies, waits for them, and re-layouts: 0.36 us -> 8.65 us
    ppermute x3 -> x0, starting transfers between devices: 5.56 us -> none  [swap_both(): return lax.ppermute(value, ('rep', 'shard'), pairs)]
    pallas_call x2 -> x4, Pallas kernels: 51.2 us -> 56.4 us  [the longest x1 29.3 us: call_feed_forward(): pl.pallas_call(functools.partial(feed_forward, shards, tokens), grid=(chu...]
    ppermute x37 -> x39, starting transfers between devices: 41.1 us -> 46.2 us  [swap(): return lax.ppermute(value, axis, [(i, i ^ bit) for i in range(n)])]
  transfers between devices with their start and end apart: 40 -> 39, of which waited for: 22 -> 23; matrix products, arithmetic and copies ran while one was open for 4% -> 7% of each run, Pallas kernels for 12% -> 19%
where the time goes in v2:
time: 231 us; the launch traced here: 229 us
  Pallas kernels  92 us (40%)
  waiting for transfers between devices  60.9 us (26%)
  starting transfers between devices  46.2 us (20%)
  other arithmetic  14.1 us (6%)
  local copies, waits for them, and re-layouts  11.8 us (5%)
  between operations  4.19 us (2%)
    ppermute x39, waiting for transfers between devices, swap(): return lax.ppermute(value, axis, [(i, i ^ bit) for i in range(n)])  60.9 us
    ppermute x39, starting transfers between devices, swap(): return lax.ppermute(value, axis, [(i, i ^ bit) for i in range(n)])  46.2 us
    pallas_call x2, Pallas kernels, call_backward(): pl.pallas_call(functools.partial(attention_backward, last, shards), grid_...  35.6 us
    pallas_call x1, Pallas kernels, call_feed_forward(): pl.pallas_call(functools.partial(feed_forward, shards, tokens), grid=(chu...  29.3 us
    pallas_call x2, Pallas kernels, call_forward(): pl.pallas_call(functools.partial(attention_forward, quad, shards), grid_s...  25 us
    unnamed x52, local copies, waits for them, and re-layouts  8.65 us
    convert_element_type x12, other arithmetic, add_low(): return sum((part.astype(F32) for part in parts)).astype(BF16)  5.47 us
  transfers between devices with their start and end apart: 39, of which 23 were waited for; matrix products, arithmetic and copies ran while one was open for 7% of the time, Pallas kernels for 19%

profile of v2, /device:TPU:13, one launch (start us, length us, event | category | flops | bytes accessed | tf_op | source)
XLA Modules:
  0.0 229.2 jit_solution(9958872310749152552)
XLA Ops:
  1.9 2.0 pack.1
  4.1 2.3 %collective-permute-start.1 = (bf16[1,144,256]{2,1,0:T(8,128)(2,1)}, bf16[1,144,256]{2,1,0:T(8,128)(2,1)S(1)}, u32[]{:S(2)}, u32[]{:S(2)}) collective-permute-start(bf16[1,144,256]{2,1,0:T(8,128)(2,1)} %bitcast.220), channel_id=1, source_target_pairs={{0,4},{1,5},{2,6},{3,7},{4,0},{5,1},{6,2},{7,3},{8,12},{9,13},{10,... | collective-permute-start | bytes 221192 | tf_op jit(solution)/shard_map/ppermute | solution.py:737
  9.5 2.8 %collective-permute-done.2 = bf16[1,144,256]{2,1,0:T(8,128)(2,1)S(1)} collective-permute-done((bf16[1,144,256]{2,1,0:T(8,128)(2,1)}, bf16[1,144,256]{2,1,0:T(8,128)(2,1)S(1)}, u32[]{:S(2)}, u32[]{:S(2)}) %collective-permute-start.2) | collective-permute-done | bytes 73760 | tf_op jit(solution)/shard_map/ppermute | solution.py:737
  15.0 1.5 collective-permute-done.8
  16.8 6.5 %collective-permute-done.7 = bf16[4,144,256]{2,1,0:T(8,128)(2,1)S(1)} collective-permute-done((bf16[4,144,256]{2,1,0:T(8,128)(2,1)S(1)}, bf16[4,144,256]{2,1,0:T(8,128)(2,1)S(1)}, u32[]{:S(2)}, u32[]{:S(2)}) %collective-permute-start.7) | collective-permute-done | bytes 294944 | tf_op jit(solution)/shard_map/ppermute | solution.py:737
  23.4 5.0 %collective-permute-start.10 = (bf16[16,144,256]{2,1,0:T(8,128)(2,1)S(1)}, bf16[16,144,256]{2,1,0:T(8,128)(2,1)}, u32[]{:S(2)}, u32[]{:S(2)}) collective-permute-start(bf16[16,144,256]{2,1,0:T(8,128)(2,1)S(1)} %constant_dynamic-update-slice_fusion.4.refs_0_), channel_id=1, source_target_pairs={{0,8},{8,0},{16,24},{24,16},{1,9},{9,1},{17,25},{25,17},{2,10},{10... | collective-permute-start | bytes 3538952 | tf_op jit(solution)/shard_map/ppermute | solution.py:737
  29.1 1.8 collective-permute-start.4
  31.1 3.7 %collective-permute-done.3 = bf16[1,288,256]{2,1,0:T(8,128)(2,1)S(1)} collective-permute-done((bf16[1,288,256]{2,1,0:T(8,128)(2,1)S(1)}, bf16[1,288,256]{2,1,0:T(8,128)(2,1)S(1)}, u32[]{:S(2)}, u32[]{:S(2)}) %collective-permute-start.3) | collective-permute-done | bytes 147488 | tf_op jit(solution)/shard_map/ppermute | solution.py:737
  34.8 5.3 %collective-permute-done.4 = bf16[1,288,256]{2,1,0:T(8,128)(2,1)S(1)} collective-permute-done((bf16[1,288,256]{2,1,0:T(8,128)(2,1)S(1)}, bf16[1,288,256]{2,1,0:T(8,128)(2,1)S(1)}, u32[]{:S(2)}, u32[]{:S(2)}) %collective-permute-start.4) | collective-permute-done | bytes 147488 | tf_op jit(solution)/shard_map/ppermute | solution.py:737
  40.1 4.2 %collective-permute-done.5 = bf16[1,288,256]{2,1,0:T(8,128)(2,1)S(1)} collective-permute-done((bf16[1,288,256]{2,1,0:T(8,128)(2,1)S(1)}, bf16[1,288,256]{2,1,0:T(8,128)(2,1)S(1)}, u32[]{:S(2)}, u32[]{:S(2)}) %collective-permute-start.5) | collective-permute-done | bytes 147488 | tf_op jit(solution)/shard_map/ppermute | solution.py:737
  49.2 13.3 %attention_forward_0.1 = (bf16[1024,256]{1,0:T(8,128)(2,1)}, bf16[1024,256]{1,0:T(8,128)(2,1)}, bf16[1024,256]{1,0:T(8,128)(2,1)}, bf16[1024,256]{1,0:T(8,128)(2...) custom-call(s32[1,1024]{1,0:T(1,128)} %refs_1_.5, ...), custom_call_target="tpu_custom_call" | custom-call | flops 1000 | bytes 1000 | tf_op jit(solution)/shard_map/attention_forward_0/pallas_call | solution.py:633
  63.9 1.7 constant_dynamic-update-slice_fusion.23
  65.7 11.7 %attention_forward_1.1 = (bf16[1024,256]{1,0:T(8,128)(2,1)}, bf16[1024,256]{1,0:T(8,128)(2,1)}, bf16[1024,256]{1,0:T(8,128)(2,1)}, bf16[1024,256]{1,0:T(8,128)(2...) custom-call(s32[1,1024]{1,0:T(1,128)} %refs_1_.5, ...), custom_call_target="tpu_custom_call" | custom-call | flops 1000 | bytes 1000 | tf_op jit(solution)/shard_map/attention_forward_1/pallas_call | solution.py:633
  79.9 3.0 %collective-permute-start.16 = (bf16[16,288,256]{2,1,0:T(8,128)(2,1)S(1)}, bf16[16,288,256]{2,1,0:T(8,128)(2,1)S(1)}, u32[]{:S(2)}, u32[]{:S(2)}) collective-permute-start(bf16[16,288,256]{2,1,0:T(8,128)(2,1)S(1)} %constant_dynamic-update-slice_fusion.18.mine_ref), channel_id=1, source_target_pairs={{0,8},{8,0},{16,24},{24,16},{1,9},{9,1},{17,25},{25,17},{2,10},{10... | collective-permute-start | bytes 7077896 | tf_op jit(solution)/shard_map/ppermute | solution.py:737
  83.9 2.2 collective-permute-done.13
  88.5 29.3 %feed_forward.1 = (bf16[1024,512]{1,0:T(8,128)(2,1)}, f32[1024,512]{1,0:T(8,128)}, bf16[1024,512]{1,0:T(8,128)(2,1)}, bf16[2,2,4,128,256]{4,3,2,1,0:T(8,128)(2,1...) custom-call(bf16[1024,512]{1,0:T(8,128)(2,1)} %bitcast.215, ...), custom_call_target="tpu_custom_call" | custom-call | flops 1000 | bytes 1000 | tf_op jit(solution)/shard_map/feed_forward/pallas_call | solution.py:650
  117.9 17.6 %attention_backward_0.1 = (f32[1024,512]{1,0:T(8,128)}, bf16[2,2,4,144,128]{4,3,2,1,0:T(8,128)(2,1)}, bf16[2,2,4,144,128]{4,3,2,1,0:T(8,128)(2,1)}) custom-call(s32[1,1024]{1,0:T(1,128)} %refs_1_.5, bf16[1024,512]{1,0:T(8,128)(2,1)} %bitcast.216, s32[1,1024]{1,0:T(1,128)} %refs_1_.5, bf16[1024,256]{1,0:T(8,128)(2,1)} %get-tuple-element.99.refs_2_, ...), custom_call_target="tpu_custom_call" | custom-call | flops 1000 | bytes 1000 | tf_op jit(solution)/shard_map/attention_backward_0/pallas_call | solution.py:725
  136.5 18.0 %attention_backward_1.1 = (f32[1024,512]{1,0:T(8,128)}, bf16[2,2,4,144,128]{4,3,2,1,0:T(8,128)(2,1)}, bf16[2,2,4,144,128]{4,3,2,1,0:T(8,128)(2,1)}) custom-call(s32[1,1024]{1,0:T(1,128)} %refs_1_.5, bf16[1024,512]{1,0:T(8,128)(2,1)} %bitcast.217, s32[1,1024]{1,0:T(1,128)} %refs_1_.5, bf16[1024,256]{1,0:T(8,128)(2,1)} %get-tuple-element.89.refs_2_, ...), custom_call_target="tpu_custom_call" | custom-call | flops 1000 | bytes 1000 | tf_op jit(solution)/shard_map/attention_backward_1/pallas_call | solution.py:725
  158.4 6.5 %collective-permute-done.29 = bf16[2,4,144,128]{3,2,1,0:T(8,128)(2,1)S(1)} collective-permute-done((bf16[2,4,144,128]{3,2,1,0:T(8,128)(2,1)}, bf16[2,4,144,128]{3,2,1,0:T(8,128)(2,1)S(1)}, u32[]{:S(2)}, u32[]{:S(2)}) %collective-permute-start.29) | collective-permute-done | bytes 294944 | tf_op jit(solution)/shard_map/ppermute | solution.py:737
  169.7 1.7 collective-permute-done.33
  171.5 1.6 fusion.3
  173.1 1.5 collective-permute-start.18
  175.2 2.4 %collective-permute-start.35 = (bf16[1,288,128]{2,1,0:T(8,128)(2,1)S(1)}, bf16[1,288,128]{2,1,0:T(8,128)(2,1)S(1)}, u32[]{:S(2)}, u32[]{:S(2)}) collective-permute-start(bf16[1,288,128]{2,1,0:T(8,128)(2,1)S(1)} %pad_maximum_fusion.16), channel_id=1, source_target_pairs={{0,4},{1,5},{2,6},{3,7},{4,0},{5,1},{6,2},{7,3},{8,12},{9,13},{10,... | collective-permute-start | bytes 221192 | tf_op jit(solution)/shard_map/ppermute | solution.py:737
  180.3 2.6 %collective-permute-done.36 = bf16[1,288,128]{2,1,0:T(8,128)(2,1)S(1)} collective-permute-done((bf16[1,288,128]{2,1,0:T(8,128)(2,1)S(1)}, bf16[1,288,128]{2,1,0:T(8,128)(2,1)S(1)}, u32[]{:S(2)}, u32[]{:S(2)}) %collective-permute-start.36) | collective-permute-done | bytes 73760 | tf_op jit(solution)/shard_map/ppermute | solution.py:737
  185.4 5.1 %collective-permute-done.21 = bf16[2,4,176,256]{3,2,1,0:T(8,128)(2,1)S(1)} collective-permute-done((bf16[2,4,176,256]{3,2,1,0:T(8,128)(2,1)S(1)}, bf16[2,4,176,256]{3,2,1,0:T(8,128)(2,1)S(1)}, u32[]{:S(2)}, u32[]{:S(2)}) %collective-permute-start.21) | collective-permute-done | bytes 720928 | tf_op jit(solution)/shard_map/ppermute | solution.py:737
  192.2 5.9 %collective-permute-start.38 = (bf16[2,288,128]{2,1,0:T(8,128)(2,1)S(1)}, bf16[2,288,128]{2,1,0:T(8,128)(2,1)S(1)}, u32[]{:S(2)}, u32[]{:S(2)}) collective-permute-start(bf16[2,288,128]{2,1,0:T(8,128)(2,1)S(1)} %pad_maximum_fusion.10), channel_id=1, source_target_pairs={{0,8},{8,0},{16,24},{24,16},{1,9},{9,1},{17,25},{25,17},{2,10},{10... | collective-permute-start | bytes 442376 | tf_op jit(solution)/shard_map/ppermute | solution.py:737
  198.2 1.6 collective-permute-start.23
  201.3 2.0 collective-permute-done.23
  203.3 2.9 %collective-permute-done.24 = bf16[1,304,256]{2,1,0:T(8,128)(2,1)S(1)} collective-permute-done((bf16[1,304,256]{2,1,0:T(8,128)(2,1)S(1)}, bf16[1,304,256]{2,1,0:T(8,128)(2,1)S(1)}, u32[]{:S(2)}, u32[]{:S(2)}) %collective-permute-start.24) | collective-permute-done | bytes 155680 | tf_op jit(solution)/shard_map/ppermute | solution.py:737
  206.2 2.9 %collective-permute-done.25 = bf16[1,304,256]{2,1,0:T(8,128)(2,1)S(1)} collective-permute-done((bf16[1,304,256]{2,1,0:T(8,128)(2,1)S(1)}, bf16[1,304,256]{2,1,0:T(8,128)(2,1)S(1)}, u32[]{:S(2)}, u32[]{:S(2)}) %collective-permute-start.25) | collective-permute-done | bytes 155680 | tf_op jit(solution)/shard_map/ppermute | solution.py:737
  209.3 4.2 %collective-permute-done.26 = bf16[304,256]{1,0:T(8,128)(2,1)S(1)} collective-permute-done((bf16[304,256]{1,0:T(8,128)(2,1)S(1)}, bf16[304,256]{1,0:T(8,128)(2,1)S(1)}, u32[]{:S(2)}, u32[]{:S(2)}) %collective-permute-start.26) | collective-permute-done | bytes 155680 | tf_op jit(solution)/shard_map/ppermute | solution.py:737
  213.6 8.1 %collective-permute-start.27 = (bf16[2,304,256]{2,1,0:T(8,128)(2,1)S(1)}, bf16[2,304,256]{2,1,0:T(8,128)(2,1)S(1)}, u32[]{:S(2)}, u32[]{:S(2)}) collective-permute-start(bf16[2,304,256]{2,1,0:T(8,128)(2,1)S(1)} %pad_maximum_fusion.1), channel_id=1, source_target_pairs={{0,8},{8,0},{16,24},{24,16},{1,9},{9,1},{17,25},{25,17},{2,10},{10... | collective-permute-start | bytes 933896 | tf_op jit(solution)/shard_map/ppermute | solution.py:737
  (154 shorter events, 44.0 us)
Async XLA Ops:
  4.1 5.5 %collective-permute-start.1 = (bf16[1,144,256]{2,1,0:T(8,128)(2,1)}, bf16[1,144,256]{2,1,0:T(8,128)(2,1)S(1)}, u32[]{:S(2)}, u32[]{:S(2)}) collective-permute-start(bf16[1,144,256]{2,1,0:T(8,128)(2,1)} %bitcast.220), channel_id=1, source_target_pairs={{0,4},{1,5},{2,6},{3,7},{4,0},{5,1},{6,2},{7,3},{8,12},{9,13},{10,... | collective-permute-start | bytes 221192 | tf_op jit(solution)/shard_map/ppermute | solution.py:737
  6.4 6.0 %collective-permute-start.2 = (bf16[1,144,256]{2,1,0:T(8,128)(2,1)}, bf16[1,144,256]{2,1,0:T(8,128)(2,1)S(1)}, u32[]{:S(2)}, u32[]{:S(2)}) collective-permute-start(bf16[1,144,256]{2,1,0:T(8,128)(2,1)} %bitcast.221), channel_id=1, source_target_pairs={{0,6},{1,7},{2,4},{3,5},{4,2},{5,3},{6,0},{7,1},{8,14},{9,15},{10,... | collective-permute-start | bytes 221192 | tf_op jit(solution)/shard_map/ppermute | solution.py:737
  8.2 5.5 %collective-permute-start.6 = (bf16[2,144,256]{2,1,0:T(8,128)(2,1)S(1)}, bf16[2,144,256]{2,1,0:T(8,128)(2,1)S(1)}, u32[]{:S(2)}, u32[]{:S(2)}) collective-permute-start(bf16[2,144,256]{2,1,0:T(8,128)(2,1)S(1)} %pad_maximum_fusion.8), channel_id=1, source_target_pairs={{0,1},{1,0},{2,3},{3,2},{4,5},{5,4},{6,7},{7,6},{8,9},{9,8},{10,11... | collective-permute-start | bytes 442376 | tf_op jit(solution)/shard_map/ppermute | solution.py:737
  14.7 8.6 %collective-permute-start.7 = (bf16[4,144,256]{2,1,0:T(8,128)(2,1)S(1)}, bf16[4,144,256]{2,1,0:T(8,128)(2,1)S(1)}, u32[]{:S(2)}, u32[]{:S(2)}) collective-permute-start(bf16[4,144,256]{2,1,0:T(8,128)(2,1)S(1)} %pad_maximum_fusion.2), channel_id=1, source_target_pairs={{0,16},{8,24},{16,0},{24,8},{1,17},{9,25},{17,1},{25,9},{2,18},{10... | collective-permute-start | bytes 884744 | tf_op jit(solution)/shard_map/ppermute | solution.py:737
  16.5 6.9 %collective-permute-start.9 = (bf16[4,144,256]{2,1,0:T(8,128)(2,1)S(1)}, bf16[4,144,256]{2,1,0:T(8,128)(2,1)S(1)}, u32[]{:S(2)}, u32[]{:S(2)}) collective-permute-start(bf16[4,144,256]{2,1,0:T(8,128)(2,1)S(1)} %pad_maximum_fusion.3), channel_id=1, source_target_pairs={{0,1},{1,0},{2,3},{3,2},{4,5},{5,4},{6,7},{7,6},{8,9},{9,8},{10,11... | collective-permute-start | bytes 884744 | tf_op jit(solution)/shard_map/ppermute | solution.py:737
  23.4 25.7 %collective-permute-start.10 = (bf16[16,144,256]{2,1,0:T(8,128)(2,1)S(1)}, bf16[16,144,256]{2,1,0:T(8,128)(2,1)}, u32[]{:S(2)}, u32[]{:S(2)}) collective-permute-start(bf16[16,144,256]{2,1,0:T(8,128)(2,1)S(1)} %constant_dynamic-update-slice_fusion.4.refs_0_), channel_id=1, source_target_pairs={{0,8},{8,0},{16,24},{24,16},{1,9},{9,1},{17,25},{25,17},{2,10},{10... | collective-permute-start | bytes 3538952 | tf_op jit(solution)/shard_map/ppermute | solution.py:737
  28.4 6.4 %collective-permute-start.3 = (bf16[1,288,256]{2,1,0:T(8,128)(2,1)S(1)}, bf16[1,288,256]{2,1,0:T(8,128)(2,1)S(1)}, u32[]{:S(2)}, u32[]{:S(2)}) collective-permute-start(bf16[1,288,256]{2,1,0:T(8,128)(2,1)S(1)} %bitcast.226), channel_id=1, source_target_pairs={{0,2},{1,3},{2,0},{3,1},{4,6},{5,7},{6,4},{7,5},{8,10},{9,11},{10,... | collective-permute-start | bytes 442376 | tf_op jit(solution)/shard_map/ppermute | solution.py:737
  29.1 10.9 %collective-permute-start.4 = (bf16[1,288,256]{2,1,0:T(8,128)(2,1)S(1)}, bf16[1,288,256]{2,1,0:T(8,128)(2,1)S(1)}, u32[]{:S(2)}, u32[]{:S(2)}) collective-permute-start(bf16[1,288,256]{2,1,0:T(8,128)(2,1)S(1)} %bitcast.227), channel_id=1, source_target_pairs={{0,4},{1,5},{2,6},{3,7},{4,0},{5,1},{6,2},{7,3},{8,12},{9,13},{10,... | collective-permute-start | bytes 442376 | tf_op jit(solution)/shard_map/ppermute | solution.py:737
  30.9 13.3 %collective-permute-start.5 = (bf16[1,288,256]{2,1,0:T(8,128)(2,1)S(1)}, bf16[1,288,256]{2,1,0:T(8,128)(2,1)S(1)}, u32[]{:S(2)}, u32[]{:S(2)}) collective-permute-start(bf16[1,288,256]{2,1,0:T(8,128)(2,1)S(1)} %bitcast.228), channel_id=1, source_target_pairs={{0,6},{1,7},{2,4},{3,5},{4,2},{5,3},{6,0},{7,1},{8,14},{9,15},{10,... | collective-permute-start | bytes 442376 | tf_op jit(solution)/shard_map/ppermute | solution.py:737
  45.6 16.9 %collective-permute-start.12 = (bf16[2,288,256]{2,1,0:T(8,128)(2,1)}, bf16[2,288,256]{2,1,0:T(8,128)(2,1)S(1)}, u32[]{:S(2)}, u32[]{:S(2)}) collective-permute-start(bf16[2,288,256]{2,1,0:T(8,128)(2,1)} %get-tuple-element.185), channel_id=1, source_target_pairs={{0,16},{8,24},{16,0},{24,8},{1,17},{9,25},{17,1},{25,9},{2,18},{10... | collective-permute-start | bytes 884744 | tf_op jit(solution)/shard_map/ppermute | solution.py:737
  48.3 14.2 %collective-permute-start.11 = (bf16[2,288,256]{2,1,0:T(8,128)(2,1)}, bf16[2,288,256]{2,1,0:T(8,128)(2,1)}, u32[]{:S(2)}, u32[]{:S(2)}) collective-permute-start(bf16[2,288,256]{2,1,0:T(8,128)(2,1)} %get-tuple-element.180), channel_id=1, source_target_pairs={{0,1},{1,0},{2,3},{3,2},{4,5},{5,4},{6,7},{7,6},{8,9},{9,8},{10,11... | collective-permute-start | bytes 884744 | tf_op jit(solution)/shard_map/ppermute | solution.py:737
  63.2 14.2 %collective-permute-start.15 = (bf16[4,288,256]{2,1,0:T(8,128)(2,1)}, bf16[4,288,256]{2,1,0:T(8,128)(2,1)S(1)}, u32[]{:S(2)}, u32[]{:S(2)}) collective-permute-start(bf16[4,288,256]{2,1,0:T(8,128)(2,1)} %constant_dynamic-update-slice_fusion.15), channel_id=1, source_target_pairs={{0,1},{1,0},{2,3},{3,2},{4,5},{5,4},{6,7},{7,6},{8,9},{9,8},{10,11... | collective-permute-start | bytes 1769480 | tf_op jit(solution)/shard_map/ppermute | solution.py:737
  65.6 13.1 %collective-permute-start.14 = (bf16[4,288,256]{2,1,0:T(8,128)(2,1)}, bf16[4,288,256]{2,1,0:T(8,128)(2,1)}, u32[]{:S(2)}, u32[]{:S(2)}) collective-permute-start(bf16[4,288,256]{2,1,0:T(8,128)(2,1)} %get-tuple-element.175), channel_id=1, source_target_pairs={{0,16},{8,24},{16,0},{24,8},{1,17},{9,25},{17,1},{25,9},{2,18},{10... | collective-permute-start | bytes 1769480 | tf_op jit(solution)/shard_map/ppermute | solution.py:737
  79.9 7.2 %collective-permute-start.16 = (bf16[16,288,256]{2,1,0:T(8,128)(2,1)S(1)}, bf16[16,288,256]{2,1,0:T(8,128)(2,1)S(1)}, u32[]{:S(2)}, u32[]{:S(2)}) collective-permute-start(bf16[16,288,256]{2,1,0:T(8,128)(2,1)S(1)} %constant_dynamic-update-slice_fusion.18.mine_ref), channel_id=1, source_target_pairs={{0,8},{8,0},{16,24},{24,16},{1,9},{9,1},{17,25},{25,17},{2,10},{10... | collective-permute-start | bytes 7077896 | tf_op jit(solution)/shard_map/ppermute | solution.py:737
  135.5 19.5 %collective-permute-start.28 = (bf16[2,2,4,144,128]{4,3,2,1,0:T(8,128)(2,1)}, bf16[2,2,4,144,128]{4,3,2,1,0:T(8,128)(2,1)S(1)}, u32[]{:S(2)}, u32[]{:S(2)}) collective-permute-start(bf16[2,2,4,144,128]{4,3,2,1,0:T(8,128)(2,1)} %get-tuple-element.120), channel_id=1, source_target_pairs={{0,8},{8,0},{16,24},{24,16},{1,9},{9,1},{17,25},{25,17},{2,10},{10... | collective-permute-start | bytes 1769480 | tf_op jit(solution)/shard_map/ppermute | solution.py:737
  154.6 20.0 %collective-permute-start.20 = (bf16[2,2,4,176,256]{4,3,2,1,0:T(8,128)(2,1)}, bf16[2,2,4,176,256]{4,3,2,1,0:T(8,128)(2,1)S(1)}, u32[]{:S(2)}, u32[]{:S(2)}) collective-permute-start(bf16[2,2,4,176,256]{4,3,2,1,0:T(8,128)(2,1)} %get-tuple-element.116), channel_id=1, source_target_pairs={{0,8},{8,0},{16,24},{24,16},{1,9},{9,1},{17,25},{25,17},{2,10},{10... | collective-permute-start | bytes 4325384 | tf_op jit(solution)/shard_map/ppermute | solution.py:737
  156.0 8.9 %collective-permute-start.29 = (bf16[2,4,144,128]{3,2,1,0:T(8,128)(2,1)}, bf16[2,4,144,128]{3,2,1,0:T(8,128)(2,1)S(1)}, u32[]{:S(2)}, u32[]{:S(2)}) collective-permute-start(bf16[2,4,144,128]{3,2,1,0:T(8,128)(2,1)} %get-tuple-element.131), channel_id=1, source_target_pairs={{0,1},{1,0},{2,3},{3,2},{4,5},{5,4},{6,7},{7,6},{8,9},{9,8},{10,11... | collective-permute-start | bytes 884744 | tf_op jit(solution)/shard_map/ppermute | solution.py:737
  157.7 8.6 %collective-permute-start.32 = (bf16[2,4,144,128]{3,2,1,0:T(8,128)(2,1)}, bf16[2,4,144,128]{3,2,1,0:T(8,128)(2,1)}, u32[]{:S(2)}, u32[]{:S(2)}) collective-permute-start(bf16[2,4,144,128]{3,2,1,0:T(8,128)(2,1)} %get-tuple-element.133), channel_id=1, source_target_pairs={{0,16},{8,24},{16,0},{24,8},{1,17},{9,25},{17,1},{25,9},{2,18},{10... | collective-permute-start | bytes 884744 | tf_op jit(solution)/shard_map/ppermute | solution.py:737
  157.8 13.7 %collective-permute-start.17 = (bf16[2,2,4,128,256]{4,3,2,1,0:T(8,128)(2,1)}, bf16[2,2,4,128,256]{4,3,2,1,0:T(8,128)(2,1)}, u32[]{:S(2)}, u32[]{:S(2)}) collective-permute-start(bf16[2,2,4,128,256]{4,3,2,1,0:T(8,128)(2,1)} %get-tuple-element.112), channel_id=1, source_target_pairs={{0,8},{8,0},{16,24},{24,16},{1,9},{9,1},{17,25},{25,17},{2,10},{10... | collective-permute-start | bytes 3145736 | tf_op jit(solution)/shard_map/ppermute | solution.py:737
  171.4 8.3 %collective-permute-start.34 = (bf16[1,288,128]{2,1,0:T(8,128)(2,1)S(1)}, bf16[1,288,128]{2,1,0:T(8,128)(2,1)S(1)}, u32[]{:S(2)}, u32[]{:S(2)}) collective-permute-start(bf16[1,288,128]{2,1,0:T(8,128)(2,1)S(1)} %pad_maximum_fusion.15), channel_id=1, source_target_pairs={{0,2},{1,3},{2,0},{3,1},{4,6},{5,7},{6,4},{7,5},{8,10},{9,11},{10,... | collective-permute-start | bytes 221192 | tf_op jit(solution)/shard_map/ppermute | solution.py:737
  173.1 11.2 %collective-permute-start.18 = (bf16[2,4,128,256]{3,2,1,0:T(8,128)(2,1)S(1)}, bf16[2,4,128,256]{3,2,1,0:T(8,128)(2,1)S(1)}, u32[]{:S(2)}, u32[]{:S(2)}) collective-permute-start(bf16[2,4,128,256]{3,2,1,0:T(8,128)(2,1)S(1)} %get-tuple-element.126), channel_id=1, source_target_pairs={{0,1},{1,0},{2,3},{3,2},{4,5},{5,4},{6,7},{7,6},{8,9},{9,8},{10,11... | collective-permute-start | bytes 1572872 | tf_op jit(solution)/shard_map/ppermute | solution.py:737
  175.0 15.5 %collective-permute-start.21 = (bf16[2,4,176,256]{3,2,1,0:T(8,128)(2,1)S(1)}, bf16[2,4,176,256]{3,2,1,0:T(8,128)(2,1)S(1)}, u32[]{:S(2)}, u32[]{:S(2)}) collective-permute-start(bf16[2,4,176,256]{3,2,1,0:T(8,128)(2,1)S(1)} %get-tuple-element.124), channel_id=1, source_target_pairs={{0,16},{8,24},{16,0},{24,8},{1,17},{9,25},{17,1},{25,9},{2,18},{10... | collective-permute-start | bytes 2162696 | tf_op jit(solution)/shard_map/ppermute | solution.py:737
  175.2 5.1 %collective-permute-start.35 = (bf16[1,288,128]{2,1,0:T(8,128)(2,1)S(1)}, bf16[1,288,128]{2,1,0:T(8,128)(2,1)S(1)}, u32[]{:S(2)}, u32[]{:S(2)}) collective-permute-start(bf16[1,288,128]{2,1,0:T(8,128)(2,1)S(1)} %pad_maximum_fusion.16), channel_id=1, source_target_pairs={{0,4},{1,5},{2,6},{3,7},{4,0},{5,1},{6,2},{7,3},{8,12},{9,13},{10,... | collective-permute-start | bytes 221192 | tf_op jit(solution)/shard_map/ppermute | solution.py:737
  177.6 5.3 %collective-permute-start.36 = (bf16[1,288,128]{2,1,0:T(8,128)(2,1)S(1)}, bf16[1,288,128]{2,1,0:T(8,128)(2,1)S(1)}, u32[]{:S(2)}, u32[]{:S(2)}) collective-permute-start(bf16[1,288,128]{2,1,0:T(8,128)(2,1)S(1)} %pad_maximum_fusion.17), channel_id=1, source_target_pairs={{0,6},{1,7},{2,4},{3,5},{4,2},{5,3},{6,0},{7,1},{8,14},{9,15},{10,... | collective-permute-start | bytes 221192 | tf_op jit(solution)/shard_map/ppermute | solution.py:737
  182.9 9.2 %collective-permute-start.37 = (bf16[288,128]{1,0:T(8,128)(2,1)S(1)}, bf16[288,128]{1,0:T(8,128)(2,1)S(1)}, u32[]{:S(2)}, u32[]{:S(2)}) collective-permute-start(bf16[288,128]{1,0:T(8,128)(2,1)S(1)} %fusion.26), channel_id=1, source_target_pairs={{0,16},{8,24},{16,0},{24,8},{1,17},{9,25},{17,1},{25,9},{2,18},{10... | collective-permute-start | bytes 221192 | tf_op jit(solution)/shard_map/ppermute | solution.py:737
  184.5 13.5 %collective-permute-start.19 = (bf16[4,128,256]{2,1,0:T(8,128)(2,1)S(1)}, bf16[4,128,256]{2,1,0:T(8,128)(2,1)S(1)}, u32[]{:S(2)}, u32[]{:S(2)}) collective-permute-start(bf16[4,128,256]{2,1,0:T(8,128)(2,1)S(1)} %get-tuple-element.134), channel_id=1, source_target_pairs={{0,16},{8,24},{16,0},{24,8},{1,17},{9,25},{17,1},{25,9},{2,18},{10... | collective-permute-start | bytes 786440 | tf_op jit(solution)/shard_map/ppermute | solution.py:737
  190.7 7.4 %collective-permute-start.22 = (bf16[4,176,256]{2,1,0:T(8,128)(2,1)S(1)}, bf16[4,176,256]{2,1,0:T(8,128)(2,1)S(1)}, u32[]{:S(2)}, u32[]{:S(2)}) collective-permute-start(bf16[4,176,256]{2,1,0:T(8,128)(2,1)S(1)} %get-tuple-element.128), channel_id=1, source_target_pairs={{0,1},{1,0},{2,3},{3,2},{4,5},{5,4},{6,7},{7,6},{8,9},{9,8},{10,11... | collective-permute-start | bytes 1081352 | tf_op jit(solution)/shard_map/ppermute | solution.py:737
  192.2 9.0 %collective-permute-start.38 = (bf16[2,288,128]{2,1,0:T(8,128)(2,1)S(1)}, bf16[2,288,128]{2,1,0:T(8,128)(2,1)S(1)}, u32[]{:S(2)}, u32[]{:S(2)}) collective-permute-start(bf16[2,288,128]{2,1,0:T(8,128)(2,1)S(1)} %pad_maximum_fusion.10), channel_id=1, source_target_pairs={{0,8},{8,0},{16,24},{24,16},{1,9},{9,1},{17,25},{25,17},{2,10},{10... | collective-permute-start | bytes 442376 | tf_op jit(solution)/shard_map/ppermute | solution.py:737
  198.2 5.0 %collective-permute-start.23 = (bf16[1,304,256]{2,1,0:T(8,128)(2,1)S(1)}, bf16[1,304,256]{2,1,0:T(8,128)(2,1)S(1)}, u32[]{:S(2)}, u32[]{:S(2)}) collective-permute-start(bf16[1,304,256]{2,1,0:T(8,128)(2,1)S(1)} %pad_maximum_fusion.5), channel_id=1, source_target_pairs={{0,2},{1,3},{2,0},{3,1},{4,6},{5,7},{6,4},{7,5},{8,10},{9,11},{10,... | collective-permute-start | bytes 466952 | tf_op jit(solution)/shard_map/ppermute | solution.py:737
  199.9 6.3 %collective-permute-start.24 = (bf16[1,304,256]{2,1,0:T(8,128)(2,1)S(1)}, bf16[1,304,256]{2,1,0:T(8,128)(2,1)S(1)}, u32[]{:S(2)}, u32[]{:S(2)}) collective-permute-start(bf16[1,304,256]{2,1,0:T(8,128)(2,1)S(1)} %pad_maximum_fusion.6), channel_id=1, source_target_pairs={{0,4},{1,5},{2,6},{3,7},{4,0},{5,1},{6,2},{7,3},{8,12},{9,13},{10,... | collective-permute-start | bytes 466952 | tf_op jit(solution)/shard_map/ppermute | solution.py:737
  200.6 8.4 %collective-permute-start.25 = (bf16[1,304,256]{2,1,0:T(8,128)(2,1)S(1)}, bf16[1,304,256]{2,1,0:T(8,128)(2,1)S(1)}, u32[]{:S(2)}, u32[]{:S(2)}) collective-permute-start(bf16[1,304,256]{2,1,0:T(8,128)(2,1)S(1)} %pad_maximum_fusion.7), channel_id=1, source_target_pairs={{0,6},{1,7},{2,4},{3,5},{4,2},{5,3},{6,0},{7,1},{8,14},{9,15},{10,... | collective-permute-start | bytes 466952 | tf_op jit(solution)/shard_map/ppermute | solution.py:737
  213.6 9.5 %collective-permute-start.27 = (bf16[2,304,256]{2,1,0:T(8,128)(2,1)S(1)}, bf16[2,304,256]{2,1,0:T(8,128)(2,1)S(1)}, u32[]{:S(2)}, u32[]{:S(2)}) collective-permute-start(bf16[2,304,256]{2,1,0:T(8,128)(2,1)S(1)} %pad_maximum_fusion.1), channel_id=1, source_target_pairs={{0,8},{8,0},{16,24},{24,16},{1,9},{9,1},{17,25},{25,17},{2,10},{10... | collective-permute-start | bytes 933896 | tf_op jit(solution)/shard_map/ppermute | solution.py:737
  (25 other events, 178.8 us)

commit v3 on v2

--- a/solution.py
+++ b/solution.py
@@ -10,6 +10,7 @@
 HEADS = 8
 EPSILON = 1e-05
 CHUNK = 256
+ROWS = 512
 QUAD = 256
 F32 = jnp.float32
 BF16 = jnp.bfloat16
@@ -19,6 +20,10 @@
 COST = pl.CostEstimate(flops=1000, bytes_accessed=1000, transcendentals=0)
 
 
+def ordered(kernel, at, count, *refs):
+    kernel(*refs[:at], *refs[at + count :])
+
+
 def place():
     rep = lax.axis_index("rep")
     return lax.axis_index("shard"), rep % 2, (rep // 2) % 2
@@ -55,8 +60,9 @@
     return jnp.where(rows == columns, 1.0, 0.0)
 
 
-def as_column(row):
-    return jnp.broadcast_to(row, (CHUNK, CHUNK)).T
+def as_column(row, width):
+    tile = jnp.broadcast_to(row, (128, row.shape[1])).T
+    return jnp.concatenate([tile] * (width // 128), axis=1)
 
 
 def causal_mask(column, row):
@@ -171,8 +177,8 @@
     if quad == 0:
         mine_ref, theirs_ref = refs[:2]
         q_ref, k_ref, v_ref, e_ref, p_ref, s_ref, rz_ref, mix_ref, one_ref, two_ref = refs[2:12]
-        w_ref, vec_ref, eb_ref = refs[12:15]
-        held, first_state, second_state, total_state, sems = refs[15:]
+        w_ref, vec_ref, eb_ref, count_ref = refs[12:16]
+        held, first_state, second_state, total_state, sems = refs[16:]
         weight = lambda m: w_ref[m, :, at]
     else:
         w_ref, vec_ref = refs[:2]
@@ -203,12 +209,15 @@
                         ],
                         sems.at[0],
                     ).start()
-                if half == 0 and x == 0:
-                    pltpu.make_async_copy(
-                        source.at[slot, pl.ds(2 * r, 16)], held.at[owner], sems.at[1]
-                    ).start()
+                pltpu.make_async_copy(
+                    source.at[slot, pl.ds(2 * r, 16)], held.at[2 * half + x, owner], sems.at[1]
+                ).start()
         pltpu.make_async_copy(held, held, sems.at[1]).wait()
-        own = [held[s].astype(F32) for s in range(shards)]
+        own = [held[0, s].astype(F32) for s in range(shards)]
+        count = sum(part[:8, :128] for part in own)
+        for k in range(1, 4):
+            count += jnp.sum(held[k, :, :8, :128].astype(F32), axis=0)
+        count_ref[...] = count
         vec_ref[...] = spread([part[:8, :128] for part in own], shards)
         width = 2048 // shards
         lane = lax.broadcasted_iota(jnp.int32, (8, 128), 1)
@@ -233,7 +242,7 @@
     segment_before = jnp.where(step == 0, -1, seg_s[0, jnp.maximum(start - 1, 0)])
     keep = jnp.where(segment_last == segment_before, 1.0, 0.0)
     row = seg_ref[...].astype(F32)
-    column = as_column(row)
+    column = as_column(row, CHUNK)
     causal = causal_mask(column, row).astype(BF16)
     enters = jnp.where(column == segment_before.astype(F32), 1.0, 0.0)
     leaves = jnp.where(column == segment_last.astype(F32), 1.0, 0.0).astype(BF16)
@@ -295,10 +304,8 @@
     out_ref,
     hidden_ref,
     grad_mix_ref,
-    keep_1_ref,
-    send_1_ref,
-    keep_2_ref,
-    send_2_ref,
+    keep_ref,
+    send_ref,
     wo,
     we,
     wc,
@@ -353,8 +360,6 @@
         for ref in (d_wo, d_we, d_wc, d_vec, d_eb):
             ref[...] = jnp.zeros_like(ref)
         pltpu.make_async_copy(wo, wo, sems.at[0]).wait()
-        pltpu.make_async_copy(we, we, sems.at[1]).wait()
-        pltpu.make_async_copy(wc, wc, sems.at[2]).wait()
 
     gain, shift, bias = vec_ref[2:3, :], vec_ref[3:4, :], vec_ref[4:5, :]
     weight_out = wo[...].reshape(512, 512)
@@ -362,18 +367,19 @@
     hidden = x_ref[...].astype(F32) + nn(mixed, weight_out)
     normal, scale = standardise(hidden)
     normed = (normal * gain + shift).astype(BF16)
+    pl.when(step == 0)(lambda: pltpu.make_async_copy(we, we, sems.at[1]).wait())
     for b in range(4):
         at = slice(b * 512, (b + 1) * 512)
         before = nn(normed, we[b]) + eb_ref[0:1, at]
         act[:, at] = jnp.maximum(before, 0.0).astype(BF16)
+    pl.when(step == 0)(lambda: pltpu.make_async_copy(wc, wc, sems.at[2]).wait())
     result = hidden + (nn(act[...], wc[...]) + bias)
     out_ref[...] = result.astype(BF16)
-    valid = as_column(valid_ref[...].astype(F32))
-    valid = jnp.concatenate([valid, valid], axis=1)
+    valid = as_column(valid_ref[...].astype(F32), 512)
     error = result - teacher_ref[...].astype(F32)
     masked = valid * error
     loss_ref[...] += jnp.sum(masked * error)
-    count = 256.0 * count_ref[0:1, 0:1] + count_ref[0:1, 1:2]
+    count = 256.0 * count_ref[6:7, 0:1] + count_ref[6:7, 1:2]
     grad_result = masked * (tokens / count)
     low = grad_result.astype(BF16)
     d_normed = None
@@ -401,10 +407,10 @@
         width = 2048 // shards
         digits = digits_of(loss_ref[...])
 
-        def write(first_ref, second_ref, at):
+        _, rows = branch_rows(shards, keep_ref.shape[0])
+
+        def write(ref, at):
             for s in range(shards):
-                y, z = (me ^ s) & 1, (me ^ s) >> 1
-                rows = slice(s * r, (s + 1) * r)
                 top = jnp.concatenate([piece_of(d_vec[...], s, r), digits], axis=1)
                 if width >= 128:
                     low_rows = d_eb[:, s * width : (s + 1) * width]
@@ -413,30 +419,31 @@
                 if low_rows.shape[1] < 256:
                     pad = jnp.zeros((8, 256 - low_rows.shape[1]), F32)
                     low_rows = jnp.concatenate([low_rows, pad], axis=1)
-                both = jnp.concatenate([top, low_rows], axis=0).astype(BF16)
-                for half in range(2):
-                    x = cross ^ half
-                    start = s * 4 * r + half * 2 * r
-                    first_ref[y, x, z] = d_wc[start : start + 2 * r, at].astype(BF16)
-                    for b in range(2):
-                        part = d_we[2 * half + b, rows, at]
-                        second_ref[x, y, z, b * r : (b + 1) * r, :] = part.astype(BF16)
-                    second_ref[x, y, z, 2 * r : 2 * r + 16, :] = both
-                    start = s * r + half * (r // 2)
-                    part = d_wo[start : start + r // 2, at]
-                    second_ref[x, y, z, 2 * r + 16 :, :] = part.astype(BF16)
+                both = jnp.concatenate([top, low_rows], axis=0)
+                for name, done, part, offset, size in rows:
+                    if name == "contract":
+                        value = d_wc[s * 4 * r + done : s * 4 * r + done + size, at]
+                    elif name == "output":
+                        value = d_wo[s * r + done : s * r + done + size, at]
+                    elif name == "vectors":
+                        value = both[done : done + size]
+                    elif name == "none":
+                        value = jnp.zeros((size, 256), F32)
+                    else:
+                        value = d_we[name, s * r + done : s * r + done + size, at]
+                    ref[part, s, offset : offset + size, :] = value.astype(BF16)
 
         left, right = slice(0, 256), slice(256, 512)
 
         @pl.when(core == 0)
         def _():
-            write(keep_1_ref, keep_2_ref, left)
-            write(send_1_ref, send_2_ref, right)
+            write(keep_ref, left)
+            write(send_ref, right)
 
         @pl.when(core == 1)
         def _():
-            write(keep_1_ref, keep_2_ref, right)
-            write(send_1_ref, send_2_ref, left)
+            write(keep_ref, right)
+            write(send_ref, left)
 
 
 def attention_backward(last, shards, seg_s, *refs):
@@ -466,7 +473,7 @@
     segment_after = jnp.where(step == 0, -1, seg_s[0, jnp.minimum(start + CHUNK, length - 1)])
     keep = jnp.where(segment_first == segment_after, 1.0, 0.0)
     row = seg_ref[...].astype(F32)
-    column = as_column(row)
+    column = as_column(row, CHUNK)
     causal = causal_mask(column, row).astype(BF16)
     turned = causal_mask_transposed(column, row).astype(BF16)
     enters = jnp.where(column == segment_before.astype(F32), 1.0, 0.0)
@@ -600,7 +607,7 @@
     )(*operands)
 
 
-def call_forward(quad, shards, segments, x, operands):
+def call_forward(quad, shards, segments, x, operands, earlier):
     length = x.shape[0]
     chunks = length // CHUNK
     wide = pl.BlockSpec((CHUNK, 512), lambda c, *_: (c, 0))
@@ -610,9 +617,10 @@
     states = shaped((chunks, QUAD, QUAD), BF16)
     if quad == 0:
         in_specs = [anywhere(), anywhere()]
-        out_specs = [whole((4, 512, 512)), whole((8, 512)), whole((8, 2048))]
-        out_shape = [shaped((4, 512, 512), BF16), shaped((8, 512), F32), shaped((8, 2048), F32)]
-        first = [pltpu.VMEM((shards, 16, 256), BF16)]
+        out_specs = [whole((4, 512, 512)), whole((8, 512)), whole((8, 2048)), whole((8, 128))]
+        out_shape = [shaped((4, 512, 512), BF16), shaped((8, 512), F32)]
+        out_shape += [shaped((8, 2048), F32), shaped((8, 128), F32)]
+        first = [pltpu.VMEM((4, shards, 16, 256), BF16)]
         last = [pltpu.SemaphoreType.DMA((2,))]
     else:
         in_specs = [pl.BlockSpec((4, 512, QUAD), lambda c, *_: (0, 0, 1)), whole((8, 512))]
@@ -620,7 +628,8 @@
     grid_spec = pltpu.PrefetchScalarGridSpec(
         num_scalar_prefetch=1,
         grid=(chunks,),
-        in_specs=[wide, pl.BlockSpec((1, CHUNK), lambda c, *_: (0, c)), *in_specs],
+        in_specs=[wide, pl.BlockSpec((1, CHUNK), lambda c, *_: (0, c)), *in_specs]
+        + [anywhere()] * len(earlier),
         out_specs=[tile] * 8 + [state] * 2 + out_specs,
         scratch_shapes=first
         + [
@@ -631,22 +640,27 @@
         + last,
     )
     return pl.pallas_call(
-        functools.partial(attention_forward, quad, shards),
+        functools.partial(
+            ordered,
+            functools.partial(attention_forward, quad, shards),
+            3 + len(operands),
+            len(earlier),
+        ),
         grid_spec=grid_spec,
-        out_shape=[low] * 6 + [shaped((length, QUAD), F32), low, states, states] + out_shape,
+        out_shape=[low] * 6 + [shaped((length, QUAD), F32), low, states, states]
+        + out_shape,
         compiler_params=params(),
         cost_estimate=COST,
         name=f"attention_forward_{quad}",
-    )(segments, x, segments, *operands)
-
-
-def call_feed_forward(shards, tokens, *operands):
+    )(segments, x, segments, *operands, *earlier)
+
+
+def call_feed_forward(shards, reps, tokens, *operands):
     length = operands[0].shape[0]
-    chunks = length // CHUNK
+    chunks = length // ROWS
     r = 512 // shards
-    tile = lambda width: pl.BlockSpec((CHUNK, width), lambda c: (c, 0))
-    first = (2, 2, shards // 2, 2 * r, 256)
-    second = (2, 2, shards // 2, 2 * r + 16 + r // 2, 256)
+    tile = lambda width: pl.BlockSpec((ROWS, width), lambda c: (c, 0))
+    payload = (reps, shards, branch_rows(shards, reps)[0], 256)
     return pl.pallas_call(
         functools.partial(feed_forward, shards, tokens),
         grid=(chunks,),
@@ -655,26 +669,25 @@
             tile(QUAD),
             tile(QUAD),
             tile(512),
-            pl.BlockSpec((1, CHUNK), lambda c: (0, c)),
+            pl.BlockSpec((1, ROWS), lambda c: (0, c)),
             whole((8, 512)),
             whole((8, 2048)),
-            whole((1, 2)),
+            whole((8, 128)),
             anywhere(),
             anywhere(),
         ],
-        out_specs=[tile(512)] * 3 + [whole(first)] * 2 + [whole(second)] * 2,
+        out_specs=[tile(512)] * 3 + [whole(payload)] * 2,
         out_shape=[
             shaped((length, 512), BF16),
             shaped((length, 512), F32),
             shaped((length, 512), BF16),
-            *[shaped(first, BF16)] * 2,
-            *[shaped(second, BF16)] * 2,
+            *[shaped(payload, BF16)] * 2,
         ],
         scratch_shapes=[
             pltpu.VMEM((2 * shards, r // 2, 512), BF16),
             pltpu.VMEM((4, 512, 512), BF16),
             pltpu.VMEM((2048, 512), BF16),
-            pltpu.VMEM((CHUNK, 2048), BF16),
+            pltpu.VMEM((ROWS, 2048), BF16),
             pltpu.VMEM((512, 512), F32),
             pltpu.VMEM((4, 512, 512), F32),
             pltpu.VMEM((2048, 512), F32),
@@ -689,7 +702,7 @@
     )(*operands)
 
 
-def call_backward(quad, shards, segments, x, saved, grad_mix, states, weights, vectors, extra):
+def call_backward(quad, shards, segments, x, *operands, extra, earlier):
     length = x.shape[0]
     chunks = length // CHUNK
     r = 512 // shards
@@ -712,6 +725,7 @@
             pl.BlockSpec((4, 512, QUAD), lambda c, *_: (0, 0, quad)),
             whole((8, 512)),
             *[wide] * len(extra),
+            *[anywhere()] * len(earlier),
         ],
         out_specs=[wide, whole(payload), whole(payload)],
         scratch_shapes=[
@@ -723,13 +737,22 @@
         ],
     )
     return pl.pallas_call(
-        functools.partial(attention_backward, last, shards),
+        functools.partial(
+            ordered,
+            functools.partial(attention_backward, last, shards),
+            3 + len(operands) + len(extra),
+            len(earlier),
+        ),
         grid_spec=grid_spec,
-        out_shape=[shaped((length, 512), F32), shaped(payload, BF16), shaped(payload, BF16)],
+        out_shape=[
+            shaped((length, 512), F32),
+            shaped(payload, BF16),
+            shaped(payload, BF16),
+        ],
         compiler_params=params(),
         cost_estimate=COST,
         name=f"attention_backward_{quad}",
-    )(segments, x, segments, *saved, grad_mix, *states, weights, vectors, *extra)
+    )(segments, x, segments, *operands, *extra, *earlier)
 
 
 def swap(value, axis, bit):
@@ -742,8 +765,129 @@
     return [(low, min(2, bits - low)) for low in range(1, bits, 2)]
 
 
+def branch_rows(shards, reps):
+    r = 512 // shards
+    piece = -(-(9 * r + 16) // (16 * reps)) * 16
+    names = [("contract", 4 * r)] + [(b, r) for b in range(4)] + [("output", r), ("vectors", 16)]
+    rows, at = [], 0
+    for name, height in names + [("none", piece * reps - 9 * r - 16)]:
+        done = 0
+        while done < height:
+            part, offset = divmod(at, piece)
+            size = min(height - done, piece - offset)
+            rows.append((name, done, part, offset, size))
+            done += size
+            at += size
+    return piece, rows
+
+
+def add_arrived(shards, *refs):
+    source, target = refs[0], refs[-1]
+    for half in range(2):
+        total = 0.0
+        for rep in range(half, source.shape[0], 2):
+            for s in range(shards):
+                total = total + source[rep, s].astype(F32)
+        target[half] = total.astype(BF16)
+
+
+def call_add_arrived(shards, arrived, *others):
+    reps, _, piece, width = arrived.shape
+    return pl.pallas_call(
+        functools.partial(add_arrived, shards),
+        in_specs=[pl.BlockSpec(memory_space=pltpu.VMEM)] + [anywhere()] * len(others),
+        out_specs=pl.BlockSpec(memory_space=pltpu.VMEM),
+        out_shape=shaped((2, piece, width), BF16),
+        compiler_params=pltpu.CompilerParams(vmem_limit_bytes=VMEM_LIMIT),
+        cost_estimate=COST,
+        name="add_arrived",
+    )(arrived, *others)
+
+
+def zero_of(arrays):
+    return sum(array[(0,) * array.ndim] for array in arrays) * jnp.zeros((), BF16)
+
+
 def after(value, *others):
     return lax.optimization_barrier((value, *others))[0]
+
+
+def quarters(refs):
+    _, core, cross = place()
+
+    def quarter(rows, half, third):
+        parts = [ref[rows, :] for ref in refs]
+        near = jnp.where(core == half, parts[0], parts[1])
+        far = jnp.where(core == half, parts[2], parts[3])
+        return jnp.where(cross == third, near, far).astype(F32)
+
+    def both(rows, third):
+        return jnp.concatenate([quarter(rows, half, third) for half in range(2)], axis=1)
+
+    return both
+
+
+def assemble_branch(shards, count_ref, *refs):
+    held = refs[-1]
+    reps = held.shape[0]
+    me = lax.axis_index("rep")
+    for a in range(reps):
+        held[me ^ a] = refs[a][...]
+    contract_ref, expand_ref, output_ref, bias_1_ref, bias_2_ref, gain_ref, shift_ref, loss_ref = (
+        refs[reps:-1]
+    )
+    r = 512 // shards
+    _, rows = branch_rows(shards, reps)
+    vectors = []
+    for name, done, part, offset, size in rows:
+        value = jnp.concatenate(
+            [held[part, half, offset : offset + size, :] for half in range(2)], axis=1
+        ).astype(F32)
+        if name == "contract":
+            contract_ref[done : done + size, :] = value
+        elif name == "output":
+            output_ref[done : done + size, :] = value
+        elif name == "vectors":
+            vectors.append(value[:, :256])
+        elif name != "none":
+            expand_ref[done : done + size, name * 512 : (name + 1) * 512] = value
+    vectors = vectors[0] if len(vectors) == 1 else jnp.concatenate(vectors, axis=0)
+    bias_1_ref[...] = vectors[8:9, : 4 * r]
+    gain_ref[...] = vectors[0:1, :r]
+    shift_ref[...] = vectors[1:2, :r]
+    bias_2_ref[...] = vectors[2:3, :r]
+    lane = lax.broadcasted_iota(jnp.int32, (1, 128), 1)
+    power = jnp.zeros((1, 128), F32)
+    for k in range(LOSS_DIGITS):
+        power = jnp.where(lane == k, 8.0 ** (k - LOSS_ZERO), power)
+    total = jnp.sum(vectors[0:1, 128:256] * power, axis=1, keepdims=True)
+    count = 256.0 * count_ref[6:7, 0:1] + count_ref[6:7, 1:2]
+    loss_ref[...] = total / (2.0 * count)
+
+
+def assemble_mixer(shards, *refs):
+    both = quarters(refs[:4])
+    gain_ref, shift_ref = refs[8:]
+    r = 512 // shards
+    for m, ref in enumerate(refs[4:8]):
+        for quad in range(2):
+            at = quad * (2 * r + 16) + (m % 2) * r
+            ref[:, quad * 256 : (quad + 1) * 256] = both(slice(at, at + r), m // 2)
+    vectors = both(slice(4 * r + 16, 4 * r + 32), 0)
+    gain_ref[...] = vectors[0:1, :r]
+    shift_ref[...] = vectors[1:2, :r]
+
+
+def assemble(body, shards, parts, shapes, scratch=()):
+    return pl.pallas_call(
+        functools.partial(body, shards),
+        in_specs=[pl.BlockSpec(memory_space=pltpu.VMEM)] * len(parts),
+        out_specs=[pl.BlockSpec(memory_space=pltpu.VMEM)] * len(shapes),
+        out_shape=[shaped(shape, F32) for shape in shapes],
+        scratch_shapes=list(scratch),
+        cost_estimate=COST,
+        name="assemble",
+    )(*parts)
 
 
 def add_low(*parts):
@@ -790,11 +934,10 @@
         return held
 
     def halves(held):
-        half = shards // 4
         if len(held) == 4:
-            groups_of = [[], held[:2], held[2:]]
             return jnp.concatenate(held[:2], axis=0), jnp.concatenate(held[2:], axis=0)
         joined = jnp.concatenate(held, axis=0)
+        half = joined.shape[0] // 2
         return joined[:half], joined[half:]
 
     def step_one(first, second):
@@ -806,42 +949,36 @@
     def step_two(first, second):
         return swap(first, "rep", 2), swap(second, "shard", 1)
 
-    held_a = along_z(mixer)
-    branch = after(branch, held_a[1:])
+    first, second = halves(along_z(mixer))
+    first, second = join(first, second, step_one(first, second))
+    arrived = step_two(first, second)
     held_b = along_z(branch)
-    first, second = halves(held_a)
-    arrived = step_one(first, second)
-    first, second = join(first, second, arrived)
-    arrived = step_two(first, second)
-    mine_a = jnp.concatenate([first, arrived[0], second, arrived[1]])
+    first_b, second_b = halves(held_b)
+    pending = step_one(first_b, second_b)
+    mine_a = jnp.concatenate([first, arrived[0] + zero_of(held_b[1:]), second, arrived[1]])
     theirs_a = swap(mine_a, "rep", 1)
 
-    first, second = halves(after(held_b, arrived))
-    pending = step_one(first, second)
-
-    own_slots = [n for n, slot in enumerate(slots_of(shards)) if slot[2] == 0]
-    count = sum(
-        part[n : n + 1, 2 * r + 6, :2].astype(F32) for part in (mine_a, theirs_a) for n in own_slots
-    )
-    bit = 2
+    x = inputs.reshape(length, width)
+    forward_0 = call_forward(
+        0, shards, segments, x, (mine_a, theirs_a), (first_b, second_b)
+    )
+    weights, vectors, bias, count = forward_0[10:]
+    bit = 4
     while bit < reps:
         count = count + swap(count, "rep", bit)
         bit *= 2
-
-    x = inputs.reshape(length, width)
-    forward_0 = call_forward(0, shards, segments, after(x, first, second), (mine_a, theirs_a))
-    weights, vectors, bias = forward_0[10:]
-    first, second = join(first, second, after(pending, forward_0[7]))
-    pending = step_two(first, second)
-    vectors = after(vectors, first, second)
-    forward_1 = call_forward(1, shards, segments, x, (weights, vectors))
+    pending = after(pending, forward_0[7])
+    first_b, second_b = join(first_b, second_b, pending)
+    pending = step_two(first_b, second_b)
+    forward_1 = call_forward(1, shards, segments, x, (weights, vectors), (first_b, second_b))
+    pending = after(pending, forward_1[7])
+    mine_b = jnp.concatenate([first_b, pending[0], second_b, pending[1]])
+    theirs_b = swap(mine_b, "rep", 1)
     mixed = (forward_0[7], forward_1[7])
-    pending = after(pending, forward_1[7])
-    mine_b = jnp.concatenate([first, pending[0], second, pending[1]])
-    theirs_b = swap(mine_b, "rep", 1)
-
-    layer_out, grad_hidden, grad_mix, keep_c, send_c, keep_e, send_e = call_feed_forward(
+
+    layer_out, grad_hidden, grad_mix, keep_f, send_f = call_feed_forward(
         shards,
+        reps,
         float(length * shards * reps),
         x,
         *mixed,
@@ -853,9 +990,6 @@
         mine_b,
         theirs_b,
     )
-
-    def core_swap(keep, send):
-        return keep, swap(send, "rep", 1)
 
     def split(parts):
         return add_low(*(part[0] for part in parts)), add_low(*(part[1] for part in parts))
@@ -892,74 +1026,60 @@
         while bit < reps:
             total = add_low(total, swap(total, "rep", bit))
             bit *= 2
-        over = swap(total, "rep", 2)
-        near = jnp.where(cross == 0, total, over)
-        far = jnp.where(cross == 0, over, total)
-        both = jnp.stack([near, far])
-        sibling = swap(both, "rep", 1)
-        left = jnp.where(core == 0, both, sibling)
-        right = jnp.where(core == 0, sibling, both)
-        return jnp.concatenate([left, right], axis=2).astype(F32)
-
-    def back(quad, saved, grad_mix, extra):
+        return [total] + [swap(total, "rep", a) for a in range(1, 4)]
+
+    def back(quad, saved, extra, earlier):
         return call_backward(
-            quad, shards, segments, x, saved[:7], grad_mix, saved[8:10], weights, vectors, extra
+            quad,
+            shards,
+            segments,
+            x,
+            *saved[:7],
+            grad_mix,
+            *saved[8:10],
+            weights,
+            vectors,
+            extra=extra,
+            earlier=earlier,
         )
 
-    c_parts = row_first(core_swap(keep_c, send_c))
-    e_parts = cross_first(core_swap(keep_e, send_e))
-    grad_mix = after(grad_mix, c_parts[0], e_parts[0])
-    part, keep_0, send_0 = back(0, forward_0, grad_mix, ())
-    c_parts = (c_parts[0], after(c_parts[1], part))
-    e_parts = (e_parts[0], after(e_parts[1], part))
-    c_parts, e_parts = cross_first(c_parts), row_first(e_parts)
-    parts_0 = core_swap(keep_0, send_0)
-    part = after(part, c_parts[0], e_parts[0])
-    grad_inputs, keep_1, send_1 = back(1, forward_1, grad_mix, (part, grad_hidden))
-
-    parts_0 = (parts_0[0], after(parts_0[1], grad_inputs))
-    c_parts = (c_parts[0], after(c_parts[1], grad_inputs))
-    e_parts = (e_parts[0], after(e_parts[1], grad_inputs))
-    parts_1 = core_swap(keep_1, send_1)
-    f_parts = z_stage([c_parts, e_parts])
-    parts_0, parts_1 = row_first(parts_0), cross_first(parts_1)
+    summed = add_low(keep_f, swap(send_f, "rep", 1))
+    every = summed.reshape(reps * shards, *summed.shape[2:])
+    arrived_f = lax.all_to_all(every, ("rep", "shard"), 0, 0).reshape(summed.shape)
+    part, keep_0, send_0 = back(0, forward_0, (), (every,))
+    late_0 = swap(send_0, "rep", 1)
+    grad_inputs, keep_1, send_1 = back(1, forward_1, (part, grad_hidden), ())
+    late_1 = swap(send_1, "rep", 1)
+    parts_0, parts_1 = row_first((keep_0, late_0)), cross_first((keep_1, late_1))
     parts_0, parts_1 = cross_first(parts_0), row_first(parts_1)
-    q_parts = z_stage([parts_0, parts_1])
-    final_f = finish(f_parts)
-    final_q = finish(q_parts)
-
-    grad_contract = final_f[:, : 2 * r].reshape(4 * r, width)
-    rest = final_f[:, 2 * r :]
-    grad_expand = jnp.concatenate(
-        [rest[h, b * r : (b + 1) * r] for h in range(2) for b in range(2)], axis=1
-    )
-    vec_f = rest[0, 2 * r : 2 * r + 16, :256]
-    grad_output = rest[:, 2 * r + 16 :].reshape(r, width)
-    mats = []
-    for m in range(4):
-        parts = [
-            final_q[m // 2, q * (2 * r + 16) + (m % 2) * r : q * (2 * r + 16) + (m % 2 + 1) * r]
-            for q in range(2)
-        ]
-        mats.append(jnp.concatenate(parts, axis=1))
-    vec_1 = final_q[0, 4 * r + 32 - 16 : 4 * r + 32, :128]
-    powers = jnp.array([8.0 ** (k - LOSS_ZERO) for k in range(LOSS_DIGITS)], F32)
-    loss_sum = jnp.sum(vec_f[0, 128 : 128 + LOSS_DIGITS] * powers)
-    loss_value = loss_sum / (2.0 * (256.0 * count[0, 0] + count[0, 1]))
+    q_pieces = z_stage([parts_0, parts_1])
+    total_f = call_add_arrived(shards, arrived_f, q_pieces[0])
+    parts_f = [total_f] + [swap(total_f, "rep", a) for a in range(1, reps)]
+    parts_q = finish(q_pieces)
+    grad_contract, grad_expand, grad_output, bias_1, bias_2, gain_2, shift_2, loss = assemble(
+        assemble_branch,
+        shards,
+        [count, *parts_f],
+        [(4 * r, 512), (r, 2048), (r, 512), (1, 4 * r), (1, r), (1, r), (1, r), (1, 1)],
+        [pltpu.VMEM((reps, *total_f.shape), BF16)],
+    )
+    *mats, gain_1, shift_1 = assemble(
+        assemble_mixer, shards, parts_q, [(r, 512)] * 4 + [(1, r)] * 2
+    )
     return (
         layer_out.reshape(inputs.shape),
         grad_inputs.reshape(inputs.shape),
-        loss_value,
+        loss.reshape(()),
         *mats,
         grad_output,
-        vec_1[0, :r],
-        vec_1[1, :r],
+        gain_1.reshape(r),
+        shift_1.reshape(r),
         grad_expand,
-        vec_f[8, : 4 * r],
+        bias_1.reshape(4 * r),
         grad_contract,
-        vec_f[2, :r],
-        vec_f[0, :r],
-        vec_f[1, :r],
+        bias_2.reshape(r),
+        gain_2.reshape(r),
+        shift_2.reshape(r),
     )
 
 

time: 231 us -> 217 us (0.939)
  starting transfers between devices: 46.2 us -> 38.4 us
  other arithmetic: 14.1 us -> 8.46 us
  waiting for transfers between devices: 60.9 us -> 55.8 us
  Pallas kernels: 92 us -> 96.3 us
  local copies, waits for them, and re-layouts: 11.8 us -> 14.5 us
    ppermute x39 -> x32, starting transfers between devices: 46.2 us -> 32.2 us  [swap(): return lax.ppermute(value, axis, [(i, i ^ bit) for i in range(n)])]
    pallas_call x4 -> x7, Pallas kernels: 60.6 us -> 67.4 us  [the longest x2 35.5 us: call_backward(): pl.pallas_call(functools.partial(ordered, functools.partial(attention_bac...]
    all_to_all x0 -> x1, starting transfers between devices: none -> 6.23 us  [local(): lax.all_to_all(every, ('rep', 'shard'), 0, 0).reshape(summed.shape)]
    ppermute x39 -> x32, waiting for transfers between devices: 60.9 us -> 55.8 us  [swap(): return lax.ppermute(value, axis, [(i, i ^ bit) for i in range(n)])]
    pallas_call x1, Pallas kernels: 29.3 us -> 26.8 us  [call_feed_forward(): pl.pallas_call(functools.partial(feed_forward, shards, tokens), grid=(chu...]
    unnamed x52 -> x49, local copies, waits for them, and re-layouts: 8.65 us -> 9.84 us
    convert_element_type x12 -> x7, other arithmetic: 5.47 us -> 5.76 us  [add_low(): return sum((part.astype(F32) for part in parts)).astype(BF16)]
  transfers between devices with their start and end apart: 39 -> 33, of which waited for: 23 -> 16; matrix products, arithmetic and copies ran while one was open for 7% -> 4% of each run, Pallas kernels for 19% -> 30%
where the time goes in v3:
time: 217 us; the launch traced here: 216 us
  Pallas kernels  96.3 us (44%)
  waiting for transfers between devices  55.8 us (26%)
  starting transfers between devices  38.4 us (18%)
  local copies, waits for them, and re-layouts  14.5 us (7%)
  other arithmetic  8.46 us (4%)
  between operations  3.03 us (1%)
    ppermute x32, waiting for transfers between devices, swap(): return lax.ppermute(value, axis, [(i, i ^ bit) for i in range(n)])  55.8 us
    pallas_call x2, Pallas kernels, call_backward(): pl.pallas_call(functools.partial(ordered, functools.partial(attention_bac...  35.5 us
    ppermute x32, starting transfers between devices, swap(): return lax.ppermute(value, axis, [(i, i ^ bit) for i in range(n)])  32.2 us
    pallas_call x1, Pallas kernels, call_feed_forward(): pl.pallas_call(functools.partial(feed_forward, shards, tokens), grid=(chu...  26.8 us
    pallas_call x2, Pallas kernels, call_forward(): pl.pallas_call(functools.partial(ordered, functools.partial(attention_for...  25.1 us
    unnamed x49, local copies, waits for them, and re-layouts  9.84 us
    all_to_all x1, starting transfers between devices, local(): lax.all_to_all(every, ('rep', 'shard'), 0, 0).reshape(summed.shape)  6.23 us
    convert_element_type x7, other arithmetic, add_low(): return sum((part.astype(F32) for part in parts)).astype(BF16)  5.76 us
  transfers between devices with their start and end apart: 33, of which 16 were waited for; matrix products, arithmetic and copies ran while one was open for 4% of the time, Pallas kernels for 30%

profile of v3, /device:TPU:13, one launch (start us, length us, event | category | flops | bytes accessed | tf_op | source)
XLA Modules:
  0.0 216.4 jit_solution(7487045124549628079)
XLA Ops:
  1.9 2.0 pack.1
  4.1 2.4 %collective-permute-start.7 = (bf16[1,144,256]{2,1,0:T(8,128)(2,1)}, bf16[1,144,256]{2,1,0:T(8,128)(2,1)S(1)}, u32[]{:S(2)}, u32[]{:S(2)}) collective-permute-start(bf16[1,144,256]{2,1,0:T(8,128)(2,1)} %bitcast.106), channel_id=1, source_target_pairs={{0,6},{1,7},{2,4},{3,5},{4,2},{5,3},{6,0},{7,1},{8,14},{9,15},{10,... | collective-permute-start | bytes 221192 | tf_op jit(solution)/shard_map/ppermute | solution.py:760
  7.5 1.3 collective-permute-start.5
  12.3 6.5 %collective-permute-done.6 = bf16[1,144,256]{2,1,0:T(8,128)(2,1)S(1)} collective-permute-done((bf16[1,144,256]{2,1,0:T(8,128)(2,1)}, bf16[1,144,256]{2,1,0:T(8,128)(2,1)S(1)}, u32[]{:S(2)}, u32[]{:S(2)}) %collective-permute-start.6) | collective-permute-done | bytes 73760 | tf_op jit(solution)/shard_map/ppermute | solution.py:760
  21.4 4.1 %collective-permute-done.4 = bf16[1,288,256]{2,1,0:T(8,128)(2,1)S(1)} collective-permute-done((bf16[1,288,256]{2,1,0:T(8,128)(2,1)}, bf16[1,288,256]{2,1,0:T(8,128)(2,1)S(1)}, u32[]{:S(2)}, u32[]{:S(2)}) %collective-permute-start.4) | collective-permute-done | bytes 147488 | tf_op jit(solution)/shard_map/ppermute | solution.py:760
  29.7 6.7 %collective-permute-done.9 = bf16[4,144,256]{2,1,0:T(8,128)(2,1)S(1)} collective-permute-done((bf16[4,144,256]{2,1,0:T(8,128)(2,1)S(1)}, bf16[4,144,256]{2,1,0:T(8,128)(2,1)S(1)}, u32[]{:S(2)}, u32[]{:S(2)}) %collective-permute-start.9) | collective-permute-done | bytes 294944 | tf_op jit(solution)/shard_map/ppermute | solution.py:760
  36.5 2.2 %collective-permute-start.10 = (bf16[16,144,256]{2,1,0:T(8,128)(2,1)S(1)}, bf16[16,144,256]{2,1,0:T(8,128)(2,1)S(1)}, u32[]{:S(2)}, u32[]{:S(2)}) collective-permute-start(bf16[16,144,256]{2,1,0:T(8,128)(2,1)S(1)} %constant_dynamic-update-slice_fusion.refs_3_), channel_id=1, source_target_pairs={{0,8},{8,0},{16,24},{24,16},{1,9},{9,1},{17,25},{25,17},{2,10},{10... | collective-permute-start | bytes 3538952 | tf_op jit(solution)/shard_map/ppermute | solution.py:760
  42.6 13.5 %attention_forward_0.1 = (bf16[1024,256]{1,0:T(8,128)(2,1)}, bf16[1024,256]{1,0:T(8,128)(2,1)}, bf16[1024,256]{1,0:T(8,128)(2,1)}, bf16[1024,256]{1,0:T(8,128)(2...) custom-call(s32[1,1024]{1,0:T(1,128)} %refs_2_.9, ...), custom_call_target="tpu_custom_call" | custom-call | flops 1000 | bytes 1000 | tf_op jit(solution)/shard_map/attention_forward_0/pallas_call | solution.py:642
  58.6 11.6 %attention_forward_1.1 = (bf16[1024,256]{1,0:T(8,128)(2,1)}, bf16[1024,256]{1,0:T(8,128)(2,1)}, bf16[1024,256]{1,0:T(8,128)(2,1)}, bf16[1024,256]{1,0:T(8,128)(2...) custom-call(s32[1,1024]{1,0:T(1,128)} %refs_2_.9, ...), custom_call_target="tpu_custom_call" | custom-call | flops 1000 | bytes 1000 | tf_op jit(solution)/shard_map/attention_forward_1/pallas_call | solution.py:642
  70.7 1.7 collective-permute-done.14
  74.7 1.6 collective-permute-start.15
  76.2 4.2 %collective-permute-done.15.theirs_ref = bf16[16,288,256]{2,1,0:T(8,128)(2,1)S(1)} collective-permute-done((bf16[16,288,256]{2,1,0:T(8,128)(2,1)S(1)}, bf16[16,288,256]{2,1,0:T(8,128)(2,1)S(1)}, u32[]{:S(2)}, u32[]{:S(2)}) %collective-permute-start.15) | collective-permute-done | bytes 2359328 | tf_op jit(solution)/shard_map/ppermute | solution.py:760
  80.4 1.5 copy-done.2
  81.9 26.8 %feed_forward.1 = (bf16[1024,512]{1,0:T(8,128)(2,1)}, f32[1024,512]{1,0:T(8,128)}, bf16[1024,512]{1,0:T(8,128)(2,1)}, bf16[4,8,160,256]{3,2,1,0:T(8,128)(2,1)}, bf16[4,8,160,256]{3,2,1,0:T(8,128)(2,1)}) custom-call(bf16[1024,512]{1,0:T(8,128)(2,1)} %bitcast.95, bf16[1024,256]{1,0:T(8,128)(2,1)} %get-tuple-element.73.mix_0_ref, ...), custom_call_target="tpu_custom_call" | custom-call | flops 1000 | bytes 1000 | tf_op jit(solution)/shard_map/feed_forward/pallas_call | solution.py:664
  109.2 4.7 %collective-permute-done.16 = bf16[4,8,160,256]{3,2,1,0:T(8,128)(2,1)S(1)} collective-permute-done((bf16[4,8,160,256]{3,2,1,0:T(8,128)(2,1)}, bf16[4,8,160,256]{3,2,1,0:T(8,128)(2,1)S(1)}, u32[]{:S(2)}, u32[]{:S(2)}) %collective-permute-start.16) | collective-permute-done | bytes 2621472 | tf_op jit(solution)/shard_map/ppermute | solution.py:760
  113.9 4.2 %add_convert_fusion = bf16[4,8,160,256]{3,2,1,0:T(8,128)(2,1)} fusion(bf16[4,8,160,256]{3,2,1,0:T(8,128)(2,1)S(1)} %collective-permute-done.16, bf16[4,8,160,256]{3,2,1,0:T(8,128)(2,1)} %get-tuple-element.103), kind=kLoop, calls=%fused_computation | loop fusion | flops 5242880 | bytes 7864320 | tf_op jit(solution)/shard_map/convert_element_type | solution.py:894
  118.1 6.2 %all-to-all-start = ((bf16[32,160,256]{2,1,0:T(8,128)(2,1)}), bf16[32,160,256]{2,1,0:T(8,128)(2,1)S(1)}, u32[]{:S(2)}, u32[]{:S(2)}) async-start(bf16[32,160,256]{2,1,0:T(8,128)(2,1)} %bitcast.11.refs_15_), calls=%async_computation | async-start | bytes 5242880 | tf_op jit(solution)/shard_map/all_to_all | solution.py:1048
  124.3 17.5 %attention_backward_0.1 = (f32[1024,512]{1,0:T(8,128)}, bf16[2,2,4,144,128]{4,3,2,1,0:T(8,128)(2,1)}, bf16[2,2,4,144,128]{4,3,2,1,0:T(8,128)(2,1)}) custom-call(s32[1,1024]{1,0:T(1,128)} %refs_2_.9, bf16[1024,512]{1,0:T(8,128)(2,1)} %bitcast.96, s32[1,1024]{1,0:T(1,128)} %refs_2_.9, bf16[1024,256]{1,0:T(8,128)(2,1)} %get-tuple-element.94.refs_3_, ...), custom_call_target="tpu_custom_call" | custom-call | flops 1000 | bytes 1000 | tf_op jit(solution)/shard_map/attention_backward_0/pallas_call | solution.py:739
  141.8 18.0 %attention_backward_1.1 = (f32[1024,512]{1,0:T(8,128)}, bf16[2,2,4,144,128]{4,3,2,1,0:T(8,128)(2,1)}, bf16[2,2,4,144,128]{4,3,2,1,0:T(8,128)(2,1)}) custom-call(s32[1,1024]{1,0:T(1,128)} %refs_2_.9, bf16[1024,512]{1,0:T(8,128)(2,1)} %bitcast.97, s32[1,1024]{1,0:T(1,128)} %refs_2_.9, bf16[1024,256]{1,0:T(8,128)(2,1)} %get-tuple-element.84.refs_3_, ...), custom_call_target="tpu_custom_call" | custom-call | flops 1000 | bytes 1000 | tf_op jit(solution)/shard_map/attention_backward_1/pallas_call | solution.py:739
  160.4 1.7 collective-permute-done.20
  165.1 7.6 %collective-permute-done.21 = bf16[2,4,144,128]{3,2,1,0:T(8,128)(2,1)S(1)} collective-permute-done((bf16[2,4,144,128]{3,2,1,0:T(8,128)(2,1)S(1)}, bf16[2,4,144,128]{3,2,1,0:T(8,128)(2,1)S(1)}, u32[]{:S(2)}, u32[]{:S(2)}) %collective-permute-start.21) | collective-permute-done | bytes 294944 | tf_op jit(solution)/shard_map/ppermute | solution.py:760
  172.7 3.2 %collective-permute-start.22 = (bf16[4,144,128]{2,1,0:T(8,128)(2,1)S(1)}, bf16[4,144,128]{2,1,0:T(8,128)(2,1)S(1)}, u32[]{:S(2)}, u32[]{:S(2)}) collective-permute-start(bf16[4,144,128]{2,1,0:T(8,128)(2,1)S(1)} %get-tuple-element.133), channel_id=1, source_target_pairs={{0,1},{1,0},{2,3},{3,2},{4,5},{5,4},{6,7},{7,6},{8,9},{9,8},{10,11... | collective-permute-start | bytes 442376 | tf_op jit(solution)/shard_map/ppermute | solution.py:760
  176.0 5.6 %collective-permute-done.18 = bf16[2,4,144,128]{3,2,1,0:T(8,128)(2,1)S(1)} collective-permute-done((bf16[2,4,144,128]{3,2,1,0:T(8,128)(2,1)S(1)}, bf16[2,4,144,128]{3,2,1,0:T(8,128)(2,1)S(1)}, u32[]{:S(2)}, u32[]{:S(2)}) %collective-permute-start.18) | collective-permute-done | bytes 294944 | tf_op jit(solution)/shard_map/ppermute | solution.py:760
  182.5 2.2 %collective-permute-done.22 = bf16[4,144,128]{2,1,0:T(8,128)(2,1)S(1)} collective-permute-done((bf16[4,144,128]{2,1,0:T(8,128)(2,1)S(1)}, bf16[4,144,128]{2,1,0:T(8,128)(2,1)S(1)}, u32[]{:S(2)}, u32[]{:S(2)}) %collective-permute-start.22) | collective-permute-done | bytes 147488 | tf_op jit(solution)/shard_map/ppermute | solution.py:760
  184.7 1.8 collective-permute-done.19
  186.7 3.4 %collective-permute-start.26 = (bf16[1,288,128]{2,1,0:T(8,128)(2,1)S(1)}, bf16[1,288,128]{2,1,0:T(8,128)(2,1)S(1)}, u32[]{:S(2)}, u32[]{:S(2)}) collective-permute-start(bf16[1,288,128]{2,1,0:T(8,128)(2,1)S(1)} %pad_maximum_fusion.7), channel_id=1, source_target_pairs={{0,2},{1,3},{2,0},{3,1},{4,6},{5,7},{6,4},{7,5},{8,10},{9,11},{10,... | collective-permute-start | bytes 221192 | tf_op jit(solution)/shard_map/ppermute | solution.py:760
  190.8 1.5 copy-done
  192.3 2.7 %add_arrived.1.refs_0_ = bf16[2,160,256]{2,1,0:T(8,128)(2,1)} custom-call(bf16[4,8,160,256]{3,2,1,0:T(8,128)(2,1)} %bitcast.98, bf16[1,288,128]{2,1,0:T(8,128)(2,1)} %pad_maximum_fusion.6.refs_1_), custom_call_target="tpu_custom_call" | custom-call | flops 1000 | bytes 1000 | tf_op jit(solution)/shard_map/add_arrived/pallas_call | solution.py:796
  195.0 3.0 %collective-permute-start.25 = (bf16[2,160,256]{2,1,0:T(8,128)(2,1)}, bf16[2,160,256]{2,1,0:T(8,128)(2,1)S(1)}, u32[]{:S(2)}, u32[]{:S(2)}) collective-permute-start(bf16[2,160,256]{2,1,0:T(8,128)(2,1)} %add_arrived.1.refs_0_), channel_id=1, source_target_pairs={{0,24},{8,16},{16,8},{24,0},{1,25},{9,17},{17,9},{25,1},{2,26},{10... | collective-permute-start | bytes 491528 | tf_op jit(solution)/shard_map/ppermute | solution.py:760
  200.7 7.4 %collective-permute-done.31.refs_3_ = bf16[288,128]{1,0:T(8,128)(2,1)S(1)} collective-permute-done((bf16[288,128]{1,0:T(8,128)(2,1)S(1)}, bf16[288,128]{1,0:T(8,128)(2,1)S(1)}, u32[]{:S(2)}, u32[]{:S(2)}) %collective-permute-start.31) | collective-permute-done | bytes 73760 | tf_op jit(solution)/shard_map/ppermute | solution.py:760
  210.9 1.8 assemble.3
  214.1 2.3 %assemble.2 = (f32[256,512]{1,0:T(8,128)}, f32[64,2048]{1,0:T(8,128)}, f32[64,512]{1,0:T(8,128)}, f32[1,256]{1,0:T(1,128)}, f32[1,64]{1,0:T(1,128)}, /*index=5*/...) custom-call(f32[8,128]{1,0:T(8,128)} %get-tuple-element.80.count_ref, bf16[2,160,256]{2,1,0:T(8,128)(2,1)} %add_arrived.1.refs_0_, ...), custom_call_target="tpu_custom_call" | custom-call | flops 1000 | bytes 1000 | tf_op jit(solution)/shard_map/assemble/pallas_call | solution.py:882
  (118 shorter events, 32.4 us)
Async XLA Ops:
  3.9 5.9 %collective-permute-start = (bf16[1,144,256]{2,1,0:T(8,128)(2,1)}, bf16[1,144,256]{2,1,0:T(8,128)(2,1)S(1)}, u32[]{:S(2)}, u32[]{:S(2)}) collective-permute-start(bf16[1,144,256]{2,1,0:T(8,128)(2,1)} %bitcast.105), channel_id=1, source_target_pairs={{0,2},{1,3},{2,0},{3,1},{4,6},{5,7},{6,4},{7,5},{8,10},{9,11},{10,... | collective-permute-start | bytes 221192 | tf_op jit(solution)/shard_map/ppermute | solution.py:760
  4.1 7.8 %collective-permute-start.7 = (bf16[1,144,256]{2,1,0:T(8,128)(2,1)}, bf16[1,144,256]{2,1,0:T(8,128)(2,1)S(1)}, u32[]{:S(2)}, u32[]{:S(2)}) collective-permute-start(bf16[1,144,256]{2,1,0:T(8,128)(2,1)} %bitcast.106), channel_id=1, source_target_pairs={{0,6},{1,7},{2,4},{3,5},{4,2},{5,3},{6,0},{7,1},{8,14},{9,15},{10,... | collective-permute-start | bytes 221192 | tf_op jit(solution)/shard_map/ppermute | solution.py:760
  6.6 12.3 %collective-permute-start.6 = (bf16[1,144,256]{2,1,0:T(8,128)(2,1)}, bf16[1,144,256]{2,1,0:T(8,128)(2,1)S(1)}, u32[]{:S(2)}, u32[]{:S(2)}) collective-permute-start(bf16[1,144,256]{2,1,0:T(8,128)(2,1)} %bitcast.107), channel_id=1, source_target_pairs={{0,4},{1,5},{2,6},{3,7},{4,0},{5,1},{6,2},{7,3},{8,12},{9,13},{10,... | collective-permute-start | bytes 221192 | tf_op jit(solution)/shard_map/ppermute | solution.py:760
  7.5 20.3 %collective-permute-start.5 = (bf16[1,288,256]{2,1,0:T(8,128)(2,1)}, bf16[1,288,256]{2,1,0:T(8,128)(2,1)S(1)}, u32[]{:S(2)}, u32[]{:S(2)}) collective-permute-start(bf16[1,288,256]{2,1,0:T(8,128)(2,1)} %bitcast.99), channel_id=1, source_target_pairs={{0,6},{1,7},{2,4},{3,5},{4,2},{5,3},{6,0},{7,1},{8,14},{9,15},{10,... | collective-permute-start | bytes 442376 | tf_op jit(solution)/shard_map/ppermute | solution.py:760
  8.8 16.7 %collective-permute-start.4 = (bf16[1,288,256]{2,1,0:T(8,128)(2,1)}, bf16[1,288,256]{2,1,0:T(8,128)(2,1)S(1)}, u32[]{:S(2)}, u32[]{:S(2)}) collective-permute-start(bf16[1,288,256]{2,1,0:T(8,128)(2,1)} %bitcast.100), channel_id=1, source_target_pairs={{0,4},{1,5},{2,6},{3,7},{4,0},{5,1},{6,2},{7,3},{8,12},{9,13},{10,... | collective-permute-start | bytes 442376 | tf_op jit(solution)/shard_map/ppermute | solution.py:760
  10.7 9.4 %collective-permute-start.1 = (bf16[2,144,256]{2,1,0:T(8,128)(2,1)S(1)}, bf16[2,144,256]{2,1,0:T(8,128)(2,1)S(1)}, u32[]{:S(2)}, u32[]{:S(2)}) collective-permute-start(bf16[2,144,256]{2,1,0:T(8,128)(2,1)S(1)} %pad_maximum_fusion.4), channel_id=1, source_target_pairs={{0,1},{1,0},{2,3},{3,2},{4,5},{5,4},{6,7},{7,6},{8,9},{9,8},{10,11... | collective-permute-start | bytes 442376 | tf_op jit(solution)/shard_map/ppermute | solution.py:760
  11.9 14.1 %collective-permute-start.3 = (bf16[1,288,256]{2,1,0:T(8,128)(2,1)}, bf16[1,288,256]{2,1,0:T(8,128)(2,1)S(1)}, u32[]{:S(2)}, u32[]{:S(2)}) collective-permute-start(bf16[1,288,256]{2,1,0:T(8,128)(2,1)} %bitcast.101), channel_id=1, source_target_pairs={{0,2},{1,3},{2,0},{3,1},{4,6},{5,7},{6,4},{7,5},{8,10},{9,11},{10,... | collective-permute-start | bytes 442376 | tf_op jit(solution)/shard_map/ppermute | solution.py:760
  18.9 10.2 %collective-permute-start.8 = (bf16[2,144,256]{2,1,0:T(8,128)(2,1)S(1)}, bf16[2,144,256]{2,1,0:T(8,128)(2,1)S(1)}, u32[]{:S(2)}, u32[]{:S(2)}) collective-permute-start(bf16[2,144,256]{2,1,0:T(8,128)(2,1)S(1)} %pad_maximum_fusion.5), channel_id=1, source_target_pairs={{0,16},{8,24},{16,0},{24,8},{1,17},{9,25},{17,1},{25,9},{2,18},{10... | collective-permute-start | bytes 442376 | tf_op jit(solution)/shard_map/ppermute | solution.py:760
  21.1 8.5 %collective-permute-start.2 = (bf16[4,144,256]{2,1,0:T(8,128)(2,1)S(1)}, bf16[4,144,256]{2,1,0:T(8,128)(2,1)S(1)}, u32[]{:S(2)}, u32[]{:S(2)}) collective-permute-start(bf16[4,144,256]{2,1,0:T(8,128)(2,1)S(1)} %pad_maximum_fusion.1), channel_id=1, source_target_pairs={{0,16},{8,24},{16,0},{24,8},{1,17},{9,25},{17,1},{25,9},{2,18},{10... | collective-permute-start | bytes 884744 | tf_op jit(solution)/shard_map/ppermute | solution.py:760
  29.1 7.3 %collective-permute-start.9 = (bf16[4,144,256]{2,1,0:T(8,128)(2,1)S(1)}, bf16[4,144,256]{2,1,0:T(8,128)(2,1)S(1)}, u32[]{:S(2)}, u32[]{:S(2)}) collective-permute-start(bf16[4,144,256]{2,1,0:T(8,128)(2,1)S(1)} %pad_maximum_fusion.2), channel_id=1, source_target_pairs={{0,1},{1,0},{2,3},{3,2},{4,5},{5,4},{6,7},{7,6},{8,9},{9,8},{10,11... | collective-permute-start | bytes 884744 | tf_op jit(solution)/shard_map/ppermute | solution.py:760
  36.5 5.1 %collective-permute-start.10 = (bf16[16,144,256]{2,1,0:T(8,128)(2,1)S(1)}, bf16[16,144,256]{2,1,0:T(8,128)(2,1)S(1)}, u32[]{:S(2)}, u32[]{:S(2)}) collective-permute-start(bf16[16,144,256]{2,1,0:T(8,128)(2,1)S(1)} %constant_dynamic-update-slice_fusion.refs_3_), channel_id=1, source_target_pairs={{0,8},{8,0},{16,24},{24,16},{1,9},{9,1},{17,25},{25,17},{2,10},{10... | collective-permute-start | bytes 3538952 | tf_op jit(solution)/shard_map/ppermute | solution.py:760
  38.7 17.4 %collective-permute-start.11 = (bf16[2,288,256]{2,1,0:T(8,128)(2,1)S(1)}, bf16[2,288,256]{2,1,0:T(8,128)(2,1)S(1)}, u32[]{:S(2)}, u32[]{:S(2)}) collective-permute-start(bf16[2,288,256]{2,1,0:T(8,128)(2,1)S(1)} %pad_maximum_fusion.3.refs_5_), channel_id=1, source_target_pairs={{0,1},{1,0},{2,3},{3,2},{4,5},{5,4},{6,7},{7,6},{8,9},{9,8},{10,11... | collective-permute-start | bytes 884744 | tf_op jit(solution)/shard_map/ppermute | solution.py:760
  40.4 15.8 %collective-permute-start.12 = (bf16[2,288,256]{2,1,0:T(8,128)(2,1)S(1)}, bf16[2,288,256]{2,1,0:T(8,128)(2,1)S(1)}, u32[]{:S(2)}, u32[]{:S(2)}) collective-permute-start(bf16[2,288,256]{2,1,0:T(8,128)(2,1)S(1)} %get-tuple-element.143.refs_6_), channel_id=1, source_target_pairs={{0,16},{8,24},{16,0},{24,8},{1,17},{9,25},{17,1},{25,9},{2,18},{10... | collective-permute-start | bytes 884744 | tf_op jit(solution)/shard_map/ppermute | solution.py:760
  56.2 14.5 %collective-permute-start.13 = (bf16[4,288,256]{2,1,0:T(8,128)(2,1)S(1)}, bf16[4,288,256]{2,1,0:T(8,128)(2,1)}, u32[]{:S(2)}, u32[]{:S(2)}) collective-permute-start(bf16[4,288,256]{2,1,0:T(8,128)(2,1)S(1)} %pad_maximum_fusion.refs_5_), channel_id=1, source_target_pairs={{0,16},{8,24},{16,0},{24,8},{1,17},{9,25},{17,1},{25,9},{2,18},{10... | collective-permute-start | bytes 1769480 | tf_op jit(solution)/shard_map/ppermute | solution.py:760
  57.8 14.5 %collective-permute-start.14 = (bf16[4,288,256]{2,1,0:T(8,128)(2,1)}, bf16[4,288,256]{2,1,0:T(8,128)(2,1)}, u32[]{:S(2)}, u32[]{:S(2)}) collective-permute-start(bf16[4,288,256]{2,1,0:T(8,128)(2,1)} %constant_dynamic-update-slice_fusion.9.refs_6_), channel_id=1, source_target_pairs={{0,1},{1,0},{2,3},{3,2},{4,5},{5,4},{6,7},{7,6},{8,9},{9,8},{10,11... | collective-permute-start | bytes 1769480 | tf_op jit(solution)/shard_map/ppermute | solution.py:760
  74.7 5.7 %collective-permute-start.15 = (bf16[16,288,256]{2,1,0:T(8,128)(2,1)S(1)}, bf16[16,288,256]{2,1,0:T(8,128)(2,1)S(1)}, u32[]{:S(2)}, u32[]{:S(2)}) collective-permute-start(bf16[16,288,256]{2,1,0:T(8,128)(2,1)S(1)} %constant_dynamic-update-slice_fusion.12.mine_ref), channel_id=1, source_target_pairs={{0,8},{8,0},{16,24},{24,16},{1,9},{9,1},{17,25},{25,17},{2,10},{10... | collective-permute-start | bytes 7077896 | tf_op jit(solution)/shard_map/ppermute | solution.py:760
  108.7 5.2 %collective-permute-start.16 = (bf16[4,8,160,256]{3,2,1,0:T(8,128)(2,1)}, bf16[4,8,160,256]{3,2,1,0:T(8,128)(2,1)S(1)}, u32[]{:S(2)}, u32[]{:S(2)}) collective-permute-start(bf16[4,8,160,256]{3,2,1,0:T(8,128)(2,1)} %get-tuple-element.104), channel_id=1, source_target_pairs={{0,8},{8,0},{16,24},{24,16},{1,9},{9,1},{17,25},{25,17},{2,10},{10... | collective-permute-start | bytes 7864328 | tf_op jit(solution)/shard_map/ppermute | solution.py:760
  118.1 72.7 %all-to-all-start = ((bf16[32,160,256]{2,1,0:T(8,128)(2,1)}), bf16[32,160,256]{2,1,0:T(8,128)(2,1)S(1)}, u32[]{:S(2)}, u32[]{:S(2)}) async-start(bf16[32,160,256]{2,1,0:T(8,128)(2,1)} %bitcast.11.refs_15_), calls=%async_computation | async-start | bytes 5242880 | tf_op jit(solution)/shard_map/all_to_all | solution.py:1048
  159.8 2.3 %collective-permute-start.20 = (bf16[2,2,4,144,128]{4,3,2,1,0:T(8,128)(2,1)}, bf16[2,2,4,144,128]{4,3,2,1,0:T(8,128)(2,1)S(1)}, u32[]{:S(2)}, u32[]{:S(2)}) collective-permute-start(bf16[2,2,4,144,128]{4,3,2,1,0:T(8,128)(2,1)} %get-tuple-element.111), channel_id=1, source_target_pairs={{0,8},{8,0},{16,24},{24,16},{1,9},{9,1},{17,25},{25,17},{2,10},{10... | collective-permute-start | bytes 1769480 | tf_op jit(solution)/shard_map/ppermute | solution.py:760
  160.3 4.3 %collective-permute-start.17 = (bf16[2,2,4,144,128]{4,3,2,1,0:T(8,128)(2,1)}, bf16[2,2,4,144,128]{4,3,2,1,0:T(8,128)(2,1)S(1)}, u32[]{:S(2)}, u32[]{:S(2)}) collective-permute-start(bf16[2,2,4,144,128]{4,3,2,1,0:T(8,128)(2,1)} %get-tuple-element.109), channel_id=1, source_target_pairs={{0,8},{8,0},{16,24},{24,16},{1,9},{9,1},{17,25},{25,17},{2,10},{10... | collective-permute-start | bytes 1769480 | tf_op jit(solution)/shard_map/ppermute | solution.py:760
  163.3 9.3 %collective-permute-start.21 = (bf16[2,4,144,128]{3,2,1,0:T(8,128)(2,1)S(1)}, bf16[2,4,144,128]{3,2,1,0:T(8,128)(2,1)S(1)}, u32[]{:S(2)}, u32[]{:S(2)}) collective-permute-start(bf16[2,4,144,128]{3,2,1,0:T(8,128)(2,1)S(1)} %get-tuple-element.129), channel_id=1, source_target_pairs={{0,16},{8,24},{16,0},{24,8},{1,17},{9,25},{17,1},{25,9},{2,18},{10... | collective-permute-start | bytes 884744 | tf_op jit(solution)/shard_map/ppermute | solution.py:760
  164.7 16.8 %collective-permute-start.18 = (bf16[2,4,144,128]{3,2,1,0:T(8,128)(2,1)S(1)}, bf16[2,4,144,128]{3,2,1,0:T(8,128)(2,1)S(1)}, u32[]{:S(2)}, u32[]{:S(2)}) collective-permute-start(bf16[2,4,144,128]{3,2,1,0:T(8,128)(2,1)S(1)} %get-tuple-element.127), channel_id=1, source_target_pairs={{0,1},{1,0},{2,3},{3,2},{4,5},{5,4},{6,7},{7,6},{8,9},{9,8},{10,11... | collective-permute-start | bytes 884744 | tf_op jit(solution)/shard_map/ppermute | solution.py:760
  172.7 12.0 %collective-permute-start.22 = (bf16[4,144,128]{2,1,0:T(8,128)(2,1)S(1)}, bf16[4,144,128]{2,1,0:T(8,128)(2,1)S(1)}, u32[]{:S(2)}, u32[]{:S(2)}) collective-permute-start(bf16[4,144,128]{2,1,0:T(8,128)(2,1)S(1)} %get-tuple-element.133), channel_id=1, source_target_pairs={{0,1},{1,0},{2,3},{3,2},{4,5},{5,4},{6,7},{7,6},{8,9},{9,8},{10,11... | collective-permute-start | bytes 442376 | tf_op jit(solution)/shard_map/ppermute | solution.py:760
  181.6 4.9 %collective-permute-start.19 = (bf16[4,144,128]{2,1,0:T(8,128)(2,1)S(1)}, bf16[4,144,128]{2,1,0:T(8,128)(2,1)S(1)}, u32[]{:S(2)}, u32[]{:S(2)}) collective-permute-start(bf16[4,144,128]{2,1,0:T(8,128)(2,1)S(1)} %get-tuple-element.131), channel_id=1, source_target_pairs={{0,16},{8,24},{16,0},{24,8},{1,17},{9,25},{17,1},{25,9},{2,18},{10... | collective-permute-start | bytes 442376 | tf_op jit(solution)/shard_map/ppermute | solution.py:760
  186.5 12.1 %collective-permute-start.27 = (bf16[1,288,128]{2,1,0:T(8,128)(2,1)S(1)}, bf16[1,288,128]{2,1,0:T(8,128)(2,1)S(1)}, u32[]{:S(2)}, u32[]{:S(2)}) collective-permute-start(bf16[1,288,128]{2,1,0:T(8,128)(2,1)S(1)} %pad_maximum_fusion.8), channel_id=1, source_target_pairs={{0,4},{1,5},{2,6},{3,7},{4,0},{5,1},{6,2},{7,3},{8,12},{9,13},{10,... | collective-permute-start | bytes 221192 | tf_op jit(solution)/shard_map/ppermute | solution.py:760
  186.6 12.0 %collective-permute-start.28 = (bf16[1,288,128]{2,1,0:T(8,128)(2,1)S(1)}, bf16[1,288,128]{2,1,0:T(8,128)(2,1)S(1)}, u32[]{:S(2)}, u32[]{:S(2)}) collective-permute-start(bf16[1,288,128]{2,1,0:T(8,128)(2,1)S(1)} %pad_maximum_fusion.9), channel_id=1, source_target_pairs={{0,6},{1,7},{2,4},{3,5},{4,2},{5,3},{6,0},{7,1},{8,14},{9,15},{10,... | collective-permute-start | bytes 221192 | tf_op jit(solution)/shard_map/ppermute | solution.py:760
  186.7 11.9 %collective-permute-start.26 = (bf16[1,288,128]{2,1,0:T(8,128)(2,1)S(1)}, bf16[1,288,128]{2,1,0:T(8,128)(2,1)S(1)}, u32[]{:S(2)}, u32[]{:S(2)}) collective-permute-start(bf16[1,288,128]{2,1,0:T(8,128)(2,1)S(1)} %pad_maximum_fusion.7), channel_id=1, source_target_pairs={{0,2},{1,3},{2,0},{3,1},{4,6},{5,7},{6,4},{7,5},{8,10},{9,11},{10,... | collective-permute-start | bytes 221192 | tf_op jit(solution)/shard_map/ppermute | solution.py:760
  195.0 17.7 %collective-permute-start.25 = (bf16[2,160,256]{2,1,0:T(8,128)(2,1)}, bf16[2,160,256]{2,1,0:T(8,128)(2,1)S(1)}, u32[]{:S(2)}, u32[]{:S(2)}) collective-permute-start(bf16[2,160,256]{2,1,0:T(8,128)(2,1)} %add_arrived.1.refs_0_), channel_id=1, source_target_pairs={{0,24},{8,16},{16,8},{24,0},{1,25},{9,17},{17,9},{25,1},{2,26},{10... | collective-permute-start | bytes 491528 | tf_op jit(solution)/shard_map/ppermute | solution.py:760
  198.0 14.7 %collective-permute-start.24 = (bf16[2,160,256]{2,1,0:T(8,128)(2,1)}, bf16[2,160,256]{2,1,0:T(8,128)(2,1)S(1)}, u32[]{:S(2)}, u32[]{:S(2)}) collective-permute-start(bf16[2,160,256]{2,1,0:T(8,128)(2,1)} %add_arrived.1.refs_0_), channel_id=1, source_target_pairs={{0,16},{8,24},{16,0},{24,8},{1,17},{9,25},{17,1},{25,9},{2,18},{10... | collective-permute-start | bytes 491528 | tf_op jit(solution)/shard_map/ppermute | solution.py:760
  198.7 14.1 %collective-permute-start.23 = (bf16[2,160,256]{2,1,0:T(8,128)(2,1)}, bf16[2,160,256]{2,1,0:T(8,128)(2,1)S(1)}, u32[]{:S(2)}, u32[]{:S(2)}) collective-permute-start(bf16[2,160,256]{2,1,0:T(8,128)(2,1)} %add_arrived.1.refs_0_), channel_id=1, source_target_pairs={{0,8},{8,0},{16,24},{24,16},{1,9},{9,1},{17,25},{25,17},{2,10},{10... | collective-permute-start | bytes 491528 | tf_op jit(solution)/shard_map/ppermute | solution.py:760
  198.7 9.3 %collective-permute-start.31 = (bf16[288,128]{1,0:T(8,128)(2,1)S(1)}, bf16[288,128]{1,0:T(8,128)(2,1)S(1)}, u32[]{:S(2)}, u32[]{:S(2)}) collective-permute-start(bf16[288,128]{1,0:T(8,128)(2,1)S(1)} %fusion.8.refs_0_), channel_id=1, source_target_pairs={{0,24},{8,16},{16,8},{24,0},{1,25},{9,17},{17,9},{25,1},{2,26},{10... | collective-permute-start | bytes 221192 | tf_op jit(solution)/shard_map/ppermute | solution.py:760
  200.0 9.6 %collective-permute-start.30 = (bf16[288,128]{1,0:T(8,128)(2,1)S(1)}, bf16[288,128]{1,0:T(8,128)(2,1)S(1)}, u32[]{:S(2)}, u32[]{:S(2)}) collective-permute-start(bf16[288,128]{1,0:T(8,128)(2,1)S(1)} %fusion.8.refs_0_), channel_id=1, source_target_pairs={{0,16},{8,24},{16,0},{24,8},{1,17},{9,25},{17,1},{25,9},{2,18},{10... | collective-permute-start | bytes 221192 | tf_op jit(solution)/shard_map/ppermute | solution.py:760
  (18 other events, 98.6 us)

commit v4 on v3

--- a/solution.py
+++ b/solution.py
@@ -10,6 +10,8 @@
 HEADS = 8
 EPSILON = 1e-05
 CHUNK = 256
+SUB = 128
+BACK = 512
 ROWS = 512
 QUAD = 256
 F32 = jnp.float32
@@ -66,15 +68,23 @@
 
 
 def causal_mask(column, row):
-    at = lax.broadcasted_iota(jnp.int32, (CHUNK, CHUNK), 0)
-    source = lax.broadcasted_iota(jnp.int32, (CHUNK, CHUNK), 1)
-    return jnp.where((column == row) & (source <= at), 1.0, 0.0)
+    at = lax.broadcasted_iota(jnp.int32, (SUB, SUB), 0)
+    source = lax.broadcasted_iota(jnp.int32, (SUB, SUB), 1)
+    return jnp.where((column[:, :SUB] == row) & (source <= at), 1.0, 0.0).astype(BF16)
 
 
 def causal_mask_transposed(column, row):
-    source = lax.broadcasted_iota(jnp.int32, (CHUNK, CHUNK), 0)
-    at = lax.broadcasted_iota(jnp.int32, (CHUNK, CHUNK), 1)
-    return jnp.where((column == row) & (source <= at), 1.0, 0.0)
+    source = lax.broadcasted_iota(jnp.int32, (SUB, SUB), 0)
+    at = lax.broadcasted_iota(jnp.int32, (SUB, SUB), 1)
+    return jnp.where((column[:, :SUB] == row) & (source <= at), 1.0, 0.0).astype(BF16)
+
+
+def head_stack(values):
+    return jnp.concatenate([values * lanes for lanes in head_lanes()], axis=0)
+
+
+def four_times(mask):
+    return jnp.concatenate([mask] * 4, axis=1)
 
 
 def per_head(values, reduce, fill):
@@ -237,55 +247,67 @@
     if quad == 0:
         pl.when(step == 0)(assemble)
 
-    start = step * CHUNK
-    segment_last = seg_s[0, start + CHUNK - 1]
-    segment_before = jnp.where(step == 0, -1, seg_s[0, jnp.maximum(start - 1, 0)])
-    keep = jnp.where(segment_last == segment_before, 1.0, 0.0)
-    row = seg_ref[...].astype(F32)
-    column = as_column(row, CHUNK)
-    causal = causal_mask(column, row).astype(BF16)
-    enters = jnp.where(column == segment_before.astype(F32), 1.0, 0.0)
-    leaves = jnp.where(column == segment_last.astype(F32), 1.0, 0.0).astype(BF16)
-    lanes = head_lanes()
+    row_all = seg_ref[...].astype(F32)
     diagonal = block_diagonal()
-
     normal, _ = standardise(x_ref[...].astype(F32))
     normed = (normal * vec_ref[0:1, :] + vec_ref[1:2, :]).astype(BF16)
-    queries = nn(normed, weight(0)).astype(BF16)
-    keys = nn(normed, weight(1)).astype(BF16)
-    values = nn(normed, weight(2)).astype(BF16)
-    slots = jnp.exp(nn(normed, weight(3))).astype(BF16)
-    q_ref[...] = queries
-    k_ref[...] = keys
-    v_ref[...] = values
-    e_ref[...] = slots
-    totals = nn(causal, slots) + enters * total_state[0:1, :]
-    total_state[0:1, :] = totals[CHUNK - 1 : CHUNK, :]
-    inverse = 1.0 / totals
-    rz_ref[...] = inverse
-    one = first_state[...].astype(BF16)
-    two = second_state[...].astype(BF16)
-    one_ref[0] = one
-    two_ref[0] = two
-    scores = jnp.concatenate(
-        [nt(queries * lanes[h], keys).astype(BF16) * causal for h in range(4)], axis=1
-    )
-    gathered = nn(scores, jnp.concatenate([slots * lanes[h] for h in range(4)], axis=0))
-    gathered += enters * nn(queries, one)
-    slot_scores = gathered * (inverse * 0.125)
-    raised = jnp.exp(slot_scores - per_head(slot_scores, jnp.max, -jnp.inf))
-    shares = raised / per_head(raised, jnp.sum, 0.0)
-    s_ref[...] = slot_scores.astype(BF16)
-    p_ref[...] = shares.astype(BF16)
-    scaled = (shares * inverse).astype(BF16)
-    mixing = jnp.concatenate(
-        [nt(scaled * lanes[h], slots).astype(BF16) * causal for h in range(4)], axis=1
-    )
-    mixed = nn(mixing, jnp.concatenate([values * lanes[h] for h in range(4)], axis=0))
-    mixed += enters * nn(scaled, two)
-    mix_ref[...] = mixed.astype(BF16)
-    first_state[...] = keep * first_state[...] + diagonal * tn(keys * leaves, slots)
-    second_state[...] = keep * second_state[...] + diagonal * tn(slots * leaves, values)
+    q_ref[...] = nn(normed, weight(0)).astype(BF16)
+    k_ref[...] = nn(normed, weight(1)).astype(BF16)
+    v_ref[...] = nn(normed, weight(2)).astype(BF16)
+    e_ref[...] = jnp.exp(nn(normed, weight(3))).astype(BF16)
+    subs = range(CHUNK // SUB)
+    spans = [slice(sub * SUB, (sub + 1) * SUB) for sub in subs]
+    q, k, v, e = ([ref[rows] for rows in spans] for ref in (q_ref, k_ref, v_ref, e_ref))
+    causal, causal_4, enters, one, two, totals = [], [], [], [], [], []
+    first, second, running = first_state[...], second_state[...], total_state[0:1, :]
+    for sub in subs:
+        start = step * CHUNK + sub * SUB
+        segment_last = seg_s[0, start + SUB - 1]
+        segment_before = jnp.where(start == 0, -1, seg_s[0, jnp.maximum(start - 1, 0)])
+        keep = jnp.where(segment_last == segment_before, 1.0, 0.0)
+        row = row_all[:, spans[sub]]
+        column = as_column(row, QUAD)
+        causal.append(causal_mask(column, row))
+        causal_4.append(four_times(causal[sub]))
+        enters.append(jnp.where(column == segment_before.astype(F32), 1.0, 0.0))
+        leaves = jnp.where(column == segment_last.astype(F32), 1.0, 0.0).astype(BF16)
+        one.append(first.astype(BF16))
+        two.append(second.astype(BF16))
+        one_ref[sub] = one[sub]
+        two_ref[sub] = two[sub]
+        totals.append(nn(causal[sub], e[sub]) + enters[sub] * running)
+        running = totals[sub][SUB - 1 : SUB, :]
+        first = keep * first + diagonal * tn(k[sub] * leaves, e[sub])
+        second = keep * second + diagonal * tn(e[sub] * leaves, v[sub])
+    first_state[...] = first
+    second_state[...] = second
+    total_state[0:1, :] = running
+
+    def each(function, *lists):
+        return [function(*values) for values in zip(*lists)]
+
+    def store(ref, values):
+        for rows, value in zip(spans, values):
+            ref[rows] = value
+
+    inverse = each(lambda a: 1.0 / a, totals)
+    store(rz_ref, inverse)
+    e_stack = each(head_stack, e)
+    scores = each(lambda a, b, c: nt(a, head_stack(b)).astype(BF16) * c, q, k, causal_4)
+    gathered = each(
+        lambda a, b, c, d, f: nn(a, b) + c * nn(d, f), scores, e_stack, enters, q, one
+    )
+    slot_scores = each(lambda a, b: a * (b * 0.125), gathered, inverse)
+    raised = each(lambda a: jnp.exp(a - per_head(a, jnp.max, -jnp.inf)), slot_scores)
+    shares = each(lambda a: a / per_head(a, jnp.sum, 0.0), raised)
+    scaled = each(lambda a, b: (a * b).astype(BF16), shares, inverse)
+    mixing = each(lambda a, b, c: nt(a, b).astype(BF16) * c, scaled, e_stack, causal_4)
+    mixed = each(
+        lambda a, b, c, d, f: nn(a, head_stack(b)) + c * nn(d, f), mixing, v, enters, scaled, two
+    )
+    store(s_ref, each(lambda a: a.astype(BF16), slot_scores))
+    store(p_ref, each(lambda a: a.astype(BF16), shares))
+    store(mix_ref, each(lambda a: a.astype(BF16), mixed))
 
 
 def feed_forward(
@@ -446,15 +468,10 @@
             write(send_ref, left)
 
 
-def attention_backward(last, shards, seg_s, *refs):
-    x_ref, seg_ref, q_ref, k_ref, v_ref, e_ref, p_ref, s_ref, rz_ref, g_ref = refs[:10]
-    one_ref, two_ref, w_ref, vec_ref = refs[10:14]
-    refs = refs[14:]
-    if last:
-        part_ref, hidden_ref = refs[:2]
-        refs = refs[2:]
-    out_ref, keep_ref, send_ref = refs[:3]
-    first_state, second_state, total_state, d_w, d_vec = refs[3:]
+def attention_backward(shards, seg_s, x_ref, seg_ref, *refs):
+    sides, refs = (refs[:9], refs[9:18]), refs[18:]
+    g_ref, w_ref, vec_ref, hidden_ref, out_ref, keep_ref, send_ref = refs[:7]
+    first_state, second_state, total_state, d_w, d_vec = refs[7:]
     step = pl.program_id(0)
     chunks = pl.num_programs(0)
     chunk = chunks - 1 - step
@@ -466,101 +483,136 @@
         for ref in (first_state, second_state, total_state, d_w, d_vec):
             ref[...] = jnp.zeros_like(ref)
 
-    start = chunk * CHUNK
-    length = chunks * CHUNK
-    segment_first = seg_s[0, start]
-    segment_before = jnp.where(chunk == 0, -1, seg_s[0, jnp.maximum(start - 1, 0)])
-    segment_after = jnp.where(step == 0, -1, seg_s[0, jnp.minimum(start + CHUNK, length - 1)])
-    keep = jnp.where(segment_first == segment_after, 1.0, 0.0)
-    row = seg_ref[...].astype(F32)
-    column = as_column(row, CHUNK)
-    causal = causal_mask(column, row).astype(BF16)
-    turned = causal_mask_transposed(column, row).astype(BF16)
-    enters = jnp.where(column == segment_before.astype(F32), 1.0, 0.0)
-    goes_on = jnp.where(column == segment_after.astype(F32), 1.0, 0.0)
-    opens = jnp.where(column == segment_first.astype(F32), 1.0, 0.0).astype(BF16)
-    lanes = head_lanes()
+    length = chunks * BACK
+    row_all = seg_ref[...].astype(F32)
     diagonal = block_diagonal()
-
-    def heads(values):
-        return [values * lanes[h] for h in range(4)]
-
-    def beside(parts):
-        return jnp.concatenate(parts, axis=1)
-
-    def stacked(parts):
-        return jnp.concatenate(parts, axis=0)
-
-    queries, keys, values, slots = q_ref[...], k_ref[...], v_ref[...], e_ref[...]
-    shares, slot_scores = p_ref[...].astype(F32), s_ref[...].astype(F32)
-    inverse, grad = rz_ref[...], g_ref[...]
-    scaled = shares * inverse
-    scaled_low = scaled.astype(BF16)
-    one, two = one_ref[0], two_ref[0]
-    one_back, two_back = first_state[...].astype(BF16), second_state[...].astype(BF16)
-    grad_heads, slot_heads, value_heads = heads(grad), heads(slots), heads(values)
-    slot_stack = stacked(slot_heads)
-
-    d_mixing = beside([nt(part, values).astype(BF16) * causal for part in grad_heads])
-    d_scaled = nn(d_mixing, slot_stack) + enters * nt(grad, two)
-    d_shares = d_scaled * inverse
-    product = shares * d_shares
-    d_scores = product - shares * per_head(product, jnp.sum, 0.0)
-    d_gathered = d_scores * inverse
-    d_totals = -(d_scaled * scaled + d_scores * slot_scores) * inverse
-    d_low = (d_gathered * 0.125).astype(BF16)
-    d_low_heads = heads(d_low)
-
-    d_raw = beside([nt(part, slots).astype(BF16) * causal for part in d_low_heads])
-    d_queries = nn(d_raw, stacked(heads(keys))) + enters * nt(d_low, one)
-    d_raw_t = beside([nt(part, d_low).astype(BF16) * turned for part in slot_heads])
-    d_keys = nn(d_raw_t, stacked(heads(queries))) + goes_on * nt(slots, one_back)
-    mixing_t = beside([nt(part, scaled_low).astype(BF16) * turned for part in slot_heads])
-    d_values = nn(mixing_t, stacked(grad_heads)) + goes_on * nn(slots, two_back)
-    scores_t = beside([nt(part, queries).astype(BF16) * turned for part in heads(keys)])
-    d_slots = nn(scores_t, stacked(d_low_heads))
-    d_mixing_t = beside([nt(part, grad).astype(BF16) * turned for part in value_heads])
-    d_slots += nn(d_mixing_t, stacked(heads(scaled_low)))
-    d_totals_low = d_totals.astype(BF16)
-    rest = (d_totals - d_totals_low.astype(F32)).astype(BF16)
-    sums = nn(turned, d_totals_low) + nn(turned, rest) + goes_on * total_state[0:1, :]
-    d_slots += goes_on * (nn(keys, one_back) + nt(values, two_back)) + sums
-    d_control = d_slots * slots.astype(F32)
-
-    total_state[0:1, :] = sums[0:1, :]
-    first_state[...] = keep * first_state[...] + diagonal * tn(queries * opens, d_low)
-    second_state[...] = keep * second_state[...] + diagonal * tn(scaled_low * opens, grad)
+    found = [[], []]
+    for sub in reversed(range(BACK // SUB)):
+        rows = slice(sub * SUB, (sub + 1) * SUB)
+        start = chunk * BACK + sub * SUB
+        segment_first = seg_s[0, start]
+        segment_before = jnp.where(start == 0, -1, seg_s[0, jnp.maximum(start - 1, 0)])
+        after_at = jnp.minimum(start + SUB, length - 1)
+        segment_after = jnp.where(start + SUB == length, -1, seg_s[0, after_at])
+        keep = jnp.where(segment_first == segment_after, 1.0, 0.0)
+        row = row_all[:, rows]
+        column = as_column(row, QUAD)
+        causal_4 = four_times(causal_mask(column, row))
+        turned = causal_mask_transposed(column, row)
+        turned_4 = four_times(turned)
+        enters = jnp.where(column == segment_before.astype(F32), 1.0, 0.0)
+        goes_on = jnp.where(column == segment_after.astype(F32), 1.0, 0.0)
+        opens = jnp.where(column == segment_first.astype(F32), 1.0, 0.0).astype(BF16)
+
+        def both(function, *lists):
+            return [function(*values) for values in zip(*lists)]
+
+        q, k, v, e = ([side[n][rows] for side in sides] for n in range(4))
+        grad = [g_ref[rows, g * QUAD : (g + 1) * QUAD] for g in range(2)]
+        shares = [side[4][rows].astype(F32) for side in sides]
+        slot_scores = [side[5][rows].astype(F32) for side in sides]
+        inverse = [side[6][rows] for side in sides]
+        one = [side[7][sub] for side in sides]
+        two = [side[8][sub] for side in sides]
+        scaled = both(lambda a, b: a * b, shares, inverse)
+        scaled_low = [a.astype(BF16) for a in scaled]
+        one_back = [first_state[g].astype(BF16) for g in range(2)]
+        two_back = [second_state[g].astype(BF16) for g in range(2)]
+        e_stack = both(head_stack, e)
+
+        d_mixing = both(lambda a, b: nt(a, head_stack(b)).astype(BF16) * causal_4, grad, v)
+        d_scaled = both(
+            lambda a, b, c, d: nn(a, b) + enters * nt(c, d), d_mixing, e_stack, grad, two
+        )
+        q_stack, grad_stack = both(head_stack, q), both(head_stack, grad)
+        scaled_stack = both(head_stack, scaled_low)
+        mixing_t = both(lambda a, b: nt(a, b).astype(BF16) * turned_4, e, scaled_stack)
+        d_mixing_t = both(lambda a, b: nt(a, b).astype(BF16) * turned_4, v, grad_stack)
+        scores_t = both(lambda a, b: nt(a, b).astype(BF16) * turned_4, k, q_stack)
+        d_shares = both(lambda a, b: a * b, d_scaled, inverse)
+        product = both(lambda a, b: a * b, shares, d_shares)
+        d_scores = both(lambda a, b: a - b * per_head(a, jnp.sum, 0.0), product, shares)
+        d_low = both(lambda a, b: (a * b * 0.125).astype(BF16), d_scores, inverse)
+        d_totals = both(
+            lambda a, b, c, d, i: -(a * b + c * d) * i,
+            d_scaled,
+            scaled,
+            d_scores,
+            slot_scores,
+            inverse,
+        )
+        d_values = both(
+            lambda a, b, c, d: nn(a, b) + goes_on * nn(c, d), mixing_t, grad_stack, e, two_back
+        )
+        d_slots = both(nn, d_mixing_t, scaled_stack)
+        d_low_stack = both(head_stack, d_low)
+        d_raw = both(lambda a, b: nt(a, b).astype(BF16) * causal_4, d_low, e_stack)
+        d_raw_t = both(lambda a, b: nt(a, b).astype(BF16) * turned_4, e, d_low_stack)
+        d_slots = both(lambda a, b, c: a + nn(b, c), d_slots, scores_t, d_low_stack)
+        d_queries = both(
+            lambda a, b, c, d: nn(a, head_stack(b)) + enters * nt(c, d), d_raw, k, d_low, one
+        )
+        d_keys = both(
+            lambda a, b, c, d: nn(a, b) + goes_on * nt(c, d), d_raw_t, q_stack, e, one_back
+        )
+        totals_low = [a.astype(BF16) for a in d_totals]
+        rest = both(lambda a, b: (a - b.astype(F32)).astype(BF16), d_totals, totals_low)
+        sums = [
+            nn(turned, totals_low[g]) + nn(turned, rest[g]) + goes_on * total_state[g, 0:1, :]
+            for g in range(2)
+        ]
+        d_slots = both(
+            lambda a, b, c, d, f, h: a + goes_on * (nn(b, c) + nt(d, f)) + h,
+            d_slots,
+            k,
+            one_back,
+            v,
+            two_back,
+            sums,
+        )
+        d_control = both(lambda a, b: a * b.astype(F32), d_slots, e)
+        for g in range(2):
+            total_state[g, 0:1, :] = sums[g][0:1, :]
+            first_state[g] = keep * first_state[g] + diagonal * tn(q[g] * opens, d_low[g])
+            second_state[g] = keep * second_state[g] + diagonal * tn(
+                scaled_low[g] * opens, grad[g]
+            )
+            parts = (d_queries[g], d_keys[g], d_values[g], d_control[g])
+            found[g].append([part.astype(BF16) for part in parts])
+    grads = [
+        jnp.concatenate([part[m] for part in reversed(found[g])], axis=0)
+        for g in range(2)
+        for m in range(4)
+    ]
 
     normal, scale = standardise(x_ref[...].astype(F32))
     gain = vec_ref[0:1, :]
     normed = (normal * gain + vec_ref[1:2, :]).astype(BF16)
-    grads = [part.astype(BF16) for part in (d_queries, d_keys, d_values, d_control)]
-    d_w[...] += tn(normed, beside(grads))
-    d_normed = sum(nt(grads[m], w_ref[m]) for m in range(4))
-    if last:
-        d_normed += part_ref[...]
-        d_vec[0:1, :] += jnp.sum(d_normed * normal, axis=0, keepdims=True)
-        d_vec[1:2, :] += jnp.sum(d_normed, axis=0, keepdims=True)
-        out_ref[...] = hidden_ref[...] + norm_backward(d_normed, gain, normal, scale)
-    else:
-        out_ref[...] = d_normed
+    d_w[...] += tn(normed, jnp.concatenate(grads, axis=1))
+    d_normed = sum(
+        nt(jnp.concatenate([grads[m], grads[4 + m]], axis=1), w_ref[m]) for m in range(4)
+    )
+    d_vec[0:1, :] += jnp.sum(d_normed * normal, axis=0, keepdims=True)
+    d_vec[1:2, :] += jnp.sum(d_normed, axis=0, keepdims=True)
+    out_ref[...] = hidden_ref[...] + norm_backward(d_normed, gain, normal, scale)
 
     @pl.when(step == chunks - 1)
     def _():
         def write(ref, half):
             for s in range(shards):
                 y, z = (me ^ s) & 1, (me ^ s) >> 1
-                for m in range(4):
-                    x = cross ^ (m // 2)
-                    lead = (x, y, z) if last else (y, x, z)
-                    at = slice(m * QUAD + half * 128, m * QUAD + half * 128 + 128)
-                    part = d_w[s * r : (s + 1) * r, at].astype(BF16)
-                    ref[(*lead, slice((m % 2) * r, (m % 2 + 1) * r), slice(None))] = part
-                for x in range(2):
-                    lead = (x, y, z) if last else (y, x, z)
-                    top = piece_of(d_vec[...], s, r)
-                    both = jnp.concatenate([top, jnp.zeros_like(top)], axis=0)
-                    ref[(*lead, slice(2 * r, 2 * r + 16), slice(None))] = both.astype(BF16)
+                top = piece_of(d_vec[...], s, r)
+                both_rows = jnp.concatenate([top, jnp.zeros_like(top)], axis=0).astype(BF16)
+                for g in range(2):
+                    for m in range(4):
+                        x = cross ^ (m // 2)
+                        lead = (g, x, y, z) if g else (g, y, x, z)
+                        at = (4 * g + m) * QUAD + half * 128
+                        part = d_w[s * r : (s + 1) * r, at : at + 128].astype(BF16)
+                        ref[(*lead, slice((m % 2) * r, (m % 2 + 1) * r), slice(None))] = part
+                    for x in range(2):
+                        lead = (g, x, y, z) if g else (g, y, x, z)
+                        ref[(*lead, slice(2 * r, 2 * r + 16), slice(None))] = both_rows
 
         @pl.when(core == 0)
         def _():
@@ -612,9 +664,9 @@
     chunks = length // CHUNK
     wide = pl.BlockSpec((CHUNK, 512), lambda c, *_: (c, 0))
     tile = pl.BlockSpec((CHUNK, QUAD), lambda c, *_: (c, 0))
-    state = pl.BlockSpec((1, QUAD, QUAD), lambda c, *_: (c, 0, 0))
+    state = pl.BlockSpec((CHUNK // SUB, QUAD, QUAD), lambda c, *_: (c, 0, 0))
     low = shaped((length, QUAD), BF16)
-    states = shaped((chunks, QUAD, QUAD), BF16)
+    states = shaped((length // SUB, QUAD, QUAD), BF16)
     if quad == 0:
         in_specs = [anywhere(), anywhere()]
         out_specs = [whole((4, 512, 512)), whole((8, 512)), whole((8, 2048)), whole((8, 128))]
@@ -702,57 +754,47 @@
     )(*operands)
 
 
-def call_backward(quad, shards, segments, x, *operands, extra, earlier):
+def call_backward(shards, segments, x, sides, operands, earlier):
     length = x.shape[0]
-    chunks = length // CHUNK
+    chunks = length // BACK
     r = 512 // shards
-    last = quad == 1
     back = lambda c: chunks - 1 - c
-    wide = pl.BlockSpec((CHUNK, 512), lambda c, *_: (back(c), 0))
-    own = pl.BlockSpec((CHUNK, QUAD), lambda c, *_: (back(c), 0))
-    tile = pl.BlockSpec((CHUNK, QUAD), lambda c, *_: (back(c), quad))
-    state = pl.BlockSpec((1, QUAD, QUAD), lambda c, *_: (back(c), 0, 0))
-    payload = (2, 2, shards // 2, 2 * r + 16, 128)
+    wide = pl.BlockSpec((BACK, 512), lambda c, *_: (back(c), 0))
+    own = pl.BlockSpec((BACK, QUAD), lambda c, *_: (back(c), 0))
+    state = pl.BlockSpec((BACK // SUB, QUAD, QUAD), lambda c, *_: (back(c), 0, 0))
+    payload = (2, 2, 2, shards // 2, 2 * r + 16, 128)
     grid_spec = pltpu.PrefetchScalarGridSpec(
         num_scalar_prefetch=1,
         grid=(chunks,),
         in_specs=[
             wide,
-            pl.BlockSpec((1, CHUNK), lambda c, *_: (0, back(c))),
-            *[own] * 7,
-            tile,
-            *[state] * 2,
-            pl.BlockSpec((4, 512, QUAD), lambda c, *_: (0, 0, quad)),
+            pl.BlockSpec((1, BACK), lambda c, *_: (0, back(c))),
+            *([own] * 7 + [state] * 2) * 2,
+            wide,
+            whole((4, 512, 512)),
             whole((8, 512)),
-            *[wide] * len(extra),
+            wide,
             *[anywhere()] * len(earlier),
         ],
         out_specs=[wide, whole(payload), whole(payload)],
         scratch_shapes=[
-            pltpu.VMEM((QUAD, QUAD), F32),
-            pltpu.VMEM((QUAD, QUAD), F32),
-            pltpu.VMEM((8, QUAD), F32),
-            pltpu.VMEM((512, 4 * QUAD), F32),
+            pltpu.VMEM((2, QUAD, QUAD), F32),
+            pltpu.VMEM((2, QUAD, QUAD), F32),
+            pltpu.VMEM((2, 8, QUAD), F32),
+            pltpu.VMEM((512, 8 * QUAD), F32),
             pltpu.VMEM((8, 512), F32),
         ],
     )
     return pl.pallas_call(
         functools.partial(
-            ordered,
-            functools.partial(attention_backward, last, shards),
-            3 + len(operands) + len(extra),
-            len(earlier),
+            ordered, functools.partial(attention_backward, shards), 25, len(earlier)
         ),
         grid_spec=grid_spec,
-        out_shape=[
-            shaped((length, 512), F32),
-            shaped(payload, BF16),
-            shaped(payload, BF16),
-        ],
+        out_shape=[shaped((length, 512), F32), shaped(payload, BF16), shaped(payload, BF16)],
         compiler_params=params(),
         cost_estimate=COST,
-        name=f"attention_backward_{quad}",
-    )(segments, x, segments, *operands, *extra, *earlier)
+        name="attention_backward",
+    )(segments, x, segments, *sides[0], *sides[1], *operands, *earlier)
 
 
 def swap(value, axis, bit):
@@ -955,7 +997,7 @@
     held_b = along_z(branch)
     first_b, second_b = halves(held_b)
     pending = step_one(first_b, second_b)
-    mine_a = jnp.concatenate([first, arrived[0] + zero_of(held_b[1:]), second, arrived[1]])
+    mine_a = jnp.concatenate([first, arrived[0], second, arrived[1] + zero_of(held_b[1:])])
     theirs_a = swap(mine_a, "rep", 1)
 
     x = inputs.reshape(length, width)
@@ -1028,29 +1070,15 @@
             bit *= 2
         return [total] + [swap(total, "rep", a) for a in range(1, 4)]
 
-    def back(quad, saved, extra, earlier):
-        return call_backward(
-            quad,
-            shards,
-            segments,
-            x,
-            *saved[:7],
-            grad_mix,
-            *saved[8:10],
-            weights,
-            vectors,
-            extra=extra,
-            earlier=earlier,
-        )
-
     summed = add_low(keep_f, swap(send_f, "rep", 1))
     every = summed.reshape(reps * shards, *summed.shape[2:])
     arrived_f = lax.all_to_all(every, ("rep", "shard"), 0, 0).reshape(summed.shape)
-    part, keep_0, send_0 = back(0, forward_0, (), (every,))
-    late_0 = swap(send_0, "rep", 1)
-    grad_inputs, keep_1, send_1 = back(1, forward_1, (part, grad_hidden), ())
-    late_1 = swap(send_1, "rep", 1)
-    parts_0, parts_1 = row_first((keep_0, late_0)), cross_first((keep_1, late_1))
+    sides = [(*saved[:7], *saved[8:10]) for saved in (forward_0, forward_1)]
+    grad_inputs, keep_q, send_q = call_backward(
+        shards, segments, x, sides, (grad_mix, weights, vectors, grad_hidden), (every,)
+    )
+    late_q = swap(send_q, "rep", 1)
+    parts_0, parts_1 = row_first((keep_q[0], late_q[0])), cross_first((keep_q[1], late_q[1]))
     parts_0, parts_1 = cross_first(parts_0), row_first(parts_1)
     q_pieces = z_stage([parts_0, parts_1])
     total_f = call_add_arrived(shards, arrived_f, q_pieces[0])

time: 217 us -> 213 us (0.982)
  Pallas kernels: 96.3 us -> 87.5 us
  waiting for transfers between devices: 55.8 us -> 60.8 us
    pallas_call x2 -> x1, Pallas kernels: 35.5 us -> 28.9 us  [call_backward(): pl.pallas_call(functools.partial(ordered, functools.partial(attention_bac...]
    ppermute x32 -> x31, waiting for transfers between devices: 55.8 us -> 60.8 us  [swap(): return lax.ppermute(value, axis, [(i, i ^ bit) for i in range(n)])]
    ppermute x32 -> x31, starting transfers between devices: 32.2 us -> 31.6 us  [swap(): return lax.ppermute(value, axis, [(i, i ^ bit) for i in range(n)])]
    unnamed x49 -> x48, local copies, waits for them, and re-layouts: 9.84 us -> 9.53 us
    convert_element_type x7 -> x6, other arithmetic: 5.76 us -> 5.96 us  [add_low(): return sum((part.astype(F32) for part in parts)).astype(BF16)]
  transfers between devices with their start and end apart: 33 -> 32, of which waited for: 16 -> 16; matrix products, arithmetic and copies ran while one was open for 4% -> 4% of each run, Pallas kernels for 30% -> 27%
where the time goes in v4:
time: 213 us; the launch traced here: 212 us
  Pallas kernels  87.5 us (41%)
  waiting for transfers between devices  60.8 us (29%)
  starting transfers between devices  37.8 us (18%)
  local copies, waits for them, and re-layouts  14.1 us (7%)
  other arithmetic  8.67 us (4%)
  between operations  3.01 us (1%)
    ppermute x31, waiting for transfers between devices, swap(): return lax.ppermute(value, axis, [(i, i ^ bit) for i in range(n)])  60.8 us
    ppermute x31, starting transfers between devices, swap(): return lax.ppermute(value, axis, [(i, i ^ bit) for i in range(n)])  31.6 us
    pallas_call x1, Pallas kernels, call_backward(): pl.pallas_call(functools.partial(ordered, functools.partial(attention_bac...  28.9 us
    pallas_call x1, Pallas kernels, call_feed_forward(): pl.pallas_call(functools.partial(feed_forward, shards, tokens), grid=(chu...  26.9 us
    pallas_call x2, Pallas kernels, call_forward(): pl.pallas_call(functools.partial(ordered, functools.partial(attention_for...  23 us
    unnamed x48, local copies, waits for them, and re-layouts  9.53 us
    all_to_all x1, starting transfers between devices, local(): lax.all_to_all(every, ('rep', 'shard'), 0, 0).reshape(summed.shape)  6.2 us
    convert_element_type x6, other arithmetic, add_low(): return sum((part.astype(F32) for part in parts)).astype(BF16)  5.96 us
  transfers between devices with their start and end apart: 32, of which 16 were waited for; matrix products, arithmetic and copies ran while one was open for 4% of the time, Pallas kernels for 27%

profile of v4, /device:TPU:13, one launch (start us, length us, event | category | flops | bytes accessed | tf_op | source)
XLA Modules:
  0.0 212.0 jit_solution(14763267664406609536)
XLA Ops:
  1.9 2.0 pack.1
  4.1 2.4 %collective-permute-start.4 = (bf16[1,144,256]{2,1,0:T(8,128)(2,1)}, bf16[1,144,256]{2,1,0:T(8,128)(2,1)S(1)}, u32[]{:S(2)}, u32[]{:S(2)}) collective-permute-start(bf16[1,144,256]{2,1,0:T(8,128)(2,1)} %bitcast.105), channel_id=1, source_target_pairs={{0,6},{1,7},{2,4},{3,5},{4,2},{5,3},{6,0},{7,1},{8,14},{9,15},{10,... | collective-permute-start | bytes 221192 | tf_op jit(solution)/shard_map/ppermute | solution.py:802
  12.3 6.5 %collective-permute-done.3 = bf16[1,144,256]{2,1,0:T(8,128)(2,1)S(1)} collective-permute-done((bf16[1,144,256]{2,1,0:T(8,128)(2,1)}, bf16[1,144,256]{2,1,0:T(8,128)(2,1)S(1)}, u32[]{:S(2)}, u32[]{:S(2)}) %collective-permute-start.3) | collective-permute-done | bytes 73760 | tf_op jit(solution)/shard_map/ppermute | solution.py:802
  21.4 4.1 %collective-permute-done.8 = bf16[1,288,256]{2,1,0:T(8,128)(2,1)S(1)} collective-permute-done((bf16[1,288,256]{2,1,0:T(8,128)(2,1)}, bf16[1,288,256]{2,1,0:T(8,128)(2,1)S(1)}, u32[]{:S(2)}, u32[]{:S(2)}) %collective-permute-start.8) | collective-permute-done | bytes 147488 | tf_op jit(solution)/shard_map/ppermute | solution.py:802
  29.6 6.8 %collective-permute-done.6 = bf16[4,144,256]{2,1,0:T(8,128)(2,1)S(1)} collective-permute-done((bf16[4,144,256]{2,1,0:T(8,128)(2,1)S(1)}, bf16[4,144,256]{2,1,0:T(8,128)(2,1)S(1)}, u32[]{:S(2)}, u32[]{:S(2)}) %collective-permute-start.6) | collective-permute-done | bytes 294944 | tf_op jit(solution)/shard_map/ppermute | solution.py:802
  36.5 2.2 %collective-permute-start.10 = (bf16[16,144,256]{2,1,0:T(8,128)(2,1)S(1)}, bf16[16,144,256]{2,1,0:T(8,128)(2,1)S(1)}, u32[]{:S(2)}, u32[]{:S(2)}) collective-permute-start(bf16[16,144,256]{2,1,0:T(8,128)(2,1)S(1)} %add_dynamic-update-slice_fusion.refs_3_), channel_id=1, source_target_pairs={{0,8},{8,0},{16,24},{24,16},{1,9},{9,1},{17,25},{25,17},{2,10},{10... | collective-permute-start | bytes 3538952 | tf_op jit(solution)/shard_map/ppermute | solution.py:802
  42.7 12.4 %attention_forward_0.1 = (bf16[1024,256]{1,0:T(8,128)(2,1)}, bf16[1024,256]{1,0:T(8,128)(2,1)}, bf16[1024,256]{1,0:T(8,128)(2,1)}, bf16[1024,256]{1,0:T(8,128)(2...) custom-call(s32[1,1024]{1,0:T(1,128)} %refs_2_.7, ...), custom_call_target="tpu_custom_call" | custom-call | flops 1000 | bytes 1000 | tf_op jit(solution)/shard_map/attention_forward_0/pallas_call | solution.py:694
  57.5 10.6 %attention_forward_1.1 = (bf16[1024,256]{1,0:T(8,128)(2,1)}, bf16[1024,256]{1,0:T(8,128)(2,1)}, bf16[1024,256]{1,0:T(8,128)(2,1)}, bf16[1024,256]{1,0:T(8,128)(2...) custom-call(s32[1,1024]{1,0:T(1,128)} %refs_2_.7, ...), custom_call_target="tpu_custom_call" | custom-call | flops 1000 | bytes 1000 | tf_op jit(solution)/shard_map/attention_forward_1/pallas_call | solution.py:694
  68.2 1.5 collective-permute-done.13
  69.6 1.6 collective-permute-done.14
  73.6 1.6 collective-permute-start.15
  75.2 4.2 %collective-permute-done.15.theirs_ref = bf16[16,288,256]{2,1,0:T(8,128)(2,1)S(1)} collective-permute-done((bf16[16,288,256]{2,1,0:T(8,128)(2,1)S(1)}, bf16[16,288,256]{2,1,0:T(8,128)(2,1)S(1)}, u32[]{:S(2)}, u32[]{:S(2)}) %collective-permute-start.15) | collective-permute-done | bytes 2359328 | tf_op jit(solution)/shard_map/ppermute | solution.py:802
  79.3 1.5 copy-done.2
  80.8 26.9 %feed_forward.1 = (bf16[1024,512]{1,0:T(8,128)(2,1)}, f32[1024,512]{1,0:T(8,128)}, bf16[1024,512]{1,0:T(8,128)(2,1)}, bf16[4,8,160,256]{3,2,1,0:T(8,128)(2,1)}, bf16[4,8,160,256]{3,2,1,0:T(8,128)(2,1)}) custom-call(bf16[1024,512]{1,0:T(8,128)(2,1)} %bitcast.95, bf16[1024,256]{1,0:T(8,128)(2,1)} %get-tuple-element.70.mix_0_ref, ...), custom_call_target="tpu_custom_call" | custom-call | flops 1000 | bytes 1000 | tf_op jit(solution)/shard_map/feed_forward/pallas_call | solution.py:716
  108.1 4.8 %collective-permute-done.16 = bf16[4,8,160,256]{3,2,1,0:T(8,128)(2,1)S(1)} collective-permute-done((bf16[4,8,160,256]{3,2,1,0:T(8,128)(2,1)}, bf16[4,8,160,256]{3,2,1,0:T(8,128)(2,1)S(1)}, u32[]{:S(2)}, u32[]{:S(2)}) %collective-permute-start.16) | collective-permute-done | bytes 2621472 | tf_op jit(solution)/shard_map/ppermute | solution.py:802
  112.9 4.2 %add_convert_fusion = bf16[4,8,160,256]{3,2,1,0:T(8,128)(2,1)} fusion(bf16[4,8,160,256]{3,2,1,0:T(8,128)(2,1)S(1)} %collective-permute-done.16, bf16[4,8,160,256]{3,2,1,0:T(8,128)(2,1)} %get-tuple-element.101), kind=kLoop, calls=%fused_computation | loop fusion | flops 5242880 | bytes 7864320 | tf_op jit(solution)/shard_map/convert_element_type | solution.py:936
  117.0 6.2 %all-to-all-start = ((bf16[32,160,256]{2,1,0:T(8,128)(2,1)}), bf16[32,160,256]{2,1,0:T(8,128)(2,1)S(1)}, u32[]{:S(2)}, u32[]{:S(2)}) async-start(bf16[32,160,256]{2,1,0:T(8,128)(2,1)} %bitcast.11.refs_25_), calls=%async_computation | async-start | bytes 5242880 | tf_op jit(solution)/shard_map/all_to_all | solution.py:1075
  123.2 28.9 %attention_backward.1 = (f32[1024,512]{1,0:T(8,128)}, bf16[2,2,2,4,144,128]{5,4,3,2,1,0:T(8,128)(2,1)}, bf16[2,2,2,4,144,128]{5,4,3,2,1,0:T(8,128)(2,1)}) custom-call(s32[1,1024]{1,0:T(1,128)} %refs_2_.7, bf16[1024,512]{1,0:T(8,128)(2,1)} %bitcast.96, s32[1,1024]{1,0:T(1,128)} %refs_2_.7, bf16[1024,256]{1,0:T(8,128)(2,1)} %get-tuple-element.81.refs_3_, ...), custom_call_target="tpu_custom_call" | custom-call | flops 1000 | bytes 1000 | tf_op jit(solution)/shard_map/attention_backward/pallas_call | solution.py:788
  152.5 2.7 %collective-permute-done.17 = bf16[2,2,2,4,144,128]{5,4,3,2,1,0:T(8,128)(2,1)S(1)} collective-permute-done((bf16[2,2,2,4,144,128]{5,4,3,2,1,0:T(8,128)(2,1)}, bf16[2,2,2,4,144,128]{5,4,3,2,1,0:T(8,128)(2,1)S(1)}, u32[]{:S(2)}, u32[]{:S(2)}) %collective-permute-start.17) | collective-permute-done | bytes 1179680 | tf_op jit(solution)/shard_map/ppermute | solution.py:802
  155.2 1.6 add_convert_fusion.4
  158.3 11.4 %collective-permute-done.20 = bf16[2,4,144,128]{3,2,1,0:T(8,128)(2,1)S(1)} collective-permute-done((bf16[2,4,144,128]{3,2,1,0:T(8,128)(2,1)S(1)}, bf16[2,4,144,128]{3,2,1,0:T(8,128)(2,1)S(1)}, u32[]{:S(2)}, u32[]{:S(2)}) %collective-permute-start.20) | collective-permute-done | bytes 294944 | tf_op jit(solution)/shard_map/ppermute | solution.py:802
  170.0 4.2 %collective-permute-done.18 = bf16[2,4,144,128]{3,2,1,0:T(8,128)(2,1)S(1)} collective-permute-done((bf16[2,4,144,128]{3,2,1,0:T(8,128)(2,1)S(1)}, bf16[2,4,144,128]{3,2,1,0:T(8,128)(2,1)S(1)}, u32[]{:S(2)}, u32[]{:S(2)}) %collective-permute-start.18) | collective-permute-done | bytes 294944 | tf_op jit(solution)/shard_map/ppermute | solution.py:802
  174.3 5.8 %collective-permute-done.21 = bf16[4,144,128]{2,1,0:T(8,128)(2,1)S(1)} collective-permute-done((bf16[4,144,128]{2,1,0:T(8,128)(2,1)S(1)}, bf16[4,144,128]{2,1,0:T(8,128)(2,1)S(1)}, u32[]{:S(2)}, u32[]{:S(2)}) %collective-permute-start.21) | collective-permute-done | bytes 147488 | tf_op jit(solution)/shard_map/ppermute | solution.py:802
  181.2 2.5 %collective-permute-start.27 = (bf16[1,288,128]{2,1,0:T(8,128)(2,1)S(1)}, bf16[1,288,128]{2,1,0:T(8,128)(2,1)S(1)}, u32[]{:S(2)}, u32[]{:S(2)}) collective-permute-start(bf16[1,288,128]{2,1,0:T(8,128)(2,1)S(1)} %pad_maximum_fusion.9), channel_id=1, source_target_pairs={{0,6},{1,7},{2,4},{3,5},{4,2},{5,3},{6,0},{7,1},{8,14},{9,15},{10,... | collective-permute-start | bytes 221192 | tf_op jit(solution)/shard_map/ppermute | solution.py:802
  185.5 1.5 copy-done
  187.0 2.7 %add_arrived.1.refs_0_ = bf16[2,160,256]{2,1,0:T(8,128)(2,1)} custom-call(bf16[4,8,160,256]{3,2,1,0:T(8,128)(2,1)} %bitcast.97, bf16[1,288,128]{2,1,0:T(8,128)(2,1)} %pad_maximum_fusion.6.refs_1_), custom_call_target="tpu_custom_call" | custom-call | flops 1000 | bytes 1000 | tf_op jit(solution)/shard_map/add_arrived/pallas_call | solution.py:838
  189.7 3.7 %collective-permute-start.24 = (bf16[2,160,256]{2,1,0:T(8,128)(2,1)}, bf16[2,160,256]{2,1,0:T(8,128)(2,1)S(1)}, u32[]{:S(2)}, u32[]{:S(2)}) collective-permute-start(bf16[2,160,256]{2,1,0:T(8,128)(2,1)} %add_arrived.1.refs_0_), channel_id=1, source_target_pairs={{0,24},{8,16},{16,8},{24,0},{1,25},{9,17},{17,9},{25,1},{2,26},{10... | collective-permute-start | bytes 491528 | tf_op jit(solution)/shard_map/ppermute | solution.py:802
  193.4 1.6 collective-permute-start.23
  197.0 5.4 %collective-permute-done.30.refs_3_ = bf16[288,128]{1,0:T(8,128)(2,1)S(1)} collective-permute-done((bf16[288,128]{1,0:T(8,128)(2,1)S(1)}, bf16[288,128]{1,0:T(8,128)(2,1)S(1)}, u32[]{:S(2)}, u32[]{:S(2)}) %collective-permute-start.30) | collective-permute-done | bytes 73760 | tf_op jit(solution)/shard_map/ppermute | solution.py:802
  202.3 2.6 %collective-permute-start.28 = (bf16[288,128]{1,0:T(8,128)(2,1)S(1)}, bf16[288,128]{1,0:T(8,128)(2,1)S(1)}, u32[]{:S(2)}, u32[]{:S(2)}) collective-permute-start(bf16[288,128]{1,0:T(8,128)(2,1)S(1)} %fusion.8.refs_0_), channel_id=1, source_target_pairs={{0,8},{8,0},{16,24},{24,16},{1,9},{9,1},{17,25},{25,17},{2,10},{10... | collective-permute-start | bytes 221192 | tf_op jit(solution)/shard_map/ppermute | solution.py:802
  206.5 1.8 assemble.3
  209.7 2.3 %assemble.2 = (f32[256,512]{1,0:T(8,128)}, f32[64,2048]{1,0:T(8,128)}, f32[64,512]{1,0:T(8,128)}, f32[1,256]{1,0:T(1,128)}, f32[1,64]{1,0:T(1,128)}, /*index=5*/...) custom-call(f32[8,128]{1,0:T(8,128)} %get-tuple-element.77.count_ref, bf16[2,160,256]{2,1,0:T(8,128)(2,1)} %add_arrived.1.refs_0_, ...), custom_call_target="tpu_custom_call" | custom-call | flops 1000 | bytes 1000 | tf_op jit(solution)/shard_map/assemble/pallas_call | solution.py:924
  (112 shorter events, 31.2 us)
Async XLA Ops:
  3.9 5.9 %collective-permute-start = (bf16[1,144,256]{2,1,0:T(8,128)(2,1)}, bf16[1,144,256]{2,1,0:T(8,128)(2,1)S(1)}, u32[]{:S(2)}, u32[]{:S(2)}) collective-permute-start(bf16[1,144,256]{2,1,0:T(8,128)(2,1)} %bitcast.104), channel_id=1, source_target_pairs={{0,2},{1,3},{2,0},{3,1},{4,6},{5,7},{6,4},{7,5},{8,10},{9,11},{10,... | collective-permute-start | bytes 221192 | tf_op jit(solution)/shard_map/ppermute | solution.py:802
  4.1 7.8 %collective-permute-start.4 = (bf16[1,144,256]{2,1,0:T(8,128)(2,1)}, bf16[1,144,256]{2,1,0:T(8,128)(2,1)S(1)}, u32[]{:S(2)}, u32[]{:S(2)}) collective-permute-start(bf16[1,144,256]{2,1,0:T(8,128)(2,1)} %bitcast.105), channel_id=1, source_target_pairs={{0,6},{1,7},{2,4},{3,5},{4,2},{5,3},{6,0},{7,1},{8,14},{9,15},{10,... | collective-permute-start | bytes 221192 | tf_op jit(solution)/shard_map/ppermute | solution.py:802
  6.6 12.3 %collective-permute-start.3 = (bf16[1,144,256]{2,1,0:T(8,128)(2,1)}, bf16[1,144,256]{2,1,0:T(8,128)(2,1)S(1)}, u32[]{:S(2)}, u32[]{:S(2)}) collective-permute-start(bf16[1,144,256]{2,1,0:T(8,128)(2,1)} %bitcast.106), channel_id=1, source_target_pairs={{0,4},{1,5},{2,6},{3,7},{4,0},{5,1},{6,2},{7,3},{8,12},{9,13},{10,... | collective-permute-start | bytes 221192 | tf_op jit(solution)/shard_map/ppermute | solution.py:802
  7.5 20.3 %collective-permute-start.9 = (bf16[1,288,256]{2,1,0:T(8,128)(2,1)}, bf16[1,288,256]{2,1,0:T(8,128)(2,1)S(1)}, u32[]{:S(2)}, u32[]{:S(2)}) collective-permute-start(bf16[1,288,256]{2,1,0:T(8,128)(2,1)} %bitcast.98), channel_id=1, source_target_pairs={{0,6},{1,7},{2,4},{3,5},{4,2},{5,3},{6,0},{7,1},{8,14},{9,15},{10,... | collective-permute-start | bytes 442376 | tf_op jit(solution)/shard_map/ppermute | solution.py:802
  8.8 16.7 %collective-permute-start.8 = (bf16[1,288,256]{2,1,0:T(8,128)(2,1)}, bf16[1,288,256]{2,1,0:T(8,128)(2,1)S(1)}, u32[]{:S(2)}, u32[]{:S(2)}) collective-permute-start(bf16[1,288,256]{2,1,0:T(8,128)(2,1)} %bitcast.99), channel_id=1, source_target_pairs={{0,4},{1,5},{2,6},{3,7},{4,0},{5,1},{6,2},{7,3},{8,12},{9,13},{10,... | collective-permute-start | bytes 442376 | tf_op jit(solution)/shard_map/ppermute | solution.py:802
  10.7 9.4 %collective-permute-start.1 = (bf16[2,144,256]{2,1,0:T(8,128)(2,1)S(1)}, bf16[2,144,256]{2,1,0:T(8,128)(2,1)S(1)}, u32[]{:S(2)}, u32[]{:S(2)}) collective-permute-start(bf16[2,144,256]{2,1,0:T(8,128)(2,1)S(1)} %pad_maximum_fusion.4), channel_id=1, source_target_pairs={{0,1},{1,0},{2,3},{3,2},{4,5},{5,4},{6,7},{7,6},{8,9},{9,8},{10,11... | collective-permute-start | bytes 442376 | tf_op jit(solution)/shard_map/ppermute | solution.py:802
  11.9 14.1 %collective-permute-start.7 = (bf16[1,288,256]{2,1,0:T(8,128)(2,1)}, bf16[1,288,256]{2,1,0:T(8,128)(2,1)S(1)}, u32[]{:S(2)}, u32[]{:S(2)}) collective-permute-start(bf16[1,288,256]{2,1,0:T(8,128)(2,1)} %bitcast.100), channel_id=1, source_target_pairs={{0,2},{1,3},{2,0},{3,1},{4,6},{5,7},{6,4},{7,5},{8,10},{9,11},{10,... | collective-permute-start | bytes 442376 | tf_op jit(solution)/shard_map/ppermute | solution.py:802
  18.9 10.2 %collective-permute-start.5 = (bf16[2,144,256]{2,1,0:T(8,128)(2,1)S(1)}, bf16[2,144,256]{2,1,0:T(8,128)(2,1)S(1)}, u32[]{:S(2)}, u32[]{:S(2)}) collective-permute-start(bf16[2,144,256]{2,1,0:T(8,128)(2,1)S(1)} %pad_maximum_fusion.5), channel_id=1, source_target_pairs={{0,16},{8,24},{16,0},{24,8},{1,17},{9,25},{17,1},{25,9},{2,18},{10... | collective-permute-start | bytes 442376 | tf_op jit(solution)/shard_map/ppermute | solution.py:802
  21.1 8.5 %collective-permute-start.2 = (bf16[4,144,256]{2,1,0:T(8,128)(2,1)S(1)}, bf16[4,144,256]{2,1,0:T(8,128)(2,1)S(1)}, u32[]{:S(2)}, u32[]{:S(2)}) collective-permute-start(bf16[4,144,256]{2,1,0:T(8,128)(2,1)S(1)} %pad_maximum_fusion.1), channel_id=1, source_target_pairs={{0,16},{8,24},{16,0},{24,8},{1,17},{9,25},{17,1},{25,9},{2,18},{10... | collective-permute-start | bytes 884744 | tf_op jit(solution)/shard_map/ppermute | solution.py:802
  29.1 7.3 %collective-permute-start.6 = (bf16[4,144,256]{2,1,0:T(8,128)(2,1)S(1)}, bf16[4,144,256]{2,1,0:T(8,128)(2,1)S(1)}, u32[]{:S(2)}, u32[]{:S(2)}) collective-permute-start(bf16[4,144,256]{2,1,0:T(8,128)(2,1)S(1)} %pad_maximum_fusion.2), channel_id=1, source_target_pairs={{0,1},{1,0},{2,3},{3,2},{4,5},{5,4},{6,7},{7,6},{8,9},{9,8},{10,11... | collective-permute-start | bytes 884744 | tf_op jit(solution)/shard_map/ppermute | solution.py:802
  36.5 5.1 %collective-permute-start.10 = (bf16[16,144,256]{2,1,0:T(8,128)(2,1)S(1)}, bf16[16,144,256]{2,1,0:T(8,128)(2,1)S(1)}, u32[]{:S(2)}, u32[]{:S(2)}) collective-permute-start(bf16[16,144,256]{2,1,0:T(8,128)(2,1)S(1)} %add_dynamic-update-slice_fusion.refs_3_), channel_id=1, source_target_pairs={{0,8},{8,0},{16,24},{24,16},{1,9},{9,1},{17,25},{25,17},{2,10},{10... | collective-permute-start | bytes 3538952 | tf_op jit(solution)/shard_map/ppermute | solution.py:802
  38.7 16.3 %collective-permute-start.11 = (bf16[2,288,256]{2,1,0:T(8,128)(2,1)S(1)}, bf16[2,288,256]{2,1,0:T(8,128)(2,1)S(1)}, u32[]{:S(2)}, u32[]{:S(2)}) collective-permute-start(bf16[2,288,256]{2,1,0:T(8,128)(2,1)S(1)} %pad_maximum_fusion.3.refs_5_), channel_id=1, source_target_pairs={{0,1},{1,0},{2,3},{3,2},{4,5},{5,4},{6,7},{7,6},{8,9},{9,8},{10,11... | collective-permute-start | bytes 884744 | tf_op jit(solution)/shard_map/ppermute | solution.py:802
  40.4 14.7 %collective-permute-start.12 = (bf16[2,288,256]{2,1,0:T(8,128)(2,1)S(1)}, bf16[2,288,256]{2,1,0:T(8,128)(2,1)S(1)}, u32[]{:S(2)}, u32[]{:S(2)}) collective-permute-start(bf16[2,288,256]{2,1,0:T(8,128)(2,1)S(1)} %get-tuple-element.137.refs_6_), channel_id=1, source_target_pairs={{0,16},{8,24},{16,0},{24,8},{1,17},{9,25},{17,1},{25,9},{2,18},{10... | collective-permute-start | bytes 884744 | tf_op jit(solution)/shard_map/ppermute | solution.py:802
  55.2 14.5 %collective-permute-start.13 = (bf16[4,288,256]{2,1,0:T(8,128)(2,1)S(1)}, bf16[4,288,256]{2,1,0:T(8,128)(2,1)}, u32[]{:S(2)}, u32[]{:S(2)}) collective-permute-start(bf16[4,288,256]{2,1,0:T(8,128)(2,1)S(1)} %pad_maximum_fusion.refs_5_), channel_id=1, source_target_pairs={{0,16},{8,24},{16,0},{24,8},{1,17},{9,25},{17,1},{25,9},{2,18},{10... | collective-permute-start | bytes 1769480 | tf_op jit(solution)/shard_map/ppermute | solution.py:802
  56.8 14.5 %collective-permute-start.14 = (bf16[4,288,256]{2,1,0:T(8,128)(2,1)}, bf16[4,288,256]{2,1,0:T(8,128)(2,1)}, u32[]{:S(2)}, u32[]{:S(2)}) collective-permute-start(bf16[4,288,256]{2,1,0:T(8,128)(2,1)} %constant_dynamic-update-slice_fusion.9.refs_6_), channel_id=1, source_target_pairs={{0,1},{1,0},{2,3},{3,2},{4,5},{5,4},{6,7},{7,6},{8,9},{9,8},{10,11... | collective-permute-start | bytes 1769480 | tf_op jit(solution)/shard_map/ppermute | solution.py:802
  73.6 5.7 %collective-permute-start.15 = (bf16[16,288,256]{2,1,0:T(8,128)(2,1)S(1)}, bf16[16,288,256]{2,1,0:T(8,128)(2,1)S(1)}, u32[]{:S(2)}, u32[]{:S(2)}) collective-permute-start(bf16[16,288,256]{2,1,0:T(8,128)(2,1)S(1)} %constant_dynamic-update-slice_fusion.12.mine_ref), channel_id=1, source_target_pairs={{0,8},{8,0},{16,24},{24,16},{1,9},{9,1},{17,25},{25,17},{2,10},{10... | collective-permute-start | bytes 7077896 | tf_op jit(solution)/shard_map/ppermute | solution.py:802
  107.7 5.2 %collective-permute-start.16 = (bf16[4,8,160,256]{3,2,1,0:T(8,128)(2,1)}, bf16[4,8,160,256]{3,2,1,0:T(8,128)(2,1)S(1)}, u32[]{:S(2)}, u32[]{:S(2)}) collective-permute-start(bf16[4,8,160,256]{3,2,1,0:T(8,128)(2,1)} %get-tuple-element.102), channel_id=1, source_target_pairs={{0,8},{8,0},{16,24},{24,16},{1,9},{9,1},{17,25},{25,17},{2,10},{10... | collective-permute-start | bytes 7864328 | tf_op jit(solution)/shard_map/ppermute | solution.py:802
  117.0 68.5 %all-to-all-start = ((bf16[32,160,256]{2,1,0:T(8,128)(2,1)}), bf16[32,160,256]{2,1,0:T(8,128)(2,1)S(1)}, u32[]{:S(2)}, u32[]{:S(2)}) async-start(bf16[32,160,256]{2,1,0:T(8,128)(2,1)} %bitcast.11.refs_25_), calls=%async_computation | async-start | bytes 5242880 | tf_op jit(solution)/shard_map/all_to_all | solution.py:1075
  152.1 3.1 %collective-permute-start.17 = (bf16[2,2,2,4,144,128]{5,4,3,2,1,0:T(8,128)(2,1)}, bf16[2,2,2,4,144,128]{5,4,3,2,1,0:T(8,128)(2,1)S(1)}, u32[]{:S(2)}, u32[]{:S(2)}) collective-permute-start(bf16[2,2,2,4,144,128]{5,4,3,2,1,0:T(8,128)(2,1)} %get-tuple-element.105), channel_id=1, source_target_pairs={{0,8},{8,0},{16,24},{24,16},{1,9},{9,1},{17,25},{25,17},{2,10},{10... | collective-permute-start | bytes 3538952 | tf_op jit(solution)/shard_map/ppermute | solution.py:802
  156.8 12.9 %collective-permute-start.20 = (bf16[2,4,144,128]{3,2,1,0:T(8,128)(2,1)S(1)}, bf16[2,4,144,128]{3,2,1,0:T(8,128)(2,1)S(1)}, u32[]{:S(2)}, u32[]{:S(2)}) collective-permute-start(bf16[2,4,144,128]{3,2,1,0:T(8,128)(2,1)S(1)} %get-tuple-element.121), channel_id=1, source_target_pairs={{0,16},{8,24},{16,0},{24,8},{1,17},{9,25},{17,1},{25,9},{2,18},{10... | collective-permute-start | bytes 884744 | tf_op jit(solution)/shard_map/ppermute | solution.py:802
  158.0 16.1 %collective-permute-start.18 = (bf16[2,4,144,128]{3,2,1,0:T(8,128)(2,1)S(1)}, bf16[2,4,144,128]{3,2,1,0:T(8,128)(2,1)S(1)}, u32[]{:S(2)}, u32[]{:S(2)}) collective-permute-start(bf16[2,4,144,128]{3,2,1,0:T(8,128)(2,1)S(1)} %get-tuple-element.123), channel_id=1, source_target_pairs={{0,1},{1,0},{2,3},{3,2},{4,5},{5,4},{6,7},{7,6},{8,9},{9,8},{10,11... | collective-permute-start | bytes 884744 | tf_op jit(solution)/shard_map/ppermute | solution.py:802
  169.8 10.3 %collective-permute-start.21 = (bf16[4,144,128]{2,1,0:T(8,128)(2,1)S(1)}, bf16[4,144,128]{2,1,0:T(8,128)(2,1)S(1)}, u32[]{:S(2)}, u32[]{:S(2)}) collective-permute-start(bf16[4,144,128]{2,1,0:T(8,128)(2,1)S(1)} %get-tuple-element.127), channel_id=1, source_target_pairs={{0,1},{1,0},{2,3},{3,2},{4,5},{5,4},{6,7},{7,6},{8,9},{9,8},{10,11... | collective-permute-start | bytes 442376 | tf_op jit(solution)/shard_map/ppermute | solution.py:802
  174.3 6.7 %collective-permute-start.19 = (bf16[4,144,128]{2,1,0:T(8,128)(2,1)S(1)}, bf16[4,144,128]{2,1,0:T(8,128)(2,1)S(1)}, u32[]{:S(2)}, u32[]{:S(2)}) collective-permute-start(bf16[4,144,128]{2,1,0:T(8,128)(2,1)S(1)} %get-tuple-element.125), channel_id=1, source_target_pairs={{0,16},{8,24},{16,0},{24,8},{1,17},{9,25},{17,1},{25,9},{2,18},{10... | collective-permute-start | bytes 442376 | tf_op jit(solution)/shard_map/ppermute | solution.py:802
  181.1 13.9 %collective-permute-start.26 = (bf16[1,288,128]{2,1,0:T(8,128)(2,1)S(1)}, bf16[1,288,128]{2,1,0:T(8,128)(2,1)S(1)}, u32[]{:S(2)}, u32[]{:S(2)}) collective-permute-start(bf16[1,288,128]{2,1,0:T(8,128)(2,1)S(1)} %pad_maximum_fusion.8), channel_id=1, source_target_pairs={{0,4},{1,5},{2,6},{3,7},{4,0},{5,1},{6,2},{7,3},{8,12},{9,13},{10,... | collective-permute-start | bytes 221192 | tf_op jit(solution)/shard_map/ppermute | solution.py:802
  181.2 13.8 %collective-permute-start.27 = (bf16[1,288,128]{2,1,0:T(8,128)(2,1)S(1)}, bf16[1,288,128]{2,1,0:T(8,128)(2,1)S(1)}, u32[]{:S(2)}, u32[]{:S(2)}) collective-permute-start(bf16[1,288,128]{2,1,0:T(8,128)(2,1)S(1)} %pad_maximum_fusion.9), channel_id=1, source_target_pairs={{0,6},{1,7},{2,4},{3,5},{4,2},{5,3},{6,0},{7,1},{8,14},{9,15},{10,... | collective-permute-start | bytes 221192 | tf_op jit(solution)/shard_map/ppermute | solution.py:802
  183.7 11.3 %collective-permute-start.25 = (bf16[1,288,128]{2,1,0:T(8,128)(2,1)S(1)}, bf16[1,288,128]{2,1,0:T(8,128)(2,1)S(1)}, u32[]{:S(2)}, u32[]{:S(2)}) collective-permute-start(bf16[1,288,128]{2,1,0:T(8,128)(2,1)S(1)} %pad_maximum_fusion.7), channel_id=1, source_target_pairs={{0,2},{1,3},{2,0},{3,1},{4,6},{5,7},{6,4},{7,5},{8,10},{9,11},{10,... | collective-permute-start | bytes 221192 | tf_op jit(solution)/shard_map/ppermute | solution.py:802
  189.7 18.6 %collective-permute-start.24 = (bf16[2,160,256]{2,1,0:T(8,128)(2,1)}, bf16[2,160,256]{2,1,0:T(8,128)(2,1)S(1)}, u32[]{:S(2)}, u32[]{:S(2)}) collective-permute-start(bf16[2,160,256]{2,1,0:T(8,128)(2,1)} %add_arrived.1.refs_0_), channel_id=1, source_target_pairs={{0,24},{8,16},{16,8},{24,0},{1,25},{9,17},{17,9},{25,1},{2,26},{10... | collective-permute-start | bytes 491528 | tf_op jit(solution)/shard_map/ppermute | solution.py:802
  193.4 14.9 %collective-permute-start.23 = (bf16[2,160,256]{2,1,0:T(8,128)(2,1)}, bf16[2,160,256]{2,1,0:T(8,128)(2,1)S(1)}, u32[]{:S(2)}, u32[]{:S(2)}) collective-permute-start(bf16[2,160,256]{2,1,0:T(8,128)(2,1)} %add_arrived.1.refs_0_), channel_id=1, source_target_pairs={{0,16},{8,24},{16,0},{24,8},{1,17},{9,25},{17,1},{25,9},{2,18},{10... | collective-permute-start | bytes 491528 | tf_op jit(solution)/shard_map/ppermute | solution.py:802
  195.0 13.3 %collective-permute-start.22 = (bf16[2,160,256]{2,1,0:T(8,128)(2,1)}, bf16[2,160,256]{2,1,0:T(8,128)(2,1)S(1)}, u32[]{:S(2)}, u32[]{:S(2)}) collective-permute-start(bf16[2,160,256]{2,1,0:T(8,128)(2,1)} %add_arrived.1.refs_0_), channel_id=1, source_target_pairs={{0,8},{8,0},{16,24},{24,16},{1,9},{9,1},{17,25},{25,17},{2,10},{10... | collective-permute-start | bytes 491528 | tf_op jit(solution)/shard_map/ppermute | solution.py:802
  195.1 7.3 %collective-permute-start.30 = (bf16[288,128]{1,0:T(8,128)(2,1)S(1)}, bf16[288,128]{1,0:T(8,128)(2,1)S(1)}, u32[]{:S(2)}, u32[]{:S(2)}) collective-permute-start(bf16[288,128]{1,0:T(8,128)(2,1)S(1)} %fusion.8.refs_0_), channel_id=1, source_target_pairs={{0,24},{8,16},{16,8},{24,0},{1,25},{9,17},{17,9},{25,1},{2,26},{10... | collective-permute-start | bytes 221192 | tf_op jit(solution)/shard_map/ppermute | solution.py:802
  195.5 9.5 %collective-permute-start.29 = (bf16[288,128]{1,0:T(8,128)(2,1)S(1)}, bf16[288,128]{1,0:T(8,128)(2,1)S(1)}, u32[]{:S(2)}, u32[]{:S(2)}) collective-permute-start(bf16[288,128]{1,0:T(8,128)(2,1)S(1)} %fusion.8.refs_0_), channel_id=1, source_target_pairs={{0,16},{8,24},{16,0},{24,8},{1,17},{9,25},{17,1},{25,9},{2,18},{10... | collective-permute-start | bytes 221192 | tf_op jit(solution)/shard_map/ppermute | solution.py:802
  202.3 3.5 %collective-permute-start.28 = (bf16[288,128]{1,0:T(8,128)(2,1)S(1)}, bf16[288,128]{1,0:T(8,128)(2,1)S(1)}, u32[]{:S(2)}, u32[]{:S(2)}) collective-permute-start(bf16[288,128]{1,0:T(8,128)(2,1)S(1)} %fusion.8.refs_0_), channel_id=1, source_target_pairs={{0,8},{8,0},{16,24},{24,16},{1,9},{9,1},{17,25},{25,17},{2,10},{10... | collective-permute-start | bytes 221192 | tf_op jit(solution)/shard_map/ppermute | solution.py:802
  (16 other events, 75.5 us)

commit v5 on v4

--- a/solution.py
+++ b/solution.py
@@ -12,7 +12,6 @@
 CHUNK = 256
 SUB = 128
 BACK = 512
-ROWS = 512
 QUAD = 256
 F32 = jnp.float32
 BF16 = jnp.bfloat16
@@ -169,6 +168,7 @@
     block = jnp.zeros((16, 256), F32)
     for k, ref in ((0, gain_1), (1, shift_1), (2, gain_2), (3, shift_2), (4, bias_2), (8, bias_1)):
         part = ref[...].astype(F32)
+        part = jnp.concatenate([part[n : n + 1] for n in range(part.shape[0])], axis=1)
         width = part.shape[1]
         if width < 256:
             part = jnp.concatenate([part, jnp.zeros((1, 256 - width), F32)], axis=1)
@@ -326,146 +326,192 @@
     out_ref,
     hidden_ref,
     grad_mix_ref,
-    keep_ref,
-    send_ref,
+    keep_out_ref,
+    send_out_ref,
+    x,
+    mix,
+    teacher,
     wo,
     we,
     wc,
     act,
+    out,
+    hidden_grad,
+    grad_mix,
+    keep_ref,
+    send_ref,
+    normed,
+    low,
+    d_normed,
     d_wo,
     d_we,
     d_wc,
     d_vec,
     d_eb,
-    loss_ref,
     sems,
 ):
-    step = pl.program_id(0)
     r = 512 // shards
     me, core, cross = place()
-
-    @pl.when(step == 0)
-    def _():
-        loss_ref[...] = jnp.zeros_like(loss_ref)
-        for half, source in enumerate((mine_ref, theirs_ref)):
-            column = pl.multiple_of(((core + half) % 2) * 256, 256)
-            for slot, (z, y, x) in enumerate(slots_of(shards)):
-                owner = me ^ (2 * z + y)
-                third = cross ^ x
+    copies = [
+        pltpu.make_async_copy(mix_0_ref, mix.at[:, pl.ds(0, QUAD)], sems.at[0]),
+        pltpu.make_async_copy(mix_1_ref, mix.at[:, pl.ds(QUAD, QUAD)], sems.at[1]),
+        pltpu.make_async_copy(x_ref, x, sems.at[2]),
+        pltpu.make_async_copy(teacher_ref, teacher, sems.at[3]),
+    ]
+    sources = list(enumerate((mine_ref, theirs_ref)))
+    columns = [pl.multiple_of(((core + half) % 2) * 256, 256) for half, _ in sources]
+    for copy in copies[:2]:
+        copy.start()
+    for half, source in sources:
+        for slot, (z, y, cross_slot) in enumerate(slots_of(shards)):
+            pltpu.make_async_copy(
+                source.at[slot, pl.ds(4 * r, r // 2)],
+                wo.at[2 * (me ^ (2 * z + y)) + (cross ^ cross_slot), :, pl.ds(columns[half], 256)],
+                sems.at[4],
+            ).start()
+    copies[2].start()
+    for half, source in sources:
+        for slot, (z, y, cross_slot) in enumerate(slots_of(shards)):
+            owner = me ^ (2 * z + y)
+
+            def expansion():
+                for b in range(4):
+                    pltpu.make_async_copy(
+                        source.at[slot, pl.ds(b * r, r)],
+                        we.at[
+                            b, pl.ds(pl.multiple_of(owner * r, r), r), pl.ds(columns[half], 256)
+                        ],
+                        sems.at[5],
+                    ).start()
+
+            def contraction():
                 pltpu.make_async_copy(
-                    source.at[slot, pl.ds(4 * r, r // 2)],
-                    wo.at[2 * owner + third, :, pl.ds(column, 256)],
-                    sems.at[0],
+                    source.at[slot, pl.ds(0, 4 * r)],
+                    wc.at[
+                        pl.ds(pl.multiple_of(owner * 4 * r, 4 * r), 4 * r),
+                        pl.ds(columns[half], 256),
+                    ],
+                    sems.at[6],
                 ).start()
 
-                def expansion():
-                    for b in range(4):
-                        pltpu.make_async_copy(
-                            source.at[slot, pl.ds(b * r, r)],
-                            we.at[
-                                b, pl.ds(pl.multiple_of(owner * r, r), r), pl.ds(column, 256)
-                            ],
-                            sems.at[1],
-                        ).start()
-
-                def contraction():
-                    pltpu.make_async_copy(
-                        source.at[slot, pl.ds(0, 4 * r)],
-                        wc.at[
-                            pl.ds(pl.multiple_of(owner * 4 * r, 4 * r), 4 * r), pl.ds(column, 256)
-                        ],
-                        sems.at[2],
-                    ).start()
-
-                pl.when(third == 0)(expansion)
-                pl.when(third == 1)(contraction)
-        for ref in (d_wo, d_we, d_wc, d_vec, d_eb):
-            ref[...] = jnp.zeros_like(ref)
-        pltpu.make_async_copy(wo, wo, sems.at[0]).wait()
+            pl.when((cross ^ cross_slot) == 0)(expansion)
+            pl.when((cross ^ cross_slot) == 1)(contraction)
+    copies[3].start()
 
     gain, shift, bias = vec_ref[2:3, :], vec_ref[3:4, :], vec_ref[4:5, :]
+    copies[0].wait()
+    copies[1].wait()
+    pltpu.make_async_copy(wo, wo, sems.at[4]).wait()
+    copies[2].wait()
     weight_out = wo[...].reshape(512, 512)
-    mixed = jnp.concatenate([mix_0_ref[...], mix_1_ref[...]], axis=1)
-    hidden = x_ref[...].astype(F32) + nn(mixed, weight_out)
+    hidden = x[...].astype(F32) + nn(mix[...], weight_out)
     normal, scale = standardise(hidden)
-    normed = (normal * gain + shift).astype(BF16)
-    pl.when(step == 0)(lambda: pltpu.make_async_copy(we, we, sems.at[1]).wait())
+    normed[...] = (normal * gain + shift).astype(BF16)
+    pltpu.make_async_copy(we, we, sems.at[5]).wait()
     for b in range(4):
-        at = slice(b * 512, (b + 1) * 512)
-        before = nn(normed, we[b]) + eb_ref[0:1, at]
-        act[:, at] = jnp.maximum(before, 0.0).astype(BF16)
-    pl.when(step == 0)(lambda: pltpu.make_async_copy(wc, wc, sems.at[2]).wait())
-    result = hidden + (nn(act[...], wc[...]) + bias)
-    out_ref[...] = result.astype(BF16)
+        before = nn(normed[...], we[b]) + eb_ref[0:1, b * 512 : (b + 1) * 512]
+        act[b] = jnp.maximum(before, 0.0).astype(BF16)
+    pltpu.make_async_copy(wc, wc, sems.at[6]).wait()
+    active = jnp.concatenate([act[b] for b in range(4)], axis=1)
+    result = hidden + (nn(active, wc[...]) + bias)
+    out[...] = result.astype(BF16)
+    out_copy = pltpu.make_async_copy(out, out_ref, sems.at[7])
+    out_copy.start()
+    copies[3].wait()
     valid = as_column(valid_ref[...].astype(F32), 512)
-    error = result - teacher_ref[...].astype(F32)
+    error = result - teacher[...].astype(F32)
     masked = valid * error
-    loss_ref[...] += jnp.sum(masked * error)
+    loss = jnp.sum(masked * error)
     count = 256.0 * count_ref[6:7, 0:1] + count_ref[6:7, 1:2]
     grad_result = masked * (tokens / count)
-    low = grad_result.astype(BF16)
-    d_normed = None
-    for b in range(4):
-        at = slice(b * 512, (b + 1) * 512)
-        active = act[:, at]
-        d_wc[at, :] += tn(active, low)
-        grad = jnp.where(active > 0, nt(low, wc[at, :]), 0.0)
-        grad = grad.astype(BF16)
-        d_we[b] += tn(normed, grad)
-        d_eb[0:1, at] += jnp.sum(grad.astype(F32), axis=0, keepdims=True)
-        part = nt(grad, we[b])
-        d_normed = part if d_normed is None else d_normed + part
-    d_vec[0:1, :] += jnp.sum(d_normed * normal, axis=0, keepdims=True)
-    d_vec[1:2, :] += jnp.sum(d_normed, axis=0, keepdims=True)
-    d_vec[2:3, :] += jnp.sum(low.astype(F32), axis=0, keepdims=True)
-    grad_hidden = grad_result + norm_backward(d_normed, gain, normal, scale)
-    hidden_ref[...] = grad_hidden
+    hidden_grad[...] = grad_result
+    low[...] = grad_result.astype(BF16)
+    d_normed[...] = jnp.zeros_like(d_normed)
+
+    @pl.loop(0, 4)
+    def _(b):
+        at = pl.ds(pl.multiple_of(b * 512, 512), 512)
+        d_wc[at, :] = tn(act[b], low[...]).astype(BF16)
+        grad = jnp.where(act[b] > 0, nt(low[...], wc[at, :]), 0.0).astype(BF16)
+        d_we[b] = tn(normed[...], grad).astype(BF16)
+        d_eb[b, 0:1, :] = jnp.sum(grad.astype(F32), axis=0, keepdims=True)
+        d_normed[...] += nt(grad, we[b])
+
+    incoming = d_normed[...]
+    hidden = x[...].astype(F32) + nn(mix[...], weight_out)
+    normal, scale = standardise(hidden)
+    d_vec[0:1, :] = jnp.sum(incoming * normal, axis=0, keepdims=True)
+    d_vec[1:2, :] = jnp.sum(incoming, axis=0, keepdims=True)
+    d_vec[2:3, :] = jnp.sum(low[...].astype(F32), axis=0, keepdims=True)
+    d_vec[3:8, :] = jnp.zeros((5, 512), F32)
+    grad_hidden = hidden_grad[...] + norm_backward(incoming, gain, normal, scale)
+    hidden_grad[...] = grad_hidden
+    hidden_copy = pltpu.make_async_copy(hidden_grad, hidden_ref, sems.at[8])
+    hidden_copy.start()
     grad_low = grad_hidden.astype(BF16)
-    d_wo[...] += tn(mixed, grad_low)
-    grad_mix_ref[...] = nt(grad_low, weight_out).astype(BF16)
-
-    @pl.when(step == pl.num_programs(0) - 1)
-    def _():
-        width = 2048 // shards
-        digits = digits_of(loss_ref[...])
-
-        _, rows = branch_rows(shards, keep_ref.shape[0])
-
-        def write(ref, at):
-            for s in range(shards):
-                top = jnp.concatenate([piece_of(d_vec[...], s, r), digits], axis=1)
-                if width >= 128:
-                    low_rows = d_eb[:, s * width : (s + 1) * width]
+    grad_mix[...] = nt(grad_low, weight_out).astype(BF16)
+    mix_copy = pltpu.make_async_copy(grad_mix, grad_mix_ref, sems.at[9])
+    mix_copy.start()
+    d_wo[...] = tn(mix[...], grad_low).astype(BF16)
+
+    width = 2048 // shards
+    digits = digits_of(jnp.zeros((8, 128), F32) + loss)
+    _, rows = branch_rows(shards, keep_ref.shape[0])
+    d_eb_all = jnp.concatenate([d_eb[b] for b in range(4)], axis=1)
+    extra = []
+    for s in range(shards):
+        top = jnp.concatenate([piece_of(d_vec[...], s, r), digits], axis=1)
+        if width >= 128:
+            low_rows = d_eb_all[:, s * width : (s + 1) * width]
+        else:
+            low_rows = piece_of(d_eb_all, s, width)
+        if low_rows.shape[1] < 256:
+            pad = jnp.zeros((8, 256 - low_rows.shape[1]), F32)
+            low_rows = jnp.concatenate([low_rows, pad], axis=1)
+        extra.append(jnp.concatenate([top, low_rows], axis=0).astype(BF16))
+
+    def write(ref, at, wanted):
+        for s in range(shards):
+            for name, done, part, offset, size in rows:
+                if part != wanted:
+                    continue
+                if name == "contract":
+                    value = d_wc[s * 4 * r + done : s * 4 * r + done + size, at]
+                elif name == "output":
+                    value = d_wo[s * r + done : s * r + done + size, at]
+                elif name == "vectors":
+                    value = extra[s][done : done + size]
+                elif name == "none":
+                    value = jnp.zeros((size, 256), BF16)
                 else:
-                    low_rows = piece_of(d_eb[...], s, width)
-                if low_rows.shape[1] < 256:
-                    pad = jnp.zeros((8, 256 - low_rows.shape[1]), F32)
-                    low_rows = jnp.concatenate([low_rows, pad], axis=1)
-                both = jnp.concatenate([top, low_rows], axis=0)
-                for name, done, part, offset, size in rows:
-                    if name == "contract":
-                        value = d_wc[s * 4 * r + done : s * 4 * r + done + size, at]
-                    elif name == "output":
-                        value = d_wo[s * r + done : s * r + done + size, at]
-                    elif name == "vectors":
-                        value = both[done : done + size]
-                    elif name == "none":
-                        value = jnp.zeros((size, 256), F32)
-                    else:
-                        value = d_we[name, s * r + done : s * r + done + size, at]
-                    ref[part, s, offset : offset + size, :] = value.astype(BF16)
-
-        left, right = slice(0, 256), slice(256, 512)
+                    value = d_we[name, s * r + done : s * r + done + size, at]
+                ref[part, s, offset : offset + size, :] = value
+
+    left, right = slice(0, 256), slice(256, 512)
+    reps = keep_ref.shape[0]
+    flights = []
+    for part in range(reps):
 
         @pl.when(core == 0)
         def _():
-            write(keep_ref, left)
-            write(send_ref, right)
+            write(send_ref, right, part)
+            write(keep_ref, left, part)
 
         @pl.when(core == 1)
         def _():
-            write(keep_ref, right)
-            write(send_ref, left)
+            write(send_ref, left, part)
+            write(keep_ref, right, part)
+
+        for n, (source, target) in enumerate(
+            ((send_ref, send_out_ref), (keep_ref, keep_out_ref))
+        ):
+            copy = pltpu.make_async_copy(
+                source.at[part], target.at[part], sems.at[10 + 2 * part + n]
+            )
+            copy.start()
+            flights.append(copy)
+    for copy in [out_copy, hidden_copy, mix_copy, *flights]:
+        copy.wait()
 
 
 def attention_backward(shards, seg_s, x_ref, seg_ref, *refs):
@@ -645,7 +691,7 @@
 
 def call_pack(shards, matrices, vectors, valid):
     r = 512 // shards
-    operands = [*matrices, *[v[None] for v in vectors], valid]
+    operands = [*matrices, *[v.reshape(-1, min(128, v.shape[0])) for v in vectors], valid]
     mixer, branch = (2 * r + 16, 256), (4 * r + r // 2, 256)
     return pl.pallas_call(
         functools.partial(pack, shards),
@@ -709,46 +755,45 @@
 
 def call_feed_forward(shards, reps, tokens, *operands):
     length = operands[0].shape[0]
-    chunks = length // ROWS
     r = 512 // shards
-    tile = lambda width: pl.BlockSpec((ROWS, width), lambda c: (c, 0))
     payload = (reps, shards, branch_rows(shards, reps)[0], 256)
+    vmem = pl.BlockSpec(memory_space=pltpu.VMEM)
+    wide = (length, 512)
     return pl.pallas_call(
         functools.partial(feed_forward, shards, tokens),
-        grid=(chunks,),
-        in_specs=[
-            tile(512),
-            tile(QUAD),
-            tile(QUAD),
-            tile(512),
-            pl.BlockSpec((1, ROWS), lambda c: (0, c)),
-            whole((8, 512)),
-            whole((8, 2048)),
-            whole((8, 128)),
-            anywhere(),
-            anywhere(),
-        ],
-        out_specs=[tile(512)] * 3 + [whole(payload)] * 2,
+        in_specs=[anywhere()] * 4 + [vmem] * 4 + [anywhere()] * 2,
+        out_specs=[anywhere()] * 5,
         out_shape=[
-            shaped((length, 512), BF16),
-            shaped((length, 512), F32),
-            shaped((length, 512), BF16),
-            *[shaped(payload, BF16)] * 2,
+            shaped(wide, BF16),
+            shaped(wide, F32),
+            shaped(wide, BF16),
+            shaped(payload, BF16),
+            shaped(payload, BF16),
         ],
         scratch_shapes=[
+            pltpu.VMEM(wide, BF16),
+            pltpu.VMEM(wide, BF16),
+            pltpu.VMEM(wide, BF16),
             pltpu.VMEM((2 * shards, r // 2, 512), BF16),
             pltpu.VMEM((4, 512, 512), BF16),
             pltpu.VMEM((2048, 512), BF16),
-            pltpu.VMEM((ROWS, 2048), BF16),
-            pltpu.VMEM((512, 512), F32),
-            pltpu.VMEM((4, 512, 512), F32),
-            pltpu.VMEM((2048, 512), F32),
+            pltpu.VMEM((4, length, 512), BF16),
+            pltpu.VMEM(wide, BF16),
+            pltpu.VMEM(wide, F32),
+            pltpu.VMEM(wide, BF16),
+            pltpu.VMEM(payload, BF16),
+            pltpu.VMEM(payload, BF16),
+            pltpu.VMEM(wide, BF16),
+            pltpu.VMEM(wide, BF16),
+            pltpu.VMEM(wide, F32),
+            pltpu.VMEM((512, 512), BF16),
+            pltpu.VMEM((4, 512, 512), BF16),
+            pltpu.VMEM((2048, 512), BF16),
             pltpu.VMEM((8, 512), F32),
-            pltpu.VMEM((8, 2048), F32),
-            pltpu.VMEM((8, 128), F32),
-            pltpu.SemaphoreType.DMA((3,)),
+            pltpu.VMEM((4, 8, 512), F32),
+            pltpu.SemaphoreType.DMA((10 + 2 * reps,)),
         ],
-        compiler_params=params(),
+        compiler_params=pltpu.CompilerParams(vmem_limit_bytes=VMEM_LIMIT),
         cost_estimate=COST,
         name="feed_forward",
     )(*operands)
@@ -920,16 +965,26 @@
     shift_ref[...] = vectors[1:2, :r]
 
 
-def assemble(body, shards, parts, shapes, scratch=()):
+def assemble_all(shards, reps, count_ref, *refs):
+    parts_q, parts_f, refs = refs[:4], refs[4 : 4 + reps], refs[4 + reps :]
+    assemble_mixer(shards, *parts_q, *refs[:6])
+    assemble_branch(shards, count_ref, *parts_f, *refs[6:])
+
+
+def assemble(shards, count, parts_q, parts_f):
+    reps = len(parts_f)
+    r = 512 // shards
+    shapes = [(r, 512)] * 4 + [(1, r)] * 2
+    shapes += [(4 * r, 512), (r, 2048), (r, 512), (1, 4 * r), (1, r), (1, r), (1, r), (1, 1)]
     return pl.pallas_call(
-        functools.partial(body, shards),
-        in_specs=[pl.BlockSpec(memory_space=pltpu.VMEM)] * len(parts),
+        functools.partial(assemble_all, shards, reps),
+        in_specs=[pl.BlockSpec(memory_space=pltpu.VMEM)] * (5 + reps),
         out_specs=[pl.BlockSpec(memory_space=pltpu.VMEM)] * len(shapes),
         out_shape=[shaped(shape, F32) for shape in shapes],
-        scratch_shapes=list(scratch),
+        scratch_shapes=[pltpu.VMEM((reps, *parts_f[0].shape), BF16)],
         cost_estimate=COST,
         name="assemble",
-    )(*parts)
+    )(count, *parts_q, *parts_f)
 
 
 def add_low(*parts):
@@ -1084,16 +1139,9 @@
     total_f = call_add_arrived(shards, arrived_f, q_pieces[0])
     parts_f = [total_f] + [swap(total_f, "rep", a) for a in range(1, reps)]
     parts_q = finish(q_pieces)
-    grad_contract, grad_expand, grad_output, bias_1, bias_2, gain_2, shift_2, loss = assemble(
-        assemble_branch,
-        shards,
-        [count, *parts_f],
-        [(4 * r, 512), (r, 2048), (r, 512), (1, 4 * r), (1, r), (1, r), (1, r), (1, 1)],
-        [pltpu.VMEM((reps, *total_f.shape), BF16)],
-    )
-    *mats, gain_1, shift_1 = assemble(
-        assemble_mixer, shards, parts_q, [(r, 512)] * 4 + [(1, r)] * 2
-    )
+    results = assemble(shards, count, parts_q, parts_f)
+    mats, (gain_1, shift_1) = results[:4], results[4:6]
+    grad_contract, grad_expand, grad_output, bias_1, bias_2, gain_2, shift_2, loss = results[6:]
     return (
         layer_out.reshape(inputs.shape),
         grad_inputs.reshape(inputs.shape),

time: 213 us -> 208 us (0.977)
  Pallas kernels: 87.5 us -> 84.9 us
    pallas_call x3 -> x2, Pallas kernels: 30.9 us -> 28.3 us  [the longest x1 25.8 us: call_feed_forward(): pl.pallas_call(functools.partial(feed_forward, shards, tokens), in_specs=...]
  transfers between devices with their start and end apart: 32 -> 32, of which waited for: 16 -> 16; matrix products, arithmetic and copies ran while one was open for 4% -> 4% of each run, Pallas kernels for 27% -> 26%
where the time goes in v5:
time: 208 us; the launch traced here: 207 us
  Pallas kernels  84.9 us (41%)
  waiting for transfers between devices  60.7 us (29%)
  starting transfers between devices  37 us (18%)
  local copies, waits for them, and re-layouts  12.3 us (6%)
  other arithmetic  8.67 us (4%)
  between operations  3.2 us (2%)
    ppermute x31, waiting for transfers between devices, swap(): return lax.ppermute(value, axis, [(i, i ^ bit) for i in range(n)])  60.7 us
    ppermute x31, starting transfers between devices, swap(): return lax.ppermute(value, axis, [(i, i ^ bit) for i in range(n)])  30.7 us
    pallas_call x1, Pallas kernels, call_backward(): pl.pallas_call(functools.partial(ordered, functools.partial(attention_bac...  28.9 us
    pallas_call x1, Pallas kernels, call_feed_forward(): pl.pallas_call(functools.partial(feed_forward, shards, tokens), in_specs=...  25.8 us
    pallas_call x2, Pallas kernels, call_forward(): pl.pallas_call(functools.partial(ordered, functools.partial(attention_for...  23 us
    unnamed x48, local copies, waits for them, and re-layouts  8.89 us
    all_to_all x1, starting transfers between devices, local(): lax.all_to_all(every, ('rep', 'shard'), 0, 0).reshape(summed.shape)  6.22 us
    convert_element_type x6, other arithmetic, add_low(): return sum((part.astype(F32) for part in parts)).astype(BF16)  5.96 us
  transfers between devices with their start and end apart: 32, of which 16 were waited for; matrix products, arithmetic and copies ran while one was open for 4% of the time, Pallas kernels for 26%

profile of v5, /device:TPU:13, one launch (start us, length us, event | category | flops | bytes accessed | tf_op | source)
XLA Modules:
  0.0 206.8 jit_solution(11213687237044299972)
XLA Ops:
  0.7 2.0 pack.1
  2.9 2.4 %collective-permute-start.4 = (bf16[1,144,256]{2,1,0:T(8,128)(2,1)}, bf16[1,144,256]{2,1,0:T(8,128)(2,1)S(1)}, u32[]{:S(2)}, u32[]{:S(2)}) collective-permute-start(bf16[1,144,256]{2,1,0:T(8,128)(2,1)} %bitcast.106), channel_id=1, source_target_pairs={{0,6},{1,7},{2,4},{3,5},{4,2},{5,3},{6,0},{7,1},{8,14},{9,15},{10,... | collective-permute-start | bytes 221192 | tf_op jit(solution)/shard_map/ppermute | solution.py:847
  11.1 6.5 %collective-permute-done.3 = bf16[1,144,256]{2,1,0:T(8,128)(2,1)S(1)} collective-permute-done((bf16[1,144,256]{2,1,0:T(8,128)(2,1)}, bf16[1,144,256]{2,1,0:T(8,128)(2,1)S(1)}, u32[]{:S(2)}, u32[]{:S(2)}) %collective-permute-start.3) | collective-permute-done | bytes 73760 | tf_op jit(solution)/shard_map/ppermute | solution.py:847
  20.2 4.1 %collective-permute-done.8 = bf16[1,288,256]{2,1,0:T(8,128)(2,1)S(1)} collective-permute-done((bf16[1,288,256]{2,1,0:T(8,128)(2,1)}, bf16[1,288,256]{2,1,0:T(8,128)(2,1)S(1)}, u32[]{:S(2)}, u32[]{:S(2)}) %collective-permute-start.8) | collective-permute-done | bytes 147488 | tf_op jit(solution)/shard_map/ppermute | solution.py:847
  28.4 6.8 %collective-permute-done.6 = bf16[4,144,256]{2,1,0:T(8,128)(2,1)S(1)} collective-permute-done((bf16[4,144,256]{2,1,0:T(8,128)(2,1)S(1)}, bf16[4,144,256]{2,1,0:T(8,128)(2,1)S(1)}, u32[]{:S(2)}, u32[]{:S(2)}) %collective-permute-start.6) | collective-permute-done | bytes 294944 | tf_op jit(solution)/shard_map/ppermute | solution.py:847
  35.3 2.2 %collective-permute-start.10 = (bf16[16,144,256]{2,1,0:T(8,128)(2,1)S(1)}, bf16[16,144,256]{2,1,0:T(8,128)(2,1)S(1)}, u32[]{:S(2)}, u32[]{:S(2)}) collective-permute-start(bf16[16,144,256]{2,1,0:T(8,128)(2,1)S(1)} %add_dynamic-update-slice_fusion.refs_3_), channel_id=1, source_target_pairs={{0,8},{8,0},{16,24},{24,16},{1,9},{9,1},{17,25},{25,17},{2,10},{10... | collective-permute-start | bytes 3538952 | tf_op jit(solution)/shard_map/ppermute | solution.py:847
  41.5 12.4 %attention_forward_0.1 = (bf16[1024,256]{1,0:T(8,128)(2,1)}, bf16[1024,256]{1,0:T(8,128)(2,1)}, bf16[1024,256]{1,0:T(8,128)(2,1)}, bf16[1024,256]{1,0:T(8,128)(2...) custom-call(s32[1,1024]{1,0:T(1,128)} %refs_2_.7, ...), custom_call_target="tpu_custom_call" | custom-call | flops 1000 | bytes 1000 | tf_op jit(solution)/shard_map/attention_forward_0/pallas_call | solution.py:740
  56.3 10.6 %attention_forward_1.1 = (bf16[1024,256]{1,0:T(8,128)(2,1)}, bf16[1024,256]{1,0:T(8,128)(2,1)}, bf16[1024,256]{1,0:T(8,128)(2,1)}, bf16[1024,256]{1,0:T(8,128)(2...) custom-call(s32[1,1024]{1,0:T(1,128)} %refs_2_.7, ...), custom_call_target="tpu_custom_call" | custom-call | flops 1000 | bytes 1000 | tf_op jit(solution)/shard_map/attention_forward_1/pallas_call | solution.py:740
  66.9 1.5 collective-permute-done.13
  68.4 1.6 collective-permute-done.14
  72.4 1.6 collective-permute-start.15
  73.9 4.2 %collective-permute-done.15.theirs_ref = bf16[16,288,256]{2,1,0:T(8,128)(2,1)S(1)} collective-permute-done((bf16[16,288,256]{2,1,0:T(8,128)(2,1)S(1)}, bf16[16,288,256]{2,1,0:T(8,128)(2,1)S(1)}, u32[]{:S(2)}, u32[]{:S(2)}) %collective-permute-start.15) | collective-permute-done | bytes 2359328 | tf_op jit(solution)/shard_map/ppermute | solution.py:847
  78.1 1.5 copy-done.2
  79.6 25.8 %feed_forward.1 = (bf16[1024,512]{1,0:T(8,128)(2,1)}, f32[1024,512]{1,0:T(8,128)}, bf16[1024,512]{1,0:T(8,128)(2,1)}, bf16[4,8,160,256]{3,2,1,0:T(8,128)(2,1)}, bf16[4,8,160,256]{3,2,1,0:T(8,128)(2,1)}) custom-call(bf16[1024,512]{1,0:T(8,128)(2,1)} %bitcast.96, bf16[1024,256]{1,0:T(8,128)(2,1)} %get-tuple-element.70.mix_0_ref, ...), custom_call_target="tpu_custom_call" | custom-call | flops 1000 | bytes 1000 | tf_op jit(solution)/shard_map/feed_forward/pallas_call | solution.py:762
  105.8 4.7 %collective-permute-done.16 = bf16[4,8,160,256]{3,2,1,0:T(8,128)(2,1)S(1)} collective-permute-done((bf16[4,8,160,256]{3,2,1,0:T(8,128)(2,1)}, bf16[4,8,160,256]{3,2,1,0:T(8,128)(2,1)S(1)}, u32[]{:S(2)}, u32[]{:S(2)}) %collective-permute-start.16) | collective-permute-done | bytes 2621472 | tf_op jit(solution)/shard_map/ppermute | solution.py:847
  110.5 4.2 %add_convert_fusion = bf16[4,8,160,256]{3,2,1,0:T(8,128)(2,1)} fusion(bf16[4,8,160,256]{3,2,1,0:T(8,128)(2,1)S(1)} %collective-permute-done.16, bf16[4,8,160,256]{3,2,1,0:T(8,128)(2,1)} %get-tuple-element.101), kind=kLoop, calls=%fused_computation | loop fusion | flops 5242880 | bytes 7864320 | tf_op jit(solution)/shard_map/convert_element_type | solution.py:991
  114.7 6.2 %all-to-all-start = ((bf16[32,160,256]{2,1,0:T(8,128)(2,1)}), bf16[32,160,256]{2,1,0:T(8,128)(2,1)S(1)}, u32[]{:S(2)}, u32[]{:S(2)}) async-start(bf16[32,160,256]{2,1,0:T(8,128)(2,1)} %bitcast.12.refs_25_), calls=%async_computation | async-start | bytes 5242880 | tf_op jit(solution)/shard_map/all_to_all | solution.py:1130
  120.9 28.9 %attention_backward.1 = (f32[1024,512]{1,0:T(8,128)}, bf16[2,2,2,4,144,128]{5,4,3,2,1,0:T(8,128)(2,1)}, bf16[2,2,2,4,144,128]{5,4,3,2,1,0:T(8,128)(2,1)}) custom-call(s32[1,1024]{1,0:T(1,128)} %refs_2_.7, bf16[1024,512]{1,0:T(8,128)(2,1)} %bitcast.97, s32[1,1024]{1,0:T(1,128)} %refs_2_.7, bf16[1024,256]{1,0:T(8,128)(2,1)} %get-tuple-element.81.refs_3_, ...), custom_call_target="tpu_custom_call" | custom-call | flops 1000 | bytes 1000 | tf_op jit(solution)/shard_map/attention_backward/pallas_call | solution.py:833
  150.2 2.7 %collective-permute-done.17 = bf16[2,2,2,4,144,128]{5,4,3,2,1,0:T(8,128)(2,1)S(1)} collective-permute-done((bf16[2,2,2,4,144,128]{5,4,3,2,1,0:T(8,128)(2,1)}, bf16[2,2,2,4,144,128]{5,4,3,2,1,0:T(8,128)(2,1)S(1)}, u32[]{:S(2)}, u32[]{:S(2)}) %collective-permute-start.17) | collective-permute-done | bytes 1179680 | tf_op jit(solution)/shard_map/ppermute | solution.py:847
  152.9 1.6 add_convert_fusion.4
  156.0 11.4 %collective-permute-done.20 = bf16[2,4,144,128]{3,2,1,0:T(8,128)(2,1)S(1)} collective-permute-done((bf16[2,4,144,128]{3,2,1,0:T(8,128)(2,1)S(1)}, bf16[2,4,144,128]{3,2,1,0:T(8,128)(2,1)S(1)}, u32[]{:S(2)}, u32[]{:S(2)}) %collective-permute-start.20) | collective-permute-done | bytes 294944 | tf_op jit(solution)/shard_map/ppermute | solution.py:847
  167.7 4.1 %collective-permute-done.18 = bf16[2,4,144,128]{3,2,1,0:T(8,128)(2,1)S(1)} collective-permute-done((bf16[2,4,144,128]{3,2,1,0:T(8,128)(2,1)S(1)}, bf16[2,4,144,128]{3,2,1,0:T(8,128)(2,1)S(1)}, u32[]{:S(2)}, u32[]{:S(2)}) %collective-permute-start.18) | collective-permute-done | bytes 294944 | tf_op jit(solution)/shard_map/ppermute | solution.py:847
  172.0 5.8 %collective-permute-done.21 = bf16[4,144,128]{2,1,0:T(8,128)(2,1)S(1)} collective-permute-done((bf16[4,144,128]{2,1,0:T(8,128)(2,1)S(1)}, bf16[4,144,128]{2,1,0:T(8,128)(2,1)S(1)}, u32[]{:S(2)}, u32[]{:S(2)}) %collective-permute-start.21) | collective-permute-done | bytes 147488 | tf_op jit(solution)/shard_map/ppermute | solution.py:847
  178.8 3.7 %collective-permute-start.23 = (bf16[1,288,128]{2,1,0:T(8,128)(2,1)S(1)}, bf16[1,288,128]{2,1,0:T(8,128)(2,1)S(1)}, u32[]{:S(2)}, u32[]{:S(2)}) collective-permute-start(bf16[1,288,128]{2,1,0:T(8,128)(2,1)S(1)} %pad_maximum_fusion.8), channel_id=1, source_target_pairs={{0,4},{1,5},{2,6},{3,7},{4,0},{5,1},{6,2},{7,3},{8,12},{9,13},{10,... | collective-permute-start | bytes 221192 | tf_op jit(solution)/shard_map/ppermute | solution.py:847
  183.1 1.5 copy-done
  184.6 2.7 %add_arrived.1.refs_4_ = bf16[2,160,256]{2,1,0:T(8,128)(2,1)} custom-call(bf16[4,8,160,256]{3,2,1,0:T(8,128)(2,1)} %bitcast.98, bf16[1,288,128]{2,1,0:T(8,128)(2,1)} %pad_maximum_fusion.6.refs_1_), custom_call_target="tpu_custom_call" | custom-call | flops 1000 | bytes 1000 | tf_op jit(solution)/shard_map/add_arrived/pallas_call | solution.py:883
  187.3 2.8 %collective-permute-start.30 = (bf16[2,160,256]{2,1,0:T(8,128)(2,1)}, bf16[2,160,256]{2,1,0:T(8,128)(2,1)S(1)}, u32[]{:S(2)}, u32[]{:S(2)}) collective-permute-start(bf16[2,160,256]{2,1,0:T(8,128)(2,1)} %add_arrived.1.refs_4_), channel_id=1, source_target_pairs={{0,24},{8,16},{16,8},{24,0},{1,25},{9,17},{17,9},{25,1},{2,26},{10... | collective-permute-start | bytes 491528 | tf_op jit(solution)/shard_map/ppermute | solution.py:847
  190.2 1.6 collective-permute-start.29
  192.3 1.5 collective-permute-start.26
  193.7 5.4 %collective-permute-done.27.refs_3_ = bf16[288,128]{1,0:T(8,128)(2,1)S(1)} collective-permute-done((bf16[288,128]{1,0:T(8,128)(2,1)S(1)}, bf16[288,128]{1,0:T(8,128)(2,1)S(1)}, u32[]{:S(2)}, u32[]{:S(2)}) %collective-permute-start.27) | collective-permute-done | bytes 73760 | tf_op jit(solution)/shard_map/ppermute | solution.py:847
  199.1 2.6 %collective-permute-start.25 = (bf16[288,128]{1,0:T(8,128)(2,1)S(1)}, bf16[288,128]{1,0:T(8,128)(2,1)S(1)}, u32[]{:S(2)}, u32[]{:S(2)}) collective-permute-start(bf16[288,128]{1,0:T(8,128)(2,1)S(1)} %fusion.8.refs_0_), channel_id=1, source_target_pairs={{0,8},{8,0},{16,24},{24,16},{1,9},{9,1},{17,25},{25,17},{2,10},{10... | collective-permute-start | bytes 221192 | tf_op jit(solution)/shard_map/ppermute | solution.py:847
  204.0 2.6 %assemble.1 = (f32[64,512]{1,0:T(8,128)}, f32[64,512]{1,0:T(8,128)}, f32[64,512]{1,0:T(8,128)}, f32[64,512]{1,0:T(8,128)}, f32[1,64]{1,0:T(1,128)}, /*index=5*/f...) custom-call(f32[8,128]{1,0:T(8,128)} %get-tuple-element.77.count_ref, ...), custom_call_target="tpu_custom_call" | custom-call | flops 1000 | bytes 1000 | tf_op jit(solution)/shard_map/assemble/pallas_call | solution.py:979
  (110 shorter events, 26.6 us)
Async XLA Ops:
  2.7 5.9 %collective-permute-start = (bf16[1,144,256]{2,1,0:T(8,128)(2,1)}, bf16[1,144,256]{2,1,0:T(8,128)(2,1)S(1)}, u32[]{:S(2)}, u32[]{:S(2)}) collective-permute-start(bf16[1,144,256]{2,1,0:T(8,128)(2,1)} %bitcast.105), channel_id=1, source_target_pairs={{0,2},{1,3},{2,0},{3,1},{4,6},{5,7},{6,4},{7,5},{8,10},{9,11},{10,... | collective-permute-start | bytes 221192 | tf_op jit(solution)/shard_map/ppermute | solution.py:847
  2.9 7.8 %collective-permute-start.4 = (bf16[1,144,256]{2,1,0:T(8,128)(2,1)}, bf16[1,144,256]{2,1,0:T(8,128)(2,1)S(1)}, u32[]{:S(2)}, u32[]{:S(2)}) collective-permute-start(bf16[1,144,256]{2,1,0:T(8,128)(2,1)} %bitcast.106), channel_id=1, source_target_pairs={{0,6},{1,7},{2,4},{3,5},{4,2},{5,3},{6,0},{7,1},{8,14},{9,15},{10,... | collective-permute-start | bytes 221192 | tf_op jit(solution)/shard_map/ppermute | solution.py:847
  5.3 12.3 %collective-permute-start.3 = (bf16[1,144,256]{2,1,0:T(8,128)(2,1)}, bf16[1,144,256]{2,1,0:T(8,128)(2,1)S(1)}, u32[]{:S(2)}, u32[]{:S(2)}) collective-permute-start(bf16[1,144,256]{2,1,0:T(8,128)(2,1)} %bitcast.107), channel_id=1, source_target_pairs={{0,4},{1,5},{2,6},{3,7},{4,0},{5,1},{6,2},{7,3},{8,12},{9,13},{10,... | collective-permute-start | bytes 221192 | tf_op jit(solution)/shard_map/ppermute | solution.py:847
  6.3 20.3 %collective-permute-start.9 = (bf16[1,288,256]{2,1,0:T(8,128)(2,1)}, bf16[1,288,256]{2,1,0:T(8,128)(2,1)S(1)}, u32[]{:S(2)}, u32[]{:S(2)}) collective-permute-start(bf16[1,288,256]{2,1,0:T(8,128)(2,1)} %bitcast.99), channel_id=1, source_target_pairs={{0,6},{1,7},{2,4},{3,5},{4,2},{5,3},{6,0},{7,1},{8,14},{9,15},{10,... | collective-permute-start | bytes 442376 | tf_op jit(solution)/shard_map/ppermute | solution.py:847
  7.6 16.7 %collective-permute-start.8 = (bf16[1,288,256]{2,1,0:T(8,128)(2,1)}, bf16[1,288,256]{2,1,0:T(8,128)(2,1)S(1)}, u32[]{:S(2)}, u32[]{:S(2)}) collective-permute-start(bf16[1,288,256]{2,1,0:T(8,128)(2,1)} %bitcast.100), channel_id=1, source_target_pairs={{0,4},{1,5},{2,6},{3,7},{4,0},{5,1},{6,2},{7,3},{8,12},{9,13},{10,... | collective-permute-start | bytes 442376 | tf_op jit(solution)/shard_map/ppermute | solution.py:847
  9.5 9.4 %collective-permute-start.1 = (bf16[2,144,256]{2,1,0:T(8,128)(2,1)S(1)}, bf16[2,144,256]{2,1,0:T(8,128)(2,1)S(1)}, u32[]{:S(2)}, u32[]{:S(2)}) collective-permute-start(bf16[2,144,256]{2,1,0:T(8,128)(2,1)S(1)} %pad_maximum_fusion.4), channel_id=1, source_target_pairs={{0,1},{1,0},{2,3},{3,2},{4,5},{5,4},{6,7},{7,6},{8,9},{9,8},{10,11... | collective-permute-start | bytes 442376 | tf_op jit(solution)/shard_map/ppermute | solution.py:847
  10.7 14.1 %collective-permute-start.7 = (bf16[1,288,256]{2,1,0:T(8,128)(2,1)}, bf16[1,288,256]{2,1,0:T(8,128)(2,1)S(1)}, u32[]{:S(2)}, u32[]{:S(2)}) collective-permute-start(bf16[1,288,256]{2,1,0:T(8,128)(2,1)} %bitcast.101), channel_id=1, source_target_pairs={{0,2},{1,3},{2,0},{3,1},{4,6},{5,7},{6,4},{7,5},{8,10},{9,11},{10,... | collective-permute-start | bytes 442376 | tf_op jit(solution)/shard_map/ppermute | solution.py:847
  17.7 10.2 %collective-permute-start.5 = (bf16[2,144,256]{2,1,0:T(8,128)(2,1)S(1)}, bf16[2,144,256]{2,1,0:T(8,128)(2,1)S(1)}, u32[]{:S(2)}, u32[]{:S(2)}) collective-permute-start(bf16[2,144,256]{2,1,0:T(8,128)(2,1)S(1)} %pad_maximum_fusion.5), channel_id=1, source_target_pairs={{0,16},{8,24},{16,0},{24,8},{1,17},{9,25},{17,1},{25,9},{2,18},{10... | collective-permute-start | bytes 442376 | tf_op jit(solution)/shard_map/ppermute | solution.py:847
  19.9 8.5 %collective-permute-start.2 = (bf16[4,144,256]{2,1,0:T(8,128)(2,1)S(1)}, bf16[4,144,256]{2,1,0:T(8,128)(2,1)S(1)}, u32[]{:S(2)}, u32[]{:S(2)}) collective-permute-start(bf16[4,144,256]{2,1,0:T(8,128)(2,1)S(1)} %pad_maximum_fusion.1), channel_id=1, source_target_pairs={{0,16},{8,24},{16,0},{24,8},{1,17},{9,25},{17,1},{25,9},{2,18},{10... | collective-permute-start | bytes 884744 | tf_op jit(solution)/shard_map/ppermute | solution.py:847
  27.9 7.3 %collective-permute-start.6 = (bf16[4,144,256]{2,1,0:T(8,128)(2,1)S(1)}, bf16[4,144,256]{2,1,0:T(8,128)(2,1)S(1)}, u32[]{:S(2)}, u32[]{:S(2)}) collective-permute-start(bf16[4,144,256]{2,1,0:T(8,128)(2,1)S(1)} %pad_maximum_fusion.2), channel_id=1, source_target_pairs={{0,1},{1,0},{2,3},{3,2},{4,5},{5,4},{6,7},{7,6},{8,9},{9,8},{10,11... | collective-permute-start | bytes 884744 | tf_op jit(solution)/shard_map/ppermute | solution.py:847
  35.3 5.1 %collective-permute-start.10 = (bf16[16,144,256]{2,1,0:T(8,128)(2,1)S(1)}, bf16[16,144,256]{2,1,0:T(8,128)(2,1)S(1)}, u32[]{:S(2)}, u32[]{:S(2)}) collective-permute-start(bf16[16,144,256]{2,1,0:T(8,128)(2,1)S(1)} %add_dynamic-update-slice_fusion.refs_3_), channel_id=1, source_target_pairs={{0,8},{8,0},{16,24},{24,16},{1,9},{9,1},{17,25},{25,17},{2,10},{10... | collective-permute-start | bytes 3538952 | tf_op jit(solution)/shard_map/ppermute | solution.py:847
  37.5 16.3 %collective-permute-start.11 = (bf16[2,288,256]{2,1,0:T(8,128)(2,1)S(1)}, bf16[2,288,256]{2,1,0:T(8,128)(2,1)S(1)}, u32[]{:S(2)}, u32[]{:S(2)}) collective-permute-start(bf16[2,288,256]{2,1,0:T(8,128)(2,1)S(1)} %pad_maximum_fusion.3.refs_5_), channel_id=1, source_target_pairs={{0,1},{1,0},{2,3},{3,2},{4,5},{5,4},{6,7},{7,6},{8,9},{9,8},{10,11... | collective-permute-start | bytes 884744 | tf_op jit(solution)/shard_map/ppermute | solution.py:847
  39.2 14.7 %collective-permute-start.12 = (bf16[2,288,256]{2,1,0:T(8,128)(2,1)S(1)}, bf16[2,288,256]{2,1,0:T(8,128)(2,1)S(1)}, u32[]{:S(2)}, u32[]{:S(2)}) collective-permute-start(bf16[2,288,256]{2,1,0:T(8,128)(2,1)S(1)} %get-tuple-element.137.refs_6_), channel_id=1, source_target_pairs={{0,16},{8,24},{16,0},{24,8},{1,17},{9,25},{17,1},{25,9},{2,18},{10... | collective-permute-start | bytes 884744 | tf_op jit(solution)/shard_map/ppermute | solution.py:847
  54.0 14.5 %collective-permute-start.13 = (bf16[4,288,256]{2,1,0:T(8,128)(2,1)S(1)}, bf16[4,288,256]{2,1,0:T(8,128)(2,1)}, u32[]{:S(2)}, u32[]{:S(2)}) collective-permute-start(bf16[4,288,256]{2,1,0:T(8,128)(2,1)S(1)} %pad_maximum_fusion.refs_5_), channel_id=1, source_target_pairs={{0,16},{8,24},{16,0},{24,8},{1,17},{9,25},{17,1},{25,9},{2,18},{10... | collective-permute-start | bytes 1769480 | tf_op jit(solution)/shard_map/ppermute | solution.py:847
  55.5 14.5 %collective-permute-start.14 = (bf16[4,288,256]{2,1,0:T(8,128)(2,1)}, bf16[4,288,256]{2,1,0:T(8,128)(2,1)}, u32[]{:S(2)}, u32[]{:S(2)}) collective-permute-start(bf16[4,288,256]{2,1,0:T(8,128)(2,1)} %constant_dynamic-update-slice_fusion.9.refs_6_), channel_id=1, source_target_pairs={{0,1},{1,0},{2,3},{3,2},{4,5},{5,4},{6,7},{7,6},{8,9},{9,8},{10,11... | collective-permute-start | bytes 1769480 | tf_op jit(solution)/shard_map/ppermute | solution.py:847
  72.4 5.7 %collective-permute-start.15 = (bf16[16,288,256]{2,1,0:T(8,128)(2,1)S(1)}, bf16[16,288,256]{2,1,0:T(8,128)(2,1)S(1)}, u32[]{:S(2)}, u32[]{:S(2)}) collective-permute-start(bf16[16,288,256]{2,1,0:T(8,128)(2,1)S(1)} %constant_dynamic-update-slice_fusion.12.mine_ref), channel_id=1, source_target_pairs={{0,8},{8,0},{16,24},{24,16},{1,9},{9,1},{17,25},{25,17},{2,10},{10... | collective-permute-start | bytes 7077896 | tf_op jit(solution)/shard_map/ppermute | solution.py:847
  105.3 5.2 %collective-permute-start.16 = (bf16[4,8,160,256]{3,2,1,0:T(8,128)(2,1)}, bf16[4,8,160,256]{3,2,1,0:T(8,128)(2,1)S(1)}, u32[]{:S(2)}, u32[]{:S(2)}) collective-permute-start(bf16[4,8,160,256]{3,2,1,0:T(8,128)(2,1)} %get-tuple-element.102), channel_id=1, source_target_pairs={{0,8},{8,0},{16,24},{24,16},{1,9},{9,1},{17,25},{25,17},{2,10},{10... | collective-permute-start | bytes 7864328 | tf_op jit(solution)/shard_map/ppermute | solution.py:847
  114.7 68.4 %all-to-all-start = ((bf16[32,160,256]{2,1,0:T(8,128)(2,1)}), bf16[32,160,256]{2,1,0:T(8,128)(2,1)S(1)}, u32[]{:S(2)}, u32[]{:S(2)}) async-start(bf16[32,160,256]{2,1,0:T(8,128)(2,1)} %bitcast.12.refs_25_), calls=%async_computation | async-start | bytes 5242880 | tf_op jit(solution)/shard_map/all_to_all | solution.py:1130
  149.8 3.1 %collective-permute-start.17 = (bf16[2,2,2,4,144,128]{5,4,3,2,1,0:T(8,128)(2,1)}, bf16[2,2,2,4,144,128]{5,4,3,2,1,0:T(8,128)(2,1)S(1)}, u32[]{:S(2)}, u32[]{:S(2)}) collective-permute-start(bf16[2,2,2,4,144,128]{5,4,3,2,1,0:T(8,128)(2,1)} %get-tuple-element.105), channel_id=1, source_target_pairs={{0,8},{8,0},{16,24},{24,16},{1,9},{9,1},{17,25},{25,17},{2,10},{10... | collective-permute-start | bytes 3538952 | tf_op jit(solution)/shard_map/ppermute | solution.py:847
  154.5 12.9 %collective-permute-start.20 = (bf16[2,4,144,128]{3,2,1,0:T(8,128)(2,1)S(1)}, bf16[2,4,144,128]{3,2,1,0:T(8,128)(2,1)S(1)}, u32[]{:S(2)}, u32[]{:S(2)}) collective-permute-start(bf16[2,4,144,128]{3,2,1,0:T(8,128)(2,1)S(1)} %get-tuple-element.121), channel_id=1, source_target_pairs={{0,16},{8,24},{16,0},{24,8},{1,17},{9,25},{17,1},{25,9},{2,18},{10... | collective-permute-start | bytes 884744 | tf_op jit(solution)/shard_map/ppermute | solution.py:847
  155.7 16.1 %collective-permute-start.18 = (bf16[2,4,144,128]{3,2,1,0:T(8,128)(2,1)S(1)}, bf16[2,4,144,128]{3,2,1,0:T(8,128)(2,1)S(1)}, u32[]{:S(2)}, u32[]{:S(2)}) collective-permute-start(bf16[2,4,144,128]{3,2,1,0:T(8,128)(2,1)S(1)} %get-tuple-element.123), channel_id=1, source_target_pairs={{0,1},{1,0},{2,3},{3,2},{4,5},{5,4},{6,7},{7,6},{8,9},{9,8},{10,11... | collective-permute-start | bytes 884744 | tf_op jit(solution)/shard_map/ppermute | solution.py:847
  167.5 10.3 %collective-permute-start.21 = (bf16[4,144,128]{2,1,0:T(8,128)(2,1)S(1)}, bf16[4,144,128]{2,1,0:T(8,128)(2,1)S(1)}, u32[]{:S(2)}, u32[]{:S(2)}) collective-permute-start(bf16[4,144,128]{2,1,0:T(8,128)(2,1)S(1)} %get-tuple-element.127), channel_id=1, source_target_pairs={{0,1},{1,0},{2,3},{3,2},{4,5},{5,4},{6,7},{7,6},{8,9},{9,8},{10,11... | collective-permute-start | bytes 442376 | tf_op jit(solution)/shard_map/ppermute | solution.py:847
  171.9 6.7 %collective-permute-start.19 = (bf16[4,144,128]{2,1,0:T(8,128)(2,1)S(1)}, bf16[4,144,128]{2,1,0:T(8,128)(2,1)S(1)}, u32[]{:S(2)}, u32[]{:S(2)}) collective-permute-start(bf16[4,144,128]{2,1,0:T(8,128)(2,1)S(1)} %get-tuple-element.125), channel_id=1, source_target_pairs={{0,16},{8,24},{16,0},{24,8},{1,17},{9,25},{17,1},{25,9},{2,18},{10... | collective-permute-start | bytes 442376 | tf_op jit(solution)/shard_map/ppermute | solution.py:847
  178.7 13.0 %collective-permute-start.22 = (bf16[1,288,128]{2,1,0:T(8,128)(2,1)S(1)}, bf16[1,288,128]{2,1,0:T(8,128)(2,1)S(1)}, u32[]{:S(2)}, u32[]{:S(2)}) collective-permute-start(bf16[1,288,128]{2,1,0:T(8,128)(2,1)S(1)} %pad_maximum_fusion.7), channel_id=1, source_target_pairs={{0,2},{1,3},{2,0},{3,1},{4,6},{5,7},{6,4},{7,5},{8,10},{9,11},{10,... | collective-permute-start | bytes 221192 | tf_op jit(solution)/shard_map/ppermute | solution.py:847
  178.8 13.0 %collective-permute-start.23 = (bf16[1,288,128]{2,1,0:T(8,128)(2,1)S(1)}, bf16[1,288,128]{2,1,0:T(8,128)(2,1)S(1)}, u32[]{:S(2)}, u32[]{:S(2)}) collective-permute-start(bf16[1,288,128]{2,1,0:T(8,128)(2,1)S(1)} %pad_maximum_fusion.8), channel_id=1, source_target_pairs={{0,4},{1,5},{2,6},{3,7},{4,0},{5,1},{6,2},{7,3},{8,12},{9,13},{10,... | collective-permute-start | bytes 221192 | tf_op jit(solution)/shard_map/ppermute | solution.py:847
  182.5 9.3 %collective-permute-start.24 = (bf16[1,288,128]{2,1,0:T(8,128)(2,1)S(1)}, bf16[1,288,128]{2,1,0:T(8,128)(2,1)S(1)}, u32[]{:S(2)}, u32[]{:S(2)}) collective-permute-start(bf16[1,288,128]{2,1,0:T(8,128)(2,1)S(1)} %pad_maximum_fusion.9), channel_id=1, source_target_pairs={{0,6},{1,7},{2,4},{3,5},{4,2},{5,3},{6,0},{7,1},{8,14},{9,15},{10,... | collective-permute-start | bytes 221192 | tf_op jit(solution)/shard_map/ppermute | solution.py:847
  187.3 15.3 %collective-permute-start.30 = (bf16[2,160,256]{2,1,0:T(8,128)(2,1)}, bf16[2,160,256]{2,1,0:T(8,128)(2,1)S(1)}, u32[]{:S(2)}, u32[]{:S(2)}) collective-permute-start(bf16[2,160,256]{2,1,0:T(8,128)(2,1)} %add_arrived.1.refs_4_), channel_id=1, source_target_pairs={{0,24},{8,16},{16,8},{24,0},{1,25},{9,17},{17,9},{25,1},{2,26},{10... | collective-permute-start | bytes 491528 | tf_op jit(solution)/shard_map/ppermute | solution.py:847
  190.2 12.5 %collective-permute-start.29 = (bf16[2,160,256]{2,1,0:T(8,128)(2,1)}, bf16[2,160,256]{2,1,0:T(8,128)(2,1)S(1)}, u32[]{:S(2)}, u32[]{:S(2)}) collective-permute-start(bf16[2,160,256]{2,1,0:T(8,128)(2,1)} %add_arrived.1.refs_4_), channel_id=1, source_target_pairs={{0,16},{8,24},{16,0},{24,8},{1,17},{9,25},{17,1},{25,9},{2,18},{10... | collective-permute-start | bytes 491528 | tf_op jit(solution)/shard_map/ppermute | solution.py:847
  191.7 10.9 %collective-permute-start.28 = (bf16[2,160,256]{2,1,0:T(8,128)(2,1)}, bf16[2,160,256]{2,1,0:T(8,128)(2,1)S(1)}, u32[]{:S(2)}, u32[]{:S(2)}) collective-permute-start(bf16[2,160,256]{2,1,0:T(8,128)(2,1)} %add_arrived.1.refs_4_), channel_id=1, source_target_pairs={{0,8},{8,0},{16,24},{24,16},{1,9},{9,1},{17,25},{25,17},{2,10},{10... | collective-permute-start | bytes 491528 | tf_op jit(solution)/shard_map/ppermute | solution.py:847
  191.8 7.3 %collective-permute-start.27 = (bf16[288,128]{1,0:T(8,128)(2,1)S(1)}, bf16[288,128]{1,0:T(8,128)(2,1)S(1)}, u32[]{:S(2)}, u32[]{:S(2)}) collective-permute-start(bf16[288,128]{1,0:T(8,128)(2,1)S(1)} %fusion.8.refs_0_), channel_id=1, source_target_pairs={{0,24},{8,16},{16,8},{24,0},{1,25},{9,17},{17,9},{25,1},{2,26},{10... | collective-permute-start | bytes 221192 | tf_op jit(solution)/shard_map/ppermute | solution.py:847
  192.3 9.5 %collective-permute-start.26 = (bf16[288,128]{1,0:T(8,128)(2,1)S(1)}, bf16[288,128]{1,0:T(8,128)(2,1)S(1)}, u32[]{:S(2)}, u32[]{:S(2)}) collective-permute-start(bf16[288,128]{1,0:T(8,128)(2,1)S(1)} %fusion.8.refs_0_), channel_id=1, source_target_pairs={{0,16},{8,24},{16,0},{24,8},{1,17},{9,25},{17,1},{25,9},{2,18},{10... | collective-permute-start | bytes 221192 | tf_op jit(solution)/shard_map/ppermute | solution.py:847
  199.1 3.5 %collective-permute-start.25 = (bf16[288,128]{1,0:T(8,128)(2,1)S(1)}, bf16[288,128]{1,0:T(8,128)(2,1)S(1)}, u32[]{:S(2)}, u32[]{:S(2)}) collective-permute-start(bf16[288,128]{1,0:T(8,128)(2,1)S(1)} %fusion.8.refs_0_), channel_id=1, source_target_pairs={{0,8},{8,0},{16,24},{24,16},{1,9},{9,1},{17,25},{25,17},{2,10},{10... | collective-permute-start | bytes 221192 | tf_op jit(solution)/shard_map/ppermute | solution.py:847
  (16 other events, 75.6 us)

commit v6 on v5

--- a/solution.py
+++ b/solution.py
@@ -36,6 +36,11 @@
     first = [(z, y, x) for x in (0, 1) for y in (0, 1) for z in low]
     second = [(z, y, x) for y in (0, 1) for x in (0, 1) for z in high]
     return first + second
+
+
+def block_of(pieces, slot):
+    each = pieces[0].shape[0]
+    return pieces[slot // each].at[slot % each]
 
 
 def nn(left, right):
@@ -185,10 +190,10 @@
     r = 512 // shards
     at = slice(quad * QUAD, (quad + 1) * QUAD)
     if quad == 0:
-        mine_ref, theirs_ref = refs[:2]
-        q_ref, k_ref, v_ref, e_ref, p_ref, s_ref, rz_ref, mix_ref, one_ref, two_ref = refs[2:12]
-        w_ref, vec_ref, eb_ref, count_ref = refs[12:16]
-        held, first_state, second_state, total_state, sems = refs[16:]
+        pieces, refs = (refs[:4], refs[4:8]), refs[8:]
+        q_ref, k_ref, v_ref, e_ref, p_ref, s_ref, rz_ref, mix_ref, one_ref, two_ref = refs[:10]
+        w_ref, vec_ref, eb_ref, count_ref = refs[10:14]
+        held, first_state, second_state, total_state, sems = refs[14:]
         weight = lambda m: w_ref[m, :, at]
     else:
         w_ref, vec_ref = refs[:2]
@@ -204,14 +209,14 @@
 
     def assemble():
         me, core, cross = place()
-        for half, source in enumerate((mine_ref, theirs_ref)):
+        for half, source in enumerate(pieces):
             column = pl.multiple_of(((core + half) % 2) * 256, 256)
             for slot, (z, y, x) in enumerate(slots_of(shards)):
                 owner = me ^ (2 * z + y)
                 third = cross ^ x
                 for m in range(2):
                     pltpu.make_async_copy(
-                        source.at[slot, pl.ds(m * r, r)],
+                        block_of(source, slot).at[pl.ds(m * r, r)],
                         w_ref.at[
                             2 * third + m,
                             pl.ds(pl.multiple_of(owner * r, r), r),
@@ -220,7 +225,7 @@
                         sems.at[0],
                     ).start()
                 pltpu.make_async_copy(
-                    source.at[slot, pl.ds(2 * r, 16)], held.at[2 * half + x, owner], sems.at[1]
+                    block_of(source, slot).at[pl.ds(2 * r, 16)], held.at[2 * half + x, owner], sems.at[1]
                 ).start()
         pltpu.make_async_copy(held, held, sems.at[1]).wait()
         own = [held[0, s].astype(F32) for s in range(shards)]
@@ -321,35 +326,12 @@
     vec_ref,
     eb_ref,
     count_ref,
-    mine_ref,
-    theirs_ref,
-    out_ref,
-    hidden_ref,
-    grad_mix_ref,
-    keep_out_ref,
-    send_out_ref,
-    x,
-    mix,
-    teacher,
-    wo,
-    we,
-    wc,
-    act,
-    out,
-    hidden_grad,
-    grad_mix,
-    keep_ref,
-    send_ref,
-    normed,
-    low,
-    d_normed,
-    d_wo,
-    d_we,
-    d_wc,
-    d_vec,
-    d_eb,
-    sems,
+    *refs,
 ):
+    pieces, refs = (refs[:4], refs[4:8]), refs[8:]
+    out_ref, hidden_ref, grad_mix_ref, keep_out_ref, send_out_ref = refs[:5]
+    x, mix, teacher, wo, we, wc, act, out, hidden_grad, grad_mix = refs[5:15]
+    keep_ref, send_ref, normed, low, d_normed, d_wo, d_we, d_wc, d_vec, d_eb, sems = refs[15:]
     r = 512 // shards
     me, core, cross = place()
     copies = [
@@ -358,14 +340,14 @@
         pltpu.make_async_copy(x_ref, x, sems.at[2]),
         pltpu.make_async_copy(teacher_ref, teacher, sems.at[3]),
     ]
-    sources = list(enumerate((mine_ref, theirs_ref)))
+    sources = list(enumerate(pieces))
     columns = [pl.multiple_of(((core + half) % 2) * 256, 256) for half, _ in sources]
     for copy in copies[:2]:
         copy.start()
     for half, source in sources:
         for slot, (z, y, cross_slot) in enumerate(slots_of(shards)):
             pltpu.make_async_copy(
-                source.at[slot, pl.ds(4 * r, r // 2)],
+                block_of(source, slot).at[pl.ds(4 * r, r // 2)],
                 wo.at[2 * (me ^ (2 * z + y)) + (cross ^ cross_slot), :, pl.ds(columns[half], 256)],
                 sems.at[4],
             ).start()
@@ -377,7 +359,7 @@
             def expansion():
                 for b in range(4):
                     pltpu.make_async_copy(
-                        source.at[slot, pl.ds(b * r, r)],
+                        block_of(source, slot).at[pl.ds(b * r, r)],
                         we.at[
                             b, pl.ds(pl.multiple_of(owner * r, r), r), pl.ds(columns[half], 256)
                         ],
@@ -386,7 +368,7 @@
 
             def contraction():
                 pltpu.make_async_copy(
-                    source.at[slot, pl.ds(0, 4 * r)],
+                    block_of(source, slot).at[pl.ds(0, 4 * r)],
                     wc.at[
                         pl.ds(pl.multiple_of(owner * 4 * r, 4 * r), 4 * r),
                         pl.ds(columns[half], 256),
@@ -714,7 +696,7 @@
     low = shaped((length, QUAD), BF16)
     states = shaped((length // SUB, QUAD, QUAD), BF16)
     if quad == 0:
-        in_specs = [anywhere(), anywhere()]
+        in_specs = [anywhere()] * 8
         out_specs = [whole((4, 512, 512)), whole((8, 512)), whole((8, 2048)), whole((8, 128))]
         out_shape = [shaped((4, 512, 512), BF16), shaped((8, 512), F32)]
         out_shape += [shaped((8, 2048), F32), shaped((8, 128), F32)]
@@ -761,7 +743,7 @@
     wide = (length, 512)
     return pl.pallas_call(
         functools.partial(feed_forward, shards, tokens),
-        in_specs=[anywhere()] * 4 + [vmem] * 4 + [anywhere()] * 2,
+        in_specs=[anywhere()] * 4 + [vmem] * 4 + [anywhere()] * 8,
         out_specs=[anywhere()] * 5,
         out_shape=[
             shaped(wide, BF16),
@@ -1047,17 +1029,18 @@
         return swap(first, "rep", 2), swap(second, "shard", 1)
 
     first, second = halves(along_z(mixer))
+    held_b = along_z(branch + zero_of([second]))
     first, second = join(first, second, step_one(first, second))
     arrived = step_two(first, second)
-    held_b = along_z(branch)
     first_b, second_b = halves(held_b)
     pending = step_one(first_b, second_b)
-    mine_a = jnp.concatenate([first, arrived[0], second, arrived[1] + zero_of(held_b[1:])])
-    theirs_a = swap(mine_a, "rep", 1)
+    last = arrived[1] + zero_of(held_b[1:])
+    mine_a = (first, arrived[0], second, last)
+    theirs_a = tuple(swap(part, "rep", 1) for part in mine_a)
 
     x = inputs.reshape(length, width)
     forward_0 = call_forward(
-        0, shards, segments, x, (mine_a, theirs_a), (first_b, second_b)
+        0, shards, segments, x, (*mine_a, *theirs_a), (first_b, second_b)
     )
     weights, vectors, bias, count = forward_0[10:]
     bit = 4
@@ -1067,10 +1050,13 @@
     pending = after(pending, forward_0[7])
     first_b, second_b = join(first_b, second_b, pending)
     pending = step_two(first_b, second_b)
-    forward_1 = call_forward(1, shards, segments, x, (weights, vectors), (first_b, second_b))
+    near_b = swap(first_b, "rep", 1), swap(second_b, "rep", 1)
+    forward_1 = call_forward(
+        1, shards, segments, x, (weights, vectors), (first_b, second_b, *near_b)
+    )
     pending = after(pending, forward_1[7])
-    mine_b = jnp.concatenate([first_b, pending[0], second_b, pending[1]])
-    theirs_b = swap(mine_b, "rep", 1)
+    mine_b = (first_b, pending[0], second_b, pending[1])
+    theirs_b = (near_b[0], swap(pending[0], "rep", 1), near_b[1], swap(pending[1], "rep", 1))
     mixed = (forward_0[7], forward_1[7])
 
     layer_out, grad_hidden, grad_mix, keep_f, send_f = call_feed_forward(
@@ -1084,8 +1070,8 @@
         vectors,
         bias,
         count,
-        mine_b,
-        theirs_b,
+        *mine_b,
+        *theirs_b,
     )
 
     def split(parts):

time: 208 us -> 200 us (0.962)
  waiting for transfers between devices: 60.7 us -> 50.2 us
  starting transfers between devices: 37 us -> 42.9 us
  local copies, waits for them, and re-layouts: 12.3 us -> 7.53 us
    ppermute x31 -> x37, waiting for transfers between devices: 60.7 us -> 50.2 us  [swap(): return lax.ppermute(value, axis, [(i, i ^ bit) for i in range(n)])]
    ppermute x31 -> x37, starting transfers between devices: 30.7 us -> 37.2 us  [swap(): return lax.ppermute(value, axis, [(i, i ^ bit) for i in range(n)])]
    unnamed x48 -> x56, local copies, waits for them, and re-layouts: 8.89 us -> 5.45 us
  transfers between devices with their start and end apart: 32 -> 38, of which waited for: 16 -> 19; matrix products, arithmetic and copies ran while one was open for 4% -> 4% of each run, Pallas kernels for 26% -> 27%
where the time goes in v6:
time: 200 us; the launch traced here: 199 us
  Pallas kernels  85 us (42%)
  waiting for transfers between devices  50.2 us (25%)
  starting transfers between devices  42.9 us (21%)
  other arithmetic  9.56 us (5%)
  local copies, waits for them, and re-layouts  7.53 us (4%)
  between operations  3.91 us (2%)
    ppermute x37, waiting for transfers between devices, swap(): return lax.ppermute(value, axis, [(i, i ^ bit) for i in range(n)])  50.2 us
    ppermute x37, starting transfers between devices, swap(): return lax.ppermute(value, axis, [(i, i ^ bit) for i in range(n)])  37.2 us
    pallas_call x1, Pallas kernels, call_backward(): pl.pallas_call(functools.partial(ordered, functools.partial(attention_bac...  28.8 us
    pallas_call x1, Pallas kernels, call_feed_forward(): pl.pallas_call(functools.partial(feed_forward, shards, tokens), in_specs=...  25.7 us
    pallas_call x2, Pallas kernels, call_forward(): pl.pallas_call(functools.partial(ordered, functools.partial(attention_for...  23.1 us
    convert_element_type x6, other arithmetic, add_low(): return sum((part.astype(F32) for part in parts)).astype(BF16)  5.99 us
    all_to_all x1, starting transfers between devices, local(): lax.all_to_all(every, ('rep', 'shard'), 0, 0).reshape(summed.shape)  5.64 us
    unnamed x56, local copies, waits for them, and re-layouts  5.45 us
  transfers between devices with their start and end apart: 38, of which 19 were waited for; matrix products, arithmetic and copies ran while one was open for 4% of the time, Pallas kernels for 27%

profile of v6, /device:TPU:13, one launch (start us, length us, event | category | flops | bytes accessed | tf_op | source)
XLA Modules:
  0.0 199.0 jit_solution(5360978503066175873)
XLA Ops:
  0.7 2.0 %pack.1 = (bf16[144,256]{1,0:T(8,128)(2,1)}, bf16[288,256]{1,0:T(8,128)(2,1)}) custom-call(bf16[64,512]{1,0:T(8,128)(2,1)} %refs_0_.4, bf16[64,512]{1,0:T(8,128)(2,1)} %refs_1_.1, bf16[64,512]{1,0:T(8,128)(2,1)} %refs_2_.4, bf16[64,512]{1,0:T(8,128)(2,1)} %refs_3_.1, bf16[64,512]{1,0:T(8,128)(2,1)} %refs_4_.1, bf16[64,2048]{1,0:T(8,128)(2,1)} %refs_5_.1, ...), custom_call_target="tpu_custom_call" | custom-call | flops 1000 | bytes 1000 | tf_op jit(solution)/shard_map/pack/pallas_call | solution.py:678
  2.7 2.3 %collective-permute-start.3 = (bf16[1,144,256]{2,1,0:T(8,128)(2,1)}, bf16[1,144,256]{2,1,0:T(8,128)(2,1)S(1)}, u32[]{:S(2)}, u32[]{:S(2)}) collective-permute-start(bf16[1,144,256]{2,1,0:T(8,128)(2,1)} %bitcast.100), channel_id=1, source_target_pairs={{0,4},{1,5},{2,6},{3,7},{4,0},{5,1},{6,2},{7,3},{8,12},{9,13},{10,... | collective-permute-start | bytes 221192 | tf_op jit(solution)/shard_map/ppermute | solution.py:829
  6.2 3.6 %collective-permute-done.3 = bf16[1,144,256]{2,1,0:T(8,128)(2,1)S(1)} collective-permute-done((bf16[1,144,256]{2,1,0:T(8,128)(2,1)}, bf16[1,144,256]{2,1,0:T(8,128)(2,1)S(1)}, u32[]{:S(2)}, u32[]{:S(2)}) %collective-permute-start.3) | collective-permute-done | bytes 73760 | tf_op jit(solution)/shard_map/ppermute | solution.py:829
  12.1 3.4 %collective-permute-start.8 = (bf16[1,288,256]{2,1,0:T(8,128)(2,1)S(1)}, bf16[1,288,256]{2,1,0:T(8,128)(2,1)S(1)}, u32[]{:S(2)}, u32[]{:S(2)}) collective-permute-start(bf16[1,288,256]{2,1,0:T(8,128)(2,1)S(1)} %add_bitcast_fusion), channel_id=1, source_target_pairs={{0,4},{1,5},{2,6},{3,7},{4,0},{5,1},{6,2},{7,3},{8,12},{9,13},{10,... | collective-permute-start | bytes 442376 | tf_op jit(solution)/shard_map/ppermute | solution.py:829
  19.1 1.9 collective-permute-done.5
  20.9 2.5 %collective-permute-start.12 = (bf16[4,144,256]{2,1,0:T(8,128)(2,1)S(1)}, bf16[4,144,256]{2,1,0:T(8,128)(2,1)S(1)}, u32[]{:S(2)}, u32[]{:S(2)}) collective-permute-start(bf16[4,144,256]{2,1,0:T(8,128)(2,1)S(1)} %constant_dynamic-update-slice_fusion.refs_5_), channel_id=1, source_target_pairs={{0,8},{8,0},{16,24},{24,16},{1,9},{9,1},{17,25},{25,17},{2,10},{10... | collective-permute-start | bytes 884744 | tf_op jit(solution)/shard_map/ppermute | solution.py:829
  24.6 1.3 collective-permute-done.7
  25.8 1.9 collective-permute-start.10
  33.6 2.9 %collective-permute-done.2.refs_4_ = bf16[4,144,256]{2,1,0:T(8,128)(2,1)S(1)} collective-permute-done((bf16[4,144,256]{2,1,0:T(8,128)(2,1)S(1)}, bf16[4,144,256]{2,1,0:T(8,128)(2,1)S(1)}, u32[]{:S(2)}, u32[]{:S(2)}) %collective-permute-start.2) | collective-permute-done | bytes 294944 | tf_op jit(solution)/shard_map/ppermute | solution.py:829
  39.5 12.6 %attention_forward_0.1 = (bf16[1024,256]{1,0:T(8,128)(2,1)}, bf16[1024,256]{1,0:T(8,128)(2,1)}, bf16[1024,256]{1,0:T(8,128)(2,1)}, bf16[1024,256]{1,0:T(8,128)(2...) custom-call(s32[1,1024]{1,0:T(1,128)} %refs_2_.7, ...), custom_call_target="tpu_custom_call" | custom-call | flops 1000 | bytes 1000 | tf_op jit(solution)/shard_map/attention_forward_0/pallas_call | solution.py:722
  55.9 10.6 %attention_forward_1.1 = (bf16[1024,256]{1,0:T(8,128)(2,1)}, bf16[1024,256]{1,0:T(8,128)(2,1)}, bf16[1024,256]{1,0:T(8,128)(2,1)}, bf16[1024,256]{1,0:T(8,128)(2...) custom-call(s32[1,1024]{1,0:T(1,128)} %refs_2_.7, ...), custom_call_target="tpu_custom_call" | custom-call | flops 1000 | bytes 1000 | tf_op jit(solution)/shard_map/attention_forward_1/pallas_call | solution.py:722
  67.6 1.5 collective-permute-start.20
  69.2 1.6 collective-permute-done.20.refs_5_
  72.5 25.7 %feed_forward.1 = (bf16[1024,512]{1,0:T(8,128)(2,1)}, f32[1024,512]{1,0:T(8,128)}, bf16[1024,512]{1,0:T(8,128)(2,1)}, bf16[4,8,160,256]{3,2,1,0:T(8,128)(2,1)}, bf16[4,8,160,256]{3,2,1,0:T(8,128)(2,1)}) custom-call(bf16[1024,512]{1,0:T(8,128)(2,1)} %bitcast.96, bf16[1024,256]{1,0:T(8,128)(2,1)} %get-tuple-element.70.mix_0_ref, ...), custom_call_target="tpu_custom_call" | custom-call | flops 1000 | bytes 1000 | tf_op jit(solution)/shard_map/feed_forward/pallas_call | solution.py:744
  98.6 4.7 %collective-permute-done.22 = bf16[4,8,160,256]{3,2,1,0:T(8,128)(2,1)S(1)} collective-permute-done((bf16[4,8,160,256]{3,2,1,0:T(8,128)(2,1)}, bf16[4,8,160,256]{3,2,1,0:T(8,128)(2,1)S(1)}, u32[]{:S(2)}, u32[]{:S(2)}) %collective-permute-start.22) | collective-permute-done | bytes 2621472 | tf_op jit(solution)/shard_map/ppermute | solution.py:829
  103.3 4.2 %add_convert_fusion = bf16[4,8,160,256]{3,2,1,0:T(8,128)(2,1)} fusion(bf16[4,8,160,256]{3,2,1,0:T(8,128)(2,1)S(1)} %collective-permute-done.22, bf16[4,8,160,256]{3,2,1,0:T(8,128)(2,1)} %get-tuple-element.101), kind=kLoop, calls=%fused_computation | loop fusion | flops 5242880 | bytes 7864320 | tf_op jit(solution)/shard_map/convert_element_type | solution.py:973
  107.5 5.6 %all-to-all-start = ((bf16[32,160,256]{2,1,0:T(8,128)(2,1)}), bf16[32,160,256]{2,1,0:T(8,128)(2,1)S(1)}, u32[]{:S(2)}, u32[]{:S(2)}) async-start(bf16[32,160,256]{2,1,0:T(8,128)(2,1)} %bitcast.13.refs_25_), calls=%async_computation | async-start | bytes 5242880 | tf_op jit(solution)/shard_map/all_to_all | solution.py:1116
  113.2 28.8 %attention_backward.1 = (f32[1024,512]{1,0:T(8,128)}, bf16[2,2,2,4,144,128]{5,4,3,2,1,0:T(8,128)(2,1)}, bf16[2,2,2,4,144,128]{5,4,3,2,1,0:T(8,128)(2,1)}) custom-call(s32[1,1024]{1,0:T(1,128)} %refs_2_.7, bf16[1024,512]{1,0:T(8,128)(2,1)} %bitcast.97, s32[1,1024]{1,0:T(1,128)} %refs_2_.7, bf16[1024,256]{1,0:T(8,128)(2,1)} %get-tuple-element.81.refs_3_, ...), custom_call_target="tpu_custom_call" | custom-call | flops 1000 | bytes 1000 | tf_op jit(solution)/shard_map/attention_backward/pallas_call | solution.py:815
  142.4 2.7 %collective-permute-done.23 = bf16[2,2,2,4,144,128]{5,4,3,2,1,0:T(8,128)(2,1)S(1)} collective-permute-done((bf16[2,2,2,4,144,128]{5,4,3,2,1,0:T(8,128)(2,1)}, bf16[2,2,2,4,144,128]{5,4,3,2,1,0:T(8,128)(2,1)S(1)}, u32[]{:S(2)}, u32[]{:S(2)}) %collective-permute-start.23) | collective-permute-done | bytes 1179680 | tf_op jit(solution)/shard_map/ppermute | solution.py:829
  145.1 1.6 add_convert_fusion.4
  148.2 11.3 %collective-permute-done.26 = bf16[2,4,144,128]{3,2,1,0:T(8,128)(2,1)S(1)} collective-permute-done((bf16[2,4,144,128]{3,2,1,0:T(8,128)(2,1)S(1)}, bf16[2,4,144,128]{3,2,1,0:T(8,128)(2,1)S(1)}, u32[]{:S(2)}, u32[]{:S(2)}) %collective-permute-start.26) | collective-permute-done | bytes 294944 | tf_op jit(solution)/shard_map/ppermute | solution.py:829
  160.0 4.1 %collective-permute-done.24 = bf16[2,4,144,128]{3,2,1,0:T(8,128)(2,1)S(1)} collective-permute-done((bf16[2,4,144,128]{3,2,1,0:T(8,128)(2,1)S(1)}, bf16[2,4,144,128]{3,2,1,0:T(8,128)(2,1)S(1)}, u32[]{:S(2)}, u32[]{:S(2)}) %collective-permute-start.24) | collective-permute-done | bytes 294944 | tf_op jit(solution)/shard_map/ppermute | solution.py:829
  164.2 5.8 %collective-permute-done.27 = bf16[4,144,128]{2,1,0:T(8,128)(2,1)S(1)} collective-permute-done((bf16[4,144,128]{2,1,0:T(8,128)(2,1)S(1)}, bf16[4,144,128]{2,1,0:T(8,128)(2,1)S(1)}, u32[]{:S(2)}, u32[]{:S(2)}) %collective-permute-start.27) | collective-permute-done | bytes 147488 | tf_op jit(solution)/shard_map/ppermute | solution.py:829
  171.0 3.7 %collective-permute-start.29 = (bf16[1,288,128]{2,1,0:T(8,128)(2,1)S(1)}, bf16[1,288,128]{2,1,0:T(8,128)(2,1)S(1)}, u32[]{:S(2)}, u32[]{:S(2)}) collective-permute-start(bf16[1,288,128]{2,1,0:T(8,128)(2,1)S(1)} %pad_maximum_fusion.7), channel_id=1, source_target_pairs={{0,4},{1,5},{2,6},{3,7},{4,0},{5,1},{6,2},{7,3},{8,12},{9,13},{10,... | collective-permute-start | bytes 221192 | tf_op jit(solution)/shard_map/ppermute | solution.py:829
  175.4 1.5 copy-done
  176.9 2.7 %add_arrived.1.refs_4_ = bf16[2,160,256]{2,1,0:T(8,128)(2,1)} custom-call(bf16[4,8,160,256]{3,2,1,0:T(8,128)(2,1)} %bitcast.98, bf16[1,288,128]{2,1,0:T(8,128)(2,1)} %pad_maximum_fusion.5.refs_1_), custom_call_target="tpu_custom_call" | custom-call | flops 1000 | bytes 1000 | tf_op jit(solution)/shard_map/add_arrived/pallas_call | solution.py:865
  179.6 2.8 %collective-permute-start.36 = (bf16[2,160,256]{2,1,0:T(8,128)(2,1)}, bf16[2,160,256]{2,1,0:T(8,128)(2,1)S(1)}, u32[]{:S(2)}, u32[]{:S(2)}) collective-permute-start(bf16[2,160,256]{2,1,0:T(8,128)(2,1)} %add_arrived.1.refs_4_), channel_id=1, source_target_pairs={{0,24},{8,16},{16,8},{24,0},{1,25},{9,17},{17,9},{25,1},{2,26},{10... | collective-permute-start | bytes 491528 | tf_op jit(solution)/shard_map/ppermute | solution.py:829
  182.4 1.6 collective-permute-start.35
  184.5 1.5 collective-permute-start.32
  186.0 5.4 %collective-permute-done.33.refs_3_ = bf16[288,128]{1,0:T(8,128)(2,1)S(1)} collective-permute-done((bf16[288,128]{1,0:T(8,128)(2,1)S(1)}, bf16[288,128]{1,0:T(8,128)(2,1)S(1)}, u32[]{:S(2)}, u32[]{:S(2)}) %collective-permute-start.33) | collective-permute-done | bytes 73760 | tf_op jit(solution)/shard_map/ppermute | solution.py:829
  191.4 2.5 %collective-permute-start.31 = (bf16[288,128]{1,0:T(8,128)(2,1)S(1)}, bf16[288,128]{1,0:T(8,128)(2,1)S(1)}, u32[]{:S(2)}, u32[]{:S(2)}) collective-permute-start(bf16[288,128]{1,0:T(8,128)(2,1)S(1)} %fusion.8.refs_0_), channel_id=1, source_target_pairs={{0,8},{8,0},{16,24},{24,16},{1,9},{9,1},{17,25},{25,17},{2,10},{10... | collective-permute-start | bytes 221192 | tf_op jit(solution)/shard_map/ppermute | solution.py:829
  196.3 2.6 %assemble.1 = (f32[64,512]{1,0:T(8,128)}, f32[64,512]{1,0:T(8,128)}, f32[64,512]{1,0:T(8,128)}, f32[64,512]{1,0:T(8,128)}, f32[1,64]{1,0:T(1,128)}, /*index=5*/f...) custom-call(f32[8,128]{1,0:T(8,128)} %get-tuple-element.77.count_ref, ...), custom_call_target="tpu_custom_call" | custom-call | flops 1000 | bytes 1000 | tf_op jit(solution)/shard_map/assemble/pallas_call | solution.py:961
  (131 shorter events, 28.3 us)
Async XLA Ops:
  2.7 7.2 %collective-permute-start.3 = (bf16[1,144,256]{2,1,0:T(8,128)(2,1)}, bf16[1,144,256]{2,1,0:T(8,128)(2,1)S(1)}, u32[]{:S(2)}, u32[]{:S(2)}) collective-permute-start(bf16[1,144,256]{2,1,0:T(8,128)(2,1)} %bitcast.100), channel_id=1, source_target_pairs={{0,4},{1,5},{2,6},{3,7},{4,0},{5,1},{6,2},{7,3},{8,12},{9,13},{10,... | collective-permute-start | bytes 221192 | tf_op jit(solution)/shard_map/ppermute | solution.py:829
  5.0 11.5 %collective-permute-start.4 = (bf16[1,144,256]{2,1,0:T(8,128)(2,1)}, bf16[1,144,256]{2,1,0:T(8,128)(2,1)S(1)}, u32[]{:S(2)}, u32[]{:S(2)}) collective-permute-start(bf16[1,144,256]{2,1,0:T(8,128)(2,1)} %bitcast.101), channel_id=1, source_target_pairs={{0,6},{1,7},{2,4},{3,5},{4,2},{5,3},{6,0},{7,1},{8,14},{9,15},{10,... | collective-permute-start | bytes 221192 | tf_op jit(solution)/shard_map/ppermute | solution.py:829
  5.0 12.8 %collective-permute-start = (bf16[1,144,256]{2,1,0:T(8,128)(2,1)}, bf16[1,144,256]{2,1,0:T(8,128)(2,1)S(1)}, u32[]{:S(2)}, u32[]{:S(2)}) collective-permute-start(bf16[1,144,256]{2,1,0:T(8,128)(2,1)} %bitcast.102), channel_id=1, source_target_pairs={{0,2},{1,3},{2,0},{3,1},{4,6},{5,7},{6,4},{7,5},{8,10},{9,11},{10,... | collective-permute-start | bytes 221192 | tf_op jit(solution)/shard_map/ppermute | solution.py:829
  12.0 19.4 %collective-permute-start.9 = (bf16[1,288,256]{2,1,0:T(8,128)(2,1)S(1)}, bf16[1,288,256]{2,1,0:T(8,128)(2,1)S(1)}, u32[]{:S(2)}, u32[]{:S(2)}) collective-permute-start(bf16[1,288,256]{2,1,0:T(8,128)(2,1)S(1)} %add_bitcast_fusion), channel_id=1, source_target_pairs={{0,6},{1,7},{2,4},{3,5},{4,2},{5,3},{6,0},{7,1},{8,14},{9,15},{10,... | collective-permute-start | bytes 442376 | tf_op jit(solution)/shard_map/ppermute | solution.py:829
  12.1 15.7 %collective-permute-start.8 = (bf16[1,288,256]{2,1,0:T(8,128)(2,1)S(1)}, bf16[1,288,256]{2,1,0:T(8,128)(2,1)S(1)}, u32[]{:S(2)}, u32[]{:S(2)}) collective-permute-start(bf16[1,288,256]{2,1,0:T(8,128)(2,1)S(1)} %add_bitcast_fusion), channel_id=1, source_target_pairs={{0,4},{1,5},{2,6},{3,7},{4,0},{5,1},{6,2},{7,3},{8,12},{9,13},{10,... | collective-permute-start | bytes 442376 | tf_op jit(solution)/shard_map/ppermute | solution.py:829
  15.4 10.4 %collective-permute-start.7 = (bf16[1,288,256]{2,1,0:T(8,128)(2,1)S(1)}, bf16[1,288,256]{2,1,0:T(8,128)(2,1)S(1)}, u32[]{:S(2)}, u32[]{:S(2)}) collective-permute-start(bf16[1,288,256]{2,1,0:T(8,128)(2,1)S(1)} %add_bitcast_fusion), channel_id=1, source_target_pairs={{0,2},{1,3},{2,0},{3,1},{4,6},{5,7},{6,4},{7,5},{8,10},{9,11},{10,... | collective-permute-start | bytes 442376 | tf_op jit(solution)/shard_map/ppermute | solution.py:829
  16.6 4.4 %collective-permute-start.5 = (bf16[2,144,256]{2,1,0:T(8,128)(2,1)S(1)}, bf16[2,144,256]{2,1,0:T(8,128)(2,1)S(1)}, u32[]{:S(2)}, u32[]{:S(2)}) collective-permute-start(bf16[2,144,256]{2,1,0:T(8,128)(2,1)S(1)} %pad_maximum_fusion.4), channel_id=1, source_target_pairs={{0,16},{8,24},{16,0},{24,8},{1,17},{9,25},{17,1},{25,9},{2,18},{10... | collective-permute-start | bytes 442376 | tf_op jit(solution)/shard_map/ppermute | solution.py:829
  18.7 4.7 %collective-permute-start.1 = (bf16[2,144,256]{2,1,0:T(8,128)(2,1)S(1)}, bf16[2,144,256]{2,1,0:T(8,128)(2,1)S(1)}, u32[]{:S(2)}, u32[]{:S(2)}) collective-permute-start(bf16[2,144,256]{2,1,0:T(8,128)(2,1)S(1)} %pad_maximum_fusion.3), channel_id=1, source_target_pairs={{0,1},{1,0},{2,3},{3,2},{4,5},{5,4},{6,7},{7,6},{8,9},{9,8},{10,11... | collective-permute-start | bytes 442376 | tf_op jit(solution)/shard_map/ppermute | solution.py:829
  20.9 16.3 %collective-permute-start.12 = (bf16[4,144,256]{2,1,0:T(8,128)(2,1)S(1)}, bf16[4,144,256]{2,1,0:T(8,128)(2,1)S(1)}, u32[]{:S(2)}, u32[]{:S(2)}) collective-permute-start(bf16[4,144,256]{2,1,0:T(8,128)(2,1)S(1)} %constant_dynamic-update-slice_fusion.refs_5_), channel_id=1, source_target_pairs={{0,8},{8,0},{16,24},{24,16},{1,9},{9,1},{17,25},{25,17},{2,10},{10... | collective-permute-start | bytes 884744 | tf_op jit(solution)/shard_map/ppermute | solution.py:829
  23.4 9.5 %collective-permute-start.6 = (bf16[4,144,256]{2,1,0:T(8,128)(2,1)S(1)}, bf16[4,144,256]{2,1,0:T(8,128)(2,1)S(1)}, u32[]{:S(2)}, u32[]{:S(2)}) collective-permute-start(bf16[4,144,256]{2,1,0:T(8,128)(2,1)S(1)} %constant_dynamic-update-slice_fusion.refs_5_), channel_id=1, source_target_pairs={{0,1},{1,0},{2,3},{3,2},{4,5},{5,4},{6,7},{7,6},{8,9},{9,8},{10,11... | collective-permute-start | bytes 884744 | tf_op jit(solution)/shard_map/ppermute | solution.py:829
  25.8 12.7 %collective-permute-start.10 = (bf16[4,144,256]{2,1,0:T(8,128)(2,1)S(1)}, bf16[4,144,256]{2,1,0:T(8,128)(2,1)S(1)}, u32[]{:S(2)}, u32[]{:S(2)}) collective-permute-start(bf16[4,144,256]{2,1,0:T(8,128)(2,1)S(1)} %pad_maximum_fusion.1.refs_3_), channel_id=1, source_target_pairs={{0,8},{8,0},{16,24},{24,16},{1,9},{9,1},{17,25},{25,17},{2,10},{10... | collective-permute-start | bytes 884744 | tf_op jit(solution)/shard_map/ppermute | solution.py:829
  27.8 8.7 %collective-permute-start.2 = (bf16[4,144,256]{2,1,0:T(8,128)(2,1)S(1)}, bf16[4,144,256]{2,1,0:T(8,128)(2,1)S(1)}, u32[]{:S(2)}, u32[]{:S(2)}) collective-permute-start(bf16[4,144,256]{2,1,0:T(8,128)(2,1)S(1)} %pad_maximum_fusion.1.refs_3_), channel_id=1, source_target_pairs={{0,16},{8,24},{16,0},{24,8},{1,17},{9,25},{17,1},{25,9},{2,18},{10... | collective-permute-start | bytes 884744 | tf_op jit(solution)/shard_map/ppermute | solution.py:829
  31.4 20.7 %collective-permute-start.14 = (bf16[2,288,256]{2,1,0:T(8,128)(2,1)S(1)}, bf16[2,288,256]{2,1,0:T(8,128)(2,1)S(1)}, u32[]{:S(2)}, u32[]{:S(2)}) collective-permute-start(bf16[2,288,256]{2,1,0:T(8,128)(2,1)S(1)} %pad_maximum_fusion.2.refs_11_), channel_id=1, source_target_pairs={{0,1},{1,0},{2,3},{3,2},{4,5},{5,4},{6,7},{7,6},{8,9},{9,8},{10,11... | collective-permute-start | bytes 884744 | tf_op jit(solution)/shard_map/ppermute | solution.py:829
  32.9 5.7 %collective-permute-start.13 = (bf16[4,144,256]{2,1,0:T(8,128)(2,1)S(1)}, bf16[4,144,256]{2,1,0:T(8,128)(2,1)S(1)}, u32[]{:S(2)}, u32[]{:S(2)}) collective-permute-start(bf16[4,144,256]{2,1,0:T(8,128)(2,1)S(1)} %broadcast_add_fusion.refs_6_), channel_id=1, source_target_pairs={{0,8},{8,0},{16,24},{24,16},{1,9},{9,1},{17,25},{25,17},{2,10},{10... | collective-permute-start | bytes 884744 | tf_op jit(solution)/shard_map/ppermute | solution.py:829
  37.3 14.8 %collective-permute-start.15 = (bf16[2,288,256]{2,1,0:T(8,128)(2,1)S(1)}, bf16[2,288,256]{2,1,0:T(8,128)(2,1)S(1)}, u32[]{:S(2)}, u32[]{:S(2)}) collective-permute-start(bf16[2,288,256]{2,1,0:T(8,128)(2,1)S(1)} %get-tuple-element.137.refs_12_), channel_id=1, source_target_pairs={{0,16},{8,24},{16,0},{24,8},{1,17},{9,25},{17,1},{25,9},{2,18},{10... | collective-permute-start | bytes 884744 | tf_op jit(solution)/shard_map/ppermute | solution.py:829
  52.9 14.6 %collective-permute-start.19 = (bf16[4,288,256]{2,1,0:T(8,128)(2,1)S(1)}, bf16[4,288,256]{2,1,0:T(8,128)(2,1)S(1)}, u32[]{:S(2)}, u32[]{:S(2)}) collective-permute-start(bf16[4,288,256]{2,1,0:T(8,128)(2,1)S(1)} %constant_dynamic-update-slice_fusion.5.refs_6_.refs_2_), channel_id=1, source_target_pairs={{0,1},{1,0},{2,3},{3,2},{4,5},{5,4},{6,7},{7,6},{8,9},{9,8},{10,11... | collective-permute-start | bytes 1769480 | tf_op jit(solution)/shard_map/ppermute | solution.py:829
  53.4 14.2 %collective-permute-start.18 = (bf16[4,288,256]{2,1,0:T(8,128)(2,1)S(1)}, bf16[4,288,256]{2,1,0:T(8,128)(2,1)S(1)}, u32[]{:S(2)}, u32[]{:S(2)}) collective-permute-start(bf16[4,288,256]{2,1,0:T(8,128)(2,1)S(1)} %pad_maximum_fusion.refs_5_.refs_0_), channel_id=1, source_target_pairs={{0,16},{8,24},{16,0},{24,8},{1,17},{9,25},{17,1},{25,9},{2,18},{10... | collective-permute-start | bytes 1769480 | tf_op jit(solution)/shard_map/ppermute | solution.py:829
  98.2 5.2 %collective-permute-start.22 = (bf16[4,8,160,256]{3,2,1,0:T(8,128)(2,1)}, bf16[4,8,160,256]{3,2,1,0:T(8,128)(2,1)S(1)}, u32[]{:S(2)}, u32[]{:S(2)}) collective-permute-start(bf16[4,8,160,256]{3,2,1,0:T(8,128)(2,1)} %get-tuple-element.102), channel_id=1, source_target_pairs={{0,8},{8,0},{16,24},{24,16},{1,9},{9,1},{17,25},{25,17},{2,10},{10... | collective-permute-start | bytes 7864328 | tf_op jit(solution)/shard_map/ppermute | solution.py:829
  107.5 67.9 %all-to-all-start = ((bf16[32,160,256]{2,1,0:T(8,128)(2,1)}), bf16[32,160,256]{2,1,0:T(8,128)(2,1)S(1)}, u32[]{:S(2)}, u32[]{:S(2)}) async-start(bf16[32,160,256]{2,1,0:T(8,128)(2,1)} %bitcast.13.refs_25_), calls=%async_computation | async-start | bytes 5242880 | tf_op jit(solution)/shard_map/all_to_all | solution.py:1116
  146.7 12.9 %collective-permute-start.26 = (bf16[2,4,144,128]{3,2,1,0:T(8,128)(2,1)S(1)}, bf16[2,4,144,128]{3,2,1,0:T(8,128)(2,1)S(1)}, u32[]{:S(2)}, u32[]{:S(2)}) collective-permute-start(bf16[2,4,144,128]{3,2,1,0:T(8,128)(2,1)S(1)} %get-tuple-element.121), channel_id=1, source_target_pairs={{0,16},{8,24},{16,0},{24,8},{1,17},{9,25},{17,1},{25,9},{2,18},{10... | collective-permute-start | bytes 884744 | tf_op jit(solution)/shard_map/ppermute | solution.py:829
  148.0 16.1 %collective-permute-start.24 = (bf16[2,4,144,128]{3,2,1,0:T(8,128)(2,1)S(1)}, bf16[2,4,144,128]{3,2,1,0:T(8,128)(2,1)S(1)}, u32[]{:S(2)}, u32[]{:S(2)}) collective-permute-start(bf16[2,4,144,128]{3,2,1,0:T(8,128)(2,1)S(1)} %get-tuple-element.123), channel_id=1, source_target_pairs={{0,1},{1,0},{2,3},{3,2},{4,5},{5,4},{6,7},{7,6},{8,9},{9,8},{10,11... | collective-permute-start | bytes 884744 | tf_op jit(solution)/shard_map/ppermute | solution.py:829
  159.7 10.3 %collective-permute-start.27 = (bf16[4,144,128]{2,1,0:T(8,128)(2,1)S(1)}, bf16[4,144,128]{2,1,0:T(8,128)(2,1)S(1)}, u32[]{:S(2)}, u32[]{:S(2)}) collective-permute-start(bf16[4,144,128]{2,1,0:T(8,128)(2,1)S(1)} %get-tuple-element.127), channel_id=1, source_target_pairs={{0,1},{1,0},{2,3},{3,2},{4,5},{5,4},{6,7},{7,6},{8,9},{9,8},{10,11... | collective-permute-start | bytes 442376 | tf_op jit(solution)/shard_map/ppermute | solution.py:829
  164.1 6.7 %collective-permute-start.25 = (bf16[4,144,128]{2,1,0:T(8,128)(2,1)S(1)}, bf16[4,144,128]{2,1,0:T(8,128)(2,1)S(1)}, u32[]{:S(2)}, u32[]{:S(2)}) collective-permute-start(bf16[4,144,128]{2,1,0:T(8,128)(2,1)S(1)} %get-tuple-element.125), channel_id=1, source_target_pairs={{0,16},{8,24},{16,0},{24,8},{1,17},{9,25},{17,1},{25,9},{2,18},{10... | collective-permute-start | bytes 442376 | tf_op jit(solution)/shard_map/ppermute | solution.py:829
  170.9 13.1 %collective-permute-start.28 = (bf16[1,288,128]{2,1,0:T(8,128)(2,1)S(1)}, bf16[1,288,128]{2,1,0:T(8,128)(2,1)S(1)}, u32[]{:S(2)}, u32[]{:S(2)}) collective-permute-start(bf16[1,288,128]{2,1,0:T(8,128)(2,1)S(1)} %pad_maximum_fusion.6), channel_id=1, source_target_pairs={{0,2},{1,3},{2,0},{3,1},{4,6},{5,7},{6,4},{7,5},{8,10},{9,11},{10,... | collective-permute-start | bytes 221192 | tf_op jit(solution)/shard_map/ppermute | solution.py:829
  171.0 13.0 %collective-permute-start.29 = (bf16[1,288,128]{2,1,0:T(8,128)(2,1)S(1)}, bf16[1,288,128]{2,1,0:T(8,128)(2,1)S(1)}, u32[]{:S(2)}, u32[]{:S(2)}) collective-permute-start(bf16[1,288,128]{2,1,0:T(8,128)(2,1)S(1)} %pad_maximum_fusion.7), channel_id=1, source_target_pairs={{0,4},{1,5},{2,6},{3,7},{4,0},{5,1},{6,2},{7,3},{8,12},{9,13},{10,... | collective-permute-start | bytes 221192 | tf_op jit(solution)/shard_map/ppermute | solution.py:829
  174.7 9.3 %collective-permute-start.30 = (bf16[1,288,128]{2,1,0:T(8,128)(2,1)S(1)}, bf16[1,288,128]{2,1,0:T(8,128)(2,1)S(1)}, u32[]{:S(2)}, u32[]{:S(2)}) collective-permute-start(bf16[1,288,128]{2,1,0:T(8,128)(2,1)S(1)} %pad_maximum_fusion.8), channel_id=1, source_target_pairs={{0,6},{1,7},{2,4},{3,5},{4,2},{5,3},{6,0},{7,1},{8,14},{9,15},{10,... | collective-permute-start | bytes 221192 | tf_op jit(solution)/shard_map/ppermute | solution.py:829
  179.6 15.3 %collective-permute-start.36 = (bf16[2,160,256]{2,1,0:T(8,128)(2,1)}, bf16[2,160,256]{2,1,0:T(8,128)(2,1)S(1)}, u32[]{:S(2)}, u32[]{:S(2)}) collective-permute-start(bf16[2,160,256]{2,1,0:T(8,128)(2,1)} %add_arrived.1.refs_4_), channel_id=1, source_target_pairs={{0,24},{8,16},{16,8},{24,0},{1,25},{9,17},{17,9},{25,1},{2,26},{10... | collective-permute-start | bytes 491528 | tf_op jit(solution)/shard_map/ppermute | solution.py:829
  182.4 12.5 %collective-permute-start.35 = (bf16[2,160,256]{2,1,0:T(8,128)(2,1)}, bf16[2,160,256]{2,1,0:T(8,128)(2,1)S(1)}, u32[]{:S(2)}, u32[]{:S(2)}) collective-permute-start(bf16[2,160,256]{2,1,0:T(8,128)(2,1)} %add_arrived.1.refs_4_), channel_id=1, source_target_pairs={{0,16},{8,24},{16,0},{24,8},{1,17},{9,25},{17,1},{25,9},{2,18},{10... | collective-permute-start | bytes 491528 | tf_op jit(solution)/shard_map/ppermute | solution.py:829
  184.0 10.9 %collective-permute-start.34 = (bf16[2,160,256]{2,1,0:T(8,128)(2,1)}, bf16[2,160,256]{2,1,0:T(8,128)(2,1)S(1)}, u32[]{:S(2)}, u32[]{:S(2)}) collective-permute-start(bf16[2,160,256]{2,1,0:T(8,128)(2,1)} %add_arrived.1.refs_4_), channel_id=1, source_target_pairs={{0,8},{8,0},{16,24},{24,16},{1,9},{9,1},{17,25},{25,17},{2,10},{10... | collective-permute-start | bytes 491528 | tf_op jit(solution)/shard_map/ppermute | solution.py:829
  184.1 7.3 %collective-permute-start.33 = (bf16[288,128]{1,0:T(8,128)(2,1)S(1)}, bf16[288,128]{1,0:T(8,128)(2,1)S(1)}, u32[]{:S(2)}, u32[]{:S(2)}) collective-permute-start(bf16[288,128]{1,0:T(8,128)(2,1)S(1)} %fusion.8.refs_0_), channel_id=1, source_target_pairs={{0,24},{8,16},{16,8},{24,0},{1,25},{9,17},{17,9},{25,1},{2,26},{10... | collective-permute-start | bytes 221192 | tf_op jit(solution)/shard_map/ppermute | solution.py:829
  184.5 9.5 %collective-permute-start.32 = (bf16[288,128]{1,0:T(8,128)(2,1)S(1)}, bf16[288,128]{1,0:T(8,128)(2,1)S(1)}, u32[]{:S(2)}, u32[]{:S(2)}) collective-permute-start(bf16[288,128]{1,0:T(8,128)(2,1)S(1)} %fusion.8.refs_0_), channel_id=1, source_target_pairs={{0,16},{8,24},{16,0},{24,8},{1,17},{9,25},{17,1},{25,9},{2,18},{10... | collective-permute-start | bytes 221192 | tf_op jit(solution)/shard_map/ppermute | solution.py:829
  191.4 3.5 %collective-permute-start.31 = (bf16[288,128]{1,0:T(8,128)(2,1)S(1)}, bf16[288,128]{1,0:T(8,128)(2,1)S(1)}, u32[]{:S(2)}, u32[]{:S(2)}) collective-permute-start(bf16[288,128]{1,0:T(8,128)(2,1)S(1)} %fusion.8.refs_0_), channel_id=1, source_target_pairs={{0,8},{8,0},{16,24},{24,16},{1,9},{9,1},{17,25},{25,17},{2,10},{10... | collective-permute-start | bytes 221192 | tf_op jit(solution)/shard_map/ppermute | solution.py:829
  (32 other events, 113.1 us)

commit v7 on v6

--- a/solution.py
+++ b/solution.py
@@ -329,9 +329,9 @@
     *refs,
 ):
     pieces, refs = (refs[:4], refs[4:8]), refs[8:]
-    out_ref, hidden_ref, grad_mix_ref, keep_out_ref, send_out_ref = refs[:5]
-    x, mix, teacher, wo, we, wc, act, out, hidden_grad, grad_mix = refs[5:15]
-    keep_ref, send_ref, normed, low, d_normed, d_wo, d_we, d_wc, d_vec, d_eb, sems = refs[15:]
+    out_ref, hidden_ref, grad_mix_ref, keep_out_ref, *sends = refs[:6]
+    x, mix, teacher, wo, we, wc, act, out, hidden_grad, grad_mix = refs[6:16]
+    keep_ref, send_ref, normed, low, d_normed, d_wo, d_we, d_wc, d_vec, d_eb, sems = refs[16:]
     r = 512 // shards
     me, core, cross = place()
     copies = [
@@ -485,11 +485,12 @@
             write(keep_ref, right, part)
 
         for n, (source, target) in enumerate(
-            ((send_ref, send_out_ref), (keep_ref, keep_out_ref))
+            (
+                (send_ref, sends[2 * part // reps].at[part % (reps // 2)]),
+                (keep_ref, keep_out_ref.at[part]),
+            )
         ):
-            copy = pltpu.make_async_copy(
-                source.at[part], target.at[part], sems.at[10 + 2 * part + n]
-            )
+            copy = pltpu.make_async_copy(source.at[part], target, sems.at[10 + 2 * part + n])
             copy.start()
             flights.append(copy)
     for copy in [out_copy, hidden_copy, mix_copy, *flights]:
@@ -744,13 +745,13 @@
     return pl.pallas_call(
         functools.partial(feed_forward, shards, tokens),
         in_specs=[anywhere()] * 4 + [vmem] * 4 + [anywhere()] * 8,
-        out_specs=[anywhere()] * 5,
+        out_specs=[anywhere()] * 6,
         out_shape=[
             shaped(wide, BF16),
             shaped(wide, F32),
             shaped(wide, BF16),
             shaped(payload, BF16),
-            shaped(payload, BF16),
+            *[shaped((reps // 2, *payload[1:]), BF16)] * 2,
         ],
         scratch_shapes=[
             pltpu.VMEM(wide, BF16),
@@ -836,7 +837,7 @@
 
 def branch_rows(shards, reps):
     r = 512 // shards
-    piece = -(-(9 * r + 16) // (16 * reps)) * 16
+    piece = -(-(9 * r + 16) // (8 * reps)) * 8
     names = [("contract", 4 * r)] + [(b, r) for b in range(4)] + [("output", r), ("vectors", 16)]
     rows, at = [], 0
     for name, height in names + [("none", piece * reps - 9 * r - 16)]:
@@ -1059,7 +1060,7 @@
     theirs_b = (near_b[0], swap(pending[0], "rep", 1), near_b[1], swap(pending[1], "rep", 1))
     mixed = (forward_0[7], forward_1[7])
 
-    layer_out, grad_hidden, grad_mix, keep_f, send_f = call_feed_forward(
+    layer_out, grad_hidden, grad_mix, keep_f, send_low, send_high = call_feed_forward(
         shards,
         reps,
         float(length * shards * reps),
@@ -1111,7 +1112,9 @@
             bit *= 2
         return [total] + [swap(total, "rep", a) for a in range(1, 4)]
 
-    summed = add_low(keep_f, swap(send_f, "rep", 1))
+    late_f = swap(send_low, "rep", 1), swap(send_high, "rep", 1)
+    halves_f = keep_f[: reps // 2], keep_f[reps // 2 :]
+    summed = jnp.concatenate([add_low(a, b) for a, b in zip(halves_f, late_f)], axis=0)
     every = summed.reshape(reps * shards, *summed.shape[2:])
     arrived_f = lax.all_to_all(every, ("rep", "shard"), 0, 0).reshape(summed.shape)
     sides = [(*saved[:7], *saved[8:10]) for saved in (forward_0, forward_1)]
@@ -1123,7 +1126,13 @@
     parts_0, parts_1 = cross_first(parts_0), row_first(parts_1)
     q_pieces = z_stage([parts_0, parts_1])
     total_f = call_add_arrived(shards, arrived_f, q_pieces[0])
-    parts_f = [total_f] + [swap(total_f, "rep", a) for a in range(1, reps)]
+    by_offset = {0: total_f}
+    bit = 2
+    while bit < reps:
+        by_offset |= {a | bit: swap(part, "rep", bit) for a, part in list(by_offset.items())}
+        bit *= 2
+    by_offset |= {a | 1: swap(part, "rep", 1) for a, part in list(by_offset.items())}
+    parts_f = [by_offset[a] for a in range(reps)]
     parts_q = finish(q_pieces)
     results = assemble(shards, count, parts_q, parts_f)
     mats, (gain_1, shift_1) = results[:4], results[4:6]

time: 200 us -> 196 us (0.980)
  waiting for transfers between devices: 50.2 us -> 46.5 us
    ppermute x37 -> x38, waiting for transfers between devices: 50.2 us -> 46.5 us  [swap(): return lax.ppermute(value, axis, [(i, i ^ bit) for i in range(n)])]
    unnamed x56 -> x58, local copies, waits for them, and re-layouts: 5.45 us -> 5.32 us
    ppermute x37 -> x38, starting transfers between devices: 37.2 us -> 37.3 us  [swap(): return lax.ppermute(value, axis, [(i, i ^ bit) for i in range(n)])]
  transfers between devices with their start and end apart: 38 -> 39, of which waited for: 19 -> 18; matrix products, arithmetic and copies ran while one was open for 4% -> 3% of each run, Pallas kernels for 27% -> 28%
where the time goes in v7:
time: 196 us; the launch traced here: 193 us
  Pallas kernels  84.8 us (43%)
  waiting for transfers between devices  46.5 us (24%)
  starting transfers between devices  42.4 us (22%)
  other arithmetic  8.36 us (4%)
  local copies, waits for them, and re-layouts  7.4 us (4%)
  between operations  3.92 us (2%)
    ppermute x38, waiting for transfers between devices, swap(): return lax.ppermute(value, axis, [(i, i ^ bit) for i in range(n)])  46.5 us
    ppermute x38, starting transfers between devices, swap(): return lax.ppermute(value, axis, [(i, i ^ bit) for i in range(n)])  37.3 us
    pallas_call x1, Pallas kernels, call_backward(): pl.pallas_call(functools.partial(ordered, functools.partial(attention_bac...  28.8 us
    pallas_call x1, Pallas kernels, call_feed_forward(): pl.pallas_call(functools.partial(feed_forward, shards, tokens), in_specs=...  25.6 us
    pallas_call x2, Pallas kernels, call_forward(): pl.pallas_call(functools.partial(ordered, functools.partial(attention_for...  23.1 us
    unnamed x58, local copies, waits for them, and re-layouts  5.32 us
    all_to_all x1, starting transfers between devices, local(): lax.all_to_all(every, ('rep', 'shard'), 0, 0).reshape(summed.shape)  5.12 us
    convert_element_type x6, other arithmetic, add_low(): return sum((part.astype(F32) for part in parts)).astype(BF16)  4.04 us
  transfers between devices with their start and end apart: 39, of which 18 were waited for; matrix products, arithmetic and copies ran while one was open for 3% of the time, Pallas kernels for 28%

profile of v7, /device:TPU:13, one launch (start us, length us, event | category | flops | bytes accessed | tf_op | source)
XLA Modules:
  0.0 193.4 jit_solution(8356394623771241479)
XLA Ops:
  0.7 2.0 %pack.1 = (bf16[144,256]{1,0:T(8,128)(2,1)}, bf16[288,256]{1,0:T(8,128)(2,1)}) custom-call(bf16[64,512]{1,0:T(8,128)(2,1)} %refs_0_.4, bf16[64,512]{1,0:T(8,128)(2,1)} %refs_1_.1, bf16[64,512]{1,0:T(8,128)(2,1)} %refs_2_.4, bf16[64,512]{1,0:T(8,128)(2,1)} %refs_3_.1, bf16[64,512]{1,0:T(8,128)(2,1)} %refs_4_.1, bf16[64,2048]{1,0:T(8,128)(2,1)} %refs_5_.1, ...), custom_call_target="tpu_custom_call" | custom-call | flops 1000 | bytes 1000 | tf_op jit(solution)/shard_map/pack/pallas_call | solution.py:679
  2.7 2.4 %collective-permute-start.3 = (bf16[1,144,256]{2,1,0:T(8,128)(2,1)}, bf16[1,144,256]{2,1,0:T(8,128)(2,1)S(1)}, u32[]{:S(2)}, u32[]{:S(2)}) collective-permute-start(bf16[1,144,256]{2,1,0:T(8,128)(2,1)} %bitcast.100), channel_id=1, source_target_pairs={{0,4},{1,5},{2,6},{3,7},{4,0},{5,1},{6,2},{7,3},{8,12},{9,13},{10,... | collective-permute-start | bytes 221192 | tf_op jit(solution)/shard_map/ppermute | solution.py:830
  6.3 3.6 %collective-permute-done.3 = bf16[1,144,256]{2,1,0:T(8,128)(2,1)S(1)} collective-permute-done((bf16[1,144,256]{2,1,0:T(8,128)(2,1)}, bf16[1,144,256]{2,1,0:T(8,128)(2,1)S(1)}, u32[]{:S(2)}, u32[]{:S(2)}) %collective-permute-start.3) | collective-permute-done | bytes 73760 | tf_op jit(solution)/shard_map/ppermute | solution.py:830
  12.1 3.4 %collective-permute-start.8 = (bf16[1,288,256]{2,1,0:T(8,128)(2,1)S(1)}, bf16[1,288,256]{2,1,0:T(8,128)(2,1)S(1)}, u32[]{:S(2)}, u32[]{:S(2)}) collective-permute-start(bf16[1,288,256]{2,1,0:T(8,128)(2,1)S(1)} %add_bitcast_fusion), channel_id=1, source_target_pairs={{0,4},{1,5},{2,6},{3,7},{4,0},{5,1},{6,2},{7,3},{8,12},{9,13},{10,... | collective-permute-start | bytes 442376 | tf_op jit(solution)/shard_map/ppermute | solution.py:830
  19.1 1.9 collective-permute-done.5
  21.0 2.5 %collective-permute-start.12 = (bf16[4,144,256]{2,1,0:T(8,128)(2,1)S(1)}, bf16[4,144,256]{2,1,0:T(8,128)(2,1)S(1)}, u32[]{:S(2)}, u32[]{:S(2)}) collective-permute-start(bf16[4,144,256]{2,1,0:T(8,128)(2,1)S(1)} %constant_dynamic-update-slice_fusion.refs_5_), channel_id=1, source_target_pairs={{0,8},{8,0},{16,24},{24,16},{1,9},{9,1},{17,25},{25,17},{2,10},{10... | collective-permute-start | bytes 884744 | tf_op jit(solution)/shard_map/ppermute | solution.py:830
  23.8 2.1 %collective-permute-done.7 = bf16[1,288,256]{2,1,0:T(8,128)(2,1)S(1)} collective-permute-done((bf16[1,288,256]{2,1,0:T(8,128)(2,1)S(1)}, bf16[1,288,256]{2,1,0:T(8,128)(2,1)S(1)}, u32[]{:S(2)}, u32[]{:S(2)}) %collective-permute-start.7) | collective-permute-done | bytes 147488 | tf_op jit(solution)/shard_map/ppermute | solution.py:830
  25.9 1.9 collective-permute-start.10
  33.6 2.9 %collective-permute-done.2.refs_4_ = bf16[4,144,256]{2,1,0:T(8,128)(2,1)S(1)} collective-permute-done((bf16[4,144,256]{2,1,0:T(8,128)(2,1)S(1)}, bf16[4,144,256]{2,1,0:T(8,128)(2,1)S(1)}, u32[]{:S(2)}, u32[]{:S(2)}) %collective-permute-start.2) | collective-permute-done | bytes 294944 | tf_op jit(solution)/shard_map/ppermute | solution.py:830
  39.6 12.5 %attention_forward_0.1 = (bf16[1024,256]{1,0:T(8,128)(2,1)}, bf16[1024,256]{1,0:T(8,128)(2,1)}, bf16[1024,256]{1,0:T(8,128)(2,1)}, bf16[1024,256]{1,0:T(8,128)(2...) custom-call(s32[1,1024]{1,0:T(1,128)} %refs_2_.7, ...), custom_call_target="tpu_custom_call" | custom-call | flops 1000 | bytes 1000 | tf_op jit(solution)/shard_map/attention_forward_0/pallas_call | solution.py:723
  55.9 10.6 %attention_forward_1.1 = (bf16[1024,256]{1,0:T(8,128)(2,1)}, bf16[1024,256]{1,0:T(8,128)(2,1)}, bf16[1024,256]{1,0:T(8,128)(2,1)}, bf16[1024,256]{1,0:T(8,128)(2...) custom-call(s32[1,1024]{1,0:T(1,128)} %refs_2_.7, ...), custom_call_target="tpu_custom_call" | custom-call | flops 1000 | bytes 1000 | tf_op jit(solution)/shard_map/attention_forward_1/pallas_call | solution.py:723
  68.9 1.6 collective-permute-done.20.refs_5_
  72.2 25.6 %feed_forward.1 = (bf16[1024,512]{1,0:T(8,128)(2,1)}, f32[1024,512]{1,0:T(8,128)}, bf16[1024,512]{1,0:T(8,128)(2,1)}, bf16[4,8,152,256]{3,2,1,0:T(8,128)(2,1)}, ...) custom-call(bf16[1024,512]{1,0:T(8,128)(2,1)} %bitcast.96, ...), custom_call_target="tpu_custom_call" | custom-call | flops 1000 | bytes 1000 | tf_op jit(solution)/shard_map/feed_forward/pallas_call | solution.py:745
  98.4 2.6 %collective-permute-done.22 = bf16[2,8,152,256]{3,2,1,0:T(8,128)(2,1)S(1)} collective-permute-done((bf16[2,8,152,256]{3,2,1,0:T(8,128)(2,1)}, bf16[2,8,152,256]{3,2,1,0:T(8,128)(2,1)S(1)}, u32[]{:S(2)}, u32[]{:S(2)}) %collective-permute-start.22) | collective-permute-done | bytes 1245216 | tf_op jit(solution)/shard_map/ppermute | solution.py:830
  101.0 1.8 collective-permute-done.23
  102.8 2.2 %add_convert_fusion.1 = (bf16[2,8,152,256]{3,2,1,0:T(8,128)(2,1)S(1)}, bf16[2,8,152,256]{3,2,1,0:T(8,128)(2,1)S(1)}) fusion(bf16[2,8,152,256]{3,2,1,0:T(8,128)(2,1)S(1)} %collective-permute-done.22, bf16[4,8,152,256]{3,2,1,0:T(8,128)(2,1)} %get-tuple-element.102, bf16[2,8,152,256]{3,2,1,0:T(8,128)(2,1)S(1)} %collective-permute-done.23), kind=kLoop, calls=%fused_computation.2 | loop fusion | flops 4980736 | bytes 7471104 | tf_op jit(solution)/shard_map/convert_element_type | solution.py:974
  105.0 1.6 pad_maximum_fusion
  106.7 5.1 %all-to-all-start = ((bf16[32,152,256]{2,1,0:T(8,128)(2,1)}), bf16[32,152,256]{2,1,0:T(8,128)(2,1)S(1)}, u32[]{:S(2)}, u32[]{:S(2)}) async-start(bf16[32,152,256]{2,1,0:T(8,128)(2,1)} %bitcast.13.refs_25_), calls=%async_computation | async-start | bytes 4980736 | tf_op jit(solution)/shard_map/all_to_all | solution.py:1119
  111.8 28.8 %attention_backward.1 = (f32[1024,512]{1,0:T(8,128)}, bf16[2,2,2,4,144,128]{5,4,3,2,1,0:T(8,128)(2,1)}, bf16[2,2,2,4,144,128]{5,4,3,2,1,0:T(8,128)(2,1)}) custom-call(s32[1,1024]{1,0:T(1,128)} %refs_2_.7, bf16[1024,512]{1,0:T(8,128)(2,1)} %bitcast.97, s32[1,1024]{1,0:T(1,128)} %refs_2_.7, bf16[1024,256]{1,0:T(8,128)(2,1)} %get-tuple-element.82.refs_3_, ...), custom_call_target="tpu_custom_call" | custom-call | flops 1000 | bytes 1000 | tf_op jit(solution)/shard_map/attention_backward/pallas_call | solution.py:816
  141.0 2.7 %collective-permute-done.24 = bf16[2,2,2,4,144,128]{5,4,3,2,1,0:T(8,128)(2,1)S(1)} collective-permute-done((bf16[2,2,2,4,144,128]{5,4,3,2,1,0:T(8,128)(2,1)}, bf16[2,2,2,4,144,128]{5,4,3,2,1,0:T(8,128)(2,1)S(1)}, u32[]{:S(2)}, u32[]{:S(2)}) %collective-permute-start.24) | collective-permute-done | bytes 1179680 | tf_op jit(solution)/shard_map/ppermute | solution.py:830
  146.8 9.5 %collective-permute-done.27 = bf16[2,4,144,128]{3,2,1,0:T(8,128)(2,1)S(1)} collective-permute-done((bf16[2,4,144,128]{3,2,1,0:T(8,128)(2,1)S(1)}, bf16[2,4,144,128]{3,2,1,0:T(8,128)(2,1)S(1)}, u32[]{:S(2)}, u32[]{:S(2)}) %collective-permute-start.27) | collective-permute-done | bytes 294944 | tf_op jit(solution)/shard_map/ppermute | solution.py:830
  156.4 1.6 collective-permute-start.28
  158.0 6.8 %collective-permute-done.25 = bf16[2,4,144,128]{3,2,1,0:T(8,128)(2,1)S(1)} collective-permute-done((bf16[2,4,144,128]{3,2,1,0:T(8,128)(2,1)S(1)}, bf16[2,4,144,128]{3,2,1,0:T(8,128)(2,1)S(1)}, u32[]{:S(2)}, u32[]{:S(2)}) %collective-permute-start.25) | collective-permute-done | bytes 294944 | tf_op jit(solution)/shard_map/ppermute | solution.py:830
  165.0 3.0 %collective-permute-done.28 = bf16[4,144,128]{2,1,0:T(8,128)(2,1)S(1)} collective-permute-done((bf16[4,144,128]{2,1,0:T(8,128)(2,1)S(1)}, bf16[4,144,128]{2,1,0:T(8,128)(2,1)S(1)}, u32[]{:S(2)}, u32[]{:S(2)}) %collective-permute-start.28) | collective-permute-done | bytes 147488 | tf_op jit(solution)/shard_map/ppermute | solution.py:830
  169.1 1.6 collective-permute-start.30
  172.8 2.7 %add_arrived.1.refs_4_ = bf16[2,152,256]{2,1,0:T(8,128)(2,1)} custom-call(bf16[4,8,152,256]{3,2,1,0:T(8,128)(2,1)} %bitcast.98, bf16[1,288,128]{2,1,0:T(8,128)(2,1)} %pad_maximum_fusion.6.refs_1_), custom_call_target="tpu_custom_call" | custom-call | flops 1000 | bytes 1000 | tf_op jit(solution)/shard_map/add_arrived/pallas_call | solution.py:866
  176.7 4.2 %collective-permute-start.35 = (bf16[2,152,256]{2,1,0:T(8,128)(2,1)}, bf16[2,152,256]{2,1,0:T(8,128)(2,1)S(1)}, u32[]{:S(2)}, u32[]{:S(2)}) collective-permute-start(bf16[2,152,256]{2,1,0:T(8,128)(2,1)} %add_arrived.1.refs_4_), channel_id=1, source_target_pairs={{0,8},{8,0},{16,24},{24,16},{1,9},{9,1},{17,25},{25,17},{2,10},{10... | collective-permute-start | bytes 466952 | tf_op jit(solution)/shard_map/ppermute | solution.py:830
  180.9 1.6 collective-permute-start.37
  182.5 2.3 %collective-permute-start.34 = (bf16[288,128]{1,0:T(8,128)(2,1)S(1)}, bf16[288,128]{1,0:T(8,128)(2,1)S(1)}, u32[]{:S(2)}, u32[]{:S(2)}) collective-permute-start(bf16[288,128]{1,0:T(8,128)(2,1)S(1)} %fusion.8.refs_0_), channel_id=1, source_target_pairs={{0,24},{8,16},{16,8},{24,0},{1,25},{9,17},{17,9},{25,1},{2,26},{10... | collective-permute-start | bytes 221192 | tf_op jit(solution)/shard_map/ppermute | solution.py:830
  185.3 2.4 %collective-permute-done.34.refs_3_ = bf16[288,128]{1,0:T(8,128)(2,1)S(1)} collective-permute-done((bf16[288,128]{1,0:T(8,128)(2,1)S(1)}, bf16[288,128]{1,0:T(8,128)(2,1)S(1)}, u32[]{:S(2)}, u32[]{:S(2)}) %collective-permute-start.34) | collective-permute-done | bytes 73760 | tf_op jit(solution)/shard_map/ppermute | solution.py:830
  187.7 1.6 collective-permute-done.33.refs_2_
  190.7 2.5 %assemble.1 = (f32[64,512]{1,0:T(8,128)}, f32[64,512]{1,0:T(8,128)}, f32[64,512]{1,0:T(8,128)}, f32[64,512]{1,0:T(8,128)}, f32[1,64]{1,0:T(1,128)}, /*index=5*/f...) custom-call(f32[8,128]{1,0:T(8,128)} %get-tuple-element.78.count_ref, ...), custom_call_target="tpu_custom_call" | custom-call | flops 1000 | bytes 1000 | tf_op jit(solution)/shard_map/assemble/pallas_call | solution.py:962
  (136 shorter events, 31.7 us)
Async XLA Ops:
  2.7 7.2 %collective-permute-start.3 = (bf16[1,144,256]{2,1,0:T(8,128)(2,1)}, bf16[1,144,256]{2,1,0:T(8,128)(2,1)S(1)}, u32[]{:S(2)}, u32[]{:S(2)}) collective-permute-start(bf16[1,144,256]{2,1,0:T(8,128)(2,1)} %bitcast.100), channel_id=1, source_target_pairs={{0,4},{1,5},{2,6},{3,7},{4,0},{5,1},{6,2},{7,3},{8,12},{9,13},{10,... | collective-permute-start | bytes 221192 | tf_op jit(solution)/shard_map/ppermute | solution.py:830
  5.1 11.5 %collective-permute-start.4 = (bf16[1,144,256]{2,1,0:T(8,128)(2,1)}, bf16[1,144,256]{2,1,0:T(8,128)(2,1)S(1)}, u32[]{:S(2)}, u32[]{:S(2)}) collective-permute-start(bf16[1,144,256]{2,1,0:T(8,128)(2,1)} %bitcast.101), channel_id=1, source_target_pairs={{0,6},{1,7},{2,4},{3,5},{4,2},{5,3},{6,0},{7,1},{8,14},{9,15},{10,... | collective-permute-start | bytes 221192 | tf_op jit(solution)/shard_map/ppermute | solution.py:830
  5.1 12.8 %collective-permute-start = (bf16[1,144,256]{2,1,0:T(8,128)(2,1)}, bf16[1,144,256]{2,1,0:T(8,128)(2,1)S(1)}, u32[]{:S(2)}, u32[]{:S(2)}) collective-permute-start(bf16[1,144,256]{2,1,0:T(8,128)(2,1)} %bitcast.102), channel_id=1, source_target_pairs={{0,2},{1,3},{2,0},{3,1},{4,6},{5,7},{6,4},{7,5},{8,10},{9,11},{10,... | collective-permute-start | bytes 221192 | tf_op jit(solution)/shard_map/ppermute | solution.py:830
  12.0 19.4 %collective-permute-start.9 = (bf16[1,288,256]{2,1,0:T(8,128)(2,1)S(1)}, bf16[1,288,256]{2,1,0:T(8,128)(2,1)S(1)}, u32[]{:S(2)}, u32[]{:S(2)}) collective-permute-start(bf16[1,288,256]{2,1,0:T(8,128)(2,1)S(1)} %add_bitcast_fusion), channel_id=1, source_target_pairs={{0,6},{1,7},{2,4},{3,5},{4,2},{5,3},{6,0},{7,1},{8,14},{9,15},{10,... | collective-permute-start | bytes 442376 | tf_op jit(solution)/shard_map/ppermute | solution.py:830
  12.1 15.7 %collective-permute-start.8 = (bf16[1,288,256]{2,1,0:T(8,128)(2,1)S(1)}, bf16[1,288,256]{2,1,0:T(8,128)(2,1)S(1)}, u32[]{:S(2)}, u32[]{:S(2)}) collective-permute-start(bf16[1,288,256]{2,1,0:T(8,128)(2,1)S(1)} %add_bitcast_fusion), channel_id=1, source_target_pairs={{0,4},{1,5},{2,6},{3,7},{4,0},{5,1},{6,2},{7,3},{8,12},{9,13},{10,... | collective-permute-start | bytes 442376 | tf_op jit(solution)/shard_map/ppermute | solution.py:830
  15.5 10.4 %collective-permute-start.7 = (bf16[1,288,256]{2,1,0:T(8,128)(2,1)S(1)}, bf16[1,288,256]{2,1,0:T(8,128)(2,1)S(1)}, u32[]{:S(2)}, u32[]{:S(2)}) collective-permute-start(bf16[1,288,256]{2,1,0:T(8,128)(2,1)S(1)} %add_bitcast_fusion), channel_id=1, source_target_pairs={{0,2},{1,3},{2,0},{3,1},{4,6},{5,7},{6,4},{7,5},{8,10},{9,11},{10,... | collective-permute-start | bytes 442376 | tf_op jit(solution)/shard_map/ppermute | solution.py:830
  16.6 4.4 %collective-permute-start.5 = (bf16[2,144,256]{2,1,0:T(8,128)(2,1)S(1)}, bf16[2,144,256]{2,1,0:T(8,128)(2,1)S(1)}, u32[]{:S(2)}, u32[]{:S(2)}) collective-permute-start(bf16[2,144,256]{2,1,0:T(8,128)(2,1)S(1)} %pad_maximum_fusion.5), channel_id=1, source_target_pairs={{0,16},{8,24},{16,0},{24,8},{1,17},{9,25},{17,1},{25,9},{2,18},{10... | collective-permute-start | bytes 442376 | tf_op jit(solution)/shard_map/ppermute | solution.py:830
  18.8 4.7 %collective-permute-start.1 = (bf16[2,144,256]{2,1,0:T(8,128)(2,1)S(1)}, bf16[2,144,256]{2,1,0:T(8,128)(2,1)S(1)}, u32[]{:S(2)}, u32[]{:S(2)}) collective-permute-start(bf16[2,144,256]{2,1,0:T(8,128)(2,1)S(1)} %pad_maximum_fusion.4), channel_id=1, source_target_pairs={{0,1},{1,0},{2,3},{3,2},{4,5},{5,4},{6,7},{7,6},{8,9},{9,8},{10,11... | collective-permute-start | bytes 442376 | tf_op jit(solution)/shard_map/ppermute | solution.py:830
  21.0 16.4 %collective-permute-start.12 = (bf16[4,144,256]{2,1,0:T(8,128)(2,1)S(1)}, bf16[4,144,256]{2,1,0:T(8,128)(2,1)S(1)}, u32[]{:S(2)}, u32[]{:S(2)}) collective-permute-start(bf16[4,144,256]{2,1,0:T(8,128)(2,1)S(1)} %constant_dynamic-update-slice_fusion.refs_5_), channel_id=1, source_target_pairs={{0,8},{8,0},{16,24},{24,16},{1,9},{9,1},{17,25},{25,17},{2,10},{10... | collective-permute-start | bytes 884744 | tf_op jit(solution)/shard_map/ppermute | solution.py:830
  23.5 9.5 %collective-permute-start.6 = (bf16[4,144,256]{2,1,0:T(8,128)(2,1)S(1)}, bf16[4,144,256]{2,1,0:T(8,128)(2,1)S(1)}, u32[]{:S(2)}, u32[]{:S(2)}) collective-permute-start(bf16[4,144,256]{2,1,0:T(8,128)(2,1)S(1)} %constant_dynamic-update-slice_fusion.refs_5_), channel_id=1, source_target_pairs={{0,1},{1,0},{2,3},{3,2},{4,5},{5,4},{6,7},{7,6},{8,9},{9,8},{10,11... | collective-permute-start | bytes 884744 | tf_op jit(solution)/shard_map/ppermute | solution.py:830
  25.9 12.8 %collective-permute-start.10 = (bf16[4,144,256]{2,1,0:T(8,128)(2,1)S(1)}, bf16[4,144,256]{2,1,0:T(8,128)(2,1)S(1)}, u32[]{:S(2)}, u32[]{:S(2)}) collective-permute-start(bf16[4,144,256]{2,1,0:T(8,128)(2,1)S(1)} %pad_maximum_fusion.2.refs_3_), channel_id=1, source_target_pairs={{0,8},{8,0},{16,24},{24,16},{1,9},{9,1},{17,25},{25,17},{2,10},{10... | collective-permute-start | bytes 884744 | tf_op jit(solution)/shard_map/ppermute | solution.py:830
  27.8 8.7 %collective-permute-start.2 = (bf16[4,144,256]{2,1,0:T(8,128)(2,1)S(1)}, bf16[4,144,256]{2,1,0:T(8,128)(2,1)S(1)}, u32[]{:S(2)}, u32[]{:S(2)}) collective-permute-start(bf16[4,144,256]{2,1,0:T(8,128)(2,1)S(1)} %pad_maximum_fusion.2.refs_3_), channel_id=1, source_target_pairs={{0,16},{8,24},{16,0},{24,8},{1,17},{9,25},{17,1},{25,9},{2,18},{10... | collective-permute-start | bytes 884744 | tf_op jit(solution)/shard_map/ppermute | solution.py:830
  31.5 20.7 %collective-permute-start.14 = (bf16[2,288,256]{2,1,0:T(8,128)(2,1)S(1)}, bf16[2,288,256]{2,1,0:T(8,128)(2,1)S(1)}, u32[]{:S(2)}, u32[]{:S(2)}) collective-permute-start(bf16[2,288,256]{2,1,0:T(8,128)(2,1)S(1)} %pad_maximum_fusion.3.refs_11_), channel_id=1, source_target_pairs={{0,1},{1,0},{2,3},{3,2},{4,5},{5,4},{6,7},{7,6},{8,9},{9,8},{10,11... | collective-permute-start | bytes 884744 | tf_op jit(solution)/shard_map/ppermute | solution.py:830
  33.0 5.7 %collective-permute-start.13 = (bf16[4,144,256]{2,1,0:T(8,128)(2,1)S(1)}, bf16[4,144,256]{2,1,0:T(8,128)(2,1)S(1)}, u32[]{:S(2)}, u32[]{:S(2)}) collective-permute-start(bf16[4,144,256]{2,1,0:T(8,128)(2,1)S(1)} %broadcast_add_fusion.refs_6_), channel_id=1, source_target_pairs={{0,8},{8,0},{16,24},{24,16},{1,9},{9,1},{17,25},{25,17},{2,10},{10... | collective-permute-start | bytes 884744 | tf_op jit(solution)/shard_map/ppermute | solution.py:830
  37.4 14.8 %collective-permute-start.15 = (bf16[2,288,256]{2,1,0:T(8,128)(2,1)S(1)}, bf16[2,288,256]{2,1,0:T(8,128)(2,1)S(1)}, u32[]{:S(2)}, u32[]{:S(2)}) collective-permute-start(bf16[2,288,256]{2,1,0:T(8,128)(2,1)S(1)} %get-tuple-element.141.refs_12_), channel_id=1, source_target_pairs={{0,16},{8,24},{16,0},{24,8},{1,17},{9,25},{17,1},{25,9},{2,18},{10... | collective-permute-start | bytes 884744 | tf_op jit(solution)/shard_map/ppermute | solution.py:830
  52.9 14.6 %collective-permute-start.19 = (bf16[4,288,256]{2,1,0:T(8,128)(2,1)S(1)}, bf16[4,288,256]{2,1,0:T(8,128)(2,1)S(1)}, u32[]{:S(2)}, u32[]{:S(2)}) collective-permute-start(bf16[4,288,256]{2,1,0:T(8,128)(2,1)S(1)} %constant_dynamic-update-slice_fusion.5.refs_6_.refs_2_), channel_id=1, source_target_pairs={{0,1},{1,0},{2,3},{3,2},{4,5},{5,4},{6,7},{7,6},{8,9},{9,8},{10,11... | collective-permute-start | bytes 1769480 | tf_op jit(solution)/shard_map/ppermute | solution.py:830
  53.1 14.4 %collective-permute-start.18 = (bf16[4,288,256]{2,1,0:T(8,128)(2,1)S(1)}, bf16[4,288,256]{2,1,0:T(8,128)(2,1)S(1)}, u32[]{:S(2)}, u32[]{:S(2)}) collective-permute-start(bf16[4,288,256]{2,1,0:T(8,128)(2,1)S(1)} %pad_maximum_fusion.1.refs_5_.refs_0_), channel_id=1, source_target_pairs={{0,16},{8,24},{16,0},{24,8},{1,17},{9,25},{17,1},{25,9},{2,18},{10... | collective-permute-start | bytes 1769480 | tf_op jit(solution)/shard_map/ppermute | solution.py:830
  98.2 4.6 %collective-permute-start.23 = (bf16[2,8,152,256]{3,2,1,0:T(8,128)(2,1)}, bf16[2,8,152,256]{3,2,1,0:T(8,128)(2,1)S(1)}, u32[]{:S(2)}, u32[]{:S(2)}) collective-permute-start(bf16[2,8,152,256]{3,2,1,0:T(8,128)(2,1)} %get-tuple-element.104), channel_id=1, source_target_pairs={{0,8},{8,0},{16,24},{24,16},{1,9},{9,1},{17,25},{25,17},{2,10},{10... | collective-permute-start | bytes 3735560 | tf_op jit(solution)/shard_map/ppermute | solution.py:830
  106.7 64.8 %all-to-all-start = ((bf16[32,152,256]{2,1,0:T(8,128)(2,1)}), bf16[32,152,256]{2,1,0:T(8,128)(2,1)S(1)}, u32[]{:S(2)}, u32[]{:S(2)}) async-start(bf16[32,152,256]{2,1,0:T(8,128)(2,1)} %bitcast.13.refs_25_), calls=%async_computation | async-start | bytes 4980736 | tf_op jit(solution)/shard_map/all_to_all | solution.py:1119
  145.3 11.0 %collective-permute-start.27 = (bf16[2,4,144,128]{3,2,1,0:T(8,128)(2,1)S(1)}, bf16[2,4,144,128]{3,2,1,0:T(8,128)(2,1)S(1)}, u32[]{:S(2)}, u32[]{:S(2)}) collective-permute-start(bf16[2,4,144,128]{3,2,1,0:T(8,128)(2,1)S(1)} %get-tuple-element.125), channel_id=1, source_target_pairs={{0,16},{8,24},{16,0},{24,8},{1,17},{9,25},{17,1},{25,9},{2,18},{10... | collective-permute-start | bytes 884744 | tf_op jit(solution)/shard_map/ppermute | solution.py:830
  146.5 18.3 %collective-permute-start.25 = (bf16[2,4,144,128]{3,2,1,0:T(8,128)(2,1)S(1)}, bf16[2,4,144,128]{3,2,1,0:T(8,128)(2,1)S(1)}, u32[]{:S(2)}, u32[]{:S(2)}) collective-permute-start(bf16[2,4,144,128]{3,2,1,0:T(8,128)(2,1)S(1)} %get-tuple-element.127), channel_id=1, source_target_pairs={{0,1},{1,0},{2,3},{3,2},{4,5},{5,4},{6,7},{7,6},{8,9},{9,8},{10,11... | collective-permute-start | bytes 884744 | tf_op jit(solution)/shard_map/ppermute | solution.py:830
  156.4 11.6 %collective-permute-start.28 = (bf16[4,144,128]{2,1,0:T(8,128)(2,1)S(1)}, bf16[4,144,128]{2,1,0:T(8,128)(2,1)S(1)}, u32[]{:S(2)}, u32[]{:S(2)}) collective-permute-start(bf16[4,144,128]{2,1,0:T(8,128)(2,1)S(1)} %get-tuple-element.131), channel_id=1, source_target_pairs={{0,1},{1,0},{2,3},{3,2},{4,5},{5,4},{6,7},{7,6},{8,9},{9,8},{10,11... | collective-permute-start | bytes 442376 | tf_op jit(solution)/shard_map/ppermute | solution.py:830
  164.9 4.1 %collective-permute-start.26 = (bf16[4,144,128]{2,1,0:T(8,128)(2,1)S(1)}, bf16[4,144,128]{2,1,0:T(8,128)(2,1)S(1)}, u32[]{:S(2)}, u32[]{:S(2)}) collective-permute-start(bf16[4,144,128]{2,1,0:T(8,128)(2,1)S(1)} %get-tuple-element.129), channel_id=1, source_target_pairs={{0,16},{8,24},{16,0},{24,8},{1,17},{9,25},{17,1},{25,9},{2,18},{10... | collective-permute-start | bytes 442376 | tf_op jit(solution)/shard_map/ppermute | solution.py:830
  169.0 13.4 %collective-permute-start.29 = (bf16[1,288,128]{2,1,0:T(8,128)(2,1)S(1)}, bf16[1,288,128]{2,1,0:T(8,128)(2,1)S(1)}, u32[]{:S(2)}, u32[]{:S(2)}) collective-permute-start(bf16[1,288,128]{2,1,0:T(8,128)(2,1)S(1)} %pad_maximum_fusion.7), channel_id=1, source_target_pairs={{0,2},{1,3},{2,0},{3,1},{4,6},{5,7},{6,4},{7,5},{8,10},{9,11},{10,... | collective-permute-start | bytes 221192 | tf_op jit(solution)/shard_map/ppermute | solution.py:830
  169.1 13.3 %collective-permute-start.30 = (bf16[1,288,128]{2,1,0:T(8,128)(2,1)S(1)}, bf16[1,288,128]{2,1,0:T(8,128)(2,1)S(1)}, u32[]{:S(2)}, u32[]{:S(2)}) collective-permute-start(bf16[1,288,128]{2,1,0:T(8,128)(2,1)S(1)} %pad_maximum_fusion.8), channel_id=1, source_target_pairs={{0,4},{1,5},{2,6},{3,7},{4,0},{5,1},{6,2},{7,3},{8,12},{9,13},{10,... | collective-permute-start | bytes 221192 | tf_op jit(solution)/shard_map/ppermute | solution.py:830
  175.5 5.3 %collective-permute-start.36 = (bf16[2,152,256]{2,1,0:T(8,128)(2,1)}, bf16[2,152,256]{2,1,0:T(8,128)(2,1)S(1)}, u32[]{:S(2)}, u32[]{:S(2)}) collective-permute-start(bf16[2,152,256]{2,1,0:T(8,128)(2,1)} %add_arrived.1.refs_4_), channel_id=1, source_target_pairs={{0,16},{8,24},{16,0},{24,8},{1,17},{9,25},{17,1},{25,9},{2,18},{10... | collective-permute-start | bytes 466952 | tf_op jit(solution)/shard_map/ppermute | solution.py:830
  175.9 6.5 %collective-permute-start.31 = (bf16[1,288,128]{2,1,0:T(8,128)(2,1)S(1)}, bf16[1,288,128]{2,1,0:T(8,128)(2,1)S(1)}, u32[]{:S(2)}, u32[]{:S(2)}) collective-permute-start(bf16[1,288,128]{2,1,0:T(8,128)(2,1)S(1)} %pad_maximum_fusion.9), channel_id=1, source_target_pairs={{0,6},{1,7},{2,4},{3,5},{4,2},{5,3},{6,0},{7,1},{8,14},{9,15},{10,... | collective-permute-start | bytes 221192 | tf_op jit(solution)/shard_map/ppermute | solution.py:830
  176.7 12.6 %collective-permute-start.35 = (bf16[2,152,256]{2,1,0:T(8,128)(2,1)}, bf16[2,152,256]{2,1,0:T(8,128)(2,1)S(1)}, u32[]{:S(2)}, u32[]{:S(2)}) collective-permute-start(bf16[2,152,256]{2,1,0:T(8,128)(2,1)} %add_arrived.1.refs_4_), channel_id=1, source_target_pairs={{0,8},{8,0},{16,24},{24,16},{1,9},{9,1},{17,25},{25,17},{2,10},{10... | collective-permute-start | bytes 466952 | tf_op jit(solution)/shard_map/ppermute | solution.py:830
  180.9 8.5 %collective-permute-start.37 = (bf16[2,152,256]{2,1,0:T(8,128)(2,1)S(1)}, bf16[2,152,256]{2,1,0:T(8,128)(2,1)S(1)}, u32[]{:S(2)}, u32[]{:S(2)}) collective-permute-start(bf16[2,152,256]{2,1,0:T(8,128)(2,1)S(1)} %collective-permute-done.36.refs_6_), channel_id=1, source_target_pairs={{0,8},{8,0},{16,24},{24,16},{1,9},{9,1},{17,25},{25,17},{2,10},{10... | collective-permute-start | bytes 466952 | tf_op jit(solution)/shard_map/ppermute | solution.py:830
  182.5 5.2 %collective-permute-start.34 = (bf16[288,128]{1,0:T(8,128)(2,1)S(1)}, bf16[288,128]{1,0:T(8,128)(2,1)S(1)}, u32[]{:S(2)}, u32[]{:S(2)}) collective-permute-start(bf16[288,128]{1,0:T(8,128)(2,1)S(1)} %fusion.8.refs_0_), channel_id=1, source_target_pairs={{0,24},{8,16},{16,8},{24,0},{1,25},{9,17},{17,9},{25,1},{2,26},{10... | collective-permute-start | bytes 221192 | tf_op jit(solution)/shard_map/ppermute | solution.py:830
  184.8 4.5 %collective-permute-start.33 = (bf16[288,128]{1,0:T(8,128)(2,1)S(1)}, bf16[288,128]{1,0:T(8,128)(2,1)S(1)}, u32[]{:S(2)}, u32[]{:S(2)}) collective-permute-start(bf16[288,128]{1,0:T(8,128)(2,1)S(1)} %fusion.8.refs_0_), channel_id=1, source_target_pairs={{0,16},{8,24},{16,0},{24,8},{1,17},{9,25},{17,1},{25,9},{2,18},{10... | collective-permute-start | bytes 221192 | tf_op jit(solution)/shard_map/ppermute | solution.py:830
  185.0 4.3 %collective-permute-start.32 = (bf16[288,128]{1,0:T(8,128)(2,1)S(1)}, bf16[288,128]{1,0:T(8,128)(2,1)S(1)}, u32[]{:S(2)}, u32[]{:S(2)}) collective-permute-start(bf16[288,128]{1,0:T(8,128)(2,1)S(1)} %fusion.8.refs_0_), channel_id=1, source_target_pairs={{0,8},{8,0},{16,24},{24,16},{1,9},{9,1},{17,25},{25,17},{2,10},{10... | collective-permute-start | bytes 221192 | tf_op jit(solution)/shard_map/ppermute | solution.py:830
  (34 other events, 132.4 us)

commit v8 on v7

--- a/solution.py
+++ b/solution.py
@@ -9,7 +9,7 @@
 
 HEADS = 8
 EPSILON = 1e-05
-CHUNK = 256
+CHUNK = 512
 SUB = 128
 BACK = 512
 QUAD = 256

time: 196 us -> 194 us (0.990)
  Pallas kernels: 84.8 us -> 81.8 us
    pallas_call x2, Pallas kernels: 23.1 us -> 20.1 us  [call_forward(): pl.pallas_call(functools.partial(ordered, functools.partial(attention_for...]
  transfers between devices with their start and end apart: 39 -> 39, of which waited for: 18 -> 18; matrix products, arithmetic and copies ran while one was open for 3% -> 3% of each run, Pallas kernels for 28% -> 27%
where the time goes in v8:
time: 194 us; the launch traced here: 192 us
  Pallas kernels  81.8 us (42%)
  waiting for transfers between devices  48.1 us (25%)
  starting transfers between devices  42.5 us (22%)
  other arithmetic  8.36 us (4%)
  local copies, waits for them, and re-layouts  7.4 us (4%)
  between operations  3.94 us (2%)
    ppermute x38, waiting for transfers between devices, swap(): return lax.ppermute(value, axis, [(i, i ^ bit) for i in range(n)])  48.1 us
    ppermute x38, starting transfers between devices, swap(): return lax.ppermute(value, axis, [(i, i ^ bit) for i in range(n)])  37.3 us
    pallas_call x1, Pallas kernels, call_backward(): pl.pallas_call(functools.partial(ordered, functools.partial(attention_bac...  28.8 us
    pallas_call x1, Pallas kernels, call_feed_forward(): pl.pallas_call(functools.partial(feed_forward, shards, tokens), in_specs=...  25.7 us
    pallas_call x2, Pallas kernels, call_forward(): pl.pallas_call(functools.partial(ordered, functools.partial(attention_for...  20.1 us
    unnamed x58, local copies, waits for them, and re-layouts  5.32 us
    all_to_all x1, starting transfers between devices, local(): lax.all_to_all(every, ('rep', 'shard'), 0, 0).reshape(summed.shape)  5.12 us
    convert_element_type x6, other arithmetic, add_low(): return sum((part.astype(F32) for part in parts)).astype(BF16)  4.04 us
  transfers between devices with their start and end apart: 39, of which 18 were waited for; matrix products, arithmetic and copies ran while one was open for 3% of the time, Pallas kernels for 27%

profile of v8, /device:TPU:13, one launch (start us, length us, event | category | flops | bytes accessed | tf_op | source)
XLA Modules:
  0.0 192.1 jit_solution(12903752633293384288)
XLA Ops:
  0.7 2.0 %pack.1 = (bf16[144,256]{1,0:T(8,128)(2,1)}, bf16[288,256]{1,0:T(8,128)(2,1)}) custom-call(bf16[64,512]{1,0:T(8,128)(2,1)} %refs_0_.4, bf16[64,512]{1,0:T(8,128)(2,1)} %refs_1_.1, bf16[64,512]{1,0:T(8,128)(2,1)} %refs_2_.4, bf16[64,512]{1,0:T(8,128)(2,1)} %refs_3_.1, bf16[64,512]{1,0:T(8,128)(2,1)} %refs_4_.1, bf16[64,2048]{1,0:T(8,128)(2,1)} %refs_5_.1, ...), custom_call_target="tpu_custom_call" | custom-call | flops 1000 | bytes 1000 | tf_op jit(solution)/shard_map/pack/pallas_call | solution.py:679
  2.7 2.4 %collective-permute-start.3 = (bf16[1,144,256]{2,1,0:T(8,128)(2,1)}, bf16[1,144,256]{2,1,0:T(8,128)(2,1)S(1)}, u32[]{:S(2)}, u32[]{:S(2)}) collective-permute-start(bf16[1,144,256]{2,1,0:T(8,128)(2,1)} %bitcast.100), channel_id=1, source_target_pairs={{0,4},{1,5},{2,6},{3,7},{4,0},{5,1},{6,2},{7,3},{8,12},{9,13},{10,... | collective-permute-start | bytes 221192 | tf_op jit(solution)/shard_map/ppermute | solution.py:830
  6.3 3.6 %collective-permute-done.3 = bf16[1,144,256]{2,1,0:T(8,128)(2,1)S(1)} collective-permute-done((bf16[1,144,256]{2,1,0:T(8,128)(2,1)}, bf16[1,144,256]{2,1,0:T(8,128)(2,1)S(1)}, u32[]{:S(2)}, u32[]{:S(2)}) %collective-permute-start.3) | collective-permute-done | bytes 73760 | tf_op jit(solution)/shard_map/ppermute | solution.py:830
  12.1 3.4 %collective-permute-start.8 = (bf16[1,288,256]{2,1,0:T(8,128)(2,1)S(1)}, bf16[1,288,256]{2,1,0:T(8,128)(2,1)S(1)}, u32[]{:S(2)}, u32[]{:S(2)}) collective-permute-start(bf16[1,288,256]{2,1,0:T(8,128)(2,1)S(1)} %add_bitcast_fusion), channel_id=1, source_target_pairs={{0,4},{1,5},{2,6},{3,7},{4,0},{5,1},{6,2},{7,3},{8,12},{9,13},{10,... | collective-permute-start | bytes 442376 | tf_op jit(solution)/shard_map/ppermute | solution.py:830
  19.1 1.9 collective-permute-done.5
  21.0 2.5 %collective-permute-start.12 = (bf16[4,144,256]{2,1,0:T(8,128)(2,1)S(1)}, bf16[4,144,256]{2,1,0:T(8,128)(2,1)S(1)}, u32[]{:S(2)}, u32[]{:S(2)}) collective-permute-start(bf16[4,144,256]{2,1,0:T(8,128)(2,1)S(1)} %constant_dynamic-update-slice_fusion.refs_5_), channel_id=1, source_target_pairs={{0,8},{8,0},{16,24},{24,16},{1,9},{9,1},{17,25},{25,17},{2,10},{10... | collective-permute-start | bytes 884744 | tf_op jit(solution)/shard_map/ppermute | solution.py:830
  23.8 2.1 %collective-permute-done.7 = bf16[1,288,256]{2,1,0:T(8,128)(2,1)S(1)} collective-permute-done((bf16[1,288,256]{2,1,0:T(8,128)(2,1)S(1)}, bf16[1,288,256]{2,1,0:T(8,128)(2,1)S(1)}, u32[]{:S(2)}, u32[]{:S(2)}) %collective-permute-start.7) | collective-permute-done | bytes 147488 | tf_op jit(solution)/shard_map/ppermute | solution.py:830
  25.9 1.9 collective-permute-start.10
  33.6 2.9 %collective-permute-done.2.refs_4_ = bf16[4,144,256]{2,1,0:T(8,128)(2,1)S(1)} collective-permute-done((bf16[4,144,256]{2,1,0:T(8,128)(2,1)S(1)}, bf16[4,144,256]{2,1,0:T(8,128)(2,1)S(1)}, u32[]{:S(2)}, u32[]{:S(2)}) %collective-permute-start.2) | collective-permute-done | bytes 294944 | tf_op jit(solution)/shard_map/ppermute | solution.py:830
  39.6 11.0 %attention_forward_0.1 = (bf16[1024,256]{1,0:T(8,128)(2,1)}, bf16[1024,256]{1,0:T(8,128)(2,1)}, bf16[1024,256]{1,0:T(8,128)(2,1)}, bf16[1024,256]{1,0:T(8,128)(2...) custom-call(s32[1,1024]{1,0:T(1,128)} %refs_2_.7, ...), custom_call_target="tpu_custom_call" | custom-call | flops 1000 | bytes 1000 | tf_op jit(solution)/shard_map/attention_forward_0/pallas_call | solution.py:723
  54.4 9.1 %attention_forward_1.1 = (bf16[1024,256]{1,0:T(8,128)(2,1)}, bf16[1024,256]{1,0:T(8,128)(2,1)}, bf16[1024,256]{1,0:T(8,128)(2,1)}, bf16[1024,256]{1,0:T(8,128)(2...) custom-call(s32[1,1024]{1,0:T(1,128)} %refs_2_.7, ...), custom_call_target="tpu_custom_call" | custom-call | flops 1000 | bytes 1000 | tf_op jit(solution)/shard_map/attention_forward_1/pallas_call | solution.py:723
  63.5 2.5 %collective-permute-done.19.refs_3_ = bf16[4,288,256]{2,1,0:T(8,128)(2,1)S(1)} collective-permute-done((bf16[4,288,256]{2,1,0:T(8,128)(2,1)S(1)}, bf16[4,288,256]{2,1,0:T(8,128)(2,1)S(1)}, u32[]{:S(2)}, u32[]{:S(2)}) %collective-permute-start.19) | collective-permute-done | bytes 589856 | tf_op jit(solution)/shard_map/ppermute | solution.py:830
  67.3 1.6 collective-permute-done.20.refs_5_
  70.6 25.7 %feed_forward.1 = (bf16[1024,512]{1,0:T(8,128)(2,1)}, f32[1024,512]{1,0:T(8,128)}, bf16[1024,512]{1,0:T(8,128)(2,1)}, bf16[4,8,152,256]{3,2,1,0:T(8,128)(2,1)}, ...) custom-call(bf16[1024,512]{1,0:T(8,128)(2,1)} %bitcast.96, ...), custom_call_target="tpu_custom_call" | custom-call | flops 1000 | bytes 1000 | tf_op jit(solution)/shard_map/feed_forward/pallas_call | solution.py:745
  96.9 2.6 %collective-permute-done.22 = bf16[2,8,152,256]{3,2,1,0:T(8,128)(2,1)S(1)} collective-permute-done((bf16[2,8,152,256]{3,2,1,0:T(8,128)(2,1)}, bf16[2,8,152,256]{3,2,1,0:T(8,128)(2,1)S(1)}, u32[]{:S(2)}, u32[]{:S(2)}) %collective-permute-start.22) | collective-permute-done | bytes 1245216 | tf_op jit(solution)/shard_map/ppermute | solution.py:830
  99.5 1.8 collective-permute-done.23
  101.3 2.2 %add_convert_fusion.1 = (bf16[2,8,152,256]{3,2,1,0:T(8,128)(2,1)S(1)}, bf16[2,8,152,256]{3,2,1,0:T(8,128)(2,1)S(1)}) fusion(bf16[2,8,152,256]{3,2,1,0:T(8,128)(2,1)S(1)} %collective-permute-done.22, bf16[4,8,152,256]{3,2,1,0:T(8,128)(2,1)} %get-tuple-element.102, bf16[2,8,152,256]{3,2,1,0:T(8,128)(2,1)S(1)} %collective-permute-done.23), kind=kLoop, calls=%fused_computation.2 | loop fusion | flops 4980736 | bytes 7471104 | tf_op jit(solution)/shard_map/convert_element_type | solution.py:974
  103.5 1.6 pad_maximum_fusion
  105.2 5.1 %all-to-all-start = ((bf16[32,152,256]{2,1,0:T(8,128)(2,1)}), bf16[32,152,256]{2,1,0:T(8,128)(2,1)S(1)}, u32[]{:S(2)}, u32[]{:S(2)}) async-start(bf16[32,152,256]{2,1,0:T(8,128)(2,1)} %bitcast.13.refs_25_), calls=%async_computation | async-start | bytes 4980736 | tf_op jit(solution)/shard_map/all_to_all | solution.py:1119
  110.3 28.8 %attention_backward.1 = (f32[1024,512]{1,0:T(8,128)}, bf16[2,2,2,4,144,128]{5,4,3,2,1,0:T(8,128)(2,1)}, bf16[2,2,2,4,144,128]{5,4,3,2,1,0:T(8,128)(2,1)}) custom-call(s32[1,1024]{1,0:T(1,128)} %refs_2_.7, bf16[1024,512]{1,0:T(8,128)(2,1)} %bitcast.97, s32[1,1024]{1,0:T(1,128)} %refs_2_.7, bf16[1024,256]{1,0:T(8,128)(2,1)} %get-tuple-element.82.refs_3_, ...), custom_call_target="tpu_custom_call" | custom-call | flops 1000 | bytes 1000 | tf_op jit(solution)/shard_map/attention_backward/pallas_call | solution.py:816
  139.5 2.7 %collective-permute-done.24 = bf16[2,2,2,4,144,128]{5,4,3,2,1,0:T(8,128)(2,1)S(1)} collective-permute-done((bf16[2,2,2,4,144,128]{5,4,3,2,1,0:T(8,128)(2,1)}, bf16[2,2,2,4,144,128]{5,4,3,2,1,0:T(8,128)(2,1)S(1)}, u32[]{:S(2)}, u32[]{:S(2)}) %collective-permute-start.24) | collective-permute-done | bytes 1179680 | tf_op jit(solution)/shard_map/ppermute | solution.py:830
  145.3 9.5 %collective-permute-done.27 = bf16[2,4,144,128]{3,2,1,0:T(8,128)(2,1)S(1)} collective-permute-done((bf16[2,4,144,128]{3,2,1,0:T(8,128)(2,1)S(1)}, bf16[2,4,144,128]{3,2,1,0:T(8,128)(2,1)S(1)}, u32[]{:S(2)}, u32[]{:S(2)}) %collective-permute-start.27) | collective-permute-done | bytes 294944 | tf_op jit(solution)/shard_map/ppermute | solution.py:830
  154.9 1.7 collective-permute-start.28
  156.5 6.8 %collective-permute-done.25 = bf16[2,4,144,128]{3,2,1,0:T(8,128)(2,1)S(1)} collective-permute-done((bf16[2,4,144,128]{3,2,1,0:T(8,128)(2,1)S(1)}, bf16[2,4,144,128]{3,2,1,0:T(8,128)(2,1)S(1)}, u32[]{:S(2)}, u32[]{:S(2)}) %collective-permute-start.25) | collective-permute-done | bytes 294944 | tf_op jit(solution)/shard_map/ppermute | solution.py:830
  163.5 3.0 %collective-permute-done.28 = bf16[4,144,128]{2,1,0:T(8,128)(2,1)S(1)} collective-permute-done((bf16[4,144,128]{2,1,0:T(8,128)(2,1)S(1)}, bf16[4,144,128]{2,1,0:T(8,128)(2,1)S(1)}, u32[]{:S(2)}, u32[]{:S(2)}) %collective-permute-start.28) | collective-permute-done | bytes 147488 | tf_op jit(solution)/shard_map/ppermute | solution.py:830
  167.6 1.6 collective-permute-start.30
  171.3 2.7 %add_arrived.1.refs_4_ = bf16[2,152,256]{2,1,0:T(8,128)(2,1)} custom-call(bf16[4,8,152,256]{3,2,1,0:T(8,128)(2,1)} %bitcast.98, bf16[1,288,128]{2,1,0:T(8,128)(2,1)} %pad_maximum_fusion.6.refs_1_), custom_call_target="tpu_custom_call" | custom-call | flops 1000 | bytes 1000 | tf_op jit(solution)/shard_map/add_arrived/pallas_call | solution.py:866
  175.2 4.2 %collective-permute-start.35 = (bf16[2,152,256]{2,1,0:T(8,128)(2,1)}, bf16[2,152,256]{2,1,0:T(8,128)(2,1)S(1)}, u32[]{:S(2)}, u32[]{:S(2)}) collective-permute-start(bf16[2,152,256]{2,1,0:T(8,128)(2,1)} %add_arrived.1.refs_4_), channel_id=1, source_target_pairs={{0,8},{8,0},{16,24},{24,16},{1,9},{9,1},{17,25},{25,17},{2,10},{10... | collective-permute-start | bytes 466952 | tf_op jit(solution)/shard_map/ppermute | solution.py:830
  181.0 2.3 %collective-permute-start.34 = (bf16[288,128]{1,0:T(8,128)(2,1)S(1)}, bf16[288,128]{1,0:T(8,128)(2,1)S(1)}, u32[]{:S(2)}, u32[]{:S(2)}) collective-permute-start(bf16[288,128]{1,0:T(8,128)(2,1)S(1)} %fusion.8.refs_0_), channel_id=1, source_target_pairs={{0,24},{8,16},{16,8},{24,0},{1,25},{9,17},{17,9},{25,1},{2,26},{10... | collective-permute-start | bytes 221192 | tf_op jit(solution)/shard_map/ppermute | solution.py:830
  183.8 2.6 %collective-permute-done.34.refs_3_ = bf16[288,128]{1,0:T(8,128)(2,1)S(1)} collective-permute-done((bf16[288,128]{1,0:T(8,128)(2,1)S(1)}, bf16[288,128]{1,0:T(8,128)(2,1)S(1)}, u32[]{:S(2)}, u32[]{:S(2)}) %collective-permute-start.34) | collective-permute-done | bytes 73760 | tf_op jit(solution)/shard_map/ppermute | solution.py:830
  186.4 1.6 collective-permute-done.33.refs_2_
  189.4 2.5 %assemble.1 = (f32[64,512]{1,0:T(8,128)}, f32[64,512]{1,0:T(8,128)}, f32[64,512]{1,0:T(8,128)}, f32[64,512]{1,0:T(8,128)}, f32[1,64]{1,0:T(1,128)}, /*index=5*/f...) custom-call(f32[8,128]{1,0:T(8,128)} %get-tuple-element.78.count_ref, ...), custom_call_target="tpu_custom_call" | custom-call | flops 1000 | bytes 1000 | tf_op jit(solution)/shard_map/assemble/pallas_call | solution.py:962
  (136 shorter events, 32.2 us)
Async XLA Ops:
  2.7 7.2 %collective-permute-start.3 = (bf16[1,144,256]{2,1,0:T(8,128)(2,1)}, bf16[1,144,256]{2,1,0:T(8,128)(2,1)S(1)}, u32[]{:S(2)}, u32[]{:S(2)}) collective-permute-start(bf16[1,144,256]{2,1,0:T(8,128)(2,1)} %bitcast.100), channel_id=1, source_target_pairs={{0,4},{1,5},{2,6},{3,7},{4,0},{5,1},{6,2},{7,3},{8,12},{9,13},{10,... | collective-permute-start | bytes 221192 | tf_op jit(solution)/shard_map/ppermute | solution.py:830
  5.1 11.5 %collective-permute-start.4 = (bf16[1,144,256]{2,1,0:T(8,128)(2,1)}, bf16[1,144,256]{2,1,0:T(8,128)(2,1)S(1)}, u32[]{:S(2)}, u32[]{:S(2)}) collective-permute-start(bf16[1,144,256]{2,1,0:T(8,128)(2,1)} %bitcast.101), channel_id=1, source_target_pairs={{0,6},{1,7},{2,4},{3,5},{4,2},{5,3},{6,0},{7,1},{8,14},{9,15},{10,... | collective-permute-start | bytes 221192 | tf_op jit(solution)/shard_map/ppermute | solution.py:830
  5.1 12.8 %collective-permute-start = (bf16[1,144,256]{2,1,0:T(8,128)(2,1)}, bf16[1,144,256]{2,1,0:T(8,128)(2,1)S(1)}, u32[]{:S(2)}, u32[]{:S(2)}) collective-permute-start(bf16[1,144,256]{2,1,0:T(8,128)(2,1)} %bitcast.102), channel_id=1, source_target_pairs={{0,2},{1,3},{2,0},{3,1},{4,6},{5,7},{6,4},{7,5},{8,10},{9,11},{10,... | collective-permute-start | bytes 221192 | tf_op jit(solution)/shard_map/ppermute | solution.py:830
  12.0 19.4 %collective-permute-start.9 = (bf16[1,288,256]{2,1,0:T(8,128)(2,1)S(1)}, bf16[1,288,256]{2,1,0:T(8,128)(2,1)S(1)}, u32[]{:S(2)}, u32[]{:S(2)}) collective-permute-start(bf16[1,288,256]{2,1,0:T(8,128)(2,1)S(1)} %add_bitcast_fusion), channel_id=1, source_target_pairs={{0,6},{1,7},{2,4},{3,5},{4,2},{5,3},{6,0},{7,1},{8,14},{9,15},{10,... | collective-permute-start | bytes 442376 | tf_op jit(solution)/shard_map/ppermute | solution.py:830
  12.1 15.7 %collective-permute-start.8 = (bf16[1,288,256]{2,1,0:T(8,128)(2,1)S(1)}, bf16[1,288,256]{2,1,0:T(8,128)(2,1)S(1)}, u32[]{:S(2)}, u32[]{:S(2)}) collective-permute-start(bf16[1,288,256]{2,1,0:T(8,128)(2,1)S(1)} %add_bitcast_fusion), channel_id=1, source_target_pairs={{0,4},{1,5},{2,6},{3,7},{4,0},{5,1},{6,2},{7,3},{8,12},{9,13},{10,... | collective-permute-start | bytes 442376 | tf_op jit(solution)/shard_map/ppermute | solution.py:830
  15.5 10.4 %collective-permute-start.7 = (bf16[1,288,256]{2,1,0:T(8,128)(2,1)S(1)}, bf16[1,288,256]{2,1,0:T(8,128)(2,1)S(1)}, u32[]{:S(2)}, u32[]{:S(2)}) collective-permute-start(bf16[1,288,256]{2,1,0:T(8,128)(2,1)S(1)} %add_bitcast_fusion), channel_id=1, source_target_pairs={{0,2},{1,3},{2,0},{3,1},{4,6},{5,7},{6,4},{7,5},{8,10},{9,11},{10,... | collective-permute-start | bytes 442376 | tf_op jit(solution)/shard_map/ppermute | solution.py:830
  16.6 4.4 %collective-permute-start.5 = (bf16[2,144,256]{2,1,0:T(8,128)(2,1)S(1)}, bf16[2,144,256]{2,1,0:T(8,128)(2,1)S(1)}, u32[]{:S(2)}, u32[]{:S(2)}) collective-permute-start(bf16[2,144,256]{2,1,0:T(8,128)(2,1)S(1)} %pad_maximum_fusion.5), channel_id=1, source_target_pairs={{0,16},{8,24},{16,0},{24,8},{1,17},{9,25},{17,1},{25,9},{2,18},{10... | collective-permute-start | bytes 442376 | tf_op jit(solution)/shard_map/ppermute | solution.py:830
  18.8 4.7 %collective-permute-start.1 = (bf16[2,144,256]{2,1,0:T(8,128)(2,1)S(1)}, bf16[2,144,256]{2,1,0:T(8,128)(2,1)S(1)}, u32[]{:S(2)}, u32[]{:S(2)}) collective-permute-start(bf16[2,144,256]{2,1,0:T(8,128)(2,1)S(1)} %pad_maximum_fusion.4), channel_id=1, source_target_pairs={{0,1},{1,0},{2,3},{3,2},{4,5},{5,4},{6,7},{7,6},{8,9},{9,8},{10,11... | collective-permute-start | bytes 442376 | tf_op jit(solution)/shard_map/ppermute | solution.py:830
  21.0 16.4 %collective-permute-start.12 = (bf16[4,144,256]{2,1,0:T(8,128)(2,1)S(1)}, bf16[4,144,256]{2,1,0:T(8,128)(2,1)S(1)}, u32[]{:S(2)}, u32[]{:S(2)}) collective-permute-start(bf16[4,144,256]{2,1,0:T(8,128)(2,1)S(1)} %constant_dynamic-update-slice_fusion.refs_5_), channel_id=1, source_target_pairs={{0,8},{8,0},{16,24},{24,16},{1,9},{9,1},{17,25},{25,17},{2,10},{10... | collective-permute-start | bytes 884744 | tf_op jit(solution)/shard_map/ppermute | solution.py:830
  23.5 9.5 %collective-permute-start.6 = (bf16[4,144,256]{2,1,0:T(8,128)(2,1)S(1)}, bf16[4,144,256]{2,1,0:T(8,128)(2,1)S(1)}, u32[]{:S(2)}, u32[]{:S(2)}) collective-permute-start(bf16[4,144,256]{2,1,0:T(8,128)(2,1)S(1)} %constant_dynamic-update-slice_fusion.refs_5_), channel_id=1, source_target_pairs={{0,1},{1,0},{2,3},{3,2},{4,5},{5,4},{6,7},{7,6},{8,9},{9,8},{10,11... | collective-permute-start | bytes 884744 | tf_op jit(solution)/shard_map/ppermute | solution.py:830
  25.9 12.8 %collective-permute-start.10 = (bf16[4,144,256]{2,1,0:T(8,128)(2,1)S(1)}, bf16[4,144,256]{2,1,0:T(8,128)(2,1)S(1)}, u32[]{:S(2)}, u32[]{:S(2)}) collective-permute-start(bf16[4,144,256]{2,1,0:T(8,128)(2,1)S(1)} %pad_maximum_fusion.2.refs_3_), channel_id=1, source_target_pairs={{0,8},{8,0},{16,24},{24,16},{1,9},{9,1},{17,25},{25,17},{2,10},{10... | collective-permute-start | bytes 884744 | tf_op jit(solution)/shard_map/ppermute | solution.py:830
  27.8 8.7 %collective-permute-start.2 = (bf16[4,144,256]{2,1,0:T(8,128)(2,1)S(1)}, bf16[4,144,256]{2,1,0:T(8,128)(2,1)S(1)}, u32[]{:S(2)}, u32[]{:S(2)}) collective-permute-start(bf16[4,144,256]{2,1,0:T(8,128)(2,1)S(1)} %pad_maximum_fusion.2.refs_3_), channel_id=1, source_target_pairs={{0,16},{8,24},{16,0},{24,8},{1,17},{9,25},{17,1},{25,9},{2,18},{10... | collective-permute-start | bytes 884744 | tf_op jit(solution)/shard_map/ppermute | solution.py:830
  31.5 19.1 %collective-permute-start.14 = (bf16[2,288,256]{2,1,0:T(8,128)(2,1)S(1)}, bf16[2,288,256]{2,1,0:T(8,128)(2,1)S(1)}, u32[]{:S(2)}, u32[]{:S(2)}) collective-permute-start(bf16[2,288,256]{2,1,0:T(8,128)(2,1)S(1)} %pad_maximum_fusion.3.refs_11_), channel_id=1, source_target_pairs={{0,1},{1,0},{2,3},{3,2},{4,5},{5,4},{6,7},{7,6},{8,9},{9,8},{10,11... | collective-permute-start | bytes 884744 | tf_op jit(solution)/shard_map/ppermute | solution.py:830
  33.0 5.7 %collective-permute-start.13 = (bf16[4,144,256]{2,1,0:T(8,128)(2,1)S(1)}, bf16[4,144,256]{2,1,0:T(8,128)(2,1)S(1)}, u32[]{:S(2)}, u32[]{:S(2)}) collective-permute-start(bf16[4,144,256]{2,1,0:T(8,128)(2,1)S(1)} %broadcast_add_fusion.refs_6_), channel_id=1, source_target_pairs={{0,8},{8,0},{16,24},{24,16},{1,9},{9,1},{17,25},{25,17},{2,10},{10... | collective-permute-start | bytes 884744 | tf_op jit(solution)/shard_map/ppermute | solution.py:830
  37.4 13.2 %collective-permute-start.15 = (bf16[2,288,256]{2,1,0:T(8,128)(2,1)S(1)}, bf16[2,288,256]{2,1,0:T(8,128)(2,1)S(1)}, u32[]{:S(2)}, u32[]{:S(2)}) collective-permute-start(bf16[2,288,256]{2,1,0:T(8,128)(2,1)S(1)} %get-tuple-element.141.refs_12_), channel_id=1, source_target_pairs={{0,16},{8,24},{16,0},{24,8},{1,17},{9,25},{17,1},{25,9},{2,18},{10... | collective-permute-start | bytes 884744 | tf_op jit(solution)/shard_map/ppermute | solution.py:830
  51.4 14.6 %collective-permute-start.19 = (bf16[4,288,256]{2,1,0:T(8,128)(2,1)S(1)}, bf16[4,288,256]{2,1,0:T(8,128)(2,1)S(1)}, u32[]{:S(2)}, u32[]{:S(2)}) collective-permute-start(bf16[4,288,256]{2,1,0:T(8,128)(2,1)S(1)} %constant_dynamic-update-slice_fusion.5.refs_6_.refs_2_), channel_id=1, source_target_pairs={{0,1},{1,0},{2,3},{3,2},{4,5},{5,4},{6,7},{7,6},{8,9},{9,8},{10,11... | collective-permute-start | bytes 1769480 | tf_op jit(solution)/shard_map/ppermute | solution.py:830
  51.6 14.4 %collective-permute-start.18 = (bf16[4,288,256]{2,1,0:T(8,128)(2,1)S(1)}, bf16[4,288,256]{2,1,0:T(8,128)(2,1)S(1)}, u32[]{:S(2)}, u32[]{:S(2)}) collective-permute-start(bf16[4,288,256]{2,1,0:T(8,128)(2,1)S(1)} %pad_maximum_fusion.1.refs_5_.refs_0_), channel_id=1, source_target_pairs={{0,16},{8,24},{16,0},{24,8},{1,17},{9,25},{17,1},{25,9},{2,18},{10... | collective-permute-start | bytes 1769480 | tf_op jit(solution)/shard_map/ppermute | solution.py:830
  96.7 4.6 %collective-permute-start.23 = (bf16[2,8,152,256]{3,2,1,0:T(8,128)(2,1)}, bf16[2,8,152,256]{3,2,1,0:T(8,128)(2,1)S(1)}, u32[]{:S(2)}, u32[]{:S(2)}) collective-permute-start(bf16[2,8,152,256]{3,2,1,0:T(8,128)(2,1)} %get-tuple-element.104), channel_id=1, source_target_pairs={{0,8},{8,0},{16,24},{24,16},{1,9},{9,1},{17,25},{25,17},{2,10},{10... | collective-permute-start | bytes 3735560 | tf_op jit(solution)/shard_map/ppermute | solution.py:830
  105.2 64.8 %all-to-all-start = ((bf16[32,152,256]{2,1,0:T(8,128)(2,1)}), bf16[32,152,256]{2,1,0:T(8,128)(2,1)S(1)}, u32[]{:S(2)}, u32[]{:S(2)}) async-start(bf16[32,152,256]{2,1,0:T(8,128)(2,1)} %bitcast.13.refs_25_), calls=%async_computation | async-start | bytes 4980736 | tf_op jit(solution)/shard_map/all_to_all | solution.py:1119
  143.8 11.0 %collective-permute-start.27 = (bf16[2,4,144,128]{3,2,1,0:T(8,128)(2,1)S(1)}, bf16[2,4,144,128]{3,2,1,0:T(8,128)(2,1)S(1)}, u32[]{:S(2)}, u32[]{:S(2)}) collective-permute-start(bf16[2,4,144,128]{3,2,1,0:T(8,128)(2,1)S(1)} %get-tuple-element.125), channel_id=1, source_target_pairs={{0,16},{8,24},{16,0},{24,8},{1,17},{9,25},{17,1},{25,9},{2,18},{10... | collective-permute-start | bytes 884744 | tf_op jit(solution)/shard_map/ppermute | solution.py:830
  145.0 18.3 %collective-permute-start.25 = (bf16[2,4,144,128]{3,2,1,0:T(8,128)(2,1)S(1)}, bf16[2,4,144,128]{3,2,1,0:T(8,128)(2,1)S(1)}, u32[]{:S(2)}, u32[]{:S(2)}) collective-permute-start(bf16[2,4,144,128]{3,2,1,0:T(8,128)(2,1)S(1)} %get-tuple-element.127), channel_id=1, source_target_pairs={{0,1},{1,0},{2,3},{3,2},{4,5},{5,4},{6,7},{7,6},{8,9},{9,8},{10,11... | collective-permute-start | bytes 884744 | tf_op jit(solution)/shard_map/ppermute | solution.py:830
  154.9 11.6 %collective-permute-start.28 = (bf16[4,144,128]{2,1,0:T(8,128)(2,1)S(1)}, bf16[4,144,128]{2,1,0:T(8,128)(2,1)S(1)}, u32[]{:S(2)}, u32[]{:S(2)}) collective-permute-start(bf16[4,144,128]{2,1,0:T(8,128)(2,1)S(1)} %get-tuple-element.131), channel_id=1, source_target_pairs={{0,1},{1,0},{2,3},{3,2},{4,5},{5,4},{6,7},{7,6},{8,9},{9,8},{10,11... | collective-permute-start | bytes 442376 | tf_op jit(solution)/shard_map/ppermute | solution.py:830
  163.4 4.1 %collective-permute-start.26 = (bf16[4,144,128]{2,1,0:T(8,128)(2,1)S(1)}, bf16[4,144,128]{2,1,0:T(8,128)(2,1)S(1)}, u32[]{:S(2)}, u32[]{:S(2)}) collective-permute-start(bf16[4,144,128]{2,1,0:T(8,128)(2,1)S(1)} %get-tuple-element.129), channel_id=1, source_target_pairs={{0,16},{8,24},{16,0},{24,8},{1,17},{9,25},{17,1},{25,9},{2,18},{10... | collective-permute-start | bytes 442376 | tf_op jit(solution)/shard_map/ppermute | solution.py:830
  167.5 13.4 %collective-permute-start.29 = (bf16[1,288,128]{2,1,0:T(8,128)(2,1)S(1)}, bf16[1,288,128]{2,1,0:T(8,128)(2,1)S(1)}, u32[]{:S(2)}, u32[]{:S(2)}) collective-permute-start(bf16[1,288,128]{2,1,0:T(8,128)(2,1)S(1)} %pad_maximum_fusion.7), channel_id=1, source_target_pairs={{0,2},{1,3},{2,0},{3,1},{4,6},{5,7},{6,4},{7,5},{8,10},{9,11},{10,... | collective-permute-start | bytes 221192 | tf_op jit(solution)/shard_map/ppermute | solution.py:830
  167.6 13.3 %collective-permute-start.30 = (bf16[1,288,128]{2,1,0:T(8,128)(2,1)S(1)}, bf16[1,288,128]{2,1,0:T(8,128)(2,1)S(1)}, u32[]{:S(2)}, u32[]{:S(2)}) collective-permute-start(bf16[1,288,128]{2,1,0:T(8,128)(2,1)S(1)} %pad_maximum_fusion.8), channel_id=1, source_target_pairs={{0,4},{1,5},{2,6},{3,7},{4,0},{5,1},{6,2},{7,3},{8,12},{9,13},{10,... | collective-permute-start | bytes 221192 | tf_op jit(solution)/shard_map/ppermute | solution.py:830
  174.0 5.4 %collective-permute-start.36 = (bf16[2,152,256]{2,1,0:T(8,128)(2,1)}, bf16[2,152,256]{2,1,0:T(8,128)(2,1)S(1)}, u32[]{:S(2)}, u32[]{:S(2)}) collective-permute-start(bf16[2,152,256]{2,1,0:T(8,128)(2,1)} %add_arrived.1.refs_4_), channel_id=1, source_target_pairs={{0,16},{8,24},{16,0},{24,8},{1,17},{9,25},{17,1},{25,9},{2,18},{10... | collective-permute-start | bytes 466952 | tf_op jit(solution)/shard_map/ppermute | solution.py:830
  174.4 6.5 %collective-permute-start.31 = (bf16[1,288,128]{2,1,0:T(8,128)(2,1)S(1)}, bf16[1,288,128]{2,1,0:T(8,128)(2,1)S(1)}, u32[]{:S(2)}, u32[]{:S(2)}) collective-permute-start(bf16[1,288,128]{2,1,0:T(8,128)(2,1)S(1)} %pad_maximum_fusion.9), channel_id=1, source_target_pairs={{0,6},{1,7},{2,4},{3,5},{4,2},{5,3},{6,0},{7,1},{8,14},{9,15},{10,... | collective-permute-start | bytes 221192 | tf_op jit(solution)/shard_map/ppermute | solution.py:830
  175.2 12.8 %collective-permute-start.35 = (bf16[2,152,256]{2,1,0:T(8,128)(2,1)}, bf16[2,152,256]{2,1,0:T(8,128)(2,1)S(1)}, u32[]{:S(2)}, u32[]{:S(2)}) collective-permute-start(bf16[2,152,256]{2,1,0:T(8,128)(2,1)} %add_arrived.1.refs_4_), channel_id=1, source_target_pairs={{0,8},{8,0},{16,24},{24,16},{1,9},{9,1},{17,25},{25,17},{2,10},{10... | collective-permute-start | bytes 466952 | tf_op jit(solution)/shard_map/ppermute | solution.py:830
  179.4 8.6 %collective-permute-start.37 = (bf16[2,152,256]{2,1,0:T(8,128)(2,1)S(1)}, bf16[2,152,256]{2,1,0:T(8,128)(2,1)S(1)}, u32[]{:S(2)}, u32[]{:S(2)}) collective-permute-start(bf16[2,152,256]{2,1,0:T(8,128)(2,1)S(1)} %collective-permute-done.36.refs_6_), channel_id=1, source_target_pairs={{0,8},{8,0},{16,24},{24,16},{1,9},{9,1},{17,25},{25,17},{2,10},{10... | collective-permute-start | bytes 466952 | tf_op jit(solution)/shard_map/ppermute | solution.py:830
  181.0 5.4 %collective-permute-start.34 = (bf16[288,128]{1,0:T(8,128)(2,1)S(1)}, bf16[288,128]{1,0:T(8,128)(2,1)S(1)}, u32[]{:S(2)}, u32[]{:S(2)}) collective-permute-start(bf16[288,128]{1,0:T(8,128)(2,1)S(1)} %fusion.8.refs_0_), channel_id=1, source_target_pairs={{0,24},{8,16},{16,8},{24,0},{1,25},{9,17},{17,9},{25,1},{2,26},{10... | collective-permute-start | bytes 221192 | tf_op jit(solution)/shard_map/ppermute | solution.py:830
  183.3 4.7 %collective-permute-start.33 = (bf16[288,128]{1,0:T(8,128)(2,1)S(1)}, bf16[288,128]{1,0:T(8,128)(2,1)S(1)}, u32[]{:S(2)}, u32[]{:S(2)}) collective-permute-start(bf16[288,128]{1,0:T(8,128)(2,1)S(1)} %fusion.8.refs_0_), channel_id=1, source_target_pairs={{0,16},{8,24},{16,0},{24,8},{1,17},{9,25},{17,1},{25,9},{2,18},{10... | collective-permute-start | bytes 221192 | tf_op jit(solution)/shard_map/ppermute | solution.py:830
  183.6 4.4 %collective-permute-start.32 = (bf16[288,128]{1,0:T(8,128)(2,1)S(1)}, bf16[288,128]{1,0:T(8,128)(2,1)S(1)}, u32[]{:S(2)}, u32[]{:S(2)}) collective-permute-start(bf16[288,128]{1,0:T(8,128)(2,1)S(1)} %fusion.8.refs_0_), channel_id=1, source_target_pairs={{0,8},{8,0},{16,24},{24,16},{1,9},{9,1},{17,25},{25,17},{2,10},{10... | collective-permute-start | bytes 221192 | tf_op jit(solution)/shard_map/ppermute | solution.py:830
  (34 other events, 132.6 us)
